TPU v7x, 32 devices: a whole 2x2x4 slice. The times are simulated.
32 devices in a mesh: dp: 8 (over z, y), mp: 4 (over x, core).
Axes of the slice: x: 2, y: 2, z: 4, core: 2. Of those that a mesh axis runs over, the one named last changes fastest.
Arguments:
- hidden_in: bfloat16 [16384, 1024], P(('dp', 'mp')), may hold values from -6 to 6
- out_grad: bfloat16 [16384, 1024], P(('dp', 'mp')), may hold values from -6 to 6
- seq_lengths: int32 [16], replicated, may hold values from 256 to 1792, as said below
- dealing: int32 [16384], replicated, may hold values from 0 to 16383, as said below
- attn_gain: float32 [1024], P(('dp', 'mp')), may hold values from 0.1 to 1.9
- mlp_gain: float32 [1024], P(('dp', 'mp')), may hold values from 0.1 to 1.9
- w_qkv: bfloat16 [3, 1024, 1024], P(None, 'dp', 'mp'), may hold values from -0.25 to 0.25
- w_out: bfloat16 [1024, 1024], P('mp', 'dp'), may hold values from -0.5 to 0.5
- w_in: bfloat16 [2, 1024, 2624], P(None, 'dp', 'mp'), may hold values from -0.1875 to 0.1875
- w_down: bfloat16 [2624, 1024], P('mp', 'dp'), may hold values from -0.25 to 0.25
Outputs:
- output: bfloat16 [16384, 1024], P(('dp', 'mp'))
- input_grad: bfloat16 [16384, 1024], P(('dp', 'mp'))
- attn_gain_grad: float32 [1024], P(('dp', 'mp'))
- mlp_gain_grad: float32 [1024], P(('dp', 'mp'))
- w_qkv_grad: float32 [3, 1024, 1024], P(None, 'dp', 'mp')
- w_out_grad: float32 [1024, 1024], P('mp', 'dp')
- w_in_grad: float32 [2, 1024, 2624], P(None, 'dp', 'mp')
- w_down_grad: float32 [2624, 1024], P('mp', 'dp')
- w_qkv_clipped: bfloat16 [3, 1024, 1024], P(None, 'dp', 'mp')
Inputs may be any that keep to these rules, and one draw needn't show every extreme that they name: `seq_lengths`: entries 2o and 2o + 1 are the lengths of owner o's two sequences and sum to 2048. `dealing`: A permutation. Cut the input order and the dealt order into blocks of 512 rows, block b standing on dp index b // 4 and mp index b % 4; each dealt block takes exactly 64 rows from each input block of the same mp index and none from others.
All inputs are finite; a program needn't handle non-finite values.
Results may differ from a plain program's by a relative error of at most 0.019.
The roundings to bfloat16 on the way count: a program that leaves them out, or rounds other values in their place, can miss the bound.
Values may be sent and summed in bfloat16 or wider, within the bound.
No kernel may reach another device: no remote copies, remote signals or barrier semaphores. Data moves between devices by JAX's collectives and lax.ppermute only.
A program may use at most 192 MiB of HBM per device.

v0:
```python
import math

import jax
import jax.numpy as jnp
from jax import lax
from jax.sharding import PartitionSpec as P

HEAD_DIM = 64


theta_base = 160000.0
norm_eps = 1e-05
clip_limit = 5.0
score_scale = 0.125


def normalize(values):
    row_mean = jnp.mean(values, axis=-1, keepdims=True)
    centered = values - row_mean
    variance = jnp.mean(centered * centered, axis=-1, keepdims=True)
    return centered * lax.rsqrt(variance + norm_eps)


def scaled_norm(values, gain_row):
    return normalize(values) * gain_row


def rope_tables(positions, head_width):
    steps = jnp.arange(head_width // 2, dtype=jnp.float32)
    freqs = jnp.exp(steps * (-2.0 * math.log(theta_base) / head_width))
    angles = positions[:, None] * freqs[None, :]
    cosine_table = jnp.cos(angles)
    sine_table = jnp.sin(angles)
    return (
        jnp.concatenate([cosine_table, cosine_table], -1),
        jnp.concatenate([sine_table, sine_table], -1),
    )


def rotate(values, cosine_table, sine_table):
    half_width = values.shape[-1] // 2
    turned = jnp.concatenate([-values[..., half_width:], values[..., :half_width]], axis=-1)
    return values * cosine_table[:, None, :] + turned * sine_table[:, None, :]


def gated_unit(gate_up):
    return jax.nn.gelu(gate_up[0], approximate=False) * gate_up[1]


def group_rows(values):
    return lax.all_gather(values, "mp", axis=0, tiled=True)


def group_sum(values):
    return lax.psum_scatter(values, "mp", scatter_dimension=0, tiled=True)


def routing(dealing, owner_index, lane_index, dp_count, mp_count, row_count):
    slot_count = row_count // dp_count
    deal_table = dealing.reshape(dp_count, mp_count, row_count)
    lane_rows = lax.dynamic_index_in_dim(deal_table, lane_index, 1, keepdims=False)
    local_row = lane_rows - (owner_index * mp_count + lane_index) * row_count
    inside = (local_row >= 0) & (local_row < row_count)
    ranked = jnp.cumsum(inside.astype(jnp.int32), axis=1) - 1
    column = jnp.where(inside, ranked, slot_count)
    target = jnp.broadcast_to(jnp.arange(dp_count, dtype=jnp.int32)[:, None], (dp_count, row_count))
    send_rows = (
        jnp.zeros((dp_count, slot_count), jnp.int32)
        .at[target, column]
        .set(local_row, mode="drop")
        .reshape(-1)
    )
    owned_rows = lax.dynamic_index_in_dim(lane_rows, owner_index, 0, keepdims=False)
    source = owned_rows // row_count // mp_count
    onehot_src = (source[:, None] == jnp.arange(dp_count, dtype=jnp.int32)[None, :]).astype(
        jnp.int32
    )
    rank_within = jnp.sum((jnp.cumsum(onehot_src, axis=0) - 1) * onehot_src, axis=1)
    recv_slot = source * slot_count + rank_within
    sequence = jnp.arange(row_count, dtype=jnp.int32)
    back_slot = jnp.zeros((row_count,), jnp.int32).at[send_rows].set(sequence)
    owner_take = jnp.zeros((row_count,), jnp.int32).at[recv_slot].set(sequence)
    return (send_rows, recv_slot, owner_take, back_slot)


def attend_forward(queries, key_rows, values, segment, block_rows):
    token_count, head_count, head_width = queries.shape
    block_count = token_count // block_rows
    q_blocks = queries.reshape(block_count, block_rows, head_count, head_width)
    s_blocks = segment.reshape(block_count, block_rows)

    def one_block(pieces):
        query_block, seg_block = pieces
        scores = (
            jnp.einsum("bhd,thd->hbt", query_block, key_rows, preferred_element_type=jnp.float32)
            * score_scale
        )
        same_seq = (seg_block[:, None] == segment[None, :])[None]
        masked = jnp.where(same_seq, scores, -jnp.inf)
        row_top = jnp.max(masked, axis=2, keepdims=True)
        weights = jnp.where(same_seq, jnp.exp(scores - row_top), 0.0)
        row_total = jnp.sum(weights, axis=2, keepdims=True)
        weights_low = (weights / row_total).astype(jnp.bfloat16)
        attended = jnp.einsum(
            "hbt,thd->bhd", weights_low, values, preferred_element_type=jnp.float32
        )
        log_total = row_top[..., 0] + jnp.log(row_total[..., 0])
        return (attended.astype(jnp.bfloat16), log_total, jnp.max(row_top[..., 0], axis=1))

    attended, log_total, peak_rows = lax.map(one_block, (q_blocks, s_blocks))
    return (
        attended.reshape(token_count, head_count, head_width),
        log_total,
        jnp.max(peak_rows, axis=0),
    )


def attend_backward(queries, key_rows, values, segment, grad_heads, log_total, block_rows):
    token_count, head_count, head_width = queries.shape
    block_count = token_count // block_rows
    q_blocks = queries.reshape(block_count, block_rows, head_count, head_width)
    g_blocks = grad_heads.reshape(block_count, block_rows, head_count, head_width)
    s_blocks = segment.reshape(block_count, block_rows)

    def one_block(running, pieces):
        key_grad, value_grad = running
        query_block, grad_block, seg_block, lse_block = pieces
        scores = (
            jnp.einsum("bhd,thd->hbt", query_block, key_rows, preferred_element_type=jnp.float32)
            * score_scale
        )
        same_seq = (seg_block[:, None] == segment[None, :])[None]
        weights = jnp.where(same_seq, jnp.exp(scores - lse_block[:, :, None]), 0.0)
        prob_grad = jnp.einsum(
            "bhd,thd->hbt", grad_block, values, preferred_element_type=jnp.float32
        )
        row_dot = jnp.sum(weights * prob_grad, axis=2, keepdims=True)
        score_grad = (weights * (prob_grad - row_dot)).astype(jnp.bfloat16)
        query_grad = (
            jnp.einsum("hbt,thd->bhd", score_grad, key_rows, preferred_element_type=jnp.float32)
            * score_scale
        )
        key_grad = (
            key_grad
            + jnp.einsum(
                "hbt,bhd->thd", score_grad, query_block, preferred_element_type=jnp.float32
            )
            * score_scale
        )
        value_grad = value_grad + jnp.einsum(
            "hbt,bhd->thd",
            weights.astype(jnp.bfloat16),
            grad_block,
            preferred_element_type=jnp.float32,
        )
        return ((key_grad, value_grad), query_grad)

    empty_grad = jnp.zeros((token_count, head_count, head_width), jnp.float32)
    (key_grad, value_grad), query_grad = lax.scan(
        one_block, (empty_grad, empty_grad), (q_blocks, g_blocks, s_blocks, log_total)
    )
    return (query_grad.reshape(token_count, head_count, head_width), key_grad, value_grad)


def local(
    hidden_in, out_grad, seq_lengths, dealing, attn_gain, mlp_gain, w_qkv, w_out, w_in, w_down
):
    dp_count = lax.axis_size("dp")
    mp_count = lax.axis_size("mp")
    owner_index = lax.axis_index("dp")
    lane_index = lax.axis_index("mp")
    row_count = hidden_in.shape[0]
    model_width = hidden_in.shape[1]
    send_rows, recv_slot, owner_take, back_slot = routing(
        dealing, owner_index, lane_index, dp_count, mp_count, row_count
    )

    def to_owners(values):
        packed = jnp.take(values, send_rows, axis=0).reshape(dp_count, -1, model_width)
        arrived = lax.all_to_all(packed, "dp", split_axis=0, concat_axis=0, tiled=True)
        return jnp.take(arrived.reshape(row_count, model_width), recv_slot, axis=0)

    def from_owners(values):
        packed = jnp.take(values, owner_take, axis=0).reshape(dp_count, -1, model_width)
        arrived = lax.all_to_all(packed, "dp", split_axis=0, concat_axis=0, tiled=True)
        return jnp.take(arrived.reshape(row_count, model_width), back_slot, axis=0)

    attn_full, mlp_full = (
        lax.all_gather(attn_gain, ("dp", "mp"), axis=0, tiled=True),
        lax.all_gather(mlp_gain, ("dp", "mp"), axis=0, tiled=True),
    )
    qkv_full, outer_full, inner_full, down_full = (
        lax.all_gather(w_qkv, "dp", axis=1, tiled=True),
        lax.all_gather(w_out, "dp", axis=1, tiled=True),
        lax.all_gather(w_in, "dp", axis=1, tiled=True),
        lax.all_gather(w_down, "dp", axis=1, tiled=True),
    )
    lane_width = qkv_full.shape[2]
    head_count = lane_width // HEAD_DIM
    base_in = hidden_in.astype(jnp.float32)
    normed_one = scaled_norm(base_in, attn_full).astype(jnp.bfloat16)
    rows_one = group_rows(to_owners(normed_one))
    token_count = rows_one.shape[0]
    block_rows = min(512, token_count)
    first_len = lax.dynamic_index_in_dim(seq_lengths, 2 * owner_index, 0, keepdims=False)
    places = jnp.arange(token_count, dtype=jnp.int32)
    second_seq = places >= first_len
    segment = second_seq.astype(jnp.int32)
    cosine_table, sine_table = rope_tables(
        jnp.where(second_seq, places - first_len, places).astype(jnp.float32), HEAD_DIM
    )
    projected = jnp.einsum("td,kdc->ktc", rows_one, qkv_full, preferred_element_type=jnp.float32)
    split_shape = (token_count, head_count, HEAD_DIM)
    queries = rotate(projected[0].reshape(split_shape), cosine_table, sine_table).astype(
        jnp.bfloat16
    )
    key_rows = rotate(projected[1].reshape(split_shape), cosine_table, sine_table).astype(
        jnp.bfloat16
    )
    values = projected[2].reshape(split_shape).astype(jnp.bfloat16)
    attended, log_total, peak_rows = attend_forward(queries, key_rows, values, segment, block_rows)
    attended_flat = attended.reshape(token_count, lane_width)
    attn_part = jnp.dot(attended_flat, outer_full, preferred_element_type=jnp.float32)
    attn_branch = from_owners(group_sum(attn_part).astype(jnp.bfloat16))
    after_attn = base_in + attn_branch.astype(jnp.float32)
    normed_two = scaled_norm(after_attn, mlp_full).astype(jnp.bfloat16)
    gate_weights, down_weights = (inner_full, down_full)
    rows_two = group_rows(normed_two)
    gate_up = jnp.einsum("td,kdf->ktf", rows_two, gate_weights, preferred_element_type=jnp.float32)
    activated = gated_unit(gate_up).astype(jnp.bfloat16)
    mlp_part = jnp.dot(activated, down_weights, preferred_element_type=jnp.float32)
    mlp_branch = group_sum(mlp_part)
    grad_rows = group_rows(out_grad)
    output = (after_attn + mlp_branch).astype(jnp.bfloat16)
    act_grad = jnp.einsum("te,fe->tf", grad_rows, down_weights, preferred_element_type=jnp.float32)
    down_grad = jnp.einsum("tf,te->fe", activated, grad_rows, preferred_element_type=jnp.float32)
    unused, unit_pullback = jax.vjp(gated_unit, gate_up)
    pair_grad = unit_pullback(act_grad)[0].astype(jnp.bfloat16)
    inner_grad = jnp.einsum("td,ktf->kdf", rows_two, pair_grad, preferred_element_type=jnp.float32)
    norm_two_part = jnp.einsum(
        "ktf,kdf->td", pair_grad, gate_weights, preferred_element_type=jnp.float32
    )
    norm_two_grad = group_sum(norm_two_part)
    unused, norm_two_pullback = jax.vjp(scaled_norm, after_attn, mlp_full)
    resid_grad, mlp_gain_part = norm_two_pullback(norm_two_grad)
    after_grad = out_grad.astype(jnp.float32) + resid_grad
    rows_grad = group_rows(to_owners(after_grad.astype(jnp.bfloat16)))
    attended_grad = jnp.einsum(
        "te,ce->tc", rows_grad, outer_full, preferred_element_type=jnp.float32
    ).astype(jnp.bfloat16)
    outer_grad = jnp.einsum(
        "tc,te->ce", attended_flat, rows_grad, preferred_element_type=jnp.float32
    )
    query_grad, key_grad, value_grad = attend_backward(
        queries,
        key_rows,
        values,
        segment,
        attended_grad.reshape(split_shape),
        log_total,
        block_rows,
    )

    def unrotate(grad_heads):
        unused_out, rope_pullback = jax.vjp(
            lambda turned: rotate(turned, cosine_table, sine_table), grad_heads
        )
        return rope_pullback(grad_heads)[0].reshape(token_count, lane_width)

    qkv_grad = jnp.stack(
        [unrotate(query_grad), unrotate(key_grad), value_grad.reshape(token_count, lane_width)]
    ).astype(jnp.bfloat16)
    proj_grad = jnp.einsum("td,ktc->kdc", rows_one, qkv_grad, preferred_element_type=jnp.float32)
    norm_one_part = jnp.einsum(
        "ktc,kdc->td", qkv_grad, qkv_full, preferred_element_type=jnp.float32
    )
    norm_one_grad = from_owners(group_sum(norm_one_part).astype(jnp.bfloat16)).astype(jnp.float32)
    unused, norm_one_pullback = jax.vjp(scaled_norm, base_in, attn_full)
    input_part, attn_gain_part = norm_one_pullback(norm_one_grad)
    input_grad = (after_grad + input_part).astype(jnp.bfloat16)
    proj_grad, outer_grad, inner_grad, down_grad = (
        lax.psum_scatter(proj_grad, "dp", scatter_dimension=1, tiled=True),
        lax.psum_scatter(outer_grad, "dp", scatter_dimension=1, tiled=True),
        lax.psum_scatter(inner_grad, "dp", scatter_dimension=1, tiled=True),
        lax.psum_scatter(down_grad, "dp", scatter_dimension=1, tiled=True),
    )
    attn_gain_grad, mlp_gain_grad = (
        lax.psum_scatter(attn_gain_part, ("dp", "mp"), scatter_dimension=0, tiled=True),
        lax.psum_scatter(mlp_gain_part, ("dp", "mp"), scatter_dimension=0, tiled=True),
    )
    head_peaks = lax.pmax(peak_rows, "dp")
    factor = jnp.sqrt(clip_limit / jnp.maximum(head_peaks, clip_limit))
    column_factor = jnp.repeat(factor, HEAD_DIM)
    scaling = jnp.stack([column_factor, column_factor, jnp.ones_like(column_factor)])[:, None, :]
    clipped = (w_qkv.astype(jnp.float32) * scaling).astype(jnp.bfloat16)
    return (
        output,
        input_grad,
        attn_gain_grad,
        mlp_gain_grad,
        proj_grad,
        outer_grad,
        inner_grad,
        down_grad,
        clipped,
    )


def solution(mesh):
    in_specs = (
        P(("dp", "mp"), None),
        P(("dp", "mp"), None),
        P(),
        P(),
        P(("dp", "mp")),
        P(("dp", "mp")),
        P(None, "dp", "mp"),
        P("mp", "dp"),
        P(None, "dp", "mp"),
        P("mp", "dp"),
    )
    out_specs = (
        P(("dp", "mp"), None),
        P(("dp", "mp"), None),
        P(("dp", "mp")),
        P(("dp", "mp")),
        P(None, "dp", "mp"),
        P("mp", "dp"),
        P(None, "dp", "mp"),
        P("mp", "dp"),
        P(None, "dp", "mp"),
    )
    return jax.shard_map(local, mesh=mesh, in_specs=in_specs, out_specs=out_specs, check_vma=False)
```

profile of v0, /device:TPU:0, one launch (start us, length us, event | category | flops | bytes accessed | tf_op | source)
XLA Modules:
  0.0 1481.6 jit_solution(17158845287569653880)
XLA Ops:
  17.8 42.3 %all-reduce.11 = (f32[1024]{0:T(1024)}, f32[1024]{0:T(1024)S(1)}) all-reduce(f32[1024]{0:T(1024)S(1)} %dynamic-update-slice.1, f32[1024]{0:T(1024)S(1)} %dynamic-update-slice), channel_id=1, replica_groups=mesh['dp'=8,'mp'=4] {'dp','mp'}, use_global_device_ids=true, to_apply=%add.7 | all-reduce | flops 2048 | bytes 16384
  60.0 15.5 %scatter_custom_fusion.2 = s32[512]{0:T(512)S(1)} fusion(s32[4096]{0:T(1024)S(1)} %bitcast.311, s32[4096]{0:T(1024)S(1)} %bitcast.312, s32[]{:T(128)} %constant.106.clone.1), kind=kCustom, calls=%fused_computation.261 | custom fusion | bytes 2052 | tf_op jit(solution)/shard_map/reshape | solution.py:71
  80.5 6.1 all-to-all-start
  88.3 22.2 %all-to-all-done = bf16[8,64,1024]{2,1,0:T(8,128)(2,1)S(1)} async-done(((bf16[8,64,1024]{2,1,0:T(8,128)(2,1)}), bf16[8,64,1024]{2,1,0:T(8,128)(2,1)S(1)}, u32[]{:S(2)}, u32[]{:S(2)}) %all-to-all-start) | async-done | bytes 1048608 | tf_op jit(solution)/shard_map/all_to_all | solution.py:180
  119.7 29.1 %all_gather.33 = bf16[256,1024]{1,0:T(8,128)(2,1)} all-gather(bf16[256,128]{1,0:T(8,128)(2,1)S(1)} %copy-done.31), channel_id=1, replica_groups=mesh['dp'=8,'mp'=4] {'dp'}, dimensions={1}, use_global_device_ids=true | all-gather | bytes 589824 | tf_op jit(solution)/shard_map/all_gather | solution.py:194
  150.9 5.7 fusion.73
  172.9 80.4 %while.30 = (s32[]{:T(128)}, bf16[4,512,4,64]{1,3,2,0:T(8,128)(2,1)}, f32[4,4,512]{2,1,0:T(4,128)}, f32[4,4]{1,0:T(4,128)}, s32[4,512]{1,0:T(4,128)S(1)}, /*inde...) while((s32[]{:T(128)}, ...), condition=%wide.region_12.14_spmd.clone, body=%wide.region_8.13_spmd.clone.sunk | while | flops 1133643776 | bytes 57235644 | solution.py:110
  177.8 7.6 select_reduce_fusion.5
  185.4 6.1 fusion.178
  197.8 7.6 select_reduce_fusion.5
  205.4 6.1 fusion.178
  217.8 7.6 select_reduce_fusion.5
  225.3 6.1 fusion.178
  237.7 7.6 select_reduce_fusion.5
  245.3 6.1 fusion.178
  267.0 64.9 %reduce-scatter.9.cloned.1.call-done = f32[512,1024]{1,0:T(8,128)} async-done(((f32[2048,1024]{1,0:T(8,128)}), f32[512,1024]{1,0:T(8,128)}) %reduce-scatter.9.cloned.1.call-update) | async-done | bytes 2097168 | tf_op jit(solution)/shard_map/reduce_scatter | solution.py:55
  336.9 5.5 all-to-all-start.1
  345.1 28.5 %all-to-all-done.1 = bf16[8,64,1024]{2,1,0:T(8,128)(2,1)S(1)} async-done(((bf16[8,64,1024]{2,1,0:T(8,128)(2,1)}), bf16[8,64,1024]{2,1,0:T(8,128)(2,1)S(1)}, u32[]{:S(2)}, u32[]{:S(2)}) %all-to-all-start.1) | async-done | bytes 1048608 | tf_op jit(solution)/shard_map/all_to_all | solution.py:185
  382.2 7.4 all-gather.16.cloned.1.call-done
  389.5 34.6 %all-gather.18.cloned.1.call-done = bf16[2048,1024]{1,0:T(8,128)(2,1)} async-done(((bf16[512,1024]{1,0:T(8,128)(2,1)}), bf16[2048,1024]{1,0:T(8,128)(2,1)}) %all-gather.18.cloned.1.call-update) | async-done | bytes 4194320 | tf_op jit(solution)/shard_map/all_gather | solution.py:51
  424.1 7.9 fusion.131
  432.1 51.8 %all-gather.14.cloned.1.call-done = bf16[2,1024,656]{1,2,0:T(8,128)(2,1)} async-done(((bf16[2,128,656]{1,2,0:T(8,128)(2,1)}), bf16[2,1024,656]{1,2,0:T(8,128)(2,1)}) %all-gather.14.cloned.1.call-update) | async-done | bytes 2686992 | tf_op jit(solution)/shard_map/all_gather | solution.py:195
  483.9 34.9 %all-gather.12.cloned.1.call-done = bf16[2048,1024]{1,0:T(8,128)(2,1)} async-done(((bf16[512,1024]{1,0:T(8,128)(2,1)}), bf16[2048,1024]{1,0:T(8,128)(2,1)}) %all-gather.12.cloned.1.call-update) | async-done | bytes 4194320 | tf_op jit(solution)/shard_map/all_gather | solution.py:51
  518.8 8.5 convolution_bitcast_fusion
  527.4 12.5 multiply_bitcast_fusion
  545.1 13.5 convolution_bitcast_fusion.2
  558.7 9.7 fusion.130
  568.9 61.6 %reduce-scatter.13.cloned.1.call-done = f32[512,1024]{1,0:T(8,128)} async-done(((f32[2048,1024]{1,0:T(8,128)}), f32[512,1024]{1,0:T(8,128)}) %reduce-scatter.13.cloned.1.call-update) | async-done | bytes 2097168 | tf_op jit(solution)/shard_map/reduce_scatter | solution.py:55
  633.8 71.1 %reduce-scatter.11.cloned.1.call-done = f32[512,1024]{1,0:T(8,128)} async-done(((f32[2048,1024]{1,0:T(8,128)}), f32[512,1024]{1,0:T(8,128)}) %reduce-scatter.11.cloned.1.call-update) | async-done | bytes 2097168 | tf_op jit(solution)/shard_map/reduce_scatter | solution.py:55
  712.5 31.1 %all_to_all.20 = bf16[8,64,1024]{2,1,0:T(8,128)(2,1)S(1)} all-to-all(bf16[8,64,1024]{2,1,0:T(8,128)(2,1)S(1)} %bitcast.298), channel_id=1, replica_groups=mesh['dp'=8,'mp'=4] {'dp'}, dimensions={0} | all-to-all | bytes 2097152 | tf_op jit(solution)/shard_map/all_to_all | solution.py:180
  746.8 32.6 %all-gather.20.cloned.1.call-done = bf16[2048,1024]{1,0:T(8,128)(2,1)} async-done(((bf16[512,1024]{1,0:T(8,128)(2,1)}), bf16[2048,1024]{1,0:T(8,128)(2,1)}) %all-gather.20.cloned.1.call-update) | async-done | bytes 4194320 | tf_op jit(solution)/shard_map/all_gather | solution.py:51
  789.7 234.1 %while.31 = (s32[]{:T(128)}, f32[2048,4,64]{0,2,1:T(8,128)}, f32[2048,4,64]{0,2,1:T(8,128)}, f32[4,512,4,64]{1,0,3,2:T(4,128)}, bf16[4,512,4,64]{1,3,2,0:T(8,128...) while((s32[]{:T(128)}, f32[2048,4,64]{0,2,1:T(8,128)}, ...), condition=%wide.region_24.26_spmd.clone, body=%wide.region_22.25_spmd.clone.sunk | while | flops 2751072256 | bytes 183122192 | solution.py:159
  796.0 6.9 fusion.191
  802.9 11.6 multiply_reduce_fusion.6
  814.4 11.2 multiply_convert_fusion.5
  825.6 6.2 fusion.192
  836.4 11.1 dynamic_update_slice.29
  853.6 7.3 fusion.191
  860.9 11.6 multiply_reduce_fusion.6
  872.4 11.2 multiply_convert_fusion.5
  883.6 6.2 fusion.192
  895.1 11.1 dynamic_update_slice.29
  912.3 7.2 fusion.191
  919.6 11.6 multiply_reduce_fusion.6
  931.2 11.2 multiply_convert_fusion.5
  942.3 6.2 fusion.192
  953.8 11.1 dynamic_update_slice.29
  971.1 7.2 fusion.191
  978.3 11.6 multiply_reduce_fusion.6
  989.9 11.2 multiply_convert_fusion.5
  1001.1 6.2 fusion.192
  1012.6 11.1 dynamic_update_slice.29
  1041.3 8.4 convolution_bitcast_fusion.1
  1049.8 8.7 fusion.93
  1058.6 7.7 fusion.133
  1066.4 11.5 fusion.81
  1077.9 43.7 %reduce-scatter.15.cloned.1.call-done = f32[512,1024]{1,0:T(8,128)} async-done(((f32[2048,1024]{1,0:T(8,128)}), f32[512,1024]{1,0:T(8,128)}) %reduce-scatter.15.cloned.1.call-update) | async-done | bytes 2097168 | tf_op jit(solution)/shard_map/reduce_scatter | solution.py:55
  1126.6 5.5 all-to-all-start.3
  1132.3 48.1 %pmax.7 = f32[4]{0:T(128)S(1)} all-reduce(f32[4]{0:T(128)S(1)} %reduce_max.27), channel_id=1, replica_groups=mesh['dp'=8,'mp'=4] {'dp'}, use_global_device_ids=true, to_apply=%region_37.39 | all-reduce | flops 4 | bytes 32 | tf_op jit(solution)/shard_map/pmax | solution.py:291
  1185.9 36.6 %reduce-scatter.17.cloned.1.call-done = f32[3,128,256]{1,2,0:T(8,128)} async-done(((f32[3,1024,256]{1,2,0:T(8,128)}), f32[3,128,256]{1,2,0:T(8,128)}) %reduce-scatter.17.cloned.1.call-update) | async-done | bytes 393232 | tf_op jit(solution)/shard_map/reduce_scatter | solution.py:282
  1231.8 40.6 %all-reduce.10 = (f32[1024]{0:T(1024)S(1)}, f32[1024]{0:T(1024)S(1)}) all-reduce(f32[1024]{0:T(1024)S(1)} %get-tuple-element.295, f32[1024]{0:T(1024)S(1)} %copy-done.55), channel_id=6, replica_groups=mesh['dp'=8,'mp'=4] {'dp','mp'}, use_global_device_ids=true, to_apply=%region_29.31.clone | all-reduce | flops 2048 | bytes 16384
  1276.8 22.1 %reduce-scatter.23.cloned.1.call-done = f32[656,128]{1,0:T(8,128)} async-done(((f32[656,1024]{1,0:T(8,128)}), f32[656,128]{1,0:T(8,128)}) %reduce-scatter.23.cloned.1.call-update) | async-done | bytes 335888 | tf_op jit(solution)/shard_map/reduce_scatter | solution.py:285
  1299.0 108.0 %reduce-scatter.21.cloned.1.call-done = f32[2,128,656]{1,2,0:T(8,128)} async-done(((f32[2,1024,656]{1,2,0:T(8,128)}), f32[2,128,656]{1,2,0:T(8,128)}) %reduce-scatter.21.cloned.1.call-update) | async-done | bytes 671760 | tf_op jit(solution)/shard_map/reduce_scatter | solution.py:284
  1407.0 67.6 %reduce-scatter.19.cloned.1.call-done = f32[256,128]{1,0:T(8,128)} async-done(((f32[256,1024]{1,0:T(8,128)}), f32[256,128]{1,0:T(8,128)}) %reduce-scatter.19.cloned.1.call-update) | async-done | bytes 131088 | tf_op jit(solution)/shard_map/reduce_scatter | solution.py:283
  (369 shorter events, 215.6 us)
Async XLA Ops:
  7.2 143.8 %all-gather.10.cloned.1.call-start = ((), (), s32[]{:S(2)}) async-start(), calls=%async_computation.13 | async-start | bytes 1769472 | tf_op jit(solution)/shard_map/all_gather | solution.py:193
  10.4 66.7 %copy-start.29 = (f32[512]{0:T(512)}, f32[512]{0:T(512)S(1)}, u32[]{:S(2)}) copy-start(f32[512]{0:T(512)S(1)} %broadcast_multiply_fusion.3) | copy-start | bytes 6148
  12.1 65.1 %copy-start.39 = (f32[512]{0:T(512)}, f32[512]{0:T(512)S(1)}, u32[]{:S(2)}) copy-start(f32[512]{0:T(512)S(1)} %fusion.111) | copy-start | bytes 6148
  13.0 73.6 %copy-start.26 = (s32[8,4,512]{2,1,0:T(4,128)}, s32[8,4,512]{2,1,0:T(4,128)S(1)}, u32[]{:S(2)}) copy-start(s32[8,4,512]{2,1,0:T(4,128)S(1)} %reshape.559) | copy-start | bytes 196612
  60.0 17.2 %copy-start.32 = (f32[1024]{0:T(1024)}, f32[1024]{0:T(1024)S(1)}, u32[]{:S(2)}) copy-start(f32[1024]{0:T(1024)S(1)} %get-tuple-element.340) | copy-start | bytes 12292
  75.5 3.8 copy-start.37
  80.5 30.0 %all-to-all-start = ((bf16[8,64,1024]{2,1,0:T(8,128)(2,1)}), bf16[8,64,1024]{2,1,0:T(8,128)(2,1)S(1)}, u32[]{:S(2)}, u32[]{:S(2)}) async-start(bf16[8,64,1024]{2,1,0:T(8,128)(2,1)} %bitcast.13), calls=%async_computation | async-start | bytes 2097152 | tf_op jit(solution)/shard_map/all_to_all | solution.py:180
  86.6 64.4 %all-gather.8.cloned.1.call-start = ((), (), s32[]{:S(2)}) async-start(), calls=%async_computation.12 | async-start | bytes 5242880 | tf_op jit(solution)/shard_map/all_gather | solution.py:51
  88.2 22.3 %copy-start.45 = (s32[512]{0:T(512)}, s32[512]{0:T(512)S(1)}, u32[]{:S(2)}) copy-start(s32[512]{0:T(512)S(1)} %fusion.100) | copy-start | bytes 6148
  88.2 24.3 %copy-start.60 = (pred[512]{0:T(512)(128)(4,1)}, pred[512]{0:T(512)(128)(4,1)S(1)}, u32[]{:S(2)}) copy-start(pred[512]{0:T(512)(128)(4,1)S(1)} %get-tuple-element.345) | copy-start | bytes 1540
  88.2 24.3 %copy-start.51 = (s32[1024]{0:T(1024)}, s32[1024]{0:T(1024)S(1)}, u32[]{:S(2)}) copy-start(s32[1024]{0:T(1024)S(1)} %pad_clamp_fusion.2) | copy-start | bytes 12292
  112.5 7.2 copy-start.31
  113.7 218.2 %reduce-scatter.9.cloned.1.call-start = ((), (), s32[]{:S(2)}) async-start(), calls=%async_computation.14 | async-start | bytes 10485760 | tf_op jit(solution)/shard_map/reduce_scatter | solution.py:55
  162.4 6.0 copy-start.14
  253.2 8.7 copy-start.5
  253.2 8.7 copy-start.7
  253.2 4.1 copy-start.22
  261.9 127.6 %all-gather.16.cloned.1.call-start = ((), (), s32[]{:S(2)}) async-start(), calls=%async_computation.17 | async-start | bytes 1511424 | tf_op jit(solution)/shard_map/all_gather | solution.py:196
  262.5 161.6 %all-gather.18.cloned.1.call-start = ((), (), s32[]{:S(2)}) async-start(), calls=%async_computation.19 | async-start | bytes 5242880 | tf_op jit(solution)/shard_map/all_gather | solution.py:51
  263.1 220.8 %all-gather.14.cloned.1.call-start = ((), (), s32[]{:S(2)}) async-start(), calls=%async_computation.16 | async-start | bytes 3022848 | tf_op jit(solution)/shard_map/all_gather | solution.py:195
  266.9 66.7 %copy-start.53 = (s32[1024]{0:T(1024)}, s32[1024]{0:T(1024)S(1)}, u32[]{:S(2)}) copy-start(s32[1024]{0:T(1024)S(1)} %pad_clamp_fusion.1) | copy-start | bytes 12292
  266.9 68.8 %copy-start.58 = (pred[512]{0:T(512)(128)(4,1)}, pred[512]{0:T(512)(128)(4,1)S(1)}, u32[]{:S(2)}) copy-start(pred[512]{0:T(512)(128)(4,1)S(1)} %compare_and_fusion.2) | copy-start | bytes 1540
  335.7 6.7 copy-start.38
  336.9 36.7 %all-to-all-start.1 = ((bf16[8,64,1024]{2,1,0:T(8,128)(2,1)}), bf16[8,64,1024]{2,1,0:T(8,128)(2,1)S(1)}, u32[]{:S(2)}, u32[]{:S(2)}) async-start(bf16[8,64,1024]{2,1,0:T(8,128)(2,1)} %bitcast.20), calls=%async_computation.2 | async-start | bytes 2097152 | tf_op jit(solution)/shard_map/all_to_all | solution.py:185
  342.4 176.4 %all-gather.12.cloned.1.call-start = ((), (), s32[]{:S(2)}) async-start(), calls=%async_computation.15 | async-start | bytes 5242880 | tf_op jit(solution)/shard_map/all_gather | solution.py:51
  345.1 28.5 %copy-start.49 = (s32[1024]{0:T(1024)}, s32[1024]{0:T(1024)S(1)}, u32[]{:S(2)}) copy-start(s32[1024]{0:T(1024)S(1)} %pad_clamp_fusion) | copy-start | bytes 12292
  345.1 359.7 %copy-start.34 = (pred[512]{0:T(512)(128)(4,1)}, pred[512]{0:T(512)(128)(4,1)S(1)}, u32[]{:S(2)}) copy-start(pred[512]{0:T(512)(128)(4,1)S(1)} %compare_and_fusion.1) | copy-start | bytes 1540
  376.4 3.8 copy-start.6
  376.4 3.8 copy-start.36
  382.1 248.4 %reduce-scatter.13.cloned.1.call-start = ((), (), s32[]{:S(2)}) async-start(), calls=%async_computation.20 | async-start | bytes 10485760 | tf_op jit(solution)/shard_map/reduce_scatter | solution.py:55
  518.8 8.6 copy-start.8
  558.7 146.2 %reduce-scatter.11.cloned.1.call-start = ((), (), s32[]{:S(2)}) async-start(), calls=%async_computation.18 | async-start | bytes 10485760 | tf_op jit(solution)/shard_map/reduce_scatter | solution.py:55
  568.5 211.0 %all-gather.20.cloned.1.call-start = ((), (), s32[]{:S(2)}) async-start(), calls=%async_computation.21 | async-start | bytes 5242880 | tf_op jit(solution)/shard_map/all_gather | solution.py:51
  704.9 5.0 copy-start.13
  712.3 31.3 %copy-start.52 = (s32[1024]{0:T(1024)S(1)}, s32[1024]{0:T(1024)}, u32[]{:S(2)}) copy-start(s32[1024]{0:T(1024)} %copy-done.51) | copy-start | bytes 12292
  746.8 374.9 %reduce-scatter.15.cloned.1.call-start = ((), (), s32[]{:S(2)}) async-start(), calls=%async_computation.22 | async-start | bytes 10485760 | tf_op jit(solution)/shard_map/reduce_scatter | solution.py:55
  792.5 3.5 copy-start.1
  825.6 6.2 copy-start
  831.9 15.6 %copy-start.28 = (s32[4,512]{1,0:T(4,128)S(1)}, s32[4,512]{1,0:T(4,128)}, u32[]{:S(2)}) copy-start(s32[4,512]{1,0:T(4,128)} %copy-done.27) | copy-start | bytes 24580 | tf_op jit(solution)/shard_map/while
  883.6 6.2 copy-start
  889.9 16.3 %copy-start.28 = (s32[4,512]{1,0:T(4,128)S(1)}, s32[4,512]{1,0:T(4,128)}, u32[]{:S(2)}) copy-start(s32[4,512]{1,0:T(4,128)} %copy-done.27) | copy-start | bytes 24580 | tf_op jit(solution)/shard_map/while
  942.3 6.2 copy-start
  948.6 16.3 %copy-start.28 = (s32[4,512]{1,0:T(4,128)S(1)}, s32[4,512]{1,0:T(4,128)}, u32[]{:S(2)}) copy-start(s32[4,512]{1,0:T(4,128)} %copy-done.27) | copy-start | bytes 24580 | tf_op jit(solution)/shard_map/while
  1001.1 6.2 copy-start
  1007.3 16.3 %copy-start.28 = (s32[4,512]{1,0:T(4,128)S(1)}, s32[4,512]{1,0:T(4,128)}, u32[]{:S(2)}) copy-start(s32[4,512]{1,0:T(4,128)} %copy-done.27) | copy-start | bytes 24580 | tf_op jit(solution)/shard_map/while
  1023.8 8.8 copy-start.4
  1023.9 8.8 copy-start.18
  1039.9 9.8 copy-start.24
  1049.8 8.8 copy-start.21
  1049.8 172.8 %reduce-scatter.17.cloned.1.call-start = ((), (), s32[]{:S(2)}) async-start(), calls=%async_computation.23 | async-start | bytes 3538944 | tf_op jit(solution)/shard_map/reduce_scatter | solution.py:282
  1058.5 240.5 %reduce-scatter.23.cloned.1.call-start = ((), (), s32[]{:S(2)}) async-start(), calls=%async_computation.26 | async-start | bytes 3022848 | tf_op jit(solution)/shard_map/reduce_scatter | solution.py:285
  1066.3 340.7 %reduce-scatter.21.cloned.1.call-start = ((), (), s32[]{:S(2)}) async-start(), calls=%async_computation.25 | async-start | bytes 6045696 | tf_op jit(solution)/shard_map/reduce_scatter | solution.py:284
  1077.9 45.5 %copy-start.54 = (s32[1024]{0:T(1024)S(1)}, s32[1024]{0:T(1024)}, u32[]{:S(2)}) copy-start(s32[1024]{0:T(1024)} %copy-done.53) | copy-start | bytes 12292
  1125.5 6.7 copy-start.62
  1125.5 54.9 %copy-start.16 = (bf16[32,8,4,512]{3,1,2,0:T(8,128)(2,1)S(1)}, bf16[32,8,4,512]{3,1,2,0:T(8,128)(2,1)}, u32[]{:S(2)}) copy-start(bf16[32,8,4,512]{3,1,2,0:T(8,128)(2,1)} %copy-done.15) | copy-start | bytes 3145732
  1126.6 97.8 %all-to-all-start.3 = ((bf16[8,64,1024]{2,1,0:T(8,128)(2,1)}), bf16[8,64,1024]{2,1,0:T(8,128)(2,1)S(1)}, u32[]{:S(2)}, u32[]{:S(2)}) async-start(bf16[8,64,1024]{2,1,0:T(8,128)(2,1)} %bitcast.36), calls=%async_computation.7 | async-start | bytes 2097152 | tf_op jit(solution)/shard_map/all_to_all | solution.py:185
  1132.2 342.4 %reduce-scatter.19.cloned.1.call-start = ((), (), s32[]{:S(2)}) async-start(), calls=%async_computation.24 | async-start | bytes 1179648 | tf_op jit(solution)/shard_map/reduce_scatter | solution.py:283
  1180.4 4.8 copy-start.25
  1180.4 44.0 %copy-start.50 = (s32[1024]{0:T(1024)S(1)}, s32[1024]{0:T(1024)}, u32[]{:S(2)}) copy-start(s32[1024]{0:T(1024)} %copy-done.49) | copy-start | bytes 12292
  1224.5 4.9 copy-start.44
  1224.5 4.9 copy-start.40
  1227.3 4.5 copy-start.55
  1227.3 46.3 %copy-start.12 = (f32[512,1024]{1,0:T(8,128)S(1)}, f32[512,1024]{1,0:T(8,128)}, u32[]{:S(2)}) copy-start(f32[512,1024]{1,0:T(8,128)} %copy-done.11) | copy-start | bytes 6291460
  1227.3 46.3 %copy-start.42 = (f32[512]{0:T(512)S(1)}, f32[512]{0:T(512)}, u32[]{:S(2)}) copy-start(f32[512]{0:T(512)} %copy-done.41) | copy-start | bytes 6148
  (30 other events, 60.8 us)
Sparse Core Ops, SparseCore 0:
  10.6 49.3 all-gather.9
  113.8 33.6 all-gather.7
  262.1 69.7 reduce-scatter.8
  334.0 55.4 all-gather.15
  391.0 33.0 all-gather.17
  426.2 57.6 all-gather.13
  486.1 32.6 all-gather.11
  558.8 71.6 reduce-scatter.12
  633.1 71.7 reduce-scatter.10
  746.9 32.5 all-gather.19
  1049.9 71.6 reduce-scatter.14
  1125.1 97.4 reduce-scatter.16
  1226.6 72.3 reduce-scatter.22
  1303.5 103.5 reduce-scatter.20
  1410.9 63.6 reduce-scatter.18
where the time goes:
time: 1490 us; the launch traced here: 1480 us
  waiting for transfers between devices  690 us (46%)
  matrix products  264 us (18%)
  blocking collectives  191 us (13%)
  other arithmetic  165 us (11%)
  local copies, waits for them, and re-layouts  137 us (9%)
  starting transfers between devices  18.1 us (1%)
  between operations  15.5 us (1%)
    reduce_scatter x4, waiting for transfers between devices, group_sum(): return lax.psum_scatter(values, 'mp', scatter_dimension=0, tiled=True)  241 us
    reduce_scatter x1, waiting for transfers between devices, local(): lax.psum_scatter(inner_grad, 'dp', scatter_dimension=1, tiled=True)  108 us
    all_gather x4, waiting for transfers between devices, group_rows(): return lax.all_gather(values, 'mp', axis=0, tiled=True)  102 us
    unnamed x2, blocking collectives  82.9 us
    reduce_scatter x1, waiting for transfers between devices, local(): lax.psum_scatter(outer_grad, 'dp', scatter_dimension=1, tiled=True)  67.6 us
    all_gather x1, waiting for transfers between devices, local(): lax.all_gather(w_in, 'dp', axis=1, tiled=True)  51.8 us
    pmax x1, blocking collectives, local(): head_peaks = lax.pmax(peak_rows, 'dp')  48.1 us
    dynamic_update_slice x8, local copies, waits for them, and re-layouts, attend_backward(): lax.scan(one_block, (empty_grad, empty_grad), (q_blocks, g_blocks, s_bloc...  46.5 us
  transfers between devices with their start and end apart: 18, of which 15 were waited for; matrix products, arithmetic and copies ran while one was open for 9% of the time, Pallas kernels for 0%

commit v1 on v0

v1 whole, which is shorter than its diff:
```python
import functools
import math

import jax
import jax.numpy as jnp
from jax import lax
from jax.experimental import pallas as pl
from jax.experimental.pallas import tpu as pltpu
from jax.sharding import PartitionSpec as P

HEAD_DIM = 64
LANES = 128
theta_base = 160000.0
norm_eps = 1e-05
clip_limit = 5.0
score_scale = 0.125
exp_scale = score_scale * math.log2(math.e)
far_away = -1e30
lowest = -3e38

BF16 = jnp.bfloat16
F32 = jnp.float32


def dot(left, right, left_dim, right_dim):
    return lax.dot_general(
        left, right, (((left_dim,), (right_dim,)), ((), ())), preferred_element_type=F32
    )


def split_three(values):
    high = values.astype(BF16).astype(F32)
    rest = values - high
    middle = rest.astype(BF16).astype(F32)
    return high, middle, rest - middle


def row_stats(values):
    mean = jnp.mean(values, axis=-1, keepdims=True)
    centered = values - mean
    variance = jnp.mean(centered * centered, axis=-1, keepdims=True)
    scale = lax.rsqrt(variance + norm_eps)
    return centered * scale, scale


def turn(values, lane):
    return jnp.where(
        lane % HEAD_DIM < HEAD_DIM // 2,
        pltpu.roll(values, LANES - HEAD_DIM // 2, 1),
        pltpu.roll(values, HEAD_DIM // 2, 1),
    )


def swap_bit(values, axis_name, bit):
    count = lax.axis_size(axis_name)
    return lax.ppermute(values, axis_name, [(i, i ^ bit) for i in range(count)])


def lane_iota(rows):
    return lax.broadcasted_iota(jnp.int32, (rows, LANES), 1)


def vmem(mib):
    return pltpu.CompilerParams(vmem_limit_bytes=mib << 20)


def resident(shape):
    zeros = (0,) * len(shape)
    return pl.BlockSpec(shape, lambda *_: zeros, pipeline_mode=pl.Buffered(1))


def qkv_kernel(step, s_ref, x_ref, gain_ref, w_ref, cos_ref, sin_ref, q_ref, k_ref, v_ref, n_ref):
    first_len = s_ref[1]
    normed, _ = row_stats(x_ref[...].astype(F32))
    n1 = (normed * gain_ref[...]).astype(BF16)
    n_ref[...] = n1
    lane = lane_iota(step)
    row = pl.program_id(0) * step + lax.broadcasted_iota(jnp.int32, (step, LANES), 0)
    second = row >= first_len
    one, zero = jnp.float32(1), jnp.float32(0)
    q_tail = jnp.where(lane == 64 + second.astype(jnp.int32), one, zero)
    k_tail = jnp.where(
        lane == 65 - second.astype(jnp.int32),
        jnp.float32(far_away),
        jnp.where((lane >= 66) & (lane < 69), one, zero),
    )
    cos, sin = cos_ref[...], sin_ref[...]
    for which, (out, tail) in enumerate(((q_ref, q_tail), (k_ref, k_tail), (v_ref, one))):
        projected = dot(n1, w_ref[which], 1, 0)
        for pair in range(projected.shape[1] // LANES):
            part = projected[:, pair * LANES : (pair + 1) * LANES]
            if which < 2:
                part = part * cos + turn(part, lane) * sin
            out[2 * pair] = jnp.where(lane < HEAD_DIM, part, tail).astype(BF16)
            out[2 * pair + 1] = jnp.where(
                lane < HEAD_DIM, pltpu.roll(part, HEAD_DIM, 1), tail
            ).astype(BF16)


def qkv_call(scalars, x_rel, gain, w_qkv, cos, sin, step=256):
    lanes, rows, width = x_rel.shape
    tokens = lanes * rows
    heads = w_qkv.shape[2] // HEAD_DIM
    per = rows // step
    ext = jax.ShapeDtypeStruct((heads, tokens, LANES), BF16)
    row_spec = lambda i, s: (i, 0)
    head_spec = pl.BlockSpec((heads, step, LANES), lambda i, s: (0, i, 0))
    return pl.pallas_call(
        functools.partial(qkv_kernel, step),
        out_shape=(ext, ext, ext, jax.ShapeDtypeStruct((tokens, width), BF16)),
        grid_spec=pltpu.PrefetchScalarGridSpec(
            num_scalar_prefetch=1,
            grid=(tokens // step,),
            in_specs=[
                pl.BlockSpec((None, step, width), lambda i, s: ((i // per) ^ s[0], i % per, 0)),
                resident(gain.shape),
                resident(w_qkv.shape),
                pl.BlockSpec((step, LANES), row_spec),
                pl.BlockSpec((step, LANES), row_spec),
            ],
            out_specs=[head_spec, head_spec, head_spec, pl.BlockSpec((step, width), row_spec)],
        ),
        compiler_params=vmem(40),
        cost_estimate=pl.CostEstimate(
            flops=2 * tokens * width * w_qkv.shape[2] * 3,
            bytes_accessed=20 << 20,
            transcendentals=tokens,
        ),
        name="qkv",
    )(scalars, x_rel, gain, w_qkv, cos, sin)


def key_range(first_len, row, q_rows, k_rows, tokens):
    low = jnp.where(row >= first_len, first_len // k_rows, 0)
    high = jnp.where(row + q_rows <= first_len, (first_len + k_rows - 1) // k_rows, tokens // k_rows)
    return low, high


def fwd_kernel(
    base, q_rows, k_rows, s_ref, q_ref, k_ref, v_ref, o_ref, q2_ref, top_ref, score, peak, acc
):
    heads, tokens, _ = k_ref.shape
    low, high = key_range(
        s_ref[1], base + pl.program_id(0) * q_rows, q_rows, k_rows, tokens
    )
    lane = lane_iota(q_rows)
    peak[...] = jnp.full(peak.shape, lowest, F32)
    acc[...] = jnp.zeros(acc.shape, F32)

    def first_pass(block, carry):
        keys = pl.ds(pl.multiple_of(block * k_rows, k_rows), k_rows)
        for h in range(heads):
            s = dot(q_ref[h], k_ref[h, keys, :], 1, 1)
            score[h, :, keys] = s
            most = peak[h]
            for t in range(k_rows // LANES):
                most = jnp.maximum(most, s[:, t * LANES : (t + 1) * LANES])
            peak[h] = most
        return carry

    lax.fori_loop(low, high, first_pass, 0)
    for h in range(heads):
        peak[h] = jnp.broadcast_to(jnp.max(peak[h], axis=1, keepdims=True), (q_rows, LANES))

    def second_pass(block, carry):
        keys = pl.ds(pl.multiple_of(block * k_rows, k_rows), k_rows)
        for h in range(heads):
            s, most = score[h, :, keys], peak[h]
            p = jnp.concatenate(
                [
                    jnp.exp2((s[:, t * LANES : (t + 1) * LANES] - most) * exp_scale).astype(BF16)
                    for t in range(k_rows // LANES)
                ],
                axis=1,
            )
            acc[h] += dot(p, v_ref[h, keys, :], 1, 0)
        return carry

    lax.fori_loop(low, high, second_pass, 0)
    held = None
    for h in range(heads):
        sums = acc[h]
        total = jnp.where(lane < HEAD_DIM, pltpu.roll(sums, HEAD_DIM, 1), sums)
        out = sums / total
        log_total = peak[h] + jnp.log2(total) * (1.0 / exp_scale)
        a, b, c = split_three(-log_total)
        q2 = q_ref[h].astype(F32)
        q2 = jnp.where(lane == 66, a, jnp.where(lane == 67, b, jnp.where(lane == 68, c, q2)))
        q2_ref[h] = q2.astype(BF16)
        top_ref[h] = jnp.broadcast_to(jnp.max(peak[h], axis=0, keepdims=True), (8, LANES))
        if h % 2 == 0:
            held = out
        else:
            both = jnp.where(lane < HEAD_DIM, held, pltpu.roll(out, HEAD_DIM, 1))
            o_ref[:, (h // 2) * LANES : (h // 2 + 1) * LANES] = both.astype(BF16)


def attend_forward(scalars, q, k, v, chunk, rows, q_rows=256, k_rows=512):
    heads, tokens, _ = k.shape
    count = rows // q_rows
    k_rows = min(k_rows, tokens)
    return pl.pallas_call(
        functools.partial(fwd_kernel, chunk * rows, q_rows, k_rows),
        out_shape=(
            jax.ShapeDtypeStruct((rows, heads * HEAD_DIM), BF16),
            jax.ShapeDtypeStruct((heads, rows, LANES), BF16),
            jax.ShapeDtypeStruct((count, heads, 8, LANES), F32),
        ),
        grid_spec=pltpu.PrefetchScalarGridSpec(
            num_scalar_prefetch=1,
            grid=(count,),
            in_specs=[
                pl.BlockSpec((heads, q_rows, LANES), lambda i, s: (0, chunk * count + i, 0)),
                resident(k.shape),
                resident(v.shape),
            ],
            out_specs=[
                pl.BlockSpec((q_rows, heads * HEAD_DIM), lambda i, s: (i, 0)),
                pl.BlockSpec((heads, q_rows, LANES), lambda i, s: (0, i, 0)),
                pl.BlockSpec((None, heads, 8, LANES), lambda i, s: (i, 0, 0, 0)),
            ],
            scratch_shapes=[
                pltpu.VMEM((heads, q_rows, tokens), F32),
                pltpu.VMEM((heads, q_rows, LANES), F32),
                pltpu.VMEM((heads, q_rows, LANES), F32),
            ],
        ),
        compiler_params=vmem(40),
        cost_estimate=pl.CostEstimate(
            flops=8 * rows * tokens * heads * LANES,
            bytes_accessed=6 << 20,
            transcendentals=rows * tokens * heads,
        ),
        name="attend_forward",
    )(scalars, q, k, v)


def bwd_kernel(
    q_rows, k_rows, s_ref, q2_ref, k_ref, v_ref, do_ref, cos_ref, sin_ref, out_ref, dk_ref, dv_ref
):
    heads, tokens, _ = k_ref.shape
    step = pl.program_id(0)
    low, high = key_range(s_ref[1], step * q_rows, q_rows, k_rows, tokens)

    @pl.when(step == 0)
    def _():
        dk_ref[...] = jnp.zeros_like(dk_ref)
        dv_ref[...] = jnp.zeros_like(dv_ref)

    def body(block, sums):
        keys = pl.ds(pl.multiple_of(block * k_rows, k_rows), k_rows)
        new = []
        for h in range(heads):
            key, q2, do = k_ref[h, keys, :], q2_ref[h], do_ref[h]
            p = jnp.exp2(dot(key, q2, 1, 1) * exp_scale)
            ds = (p * dot(v_ref[h, keys, :], do, 1, 1)).astype(BF16)
            dv_ref[h, keys, :] += dot(p.astype(BF16), do, 1, 0)
            dk_ref[h, keys, :] += dot(ds, q2, 1, 0)
            new.append(sums[h] + dot(key, ds, 0, 0))
        return tuple(new)

    sums = lax.fori_loop(
        low, high, body, tuple(jnp.zeros((LANES, q_rows), F32) for _ in range(heads))
    )
    lane = lane_iota(q_rows)

    def unrotate(first, second, rows):
        both = jnp.where(lane < HEAD_DIM, first, pltpu.roll(second, HEAD_DIM, 1)) * score_scale
        return both * cos_ref[rows, :] - turn(both, lane) * sin_ref[rows, :]

    here = pl.ds(pl.multiple_of(step * q_rows, q_rows), q_rows)
    for pair in range(heads // 2):
        cols = slice(pair * LANES, (pair + 1) * LANES)
        out_ref[0, here, cols] = unrotate(sums[2 * pair].T, sums[2 * pair + 1].T, here).astype(BF16)

    @pl.when(step == pl.num_programs(0) - 1)
    def _():
        def finish(block, carry):
            rows = pl.ds(pl.multiple_of(block * q_rows, q_rows), q_rows)
            for pair in range(heads // 2):
                cols = slice(pair * LANES, (pair + 1) * LANES)
                one, two = 2 * pair, 2 * pair + 1
                out_ref[1, rows, cols] = unrotate(
                    dk_ref[one, rows, :], dk_ref[two, rows, :], rows
                ).astype(BF16)
                out_ref[2, rows, cols] = jnp.where(
                    lane < HEAD_DIM,
                    dv_ref[one, rows, :],
                    pltpu.roll(dv_ref[two, rows, :], HEAD_DIM, 1),
                ).astype(BF16)
            return carry

        lax.fori_loop(0, tokens // q_rows, finish, 0)


def attend_backward(scalars, q2, k, v, do, cos, sin, q_rows=256, k_rows=256):
    heads, tokens, _ = k.shape
    block = lambda: pl.BlockSpec((heads, q_rows, LANES), lambda i, s: (0, i, 0))
    out = (3, tokens, heads * HEAD_DIM)
    return pl.pallas_call(
        functools.partial(bwd_kernel, q_rows, k_rows),
        out_shape=jax.ShapeDtypeStruct(out, BF16),
        grid_spec=pltpu.PrefetchScalarGridSpec(
            num_scalar_prefetch=1,
            grid=(tokens // q_rows,),
            in_specs=[
                block(),
                resident(k.shape),
                resident(v.shape),
                block(),
                resident(cos.shape),
                resident(sin.shape),
            ],
            out_specs=resident(out),
            scratch_shapes=[
                pltpu.VMEM((heads, tokens, LANES), F32),
                pltpu.VMEM((heads, tokens, LANES), F32),
            ],
        ),
        compiler_params=vmem(48),
        cost_estimate=pl.CostEstimate(
            flops=20 * tokens * tokens * heads * LANES,
            bytes_accessed=14 << 20,
            transcendentals=tokens * tokens * heads,
        ),
        name="attend_backward",
    )(scalars, q2, k, v, do, cos, sin)


def mlp_kernel(
    s_ref, x_ref, g_ref, o0, o1, o2, o3, w0, w1, w2, w3, gain_ref, win_ref, wdown_ref, *rest
):
    a_ref, n_ref, act_ref, dgate_ref, dup_ref, keep_ref, send_ref = rest[-7:]
    branch = dot(o0[...], w0[...], 1, 0) + dot(o1[...], w1[...], 1, 0)
    branch = branch + dot(o2[...], w2[...], 1, 0) + dot(o3[...], w3[...], 1, 0)
    branch = branch.astype(BF16)
    a_ref[...] = branch
    normed, _ = row_stats(x_ref[...].astype(F32) + branch.astype(F32))
    n2 = (normed * gain_ref[...]).astype(BF16)
    n_ref[...] = n2
    gate = dot(n2, win_ref[0], 1, 0)
    up = dot(n2, win_ref[1], 1, 0)
    dact = dot(g_ref[...], wdown_ref[...], 1, 1)
    phi = 0.5 + 0.5 * lax.erf(gate * math.sqrt(0.5))
    gelu = gate * phi
    act_ref[...] = (gelu * up).astype(BF16)
    density = jnp.exp(-0.5 * gate * gate) * (1.0 / math.sqrt(2.0 * math.pi))
    dgate = (dact * up * (phi + gate * density)).astype(BF16)
    dup = (dact * gelu).astype(BF16)
    dgate_ref[...] = dgate
    dup_ref[...] = dup
    partial = dot(dgate, win_ref[0], 1, 1) + dot(dup, win_ref[1], 1, 1)
    mine = pl.program_id(0) == s_ref[2]

    @pl.when(mine)
    def _():
        keep_ref[...] = partial

    @pl.when(jnp.logical_not(mine))
    def _():
        send_ref[...] = partial.astype(BF16)


def mlp_call(scalars, x_rel, g_rel, heads_rel, w_out_rel, gain, w_in, w_down, chunk, held):
    lanes, rows, width = x_rel.shape
    units = w_down.shape[0]
    step = rows // 2
    rel = lambda i, s: (s[0] ^ chunk, i, 0)
    wide = pl.BlockSpec((None, step, width), rel)
    narrow = pl.BlockSpec((None, step, units), rel)
    wide_out = jax.ShapeDtypeStruct(x_rel.shape, BF16)
    narrow_out = jax.ShapeDtypeStruct((lanes, rows, units), BF16)
    half = pl.BlockSpec((step, width), lambda i, s: (0, 0))
    head_spec = pl.BlockSpec((step, heads_rel[0].shape[1]), lambda i, s: (i, 0))
    held = list(held)
    first = 1 + 2 + len(heads_rel) + len(w_out_rel) + 3
    return pl.pallas_call(
        mlp_kernel,
        out_shape=(
            wide_out,
            wide_out,
            narrow_out,
            narrow_out,
            narrow_out,
            jax.ShapeDtypeStruct((step, width), F32),
            jax.ShapeDtypeStruct((step, width), BF16),
        ),
        grid_spec=pltpu.PrefetchScalarGridSpec(
            num_scalar_prefetch=1,
            grid=(2,),
            in_specs=[wide, wide]
            + [head_spec] * len(heads_rel)
            + [resident(w.shape) for w in w_out_rel]
            + [resident(gain.shape), resident(w_in.shape), resident(w_down.shape)]
            + [pl.BlockSpec(memory_space=pl.ANY)] * len(held),
            out_specs=[wide, wide, narrow, narrow, narrow, half, half],
        ),
        input_output_aliases={first + i: i for i in range(len(held))},
        compiler_params=vmem(48),
        cost_estimate=pl.CostEstimate(
            flops=2 * rows * width * (width + 5 * units),
            bytes_accessed=16 << 20,
            transcendentals=2 * rows * units,
        ),
        name="mlp",
    )(scalars, x_rel, g_rel, *heads_rel, *w_out_rel, gain, w_in, w_down, *held)


def pull_norm(normed, scale, cotangent):
    mean = jnp.mean(cotangent, axis=-1, keepdims=True)
    along = jnp.mean(cotangent * normed, axis=-1, keepdims=True)
    return (cotangent - mean - normed * along) * scale


def fold_rows(values):
    rows, width = values.shape
    return jnp.sum(values.reshape(rows // 8, 8, width), axis=0)


def resid_kernel(s_ref, mine_ref, other_ref, x_ref, a_ref, g_ref, gain_ref, da_ref, gain_out):
    dn = mine_ref[...].astype(F32) + other_ref[...].astype(F32)
    normed, scale = row_stats(x_ref[...].astype(F32) + a_ref[...].astype(F32))
    gain_out[...] = fold_rows(dn * normed)
    dx = g_ref[...].astype(F32) + pull_norm(normed, scale, dn * gain_ref[...])
    da_ref[...] = dx.astype(BF16)


def resid_call(scalars, mine, other, x_rel, a_rel, g_rel, gain, chunk):
    rows, width = mine.shape
    flat = pl.BlockSpec((rows, width), lambda i, s: (0, 0))
    rel = pl.BlockSpec((None, rows, width), lambda i, s: (s[0] ^ chunk, s[2], 0))
    return pl.pallas_call(
        resid_kernel,
        out_shape=(
            jax.ShapeDtypeStruct((rows, width), BF16),
            jax.ShapeDtypeStruct((8, width), F32),
        ),
        grid_spec=pltpu.PrefetchScalarGridSpec(
            num_scalar_prefetch=1,
            grid=(1,),
            in_specs=[flat, flat, rel, rel, rel, resident(gain.shape)],
            out_specs=[flat, pl.BlockSpec((8, width), lambda i, s: (0, 0))],
        ),
        compiler_params=vmem(32),
        cost_estimate=pl.CostEstimate(
            flops=20 * rows * width, bytes_accessed=12 * rows * width, transcendentals=rows
        ),
        name="resid",
    )(scalars, mine, other, x_rel, a_rel, g_rel, gain)


def head_grad_kernel(s_ref, own_ref, other_ref, w_ref, o_ref, *rest):
    do_ref, da_ref = rest[-2:]
    own = pl.program_id(0) == s_ref[2]
    da = jnp.where(own, own_ref[...], other_ref[...])
    da_ref[...] = da
    do = dot(da, w_ref[...], 1, 1).astype(BF16).astype(F32)
    rows = do.shape[0]
    lane = lane_iota(rows)
    product = do * o_ref[...].astype(F32)
    for pair in range(do.shape[1] // LANES):
        cols = slice(pair * LANES, (pair + 1) * LANES)
        part = do[:, cols]
        for odd in range(2):
            inside = (lane >= HEAD_DIM) if odd else (lane < HEAD_DIM)
            delta = jnp.sum(jnp.where(inside, product[:, cols], 0.0), axis=1, keepdims=True)
            a, b, c = split_three(jnp.broadcast_to(-delta, (rows, LANES)))
            head = pltpu.roll(part, HEAD_DIM, 1) if odd else part
            tail = jnp.where(
                lane == 64, a, jnp.where(lane == 65, b, jnp.where(lane == 66, c, 0.0))
            )
            do_ref[2 * pair + odd] = jnp.where(lane < HEAD_DIM, head, tail).astype(BF16)


def head_grad_call(scalars, own, other, w_out, o_chunk, chunk, tokens, held):
    rows, width = own.shape
    heads = o_chunk.shape[1] // HEAD_DIM
    flat = pl.BlockSpec((rows, width), lambda i, s: (0, 0))
    held = list(held)
    return pl.pallas_call(
        head_grad_kernel,
        out_shape=(
            jax.ShapeDtypeStruct((heads, tokens, LANES), BF16),
            jax.ShapeDtypeStruct((tokens, width), BF16),
        ),
        grid_spec=pltpu.PrefetchScalarGridSpec(
            num_scalar_prefetch=1,
            grid=(2,),
            in_specs=[
                flat,
                flat,
                resident(w_out.shape),
                pl.BlockSpec((rows, o_chunk.shape[1]), lambda i, s: (i, 0)),
            ]
            + [pl.BlockSpec(memory_space=pl.ANY)] * len(held),
            out_specs=[
                pl.BlockSpec((heads, rows, LANES), lambda i, s: (0, 2 * chunk + i, 0)),
                pl.BlockSpec((rows, width), lambda i, s: (2 * chunk + i, 0)),
            ],
        ),
        input_output_aliases={5 + i: i for i in range(len(held))},
        compiler_params=vmem(32),
        cost_estimate=pl.CostEstimate(
            flops=4 * rows * width * heads * HEAD_DIM,
            bytes_accessed=5 << 20,
            transcendentals=0,
        ),
        name="head_grad",
    )(scalars, own, other, w_out, o_chunk, *held)


def dn_kernel(p_ref, w_ref, out_ref):
    total = dot(p_ref[0], w_ref[0], 1, 1) + dot(p_ref[1], w_ref[1], 1, 1)
    out_ref[...] = (total + dot(p_ref[2], w_ref[2], 1, 1)).astype(BF16)


def dn_call(scalars, dproj, w_qkv, parity, rows, step=256):
    kinds, tokens, cols = dproj.shape
    width = w_qkv.shape[1]
    per = rows // step
    return pl.pallas_call(
        lambda s_ref, p_ref, w_ref, out_ref: dn_kernel(p_ref, w_ref, out_ref),
        out_shape=jax.ShapeDtypeStruct((2 * rows, width), BF16),
        grid_spec=pltpu.PrefetchScalarGridSpec(
            num_scalar_prefetch=1,
            grid=(2 * per,),
            in_specs=[
                pl.BlockSpec(
                    (kinds, step, cols),
                    lambda i, s: (0, ((2 * (i // per) + parity) ^ s[0]) * per + i % per, 0),
                ),
                resident(w_qkv.shape),
            ],
            out_specs=pl.BlockSpec((step, width), lambda i, s: (i, 0)),
        ),
        compiler_params=vmem(32),
        cost_estimate=pl.CostEstimate(
            flops=4 * rows * width * cols * kinds, bytes_accessed=8 << 20, transcendentals=0
        ),
        name="dn",
    )(scalars, dproj, w_qkv)


def last_kernel(mine_ref, other_ref, x_ref, da_ref, gain_ref, out_ref, gain_out):
    dn = (mine_ref[...] + other_ref[...].astype(F32)).astype(BF16).astype(F32)
    normed, scale = row_stats(x_ref[...].astype(F32))
    gain_out[...] = fold_rows(dn * normed)
    dx = da_ref[...].astype(F32) + pull_norm(normed, scale, dn * gain_ref[...])
    out_ref[...] = dx.astype(BF16)


def last_call(scalars, mine, other, x_rel, da, gain, step=256):
    rows, width = mine.shape
    per = rows // step
    flat = pl.BlockSpec((step, width), lambda i, s: (i, 0))
    return pl.pallas_call(
        lambda s_ref, *refs: last_kernel(*refs),
        out_shape=(
            jax.ShapeDtypeStruct((rows, width), BF16),
            jax.ShapeDtypeStruct((per, 8, width), F32),
        ),
        grid_spec=pltpu.PrefetchScalarGridSpec(
            num_scalar_prefetch=1,
            grid=(per,),
            in_specs=[
                flat,
                flat,
                pl.BlockSpec((None, step, width), lambda i, s: (0, i, 0)),
                pl.BlockSpec((step, width), lambda i, s: (s[0] * per + i, 0)),
                resident(gain.shape),
            ],
            out_specs=[flat, pl.BlockSpec((None, 8, width), lambda i, s: (i, 0, 0))],
        ),
        compiler_params=vmem(32),
        cost_estimate=pl.CostEstimate(
            flops=20 * rows * width, bytes_accessed=12 * rows * width, transcendentals=rows
        ),
        name="last",
    )(scalars, mine, other, x_rel, da, gain)


def bits_of(count):
    return [1 << i for i in range(count.bit_length() - 1)]


def pick(values, axis, index):
    return lax.dynamic_index_in_dim(values, index, axis, keepdims=False)


def halve(values, axis, axis_name):
    me = lax.axis_index(axis_name)
    carried = values
    for bit in bits_of(lax.axis_size(axis_name)):
        shape = carried.shape
        view = carried.reshape(shape[:axis] + (shape[axis] // 2, 2) + shape[axis + 1 :])
        mine = (me // bit) % 2
        arrived = swap_bit(pick(view, axis + 1, 1 - mine).astype(BF16), axis_name, bit)
        carried = pick(view, axis + 1, mine).astype(F32) + arrived.astype(F32)
    return lax.squeeze(carried, (axis,))


def spread(values, axes):
    for axis_name in reversed(axes):
        me = lax.axis_index(axis_name)
        for bit in bits_of(lax.axis_size(axis_name)):
            other = swap_bit(values, axis_name, bit)
            high = (me // bit) % 2 == 1
            values = jnp.concatenate(
                [jnp.where(high, other, values), jnp.where(high, values, other)], axis=-1
            )
    return values


def gather_sum(values, axes):
    for axis_name in axes:
        me = lax.axis_index(axis_name)
        for bit in reversed(bits_of(lax.axis_size(axis_name))):
            half = values.shape[-1] // 2
            low, top = values[..., :half], values[..., half:]
            high = (me // bit) % 2 == 1
            other = swap_bit(jnp.where(high, low, top), axis_name, bit)
            values = jnp.where(high, top, low) + other
    return values


def local(
    hidden_in, out_grad, seq_lengths, dealing, attn_gain, mlp_gain, w_qkv, w_out, w_in, w_down
):
    dp_count = lax.axis_size("dp")
    mp_count = lax.axis_size("mp")
    owner = lax.axis_index("dp")
    lane = lax.axis_index("mp")
    rows, width = hidden_in.shape
    tokens = rows * mp_count
    slots = rows // dp_count
    first_len = pick(seq_lengths, 0, 2 * owner)
    scalars = jnp.stack([lane, first_len, lane % 2]).astype(jnp.int32)

    lane_rows = pick(dealing.reshape(dp_count, mp_count, rows), 1, lane)
    local_row = lane_rows - (owner * mp_count + lane) * rows
    inside = (local_row >= 0) & (local_row < rows)
    order = jnp.arange(rows, dtype=jnp.int32)
    upto = (order[:, None] <= order[None, :]).astype(BF16)
    rank = dot(inside.astype(BF16), upto, 1, 0).astype(jnp.int32) - 1
    slot_hit = inside[:, None, :] & (rank[:, None, :] == jnp.arange(slots)[None, :, None])
    send_row = jnp.sum(jnp.where(slot_hit, local_row[:, None, :], 0), axis=2).reshape(rows)
    to_slot = (send_row[:, None] == order[None, :]).astype(BF16)
    source = pick(lane_rows, 0, owner) // (rows * mp_count)
    from_src = source[None, :] == jnp.arange(dp_count, dtype=jnp.int32)[:, None]
    src_rank = dot(from_src.astype(BF16), upto, 1, 0).astype(jnp.int32) - 1
    slot_of = source * slots + jnp.sum(jnp.where(from_src, src_rank, 0), axis=0)
    to_dealt = (slot_of[:, None] == order[None, :]).astype(BF16)

    def exchange(values):
        packed = values.reshape(dp_count, slots, width)
        arrived = lax.all_to_all(packed, "dp", split_axis=0, concat_axis=0, tiled=True)
        return arrived.reshape(rows, width)

    def to_owners(values):
        return dot(to_dealt, exchange(dot(to_slot, values, 1, 0).astype(BF16)), 1, 0).astype(BF16)

    def from_owners(values):
        return dot(to_slot, exchange(dot(to_dealt, values, 0, 0).astype(BF16)), 0, 0).astype(BF16)

    def group(values):
        across = swap_bit(values, "mp", 2)
        return [values, swap_bit(values, "mp", 1), across, swap_bit(across, "mp", 1)]

    x_rel = jnp.stack(group(to_owners(hidden_in)))
    gains = spread(jnp.stack([attn_gain, mlp_gain]), ("dp", "mp"))
    gain_one, gain_two = gains[0:1], gains[1:2]
    qkv_full = lax.all_gather(w_qkv, "dp", axis=1, tiled=True)
    outer_own = lax.all_gather(w_out, "dp", axis=1, tiled=True)
    inner_full = lax.all_gather(w_in, "dp", axis=1, tiled=True)
    down_full = lax.all_gather(w_down, "dp", axis=1, tiled=True)
    outer_rel = group(outer_own)
    g_rel = jnp.stack(group(to_owners(out_grad)))

    place = jnp.arange(tokens, dtype=jnp.int32)
    place = jnp.where(place >= first_len, place - first_len, place).astype(F32)
    freq_index = jnp.arange(LANES, dtype=jnp.int32) % (HEAD_DIM // 2)
    freqs = jnp.exp(freq_index.astype(F32) * (-2.0 * math.log(theta_base) / HEAD_DIM))
    angles = place[:, None] * freqs[None, :]
    first_half = jnp.arange(LANES) % HEAD_DIM < HEAD_DIM // 2
    cos = jnp.cos(angles)
    sin = jnp.sin(angles) * jnp.where(first_half, -1.0, 1.0)[None, :]

    q, k, v, n1 = qkv_call(scalars, x_rel, gain_one, qkv_full, cos, sin)
    o_chunks, q2_chunks, peaks, sums = [], [], [], []
    held = ()
    for chunk in range(mp_count):
        o, q2, top = attend_forward(scalars, q, k, v, chunk, rows)
        o_chunks.append(o)
        q2_chunks.append(q2)
        peaks.append(top)
        *held, keep, send = mlp_call(
            scalars, x_rel, g_rel, group(o), outer_rel, gain_two, inner_full, down_full, chunk, held
        )
        sums.append((keep, send))
    a_rel, n2, act, dgate, dup = held
    flat = lambda values: values.reshape(tokens, values.shape[2])

    held = ()
    gain_parts = []
    for chunk in range(mp_count):
        keep, send = sums[chunk]
        mine = (keep + swap_bit(send, "mp", 1).astype(F32)).astype(BF16)
        own, gain_part = resid_call(
            scalars, mine, swap_bit(mine, "mp", 2), x_rel, a_rel, g_rel, gain_two, chunk
        )
        gain_parts.append(gain_part)
        held = head_grad_call(
            scalars, own, swap_bit(own, "mp", 1), outer_own, o_chunks[chunk], chunk, tokens, held
        )
    do, da = held
    mlp_gain_part = 0.5 * jnp.sum(jnp.stack(gain_parts), axis=(0, 1))

    g_flat, n2_flat, act_flat = flat(g_rel), flat(n2), flat(act)
    units = act_flat.shape[1]
    shards = width // dp_count
    down_grad = halve(dot(act_flat, g_flat, 0, 0).reshape(units, dp_count, shards), 1, "dp")
    inner_grad = jnp.stack([dot(n2_flat, flat(dgate), 0, 0), dot(n2_flat, flat(dup), 0, 0)])
    inner_grad = halve(inner_grad.reshape(2, dp_count, shards, units), 1, "dp")
    o_all = jnp.concatenate(o_chunks, axis=0)
    outer_grad = dot(o_all, da, 0, 0).reshape(o_all.shape[1], dp_count, shards)
    outer_grad = halve(outer_grad, 1, "dp")

    def sum_lanes(keep, send):
        both = keep.astype(F32) + swap_bit(send, "mp", 1).astype(F32)
        return both[:rows], swap_bit(both[rows:].astype(BF16), "mp", 2)

    def down_part(one, two):
        pair = jnp.concatenate([act[one], act[two]], axis=0)
        return dot(pair, down_full, 1, 0).astype(BF16)

    mlp_own, mlp_other = sum_lanes(down_part(0, 2), down_part(1, 3))
    after = x_rel[0].astype(F32) + a_rel[0].astype(F32)
    output = from_owners((after + (mlp_own + mlp_other.astype(F32))).astype(BF16))

    head_peaks = jnp.max(jnp.stack(peaks), axis=(0, 1, 3, 4)) * score_scale
    for bit in bits_of(dp_count):
        head_peaks = jnp.maximum(head_peaks, swap_bit(head_peaks, "dp", bit))
    factor = jnp.sqrt(clip_limit / jnp.maximum(head_peaks, clip_limit))
    column_factor = jnp.repeat(factor, HEAD_DIM)
    scaling = jnp.stack([column_factor, column_factor, jnp.ones_like(column_factor)])[:, None, :]
    clipped = (w_qkv.astype(F32) * scaling).astype(BF16)

    dproj = attend_backward(scalars, jnp.concatenate(q2_chunks, axis=1), k, v, do, cos, sin)
    send = dn_call(scalars, dproj, qkv_full, 1, rows)
    keep = dn_call(scalars, dproj, qkv_full, 0, rows)
    proj_grad = jnp.einsum("td,ktc->kdc", n1, dproj, preferred_element_type=F32)
    proj_grad = halve(proj_grad.reshape(3, dp_count, shards, dproj.shape[2]), 1, "dp")
    dn_own, dn_other = sum_lanes(keep, send)
    dx, attn_gain_part = last_call(scalars, dn_own, dn_other, x_rel, da, gain_one)
    input_grad = from_owners(dx)
    gain_grads = jnp.stack([jnp.sum(attn_gain_part, axis=(0, 1)), mlp_gain_part])
    gain_grads = gather_sum(gain_grads, ("dp", "mp"))
    return (
        output,
        input_grad,
        gain_grads[0],
        gain_grads[1],
        proj_grad,
        outer_grad,
        inner_grad,
        down_grad,
        clipped,
    )


def solution(mesh):
    in_specs = (
        P(("dp", "mp"), None),
        P(("dp", "mp"), None),
        P(),
        P(),
        P(("dp", "mp")),
        P(("dp", "mp")),
        P(None, "dp", "mp"),
        P("mp", "dp"),
        P(None, "dp", "mp"),
        P("mp", "dp"),
    )
    out_specs = (
        P(("dp", "mp"), None),
        P(("dp", "mp"), None),
        P(("dp", "mp")),
        P(("dp", "mp")),
        P(None, "dp", "mp"),
        P("mp", "dp"),
        P(None, "dp", "mp"),
        P("mp", "dp"),
        P(None, "dp", "mp"),
    )
    return jax.shard_map(local, mesh=mesh, in_specs=in_specs, out_specs=out_specs, check_vma=False)
```

time: 1490 us -> 693 us (0.47)
  waiting for transfers between devices: 690 us -> 135 us
  matrix products: 264 us -> 51.5 us
  Pallas kernels: 0 us -> 190 us
  blocking collectives: 191 us -> 58.3 us
  other arithmetic: 165 us -> 40.3 us
  starting transfers between devices: 18.1 us -> 76.7 us
  local copies, waits for them, and re-layouts: 137 us -> 121 us
    reduce_scatter x8 -> x0, waiting for transfers between devices: 476 us -> none  [the longest x4 241 us: group_sum(): return lax.psum_scatter(values, 'mp', scatter_dimension=0, tiled=True)]
    dot_general x40 -> x17, matrix products: 264 us -> 51.5 us  [the longest x16 46.4 us: dot(): lax.dot_general(left, right, (((left_dim,), (right_dim,)), ((), ())), pre...]
    pallas_call x0 -> x21, Pallas kernels: none -> 190 us  [the longest x1 63.9 us: attend_backward(): pl.pallas_call(functools.partial(bwd_kernel, q_rows, k_rows), out_shape=j...]
    all_gather x7 -> x3, waiting for transfers between devices: 161 us -> 0.01 us  [the longest x1 0.01 us: local(): qkv_full = lax.all_gather(w_qkv, 'dp', axis=1, tiled=True)]
    ppermute x0 -> x62, waiting for transfers between devices: none -> 106 us  [swap_bit(): return lax.ppermute(values, axis_name, [(i, i ^ bit) for i in range(count)])]
    unnamed x2 -> x0, blocking collectives: 82.9 us -> none
    convert_element_type x26 -> x6, other arithmetic: 66.5 us -> 7.13 us  [the longest x4 5.76 us: local(): mine = (keep + swap_bit(send, 'mp', 1).astype(F32)).astype(BF16)]
    ppermute x0 -> x62, starting transfers between devices: none -> 57.3 us  [swap_bit(): return lax.ppermute(values, axis_name, [(i, i ^ bit) for i in range(count)])]
  transfers between devices with their start and end apart: 18 -> 69, of which waited for: 15 -> 20; matrix products, arithmetic and copies ran while one was open for 9% -> 22% of each run, Pallas kernels for 0% -> 26%
where the time goes in v1:
time: 693 us; the launch traced here: 687 us
  Pallas kernels  190 us (27%)
  waiting for transfers between devices  135 us (19%)
  local copies, waits for them, and re-layouts  121 us (17%)
  starting transfers between devices  76.7 us (11%)
  blocking collectives  58.3 us (8%)
  matrix products  51.5 us (7%)
  other arithmetic  40.3 us (6%)
  between operations  15.2 us (2%)
    ppermute x62, waiting for transfers between devices, swap_bit(): return lax.ppermute(values, axis_name, [(i, i ^ bit) for i in range(count)])  106 us
    pallas_call x1, Pallas kernels, attend_backward(): pl.pallas_call(functools.partial(bwd_kernel, q_rows, k_rows), out_shape=j...  63.9 us
    unnamed x178, local copies, waits for them, and re-layouts  62.5 us
    all_gather x1, blocking collectives, local(): outer_own = lax.all_gather(w_out, 'dp', axis=1, tiled=True)  58.3 us
    ppermute x62, starting transfers between devices, swap_bit(): return lax.ppermute(values, axis_name, [(i, i ^ bit) for i in range(count)])  57.3 us
    pallas_call x4, Pallas kernels, mlp_call(): pl.pallas_call(mlp_kernel, out_shape=(wide_out, wide_out, narrow_out, nar...  50.6 us
    dot_general x16, matrix products, dot(): lax.dot_general(left, right, (((left_dim,), (right_dim,)), ((), ())), pre...  46.4 us
    pallas_call x4, Pallas kernels, attend_forward(): pl.pallas_call(functools.partial(fwd_kernel, chunk * rows, q_rows, k_rows...  31 us
  transfers between devices with their start and end apart: 69, of which 20 were waited for; matrix products, arithmetic and copies ran while one was open for 22% of the time, Pallas kernels for 26%

profile of v1, /device:TPU:0, one launch (start us, length us, event | category | flops | bytes accessed | tf_op | source)
XLA Modules:
  0.0 687.4 jit_solution(2984138926272082268)
XLA Ops:
  12.0 7.3 %all-to-all-start = ((bf16[8,64,1024]{2,1,0:T(8,128)(2,1)}), bf16[8,64,1024]{2,1,0:T(8,128)(2,1)S(1)}, u32[]{:S(2)}, u32[]{:S(2)}) async-start(bf16[8,64,1024]{2,1,0:T(8,128)(2,1)} %bitcast.1), calls=%async_computation | async-start | bytes 2097152 | tf_op jit(solution)/shard_map/all_to_all | solution.py:656
  19.5 58.3 %all_gather.13.w0.w_ref = bf16[256,1024]{1,0:T(8,128)(2,1)S(1)} all-gather(bf16[256,128]{1,0:T(8,128)(2,1)S(1)} %copy-done.78), channel_id=1, replica_groups=mesh['dp'=8,'mp'=4] {'dp'}, dimensions={1}, use_global_device_ids=true | all-gather | bytes 589824 | tf_op jit(solution)/shard_map/all_gather | solution.py:673
  80.9 3.0 convolution_convert_fusion.6
  83.9 4.0 all-to-all-start.1
  98.5 27.0 %all-to-all-done.1 = bf16[8,64,1024]{2,1,0:T(8,128)(2,1)S(1)} async-done(((bf16[8,64,1024]{2,1,0:T(8,128)(2,1)}), bf16[8,64,1024]{2,1,0:T(8,128)(2,1)S(1)}, u32[]{:S(2)}, u32[]{:S(2)}) %all-to-all-start.1) | async-done | bytes 1048608 | tf_op jit(solution)/shard_map/all_to_all | solution.py:656
  128.0 5.0 fusion.18
  133.9 3.7 collective-permute-done.10
  138.3 8.3 %collective-permute-done.4 = bf16[512,1024]{1,0:T(8,128)(2,1)} collective-permute-done((bf16[512,1024]{1,0:T(8,128)(2,1)}, bf16[512,1024]{1,0:T(8,128)(2,1)}, u32[]{:S(2)}, u32[]{:S(2)}) %collective-permute-start.4) | collective-permute-done | bytes 1048608 | tf_op jit(solution)/shard_map/ppermute | solution.py:56
  146.6 3.8 pad_maximum_fusion.x_ref.refs_2_
  153.0 10.9 %qkv.1 = (bf16[4,2048,128]{2,1,0:T(8,128)(2,1)S(1)}, bf16[4,2048,128]{2,1,0:T(8,128)(2,1)S(1)}, bf16[4,2048,128]{2,1,0:T(8,128)(2,1)S(1)}, bf16[2048,1024]{1,0:T(8,128)(2,1)S(1)}) custom-call(s32[3]{0:T(128)S(1)} %pad_add_fusion.s_ref, bf16[4,512,1024]{2,1,0:T(8,128)(2,1)} %pad_maximum_fusion.x_ref.refs_2_, ...), custom_call_target="tpu_custom_call" | custom-call | flops 3221225472 | bytes 20971520 | tf_op jit(solution)/shard_map/qkv/pallas_call | solution.py:108
  165.9 6.3 attend_forward.7
  172.7 7.5 %attend_forward.4 = (bf16[512,256]{1,0:T(8,128)(2,1)S(1)}, bf16[4,512,128]{2,1,0:T(8,128)(2,1)S(1)}, f32[2,4,8,128]{3,2,1,0:T(8,128)S(1)}) custom-call(s32[3]{0:T(128)S(1)} %pad_add_fusion.s_ref, bf16[4,2048,128]{2,1,0:T(8,128)(2,1)S(1)} %get-tuple-element.71.q_ref, bf16[4,2048,128]{2,1,0:T(8,128)(2,1)S(1)} %get-tuple-element.72.k_ref, ...), custom_call_target="tpu_custom_call" | custom-call | flops 4294967296 | bytes 6291456 | tf_op jit(solution)/shard_map/attend_forward/pallas_call | solution.py:202
  185.1 8.1 %attend_forward.5 = (bf16[512,256]{1,0:T(8,128)(2,1)}, bf16[4,512,128]{2,1,0:T(8,128)(2,1)S(1)}, f32[2,4,8,128]{3,2,1,0:T(8,128)S(1)}) custom-call(s32[3]{0:T(128)S(1)} %pad_add_fusion.s_ref, bf16[4,2048,128]{2,1,0:T(8,128)(2,1)S(1)} %copy-done.58, bf16[4,2048,128]{2,1,0:T(8,128)(2,1)S(1)} %copy-done.52, bf16[4,2048,128]{2,1,0:T(8,128)(2,1)S(1)} %copy-done.55), custom_call_target="tpu_custom_call" | custom-call | flops 4294967296 | bytes 6291456 | tf_op jit(solution)/shard_map/attend_forward/pallas_call | solution.py:202
  199.1 9.0 %attend_forward.6 = (bf16[512,256]{1,0:T(8,128)(2,1)}, bf16[4,512,128]{2,1,0:T(8,128)(2,1)S(1)}, f32[2,4,8,128]{3,2,1,0:T(8,128)S(1)}) custom-call(s32[3]{0:T(128)S(1)} %pad_add_fusion.s_ref, bf16[4,2048,128]{2,1,0:T(8,128)(2,1)S(1)} %copy-done.59, bf16[4,2048,128]{2,1,0:T(8,128)(2,1)S(1)} %copy-done.53, bf16[4,2048,128]{2,1,0:T(8,128)(2,1)S(1)} %copy-done.56), custom_call_target="tpu_custom_call" | custom-call | flops 4294967296 | bytes 6291456 | tf_op jit(solution)/shard_map/attend_forward/pallas_call | solution.py:202
  213.4 4.0 pad_maximum_fusion.1.g_ref
  217.4 6.5 copy.83
  223.9 10.0 %collective-permute-start.59 = (f32[4]{0:T(128)S(1)}, f32[4]{0:T(128)S(1)}, u32[]{:S(2)}, u32[]{:S(2)}) collective-permute-start(f32[4]{0:T(128)S(1)} %maximum_multiply_fusion), channel_id=1, source_target_pairs={{0,4},{4,0},{8,12},{12,8},{16,20},{20,16},{24,28},{28,24},{1,5},{5... | collective-permute-start | bytes 56 | tf_op jit(solution)/shard_map/ppermute | solution.py:56
  235.4 3.5 collective-permute-done.60
  239.0 4.4 collective-permute-done.61
  246.9 4.4 collective-permute-done.21.o2
  256.9 12.7 %mlp.4 = (bf16[4,512,1024]{2,1,0:T(8,128)(2,1)}, bf16[4,512,1024]{2,1,0:T(8,128)(2,1)}, bf16[4,512,656]{2,1,0:T(8,128)(2,1)}, bf16[4,512,656]{2,1,0:T(8,128)(2,1...) custom-call(s32[3]{0:T(128)S(1)} %pad_add_fusion.s_ref, ...), custom_call_target="tpu_custom_call" | custom-call | flops 4513071104 | bytes 16777216 | tf_op jit(solution)/shard_map/mlp/pallas_call | solution.py:377
  271.4 12.7 %mlp.5 = (bf16[4,512,1024]{2,1,0:T(8,128)(2,1)}, bf16[4,512,1024]{2,1,0:T(8,128)(2,1)}, bf16[4,512,656]{2,1,0:T(8,128)(2,1)}, bf16[4,512,656]{2,1,0:T(8,128)(2,1...) custom-call(s32[3]{0:T(128)S(1)} %pad_add_fusion.s_ref, ...), custom_call_target="tpu_custom_call", output_to_operand_aliasing={{0}: (14, {}), {1}: (15, {}), {2}: (16, {}), {3}: (17, {}),... | custom-call | flops 4513071104 | bytes 16777216 | tf_op jit(solution)/shard_map/mlp/pallas_call | solution.py:377
  285.1 12.6 %mlp.6 = (bf16[4,512,1024]{2,1,0:T(8,128)(2,1)}, bf16[4,512,1024]{2,1,0:T(8,128)(2,1)}, bf16[4,512,656]{2,1,0:T(8,128)(2,1)}, bf16[4,512,656]{2,1,0:T(8,128)(2,1...) custom-call(s32[3]{0:T(128)S(1)} %pad_add_fusion.s_ref, ...), custom_call_target="tpu_custom_call", output_to_operand_aliasing={{0}: (14, {}), {1}: (15, {}), {2}: (16, {}), {3}: (17, {}),... | custom-call | flops 4513071104 | bytes 16777216 | tf_op jit(solution)/shard_map/mlp/pallas_call | solution.py:377
  298.7 12.6 %mlp.7 = (bf16[4,512,1024]{2,1,0:T(8,128)(2,1)}, bf16[4,512,1024]{2,1,0:T(8,128)(2,1)}, bf16[4,512,656]{2,1,0:T(8,128)(2,1)}, bf16[4,512,656]{2,1,0:T(8,128)(2,1...) custom-call(s32[3]{0:T(128)S(1)} %pad_add_fusion.s_ref, ...), custom_call_target="tpu_custom_call", output_to_operand_aliasing={{0}: (14, {}), {1}: (15, {}), {2}: (16, {}), {3}: (17, {}),... | custom-call | flops 4513071104 | bytes 16777216 | tf_op jit(solution)/shard_map/mlp/pallas_call | solution.py:377
  311.3 4.0 slice_bitcast_fusion.3
  316.3 6.4 convolution_bitcast_fusion.1
  322.7 5.1 stack.96
  327.9 3.9 copy_dynamic-update-slice_fusion.1
  331.8 6.6 convolution_bitcast_fusion
  338.4 3.5 fusion.56
  343.5 5.1 stack.97
  350.7 3.8 copy_dynamic-update-slice_fusion
  354.5 3.2 fusion.13
  361.0 5.6 collective-permute-done.56
  372.4 3.6 collective-permute-done.57
  377.6 3.1 convolution_convert_fusion
  403.0 3.3 resid.6
  416.8 3.0 head_grad.4
  419.8 3.4 head_grad.5
  425.1 3.0 head_grad.6
  428.2 3.4 head_grad.7
  435.0 63.9 %attend_backward.1.p_ref = bf16[3,2048,256]{2,1,0:T(8,128)(2,1)} custom-call(s32[3]{0:T(128)S(1)} %pad_add_fusion.s_ref, bf16[4,2048,128]{2,1,0:T(8,128)(2,1)S(1)} %copy-done.22, bf16[4,2048,128]{2,1,0:T(8,128)(2,1)} %copy-done.51, bf16[4,2048,128]{2,1,0:T(8,128)(2,1)} %copy-done.54, bf16[4,2048,128]{2,1,0:T(8,128)(2,1)} %copy-done.14, ...), custom_call_target="tpu_custom_call" | custom-call | flops 42949672960 | bytes 14680064 | tf_op jit(solution)/shard_map/attend_backward/pallas_call | solution.py:300
  500.8 4.1 dn.3
  505.2 5.1 fusion.4
  510.4 5.6 reshape_reshape.8
  516.0 4.7 fusion.20
  522.8 4.6 constant_dynamic-slice_fusion.3
  527.8 5.0 copy.75
  532.9 11.0 %collective-permute-start.50 = (bf16[256,4,128]{2,0,1:T(8,128)(2,1)S(1)}, bf16[256,4,128]{2,0,1:T(8,128)(2,1)}, u32[]{:S(2)}, u32[]{:S(2)}) collective-permute-start(bf16[256,4,128]{2,0,1:T(8,128)(2,1)S(1)} %bitcast.156), channel_id=1, source_target_pairs={{0,4},{4,0},{8,12},{12,8},{16,20},{20,16},{24,28},{28,24},{1,5},{5... | collective-permute-start | bytes 786440 | tf_op jit(solution)/shard_map/ppermute | solution.py:56
  543.8 4.5 constant_dynamic-slice_fusion.2
  548.3 4.6 copy.93
  556.4 3.2 dn.2
  560.1 3.2 collective-permute-start.52
  563.3 3.5 convert_add_fusion.1
  575.1 10.7 %collective-permute-done.55 = bf16[2,1,128,656]{2,3,1,0:T(8,128)(2,1)S(1)} collective-permute-done((bf16[2,1,128,656]{2,3,1,0:T(8,128)(2,1)S(1)}, bf16[2,1,128,656]{2,3,1,0:T(8,128)(2,1)S(1)}, u32[]{:S(2)}, u32[]{:S(2)}) %collective-permute-start.55) | collective-permute-done | bytes 335904 | tf_op jit(solution)/shard_map/ppermute | solution.py:56
  586.7 6.5 collective-permute-done.27
  593.2 3.4 convolution_convert_fusion.4
  596.6 4.2 all-to-all-start.2
  605.3 9.0 %collective-permute-done.41.refs_1_ = bf16[512,1024]{1,0:T(8,128)(2,1)S(1)} collective-permute-done((bf16[512,1024]{1,0:T(8,128)(2,1)}, bf16[512,1024]{1,0:T(8,128)(2,1)S(1)}, u32[]{:S(2)}, u32[]{:S(2)}) %collective-permute-start.41) | collective-permute-done | bytes 1048608 | tf_op jit(solution)/shard_map/ppermute | solution.py:56
  621.5 3.3 collective-permute-done.42
  625.0 8.2 %collective-permute-done.48 = bf16[3,2,128,256]{3,2,1,0:T(8,128)(2,1)S(1)} collective-permute-done((bf16[3,2,128,256]{3,2,1,0:T(8,128)(2,1)S(1)}, bf16[3,2,128,256]{3,2,1,0:T(8,128)(2,1)S(1)}, u32[]{:S(2)}, u32[]{:S(2)}) %collective-permute-start.48) | collective-permute-done | bytes 393248 | tf_op jit(solution)/shard_map/ppermute | solution.py:56
  636.6 3.8 all-to-all-start.3
  644.2 30.2 %collective-permute-done.49 = bf16[3,1,128,256]{3,2,1,0:T(8,128)(2,1)S(1)} collective-permute-done((bf16[3,1,128,256]{3,2,1,0:T(8,128)(2,1)S(1)}, bf16[3,1,128,256]{3,2,1,0:T(8,128)(2,1)S(1)}, u32[]{:S(2)}, u32[]{:S(2)}) %collective-permute-start.49) | collective-permute-done | bytes 196640 | tf_op jit(solution)/shard_map/ppermute | solution.py:56
  675.8 3.0 convolution_convert_fusion.3
  (392 shorter events, 151.3 us)
Async XLA Ops:
  7.2 143.2 %all-gather.4.cloned.1.call-start = ((), (), s32[]{:S(2)}) async-start(), calls=%async_computation.4 | async-start | bytes 1769472 | tf_op jit(solution)/shard_map/all_gather | solution.py:672
  8.0 246.7 %all-gather.8.cloned.1.call-start = ((), (), s32[]{:S(2)}) async-start(), calls=%async_computation.6 | async-start | bytes 1511424 | tf_op jit(solution)/shard_map/all_gather | solution.py:675
  12.0 71.8 %all-to-all-start = ((bf16[8,64,1024]{2,1,0:T(8,128)(2,1)}), bf16[8,64,1024]{2,1,0:T(8,128)(2,1)S(1)}, u32[]{:S(2)}, u32[]{:S(2)}) async-start(bf16[8,64,1024]{2,1,0:T(8,128)(2,1)} %bitcast.1), calls=%async_computation | async-start | bytes 2097152 | tf_op jit(solution)/shard_map/all_to_all | solution.py:656
  19.3 235.3 %all-gather.6.cloned.1.call-start = ((), (), s32[]{:S(2)}) async-start(), calls=%async_computation.5 | async-start | bytes 3538944 | tf_op jit(solution)/shard_map/all_gather | solution.py:674
  19.4 69.4 %collective-permute-start.6 = (f32[2,32]{1,0:T(2,128)S(1)}, f32[2,32]{1,0:T(2,128)S(1)}, u32[]{:S(2)}, u32[]{:S(2)}) collective-permute-start(f32[2,32]{1,0:T(2,128)S(1)} %pad_maximum_fusion.7), channel_id=1, source_target_pairs={{0,1},{1,0},{2,3},{3,2},{4,5},{5,4},{6,7},{7,6},{8,9},{9,8},{10,11... | collective-permute-start | bytes 776 | tf_op jit(solution)/shard_map/ppermute | solution.py:56
  77.8 59.9 %collective-permute-start.15 = (bf16[256,1024]{1,0:T(8,128)(2,1)S(1)}, bf16[256,1024]{1,0:T(8,128)(2,1)S(1)}, u32[]{:S(2)}, u32[]{:S(2)}) collective-permute-start(bf16[256,1024]{1,0:T(8,128)(2,1)S(1)} %all_gather.13.w0.w_ref), channel_id=1, source_target_pairs={{0,2},{1,3},{2,0},{3,1},{4,6},{5,7},{6,4},{7,5},{8,10},{9,11},{10,... | collective-permute-start | bytes 1572872 | tf_op jit(solution)/shard_map/ppermute | solution.py:56
  83.9 41.6 %all-to-all-start.1 = ((bf16[8,64,1024]{2,1,0:T(8,128)(2,1)}), bf16[8,64,1024]{2,1,0:T(8,128)(2,1)S(1)}, u32[]{:S(2)}, u32[]{:S(2)}) async-start(bf16[8,64,1024]{2,1,0:T(8,128)(2,1)} %bitcast.9), calls=%async_computation.1 | async-start | bytes 2097152 | tf_op jit(solution)/shard_map/all_to_all | solution.py:656
  90.9 37.1 %collective-permute-start.1 = (bf16[512,1024]{1,0:T(8,128)(2,1)}, bf16[512,1024]{1,0:T(8,128)(2,1)}, u32[]{:S(2)}, u32[]{:S(2)}) collective-permute-start(bf16[512,1024]{1,0:T(8,128)(2,1)} %convolution_convert_fusion.7), channel_id=1, source_target_pairs={{0,2},{1,3},{2,0},{3,1},{4,6},{5,7},{6,4},{7,5},{8,10},{9,11},{10,... | collective-permute-start | bytes 3145736 | tf_op jit(solution)/shard_map/ppermute | solution.py:56
  96.4 36.5 %collective-permute-start.9 = (f32[2,256]{1,0:T(2,128)S(1)}, f32[2,256]{1,0:T(2,128)S(1)}, u32[]{:S(2)}, u32[]{:S(2)}) collective-permute-start(f32[2,256]{1,0:T(2,128)S(1)} %pad_maximum_fusion.6), channel_id=1, source_target_pairs={{0,8},{4,12},{8,0},{12,4},{16,24},{20,28},{24,16},{28,20},{1,9},{5... | collective-permute-start | bytes 6152 | tf_op jit(solution)/shard_map/ppermute | solution.py:56
  98.5 39.7 %collective-permute-start = (bf16[512,1024]{1,0:T(8,128)(2,1)}, bf16[512,1024]{1,0:T(8,128)(2,1)}, u32[]{:S(2)}, u32[]{:S(2)}) collective-permute-start(bf16[512,1024]{1,0:T(8,128)(2,1)} %convolution_convert_fusion.7), channel_id=1, source_target_pairs={{0,1},{1,0},{2,3},{3,2},{4,5},{5,4},{6,7},{7,6},{8,9},{9,8},{10,11... | collective-permute-start | bytes 3145736 | tf_op jit(solution)/shard_map/ppermute | solution.py:56
  127.2 19.4 %collective-permute-start.4 = (bf16[512,1024]{1,0:T(8,128)(2,1)}, bf16[512,1024]{1,0:T(8,128)(2,1)}, u32[]{:S(2)}, u32[]{:S(2)}) collective-permute-start(bf16[512,1024]{1,0:T(8,128)(2,1)} %convolution_convert_fusion.5), channel_id=1, source_target_pairs={{0,2},{1,3},{2,0},{3,1},{4,6},{5,7},{6,4},{7,5},{8,10},{9,11},{10,... | collective-permute-start | bytes 3145736 | tf_op jit(solution)/shard_map/ppermute | solution.py:56
  128.0 18.6 %collective-permute-start.2 = (bf16[512,1024]{1,0:T(8,128)(2,1)}, bf16[512,1024]{1,0:T(8,128)(2,1)}, u32[]{:S(2)}, u32[]{:S(2)}) collective-permute-start(bf16[512,1024]{1,0:T(8,128)(2,1)} %collective-permute-done.1), channel_id=1, source_target_pairs={{0,1},{1,0},{2,3},{3,2},{4,5},{5,4},{6,7},{7,6},{8,9},{9,8},{10,11... | collective-permute-start | bytes 3145736 | tf_op jit(solution)/shard_map/ppermute | solution.py:56
  133.0 4.6 collective-permute-start.10
  137.6 108.4 %collective-permute-start.14 = (bf16[256,1024]{1,0:T(8,128)(2,1)S(1)}, bf16[256,1024]{1,0:T(8,128)(2,1)S(1)}, u32[]{:S(2)}, u32[]{:S(2)}) collective-permute-start(bf16[256,1024]{1,0:T(8,128)(2,1)S(1)} %all_gather.13.w0.w_ref), channel_id=1, source_target_pairs={{0,1},{1,0},{2,3},{3,2},{4,5},{5,4},{6,7},{7,6},{8,9},{9,8},{10,11... | collective-permute-start | bytes 1572872 | tf_op jit(solution)/shard_map/ppermute | solution.py:56
  137.6 108.9 %collective-permute-start.16 = (bf16[256,1024]{1,0:T(8,128)(2,1)S(1)}, bf16[256,1024]{1,0:T(8,128)(2,1)S(1)}, u32[]{:S(2)}, u32[]{:S(2)}) collective-permute-start(bf16[256,1024]{1,0:T(8,128)(2,1)S(1)} %collective-permute-done.15.w2), channel_id=1, source_target_pairs={{0,1},{1,0},{2,3},{3,2},{4,5},{5,4},{6,7},{7,6},{8,9},{9,8},{10,11... | collective-permute-start | bytes 1572872 | tf_op jit(solution)/shard_map/ppermute | solution.py:56
  138.2 73.5 %collective-permute-start.3 = (bf16[512,1024]{1,0:T(8,128)(2,1)}, bf16[512,1024]{1,0:T(8,128)(2,1)}, u32[]{:S(2)}, u32[]{:S(2)}) collective-permute-start(bf16[512,1024]{1,0:T(8,128)(2,1)} %convolution_convert_fusion.5), channel_id=1, source_target_pairs={{0,1},{1,0},{2,3},{3,2},{4,5},{5,4},{6,7},{7,6},{8,9},{9,8},{10,11... | collective-permute-start | bytes 3145736 | tf_op jit(solution)/shard_map/ppermute | solution.py:56
  146.6 66.8 %collective-permute-start.5 = (bf16[512,1024]{1,0:T(8,128)(2,1)}, bf16[512,1024]{1,0:T(8,128)(2,1)}, u32[]{:S(2)}, u32[]{:S(2)}) collective-permute-start(bf16[512,1024]{1,0:T(8,128)(2,1)} %collective-permute-done.4), channel_id=1, source_target_pairs={{0,1},{1,0},{2,3},{3,2},{4,5},{5,4},{6,7},{7,6},{8,9},{9,8},{10,11... | collective-permute-start | bytes 3145736 | tf_op jit(solution)/shard_map/ppermute | solution.py:56
  172.2 79.1 %collective-permute-start.23 = (bf16[512,256]{1,0:T(8,128)(2,1)}, bf16[512,256]{1,0:T(8,128)(2,1)}, u32[]{:S(2)}, u32[]{:S(2)}) collective-permute-start(bf16[512,256]{1,0:T(8,128)(2,1)} %get-tuple-element.77.o0.o_ref), channel_id=1, source_target_pairs={{0,1},{1,0},{2,3},{3,2},{4,5},{5,4},{6,7},{7,6},{8,9},{9,8},{10,11... | collective-permute-start | bytes 786440 | tf_op jit(solution)/shard_map/ppermute | solution.py:56
  211.7 33.5 %collective-permute-start.24 = (bf16[512,256]{1,0:T(8,128)(2,1)}, bf16[512,256]{1,0:T(8,128)(2,1)}, u32[]{:S(2)}, u32[]{:S(2)}) collective-permute-start(bf16[512,256]{1,0:T(8,128)(2,1)} %get-tuple-element.77.o0.o_ref), channel_id=1, source_target_pairs={{0,2},{1,3},{2,0},{3,1},{4,6},{5,7},{6,4},{7,5},{8,10},{9,11},{10,... | collective-permute-start | bytes 786440 | tf_op jit(solution)/shard_map/ppermute | solution.py:56
  223.9 11.5 %collective-permute-start.59 = (f32[4]{0:T(128)S(1)}, f32[4]{0:T(128)S(1)}, u32[]{:S(2)}, u32[]{:S(2)}) collective-permute-start(f32[4]{0:T(128)S(1)} %maximum_multiply_fusion), channel_id=1, source_target_pairs={{0,4},{4,0},{8,12},{12,8},{16,20},{20,16},{24,28},{28,24},{1,5},{5... | collective-permute-start | bytes 56 | tf_op jit(solution)/shard_map/ppermute | solution.py:56
  243.4 7.9 %collective-permute-start.21 = (bf16[512,256]{1,0:T(8,128)(2,1)}, bf16[512,256]{1,0:T(8,128)(2,1)S(1)}, u32[]{:S(2)}, u32[]{:S(2)}) collective-permute-start(bf16[512,256]{1,0:T(8,128)(2,1)} %get-tuple-element.76.o0.o_ref), channel_id=1, source_target_pairs={{0,2},{1,3},{2,0},{3,1},{4,6},{5,7},{6,4},{7,5},{8,10},{9,11},{10,... | collective-permute-start | bytes 786440 | tf_op jit(solution)/shard_map/ppermute | solution.py:56
  245.2 8.5 %collective-permute-start.25 = (bf16[512,256]{1,0:T(8,128)(2,1)}, bf16[512,256]{1,0:T(8,128)(2,1)S(1)}, u32[]{:S(2)}, u32[]{:S(2)}) collective-permute-start(bf16[512,256]{1,0:T(8,128)(2,1)} %collective-permute-done.24.o2), channel_id=1, source_target_pairs={{0,1},{1,0},{2,3},{3,2},{4,5},{5,4},{6,7},{7,6},{8,9},{9,8},{10,11... | collective-permute-start | bytes 786440 | tf_op jit(solution)/shard_map/ppermute | solution.py:56
  246.0 52.7 %collective-permute-start.11 = (bf16[512,256]{1,0:T(8,128)(2,1)S(1)}, bf16[512,256]{1,0:T(8,128)(2,1)S(1)}, u32[]{:S(2)}, u32[]{:S(2)}) collective-permute-start(bf16[512,256]{1,0:T(8,128)(2,1)S(1)} %get-tuple-element.74.o0.o_ref), channel_id=1, source_target_pairs={{0,1},{1,0},{2,3},{3,2},{4,5},{5,4},{6,7},{7,6},{8,9},{9,8},{10,11... | collective-permute-start | bytes 786440 | tf_op jit(solution)/shard_map/ppermute | solution.py:56
  246.5 24.1 %collective-permute-start.12 = (bf16[512,256]{1,0:T(8,128)(2,1)S(1)}, bf16[512,256]{1,0:T(8,128)(2,1)S(1)}, u32[]{:S(2)}, u32[]{:S(2)}) collective-permute-start(bf16[512,256]{1,0:T(8,128)(2,1)S(1)} %get-tuple-element.74.o0.o_ref), channel_id=1, source_target_pairs={{0,2},{1,3},{2,0},{3,1},{4,6},{5,7},{6,4},{7,5},{8,10},{9,11},{10,... | collective-permute-start | bytes 786440 | tf_op jit(solution)/shard_map/ppermute | solution.py:56
  251.3 19.8 %collective-permute-start.20 = (bf16[512,256]{1,0:T(8,128)(2,1)}, bf16[512,256]{1,0:T(8,128)(2,1)}, u32[]{:S(2)}, u32[]{:S(2)}) collective-permute-start(bf16[512,256]{1,0:T(8,128)(2,1)} %get-tuple-element.76.o0.o_ref), channel_id=1, source_target_pairs={{0,1},{1,0},{2,3},{3,2},{4,5},{5,4},{6,7},{7,6},{8,9},{9,8},{10,11... | collective-permute-start | bytes 786440 | tf_op jit(solution)/shard_map/ppermute | solution.py:56
  251.3 19.6 %collective-permute-start.18 = (bf16[512,256]{1,0:T(8,128)(2,1)}, bf16[512,256]{1,0:T(8,128)(2,1)S(1)}, u32[]{:S(2)}, u32[]{:S(2)}) collective-permute-start(bf16[512,256]{1,0:T(8,128)(2,1)} %get-tuple-element.75.o0.o_ref), channel_id=1, source_target_pairs={{0,2},{1,3},{2,0},{3,1},{4,6},{5,7},{6,4},{7,5},{8,10},{9,11},{10,... | collective-permute-start | bytes 786440 | tf_op jit(solution)/shard_map/ppermute | solution.py:56
  254.4 17.0 %collective-permute-start.22 = (bf16[512,256]{1,0:T(8,128)(2,1)S(1)}, bf16[512,256]{1,0:T(8,128)(2,1)}, u32[]{:S(2)}, u32[]{:S(2)}) collective-permute-start(bf16[512,256]{1,0:T(8,128)(2,1)S(1)} %collective-permute-done.21.o2), channel_id=1, source_target_pairs={{0,1},{1,0},{2,3},{3,2},{4,5},{5,4},{6,7},{7,6},{8,9},{9,8},{10,11... | collective-permute-start | bytes 786440 | tf_op jit(solution)/shard_map/ppermute | solution.py:56
  270.6 14.5 %collective-permute-start.17 = (bf16[512,256]{1,0:T(8,128)(2,1)}, bf16[512,256]{1,0:T(8,128)(2,1)S(1)}, u32[]{:S(2)}, u32[]{:S(2)}) collective-permute-start(bf16[512,256]{1,0:T(8,128)(2,1)} %get-tuple-element.75.o0.o_ref), channel_id=1, source_target_pairs={{0,1},{1,0},{2,3},{3,2},{4,5},{5,4},{6,7},{7,6},{8,9},{9,8},{10,11... | collective-permute-start | bytes 786440 | tf_op jit(solution)/shard_map/ppermute | solution.py:56
  270.9 27.8 %collective-permute-start.13 = (bf16[512,256]{1,0:T(8,128)(2,1)S(1)}, bf16[512,256]{1,0:T(8,128)(2,1)S(1)}, u32[]{:S(2)}, u32[]{:S(2)}) collective-permute-start(bf16[512,256]{1,0:T(8,128)(2,1)S(1)} %collective-permute-done.12.o2), channel_id=1, source_target_pairs={{0,1},{1,0},{2,3},{3,2},{4,5},{5,4},{6,7},{7,6},{8,9},{9,8},{10,11... | collective-permute-start | bytes 786440 | tf_op jit(solution)/shard_map/ppermute | solution.py:56
  271.1 14.0 %collective-permute-start.19 = (bf16[512,256]{1,0:T(8,128)(2,1)S(1)}, bf16[512,256]{1,0:T(8,128)(2,1)S(1)}, u32[]{:S(2)}, u32[]{:S(2)}) collective-permute-start(bf16[512,256]{1,0:T(8,128)(2,1)S(1)} %collective-permute-done.18.o2), channel_id=1, source_target_pairs={{0,1},{1,0},{2,3},{3,2},{4,5},{5,4},{6,7},{7,6},{8,9},{9,8},{10,11... | collective-permute-start | bytes 786440 | tf_op jit(solution)/shard_map/ppermute | solution.py:56
  315.3 42.3 %collective-permute-start.28 = (bf16[256,1024]{1,0:T(8,128)(2,1)S(1)}, bf16[256,1024]{1,0:T(8,128)(2,1)}, u32[]{:S(2)}, u32[]{:S(2)}) collective-permute-start(bf16[256,1024]{1,0:T(8,128)(2,1)S(1)} %get-tuple-element.100), channel_id=1, source_target_pairs={{0,1},{1,0},{2,3},{3,2},{4,5},{5,4},{6,7},{7,6},{8,9},{9,8},{10,11... | collective-permute-start | bytes 1572872 | tf_op jit(solution)/shard_map/ppermute | solution.py:56
  315.4 43.5 %collective-permute-start.31 = (bf16[256,1024]{1,0:T(8,128)(2,1)}, bf16[256,1024]{1,0:T(8,128)(2,1)S(1)}, u32[]{:S(2)}, u32[]{:S(2)}) collective-permute-start(bf16[256,1024]{1,0:T(8,128)(2,1)} %get-tuple-element.103), channel_id=1, source_target_pairs={{0,1},{1,0},{2,3},{3,2},{4,5},{5,4},{6,7},{7,6},{8,9},{9,8},{10,11... | collective-permute-start | bytes 1572872 | tf_op jit(solution)/shard_map/ppermute | solution.py:56
  315.8 51.1 %collective-permute-start.34 = (bf16[256,1024]{1,0:T(8,128)(2,1)}, bf16[256,1024]{1,0:T(8,128)(2,1)}, u32[]{:S(2)}, u32[]{:S(2)}) collective-permute-start(bf16[256,1024]{1,0:T(8,128)(2,1)} %get-tuple-element.106), channel_id=1, source_target_pairs={{0,1},{1,0},{2,3},{3,2},{4,5},{5,4},{6,7},{7,6},{8,9},{9,8},{10,11... | collective-permute-start | bytes 1572872 | tf_op jit(solution)/shard_map/ppermute | solution.py:56
  316.0 52.4 %collective-permute-start.37 = (bf16[256,1024]{1,0:T(8,128)(2,1)}, bf16[256,1024]{1,0:T(8,128)(2,1)}, u32[]{:S(2)}, u32[]{:S(2)}) collective-permute-start(bf16[256,1024]{1,0:T(8,128)(2,1)} %get-tuple-element.109), channel_id=1, source_target_pairs={{0,1},{1,0},{2,3},{3,2},{4,5},{5,4},{6,7},{7,6},{8,9},{9,8},{10,11... | collective-permute-start | bytes 1572872 | tf_op jit(solution)/shard_map/ppermute | solution.py:56
  348.6 18.0 %collective-permute-start.56 = (bf16[656,4,128]{2,0,1:T(8,128)(2,1)S(1)}, bf16[656,4,128]{2,0,1:T(8,128)(2,1)S(1)}, u32[]{:S(2)}, u32[]{:S(2)}) collective-permute-start(bf16[656,4,128]{2,0,1:T(8,128)(2,1)S(1)} %fusion.32), channel_id=1, source_target_pairs={{0,4},{4,0},{8,12},{12,8},{16,20},{20,16},{24,28},{28,24},{1,5},{5... | collective-permute-start | bytes 2015240 | tf_op jit(solution)/shard_map/ppermute | solution.py:56
  357.6 54.8 %collective-permute-start.53 = (bf16[2,4,128,656]{2,3,1,0:T(8,128)(2,1)}, bf16[2,4,128,656]{2,3,1,0:T(8,128)(2,1)}, u32[]{:S(2)}, u32[]{:S(2)}) collective-permute-start(bf16[2,4,128,656]{2,3,1,0:T(8,128)(2,1)} %fusion.13), channel_id=1, source_target_pairs={{0,4},{4,0},{8,12},{12,8},{16,20},{20,16},{24,28},{28,24},{1,5},{5... | collective-permute-start | bytes 4030472 | tf_op jit(solution)/shard_map/ppermute | solution.py:56
  359.0 21.9 %collective-permute-start.29 = (bf16[256,1024]{1,0:T(8,128)(2,1)S(1)}, bf16[256,1024]{1,0:T(8,128)(2,1)S(1)}, u32[]{:S(2)}, u32[]{:S(2)}) collective-permute-start(bf16[256,1024]{1,0:T(8,128)(2,1)S(1)} %add_convert_fusion.3.mine_ref), channel_id=1, source_target_pairs={{0,2},{1,3},{2,0},{3,1},{4,6},{5,7},{6,4},{7,5},{8,10},{9,11},{10,... | collective-permute-start | bytes 1572872 | tf_op jit(solution)/shard_map/ppermute | solution.py:56
  366.6 19.0 %collective-permute-start.32 = (bf16[256,1024]{1,0:T(8,128)(2,1)S(1)}, bf16[256,1024]{1,0:T(8,128)(2,1)}, u32[]{:S(2)}, u32[]{:S(2)}) collective-permute-start(bf16[256,1024]{1,0:T(8,128)(2,1)S(1)} %add_convert_fusion.2.mine_ref), channel_id=1, source_target_pairs={{0,2},{1,3},{2,0},{3,1},{4,6},{5,7},{6,4},{7,5},{8,10},{9,11},{10,... | collective-permute-start | bytes 1572872 | tf_op jit(solution)/shard_map/ppermute | solution.py:56
  366.9 9.0 %collective-permute-start.57 = (bf16[656,2,128]{2,0,1:T(8,128)(2,1)S(1)}, bf16[656,2,128]{2,0,1:T(8,128)(2,1)S(1)}, u32[]{:S(2)}, u32[]{:S(2)}) collective-permute-start(bf16[656,2,128]{2,0,1:T(8,128)(2,1)S(1)} %fusion.42), channel_id=1, source_target_pairs={{0,8},{4,12},{8,0},{12,4},{16,24},{20,28},{24,16},{28,20},{1,9},{5... | collective-permute-start | bytes 1007624 | tf_op jit(solution)/shard_map/ppermute | solution.py:56
  368.4 28.0 %collective-permute-start.35 = (bf16[256,1024]{1,0:T(8,128)(2,1)S(1)}, bf16[256,1024]{1,0:T(8,128)(2,1)}, u32[]{:S(2)}, u32[]{:S(2)}) collective-permute-start(bf16[256,1024]{1,0:T(8,128)(2,1)S(1)} %add_convert_fusion.1.mine_ref), channel_id=1, source_target_pairs={{0,2},{1,3},{2,0},{3,1},{4,6},{5,7},{6,4},{7,5},{8,10},{9,11},{10,... | collective-permute-start | bytes 1572872 | tf_op jit(solution)/shard_map/ppermute | solution.py:56
  376.0 30.6 %collective-permute-start.38 = (bf16[256,1024]{1,0:T(8,128)(2,1)}, bf16[256,1024]{1,0:T(8,128)(2,1)}, u32[]{:S(2)}, u32[]{:S(2)}) collective-permute-start(bf16[256,1024]{1,0:T(8,128)(2,1)} %add_convert_fusion.mine_ref), channel_id=1, source_target_pairs={{0,2},{1,3},{2,0},{3,1},{4,6},{5,7},{6,4},{7,5},{8,10},{9,11},{10,... | collective-permute-start | bytes 1572872 | tf_op jit(solution)/shard_map/ppermute | solution.py:56
  380.9 182.4 %collective-permute-start.26 = (bf16[1024,1024]{1,0:T(8,128)(2,1)}, bf16[1024,1024]{1,0:T(8,128)(2,1)}, u32[]{:S(2)}, u32[]{:S(2)}) collective-permute-start(bf16[1024,1024]{1,0:T(8,128)(2,1)} %convolution_convert_fusion), channel_id=1, source_target_pairs={{0,1},{1,0},{2,3},{3,2},{4,5},{5,4},{6,7},{7,6},{8,9},{9,8},{10,11... | collective-permute-start | bytes 6291464 | tf_op jit(solution)/shard_map/ppermute | solution.py:56
  385.5 24.8 %collective-permute-start.58 = (bf16[656,1,128]{2,0,1:T(8,128)(2,1)S(1)}, bf16[656,1,128]{2,0,1:T(8,128)(2,1)S(1)}, u32[]{:S(2)}, u32[]{:S(2)}) collective-permute-start(bf16[656,1,128]{2,0,1:T(8,128)(2,1)S(1)} %dynamic-slice_convert_fusion.6), channel_id=1, source_target_pairs={{0,16},{4,20},{8,24},{12,28},{16,0},{20,4},{24,8},{28,12},{1,17},{... | collective-permute-start | bytes 503816 | tf_op jit(solution)/shard_map/ppermute | solution.py:56
  396.4 26.8 %collective-permute-start.33 = (bf16[256,1024]{1,0:T(8,128)(2,1)}, bf16[256,1024]{1,0:T(8,128)(2,1)S(1)}, u32[]{:S(2)}, u32[]{:S(2)}) collective-permute-start(bf16[256,1024]{1,0:T(8,128)(2,1)} %copy-done.37), channel_id=1, source_target_pairs={{0,1},{1,0},{2,3},{3,2},{4,5},{5,4},{6,7},{7,6},{8,9},{9,8},{10,11... | collective-permute-start | bytes 1572872 | tf_op jit(solution)/shard_map/ppermute | solution.py:56
  406.6 13.2 %collective-permute-start.36 = (bf16[256,1024]{1,0:T(8,128)(2,1)}, bf16[256,1024]{1,0:T(8,128)(2,1)}, u32[]{:S(2)}, u32[]{:S(2)}) collective-permute-start(bf16[256,1024]{1,0:T(8,128)(2,1)} %get-tuple-element.107.own_ref), channel_id=1, source_target_pairs={{0,1},{1,0},{2,3},{3,2},{4,5},{5,4},{6,7},{7,6},{8,9},{9,8},{10,11... | collective-permute-start | bytes 1572872 | tf_op jit(solution)/shard_map/ppermute | solution.py:56
  410.3 5.8 collective-permute-start.39
  412.4 15.8 %collective-permute-start.30 = (bf16[256,1024]{1,0:T(8,128)(2,1)}, bf16[256,1024]{1,0:T(8,128)(2,1)S(1)}, u32[]{:S(2)}, u32[]{:S(2)}) collective-permute-start(bf16[256,1024]{1,0:T(8,128)(2,1)} %get-tuple-element.101.own_ref), channel_id=1, source_target_pairs={{0,1},{1,0},{2,3},{3,2},{4,5},{5,4},{6,7},{7,6},{8,9},{9,8},{10,11... | collective-permute-start | bytes 1572872 | tf_op jit(solution)/shard_map/ppermute | solution.py:56
  416.8 150.6 %collective-permute-start.54 = (bf16[2,2,128,656]{2,3,1,0:T(8,128)(2,1)}, bf16[2,2,128,656]{2,3,1,0:T(8,128)(2,1)}, u32[]{:S(2)}, u32[]{:S(2)}) collective-permute-start(bf16[2,2,128,656]{2,3,1,0:T(8,128)(2,1)} %fusion.31), channel_id=1, source_target_pairs={{0,8},{4,12},{8,0},{12,4},{16,24},{20,28},{24,16},{28,20},{1,9},{5... | collective-permute-start | bytes 2015240 | tf_op jit(solution)/shard_map/ppermute | solution.py:56
  505.0 63.8 %collective-permute-start.40 = (bf16[1024,1024]{1,0:T(8,128)(2,1)}, bf16[1024,1024]{1,0:T(8,128)(2,1)}, u32[]{:S(2)}, u32[]{:S(2)}) collective-permute-start(bf16[1024,1024]{1,0:T(8,128)(2,1)} %dn.3), channel_id=1, source_target_pairs={{0,1},{1,0},{2,3},{3,2},{4,5},{5,4},{6,7},{7,6},{8,9},{9,8},{10,11... | collective-permute-start | bytes 6291464 | tf_op jit(solution)/shard_map/ppermute | solution.py:56
  532.9 20.5 %collective-permute-start.50 = (bf16[256,4,128]{2,0,1:T(8,128)(2,1)S(1)}, bf16[256,4,128]{2,0,1:T(8,128)(2,1)}, u32[]{:S(2)}, u32[]{:S(2)}) collective-permute-start(bf16[256,4,128]{2,0,1:T(8,128)(2,1)S(1)} %bitcast.156), channel_id=1, source_target_pairs={{0,4},{4,0},{8,12},{12,8},{16,20},{20,16},{24,28},{28,24},{1,5},{5... | collective-permute-start | bytes 786440 | tf_op jit(solution)/shard_map/ppermute | solution.py:56
  552.9 47.9 %collective-permute-start.47 = (bf16[3,4,128,256]{3,2,1,0:T(8,128)(2,1)}, bf16[3,4,128,256]{3,2,1,0:T(8,128)(2,1)}, u32[]{:S(2)}, u32[]{:S(2)}) collective-permute-start(bf16[3,4,128,256]{3,2,1,0:T(8,128)(2,1)} %bitcast.119), channel_id=1, source_target_pairs={{0,4},{4,0},{8,12},{12,8},{16,20},{20,16},{24,28},{28,24},{1,5},{5... | collective-permute-start | bytes 2359304 | tf_op jit(solution)/shard_map/ppermute | solution.py:56
  554.5 5.5 collective-permute-start.51
  560.1 14.3 %collective-permute-start.52 = (bf16[256,1,128]{2,0,1:T(8,128)(2,1)S(1)}, bf16[256,1,128]{2,0,1:T(8,128)(2,1)S(1)}, u32[]{:S(2)}, u32[]{:S(2)}) collective-permute-start(bf16[256,1,128]{2,0,1:T(8,128)(2,1)S(1)} %dynamic-slice_convert_fusion.8), channel_id=1, source_target_pairs={{0,16},{4,20},{8,24},{12,28},{16,0},{20,4},{24,8},{28,12},{1,17},{... | collective-permute-start | bytes 196616 | tf_op jit(solution)/shard_map/ppermute | solution.py:56
  567.0 26.1 %collective-permute-start.27 = (bf16[512,1024]{1,0:T(8,128)(2,1)S(1)}, bf16[512,1024]{1,0:T(8,128)(2,1)S(1)}, u32[]{:S(2)}, u32[]{:S(2)}) collective-permute-start(bf16[512,1024]{1,0:T(8,128)(2,1)S(1)} %slice.161), channel_id=1, source_target_pairs={{0,2},{1,3},{2,0},{3,1},{4,6},{5,7},{6,4},{7,5},{8,10},{9,11},{10,... | collective-permute-start | bytes 3145736 | tf_op jit(solution)/shard_map/ppermute | solution.py:56
  568.7 17.1 %collective-permute-start.55 = (bf16[2,1,128,656]{2,3,1,0:T(8,128)(2,1)S(1)}, bf16[2,1,128,656]{2,3,1,0:T(8,128)(2,1)S(1)}, u32[]{:S(2)}, u32[]{:S(2)}) collective-permute-start(bf16[2,1,128,656]{2,3,1,0:T(8,128)(2,1)S(1)} %dynamic-slice_convert_fusion.4), channel_id=1, source_target_pairs={{0,16},{4,20},{8,24},{12,28},{16,0},{20,4},{24,8},{28,12},{1,17},{... | collective-permute-start | bytes 1007624 | tf_op jit(solution)/shard_map/ppermute | solution.py:56
  572.7 41.6 %collective-permute-start.41 = (bf16[512,1024]{1,0:T(8,128)(2,1)}, bf16[512,1024]{1,0:T(8,128)(2,1)S(1)}, u32[]{:S(2)}, u32[]{:S(2)}) collective-permute-start(bf16[512,1024]{1,0:T(8,128)(2,1)} %slice.160), channel_id=1, source_target_pairs={{0,2},{1,3},{2,0},{3,1},{4,6},{5,7},{6,4},{7,5},{8,10},{9,11},{10,... | collective-permute-start | bytes 3145736 | tf_op jit(solution)/shard_map/ppermute | solution.py:56
  596.6 40.0 %all-to-all-start.2 = ((bf16[8,64,1024]{2,1,0:T(8,128)(2,1)}), bf16[8,64,1024]{2,1,0:T(8,128)(2,1)}, u32[]{:S(2)}, u32[]{:S(2)}) async-start(bf16[8,64,1024]{2,1,0:T(8,128)(2,1)} %bitcast.154), calls=%async_computation.2 | async-start | bytes 2097152 | tf_op jit(solution)/shard_map/all_to_all | solution.py:656
  618.9 5.9 collective-permute-start.42
  620.5 12.7 %collective-permute-start.48 = (bf16[3,2,128,256]{3,2,1,0:T(8,128)(2,1)S(1)}, bf16[3,2,128,256]{3,2,1,0:T(8,128)(2,1)S(1)}, u32[]{:S(2)}, u32[]{:S(2)}) collective-permute-start(bf16[3,2,128,256]{3,2,1,0:T(8,128)(2,1)S(1)} %fusion.41), channel_id=1, source_target_pairs={{0,8},{4,12},{8,0},{12,4},{16,24},{20,28},{24,16},{28,20},{1,9},{5... | collective-permute-start | bytes 1179656 | tf_op jit(solution)/shard_map/ppermute | solution.py:56
  624.9 9.5 %collective-permute-start.43 = (f32[2,256]{1,0:T(2,128)S(1)}, f32[2,256]{1,0:T(2,128)S(1)}, u32[]{:S(2)}, u32[]{:S(2)}) collective-permute-start(f32[2,256]{1,0:T(2,128)S(1)} %broadcast_select_fusion.3), channel_id=1, source_target_pairs={{0,8},{4,12},{8,0},{12,4},{16,24},{20,28},{24,16},{28,20},{1,9},{5... | collective-permute-start | bytes 6152 | tf_op jit(solution)/shard_map/ppermute | solution.py:56
  634.4 6.0 collective-permute-start.44
  636.6 42.3 %all-to-all-start.3 = ((bf16[8,64,1024]{2,1,0:T(8,128)(2,1)}), bf16[8,64,1024]{2,1,0:T(8,128)(2,1)S(1)}, u32[]{:S(2)}, u32[]{:S(2)}) async-start(bf16[8,64,1024]{2,1,0:T(8,128)(2,1)} %bitcast.25), calls=%async_computation.3 | async-start | bytes 2097152 | tf_op jit(solution)/shard_map/all_to_all | solution.py:656
  640.8 33.7 %collective-permute-start.49 = (bf16[3,1,128,256]{3,2,1,0:T(8,128)(2,1)S(1)}, bf16[3,1,128,256]{3,2,1,0:T(8,128)(2,1)S(1)}, u32[]{:S(2)}, u32[]{:S(2)}) collective-permute-start(bf16[3,1,128,256]{3,2,1,0:T(8,128)(2,1)S(1)} %dynamic-slice_convert_fusion.5), channel_id=1, source_target_pairs={{0,16},{4,20},{8,24},{12,28},{16,0},{20,4},{24,8},{28,12},{1,17},{... | collective-permute-start | bytes 589832 | tf_op jit(solution)/shard_map/ppermute | solution.py:56
  644.2 31.0 %collective-permute-start.46 = (f32[2,32]{1,0:T(2,128)S(1)}, f32[2,32]{1,0:T(2,128)S(1)}, u32[]{:S(2)}, u32[]{:S(2)}) collective-permute-start(f32[2,32]{1,0:T(2,128)S(1)} %broadcast_select_fusion.6), channel_id=1, source_target_pairs={{0,1},{1,0},{2,3},{3,2},{4,5},{5,4},{6,7},{7,6},{8,9},{9,8},{10,11... | collective-permute-start | bytes 776 | tf_op jit(solution)/shard_map/ppermute | solution.py:56
  (91 other events, 935.4 us)
Sparse Core Ops, SparseCore 0:
  10.2 59.8 all-gather.3
  72.2 53.7 all-gather.7
  128.7 59.6 all-gather.5

commit v2 on v1

v2 whole, which is shorter than its diff:
```python
import functools
import math

import jax
import jax.numpy as jnp
from jax import lax
from jax.experimental import pallas as pl
from jax.experimental.pallas import tpu as pltpu
from jax.sharding import PartitionSpec as P

HEAD_DIM = 64
LANES = 128
theta_base = 160000.0
norm_eps = 1e-05
clip_limit = 5.0
score_scale = 0.125
exp_scale = score_scale * math.log2(math.e)
far_away = -1e30
lowest = -3e38

BF16 = jnp.bfloat16
F32 = jnp.float32


def dot(left, right, left_dim, right_dim):
    return lax.dot_general(
        left, right, (((left_dim,), (right_dim,)), ((), ())), preferred_element_type=F32
    )


def split_three(values):
    high = values.astype(BF16).astype(F32)
    rest = values - high
    middle = rest.astype(BF16).astype(F32)
    return high, middle, rest - middle


def row_stats(values):
    mean = jnp.mean(values, axis=-1, keepdims=True)
    centered = values - mean
    variance = jnp.mean(centered * centered, axis=-1, keepdims=True)
    scale = lax.rsqrt(variance + norm_eps)
    return centered * scale, scale


def turn(values, lane):
    return jnp.where(
        lane % HEAD_DIM < HEAD_DIM // 2,
        pltpu.roll(values, LANES - HEAD_DIM // 2, 1),
        pltpu.roll(values, HEAD_DIM // 2, 1),
    )


def swap_bit(values, axis_name, bit):
    count = lax.axis_size(axis_name)
    return lax.ppermute(values, axis_name, [(i, i ^ bit) for i in range(count)])


def lane_iota(rows):
    return lax.broadcasted_iota(jnp.int32, (rows, LANES), 1)


def vmem(mib):
    return pltpu.CompilerParams(vmem_limit_bytes=mib << 20)


def takes(micros):
    return pl.CostEstimate(flops=micros * 1_100_000_000, bytes_accessed=1 << 20, transcendentals=0)


def resident(shape):
    zeros = (0,) * len(shape)
    return pl.BlockSpec(shape, lambda *_: zeros, pipeline_mode=pl.Buffered(1))


def qkv_kernel(step, per, first, s_ref, xa_ref, xb_ref, gain_ref, w_ref, cos_ref, sin_ref, *rest):
    q_ref, k_ref, v_ref, n_ref = rest[-4:]
    first_len = s_ref[1]
    at = pl.program_id(0)
    x = jnp.where(at < per, xa_ref[...], xb_ref[...])
    normed, _ = row_stats(x.astype(F32))
    n1 = (normed * gain_ref[...]).astype(BF16)
    n_ref[...] = n1
    lane = lane_iota(step)
    start = (((first + at // per) ^ s_ref[0]) * per + at % per) * step
    row = start + lax.broadcasted_iota(jnp.int32, (step, LANES), 0)
    second = row >= first_len
    one, zero = jnp.float32(1), jnp.float32(0)
    q_tail = jnp.where(lane == 64 + second.astype(jnp.int32), one, zero)
    k_tail = jnp.where(
        lane == 65 - second.astype(jnp.int32),
        jnp.float32(far_away),
        jnp.where((lane >= 66) & (lane < 69), one, zero),
    )
    cos, sin = cos_ref[...], sin_ref[...]
    for which, (out, tail) in enumerate(((q_ref, q_tail), (k_ref, k_tail), (v_ref, one))):
        projected = dot(n1, w_ref[which], 1, 0)
        for pair in range(projected.shape[1] // LANES):
            part = projected[:, pair * LANES : (pair + 1) * LANES]
            if which < 2:
                part = part * cos + turn(part, lane) * sin
            out[2 * pair] = jnp.where(lane < HEAD_DIM, part, tail).astype(BF16)
            out[2 * pair + 1] = jnp.where(
                lane < HEAD_DIM, pltpu.roll(part, HEAD_DIM, 1), tail
            ).astype(BF16)


def qkv_call(scalars, xa, xb, gain, w_qkv, cos, sin, first, held, step=512):
    rows, width = xa.shape
    tokens = cos.shape[0]
    cols = w_qkv.shape[2]
    heads = cols // HEAD_DIM
    per = rows // step
    ext = jax.ShapeDtypeStruct((heads, tokens, LANES), BF16)
    place = lambda i, s: (((first + i // per) ^ s[0]) * per + i % per, 0)
    head_spec = pl.BlockSpec((heads, step, LANES), lambda i, s: (0, *place(i, s)))
    held = list(held)
    return pl.pallas_call(
        functools.partial(qkv_kernel, step, per, first),
        out_shape=(ext, ext, ext, jax.ShapeDtypeStruct((tokens, width), BF16)),
        grid_spec=pltpu.PrefetchScalarGridSpec(
            num_scalar_prefetch=1,
            grid=(2 * per,),
            in_specs=[
                pl.BlockSpec((step, width), lambda i, s: (jnp.minimum(i, per - 1), 0)),
                pl.BlockSpec((step, width), lambda i, s: (jnp.maximum(i - per, 0), 0)),
                resident(gain.shape),
                resident((3, width, cols)),
                pl.BlockSpec((step, LANES), place),
                pl.BlockSpec((step, LANES), place),
            ]
            + [pl.BlockSpec(memory_space=pl.ANY)] * len(held),
            out_specs=[head_spec] * 3 + [pl.BlockSpec((step, width), place)],
        ),
        input_output_aliases={7 + i: i for i in range(len(held))},
        compiler_params=vmem(60),
        cost_estimate=takes(9),
        name="qkv",
    )(scalars, xa, xb, gain, w_qkv, cos, sin, *held)


def key_range(first_len, row, q_rows, k_rows, tokens):
    low = jnp.where(row >= first_len, first_len // k_rows, 0)
    high = jnp.where(row + q_rows <= first_len, (first_len + k_rows - 1) // k_rows, tokens // k_rows)
    return low, high


def fwd_kernel(
    far, q_rows, k_rows, s_ref, q_ref, k_ref, v_ref, *rest
):
    o_ref, q2_ref, top_ref, score, peak, acc = rest[-6:]
    heads, tokens, _ = k_ref.shape
    low, high = key_range(
        s_ref[1],
        ((s_ref[3] ^ far) * pl.num_programs(0) + pl.program_id(0)) * q_rows,
        q_rows,
        k_rows,
        tokens,
    )
    lane = lane_iota(q_rows)
    peak[...] = jnp.full(peak.shape, lowest, F32)
    acc[...] = jnp.zeros(acc.shape, F32)

    def first_pass(block, carry):
        keys = pl.ds(pl.multiple_of(block * k_rows, k_rows), k_rows)
        for h in range(heads):
            s = dot(q_ref[h], k_ref[h, keys, :], 1, 1)
            score[h, :, keys] = s
            most = peak[h]
            for t in range(k_rows // LANES):
                most = jnp.maximum(most, s[:, t * LANES : (t + 1) * LANES])
            peak[h] = most
        return carry

    lax.fori_loop(low, high, first_pass, 0)
    for h in range(heads):
        peak[h] = jnp.broadcast_to(jnp.max(peak[h], axis=1, keepdims=True), (q_rows, LANES))

    def second_pass(block, carry):
        keys = pl.ds(pl.multiple_of(block * k_rows, k_rows), k_rows)
        for h in range(heads):
            s, most = score[h, :, keys], peak[h]
            p = jnp.concatenate(
                [
                    jnp.exp2((s[:, t * LANES : (t + 1) * LANES] - most) * exp_scale).astype(BF16)
                    for t in range(k_rows // LANES)
                ],
                axis=1,
            )
            acc[h] += dot(p, v_ref[h, keys, :], 1, 0)
        return carry

    lax.fori_loop(low, high, second_pass, 0)
    held = None
    for h in range(heads):
        sums = acc[h]
        total = jnp.where(lane < HEAD_DIM, pltpu.roll(sums, HEAD_DIM, 1), sums)
        out = sums / total
        log_total = peak[h] + jnp.log2(total) * (1.0 / exp_scale)
        a, b, c = split_three(-log_total)
        q2 = q_ref[h].astype(F32)
        q2 = jnp.where(lane == 66, a, jnp.where(lane == 67, b, jnp.where(lane == 68, c, q2)))
        q2_ref[h] = q2.astype(BF16)
        top_ref[h] = jnp.broadcast_to(jnp.max(peak[h], axis=0, keepdims=True), (8, LANES))
        if h % 2 == 0:
            held = out
        else:
            both = jnp.where(lane < HEAD_DIM, held, pltpu.roll(out, HEAD_DIM, 1))
            o_ref[:, (h // 2) * LANES : (h // 2 + 1) * LANES] = both.astype(BF16)


def attend_forward(scalars, q, k, v, far, rows, held, q_rows=256, k_rows=512):
    heads, tokens, _ = k.shape
    count = rows // q_rows
    k_rows = min(k_rows, tokens)
    return pl.pallas_call(
        functools.partial(fwd_kernel, far, q_rows, k_rows),
        out_shape=(
            jax.ShapeDtypeStruct((rows, heads * HEAD_DIM), BF16),
            jax.ShapeDtypeStruct(q.shape, BF16),
            jax.ShapeDtypeStruct((count, heads, 8, LANES), F32),
        ),
        grid_spec=pltpu.PrefetchScalarGridSpec(
            num_scalar_prefetch=1,
            grid=(count,),
            in_specs=[
                pl.BlockSpec((heads, q_rows, LANES), lambda i, s: (0, (s[3] ^ far) * count + i, 0)),
                resident(k.shape),
                resident(v.shape),
            ]
            + [pl.BlockSpec(memory_space=pl.ANY)] * len(held),
            out_specs=[
                pl.BlockSpec((q_rows, heads * HEAD_DIM), lambda i, s: (i, 0)),
                pl.BlockSpec((heads, q_rows, LANES), lambda i, s: (0, (s[3] ^ far) * count + i, 0)),
                pl.BlockSpec((None, heads, 8, LANES), lambda i, s: (i, 0, 0, 0)),
            ],
            scratch_shapes=[
                pltpu.VMEM((heads, q_rows, tokens), F32),
                pltpu.VMEM((heads, q_rows, LANES), F32),
                pltpu.VMEM((heads, q_rows, LANES), F32),
            ],
        ),
        compiler_params=vmem(60),
        cost_estimate=takes(20),
        input_output_aliases={4 + i: 1 + i for i in range(len(held))},
        name="attend_forward",
    )(scalars, q, k, v, *held)


def bwd_kernel(
    q_rows, k_rows, s_ref, q2_ref, k_ref, v_ref, do_ref, cos_ref, sin_ref, out_ref, dk_ref, dv_ref
):
    heads, tokens, _ = k_ref.shape
    step = pl.program_id(0)
    low, high = key_range(s_ref[1], step * q_rows, q_rows, k_rows, tokens)

    @pl.when(step == 0)
    def _():
        dk_ref[...] = jnp.zeros_like(dk_ref)
        dv_ref[...] = jnp.zeros_like(dv_ref)

    def body(block, sums):
        keys = pl.ds(pl.multiple_of(block * k_rows, k_rows), k_rows)
        new = []
        for h in range(heads):
            key, q2, do = k_ref[h, keys, :], q2_ref[h], do_ref[h]
            p = jnp.exp2(dot(key, q2, 1, 1) * exp_scale)
            ds = (p * dot(v_ref[h, keys, :], do, 1, 1)).astype(BF16)
            dv_ref[h, keys, :] += dot(p.astype(BF16), do, 1, 0)
            dk_ref[h, keys, :] += dot(ds, q2, 1, 0)
            new.append(sums[h] + dot(key, ds, 0, 0))
        return tuple(new)

    sums = lax.fori_loop(
        low, high, body, tuple(jnp.zeros((LANES, q_rows), F32) for _ in range(heads))
    )
    lane = lane_iota(q_rows)

    def unrotate(first, second, rows):
        both = jnp.where(lane < HEAD_DIM, first, pltpu.roll(second, HEAD_DIM, 1)) * score_scale
        return both * cos_ref[rows, :] - turn(both, lane) * sin_ref[rows, :]

    here = pl.ds(pl.multiple_of(step * q_rows, q_rows), q_rows)
    for pair in range(heads // 2):
        cols = slice(pair * LANES, (pair + 1) * LANES)
        out_ref[0, here, cols] = unrotate(sums[2 * pair].T, sums[2 * pair + 1].T, here).astype(BF16)

    @pl.when(step == pl.num_programs(0) - 1)
    def _():
        def finish(block, carry):
            rows = pl.ds(pl.multiple_of(block * q_rows, q_rows), q_rows)
            for pair in range(heads // 2):
                cols = slice(pair * LANES, (pair + 1) * LANES)
                one, two = 2 * pair, 2 * pair + 1
                out_ref[1, rows, cols] = unrotate(
                    dk_ref[one, rows, :], dk_ref[two, rows, :], rows
                ).astype(BF16)
                out_ref[2, rows, cols] = jnp.where(
                    lane < HEAD_DIM,
                    dv_ref[one, rows, :],
                    pltpu.roll(dv_ref[two, rows, :], HEAD_DIM, 1),
                ).astype(BF16)
            return carry

        lax.fori_loop(0, tokens // q_rows, finish, 0)


def attend_backward(scalars, q2, k, v, do, cos, sin, q_rows=256, k_rows=512):
    heads, tokens, _ = k.shape
    block = lambda: pl.BlockSpec((heads, q_rows, LANES), lambda i, s: (0, i, 0))
    out = (3, tokens, heads * HEAD_DIM)
    return pl.pallas_call(
        functools.partial(bwd_kernel, q_rows, k_rows),
        out_shape=jax.ShapeDtypeStruct(out, BF16),
        grid_spec=pltpu.PrefetchScalarGridSpec(
            num_scalar_prefetch=1,
            grid=(tokens // q_rows,),
            in_specs=[
                block(),
                resident(k.shape),
                resident(v.shape),
                block(),
                resident(cos.shape),
                resident(sin.shape),
            ],
            out_specs=resident(out),
            scratch_shapes=[
                pltpu.VMEM((heads, tokens, LANES), F32),
                pltpu.VMEM((heads, tokens, LANES), F32),
            ],
        ),
        compiler_params=vmem(60),
        cost_estimate=takes(57),
        name="attend_backward",
    )(scalars, q2, k, v, do, cos, sin)


def mlp_kernel(
    s_ref, xs_ref, xk_ref, gs_ref, gk_ref, o0, o1, o2, o3, w0, w1, w2, w3, gain_ref, w_ref, *rest
):
    a_ref, n_ref, act_ref, dgate_ref, dup_ref, keep_ref, send_ref, keep_out, send_out = rest[-9:]
    units = w_ref.shape[2]
    sending = pl.program_id(0) < pl.num_programs(0) // 2
    x = jnp.where(sending, xs_ref[...], xk_ref[...])
    g = jnp.where(sending, gs_ref[...], gk_ref[...])
    branch = dot(o0[...], w0[...], 1, 1) + dot(o1[...], w1[...], 1, 1)
    branch = branch + dot(o2[...], w2[...], 1, 1) + dot(o3[...], w3[...], 1, 1)
    branch = branch.astype(BF16)
    a_ref[...] = branch
    normed, _ = row_stats(x.astype(F32) + branch.astype(F32))
    n2 = (normed * gain_ref[...]).astype(BF16)
    n_ref[...] = n2
    partial = out_partial = 0.0
    for low in range(0, units, 256):
        cols = slice(low, min(low + 256, units))
        gate = dot(n2, w_ref[0, :, cols], 1, 0)
        up = dot(n2, w_ref[1, :, cols], 1, 0)
        dact = dot(g, w_ref[2, :, cols], 1, 0)
        phi = 0.5 + 0.5 * lax.erf(gate * math.sqrt(0.5))
        gelu = gate * phi
        act = (gelu * up).astype(BF16)
        act_ref[:, cols] = act
        density = jnp.exp(-0.5 * gate * gate) * (1.0 / math.sqrt(2.0 * math.pi))
        dgate = (dact * up * (phi + gate * density)).astype(BF16)
        dup = (dact * gelu).astype(BF16)
        dgate_ref[:, cols] = dgate
        dup_ref[:, cols] = dup
        partial = partial + dot(dgate, w_ref[0, :, cols], 1, 1) + dot(dup, w_ref[1, :, cols], 1, 1)
        out_partial = out_partial + dot(act, w_ref[2, :, cols], 1, 1)

    @pl.when(sending)
    def _():
        send_ref[...] = partial.astype(BF16)
        send_out[...] = out_partial.astype(BF16)

    @pl.when(jnp.logical_not(sending))
    def _():
        keep_ref[...] = partial
        keep_out[...] = out_partial.astype(BF16)


def mlp_call(scalars, x_pair, g_pair, heads_rel, w_out_rel, gain, w_mlp, first, held, step=256):
    rows, width = x_pair[0].shape
    units = w_mlp.shape[2]
    per = rows // step
    rel = lambda i, s: (first + 1 - i // per, i % per, 0)
    wide = pl.BlockSpec((None, step, width), rel)
    narrow = pl.BlockSpec((None, step, units), rel)
    wide_out = jax.ShapeDtypeStruct((4, rows, width), BF16)
    narrow_out = jax.ShapeDtypeStruct((4, rows, units), BF16)
    send = pl.BlockSpec((step, width), lambda i, s: (jnp.minimum(i, per - 1), 0))
    keep = pl.BlockSpec((step, width), lambda i, s: (jnp.maximum(i - per, 0), 0))
    head_spec = pl.BlockSpec(
        (step, heads_rel[0].shape[1]), lambda i, s: (((i // per) ^ 1 ^ s[2]) * per + i % per, 0)
    )
    held = list(held)
    half = lambda kind: jax.ShapeDtypeStruct((rows, width), kind)
    return pl.pallas_call(
        mlp_kernel,
        out_shape=(
            wide_out,
            wide_out,
            narrow_out,
            narrow_out,
            narrow_out,
            half(F32),
            half(BF16),
            half(BF16),
            half(BF16),
        ),
        grid_spec=pltpu.PrefetchScalarGridSpec(
            num_scalar_prefetch=1,
            grid=(2 * per,),
            in_specs=[send, keep, send, keep]
            + [head_spec] * len(heads_rel)
            + [resident(w.shape) for w in w_out_rel]
            + [resident(gain.shape), resident(w_mlp.shape)]
            + [pl.BlockSpec(memory_space=pl.ANY)] * len(held),
            out_specs=[wide, wide, narrow, narrow, narrow, keep, send, keep, send],
        ),
        input_output_aliases={15 + i: i for i in range(len(held))},
        compiler_params=vmem(60),
        cost_estimate=takes(24),
        name="mlp",
    )(scalars, *x_pair, *g_pair, *heads_rel, *w_out_rel, gain, w_mlp, *held)


def pull_norm(normed, scale, cotangent):
    mean = jnp.mean(cotangent, axis=-1, keepdims=True)
    along = jnp.mean(cotangent * normed, axis=-1, keepdims=True)
    return (cotangent - mean - normed * along) * scale


def resid_kernel(mine_ref, arrived_ref, x_ref, a_ref, g_ref, gain_ref, dx_ref, da_ref):
    dn = mine_ref[...] + arrived_ref[...].astype(F32)
    normed, scale = row_stats(x_ref[...].astype(F32) + a_ref[...].astype(F32))
    dx = g_ref[...].astype(F32) + pull_norm(normed, scale, dn * gain_ref[...])
    dx_ref[...] = dx
    da_ref[...] = dx.astype(BF16)


def resid_call(mine, arrived, x, a_rel, g, gain, step=256):
    rows, width = mine.shape
    per = rows // step
    flat = pl.BlockSpec((step, width), lambda i: (i, 0))
    return pl.pallas_call(
        resid_kernel,
        out_shape=(
            jax.ShapeDtypeStruct((rows, width), F32),
            jax.ShapeDtypeStruct((rows, width), BF16),
        ),
        grid=(per,),
        in_specs=[
            flat,
            flat,
            flat,
            pl.BlockSpec((None, step, width), lambda i: (0, i, 0)),
            flat,
            resident(gain.shape),
        ],
        out_specs=[flat, flat],
        compiler_params=vmem(60),
        cost_estimate=takes(5),
        name="resid",
    )(mine, arrived, x, a_rel, g, gain)


def head_grad_kernel(s_ref, even_ref, odd_ref, w_ref, o_ref, *rest):
    do_ref, da_ref = rest[-2:]
    own = pl.program_id(0) == s_ref[2]
    da = jnp.where(own, even_ref[...], odd_ref[...])
    da_ref[...] = da
    do = dot(da, w_ref[...], 1, 0).astype(BF16).astype(F32)
    rows = do.shape[0]
    lane = lane_iota(rows)
    product = do * o_ref[...].astype(F32)
    for pair in range(do.shape[1] // LANES):
        cols = slice(pair * LANES, (pair + 1) * LANES)
        part = do[:, cols]
        for odd in range(2):
            inside = (lane >= HEAD_DIM) if odd else (lane < HEAD_DIM)
            delta = jnp.sum(jnp.where(inside, product[:, cols], 0.0), axis=1, keepdims=True)
            a, b, c = split_three(jnp.broadcast_to(-delta, (rows, LANES)))
            head = pltpu.roll(part, HEAD_DIM, 1) if odd else part
            tail = jnp.where(
                lane == 64, a, jnp.where(lane == 65, b, jnp.where(lane == 66, c, 0.0))
            )
            do_ref[2 * pair + odd] = jnp.where(lane < HEAD_DIM, head, tail).astype(BF16)


def head_grad_call(scalars, even, odd, w_out, o_chunk, far, tokens, held):
    rows, width = even.shape
    heads = o_chunk.shape[1] // HEAD_DIM
    held = list(held)
    return pl.pallas_call(
        head_grad_kernel,
        out_shape=(
            jax.ShapeDtypeStruct((heads, tokens, LANES), BF16),
            jax.ShapeDtypeStruct((2 * rows, width), BF16),
        ),
        grid_spec=pltpu.PrefetchScalarGridSpec(
            num_scalar_prefetch=1,
            grid=(2,),
            in_specs=[
                resident(even.shape),
                resident(odd.shape),
                resident(w_out.shape),
                pl.BlockSpec((rows, o_chunk.shape[1]), lambda i, s: (i, 0)),
            ]
            + [pl.BlockSpec(memory_space=pl.ANY)] * len(held),
            out_specs=[
                pl.BlockSpec((heads, rows, LANES), lambda i, s: (0, 2 * (s[3] ^ far) + i, 0)),
                pl.BlockSpec((rows, width), lambda i, s: (i, 0)),
            ],
        ),
        input_output_aliases={5 + i: i for i in range(len(held))},
        compiler_params=vmem(60),
        cost_estimate=takes(6),
        name="head_grad",
    )(scalars, even, odd, w_out, o_chunk, *held)


def inner_kernel(n_ref, g0, g1, g2, g3, dgate_ref, dup_ref, act_ref, out_ref):
    n2 = n_ref[...]
    out_ref[0] = dot(n2, dgate_ref[...], 0, 0).astype(BF16)
    out_ref[1] = dot(n2, dup_ref[...], 0, 0).astype(BF16)
    rows = g0.shape[0]
    g = jnp.concatenate([g0[...], g1[...], g2[...], g3[...]], axis=0)
    out_ref[2] = dot(g, act_ref[...], 0, 0).astype(BF16)


def inner_call(n2, g_rel, dgate, dup, act):
    tokens, width = n2.shape
    units = act.shape[1]
    rows = g_rel[0].shape[0]
    count = width // LANES
    return pl.pallas_call(
        inner_kernel,
        out_shape=jax.ShapeDtypeStruct((count, 3, LANES, units), BF16),
        grid=(count,),
        in_specs=[pl.BlockSpec((tokens, LANES), lambda i: (0, i))]
        + [pl.BlockSpec((rows, LANES), lambda i: (0, i))] * 4
        + [resident(act.shape)] * 3,
        out_specs=pl.BlockSpec((None, 3, LANES, units), lambda i: (i, 0, 0, 0)),
        compiler_params=vmem(60),
        cost_estimate=takes(17),
        name="inner_grads",
    )(n2, *g_rel, dgate, dup, act)


def store_slices(out_ref, at, sums):
    for i in range(out_ref.shape[0]):
        out_ref[i, at] = sums[:, i * LANES : (i + 1) * LANES].astype(BF16)


def outer_kernel(o0, o1, da0, da1, out_ref):
    store_slices(out_ref, 0, dot(o0[...], da0[...], 0, 0) + dot(o1[...], da1[...], 0, 0))


def outer_call(o_chunks, da_chunks):
    rows, width = da_chunks[0].shape
    cols = o_chunks[0].shape[1]
    out = (width // LANES, 1, cols, LANES)
    return pl.pallas_call(
        outer_kernel,
        out_shape=jax.ShapeDtypeStruct(out, BF16),
        compiler_params=vmem(60),
        cost_estimate=takes(5),
        name="outer_grad",
    )(*o_chunks, *da_chunks)


def proj_kernel(n_ref, d_ref, out_ref, acc):
    step = pl.program_id(0)
    for at in range(d_ref.shape[0]):
        sums = dot(d_ref[at], n_ref[...], 0, 0)

        @pl.when(step == 0)
        def _(sums=sums, at=at):
            acc[at] = sums

        @pl.when(step > 0)
        def _(sums=sums, at=at):
            store_slices(out_ref, at, acc[at] + sums)


def proj_call(n1, dproj):
    tokens, width = n1.shape
    kinds, _, cols = dproj.shape
    step = tokens // 2
    out = (width // LANES, kinds, cols, LANES)
    return pl.pallas_call(
        proj_kernel,
        out_shape=jax.ShapeDtypeStruct(out, BF16),
        grid=(2,),
        in_specs=[
            pl.BlockSpec((step, width), lambda i: (i, 0)),
            pl.BlockSpec((kinds, step, cols), lambda i: (0, i, 0)),
        ],
        out_specs=resident(out),
        scratch_shapes=[pltpu.VMEM((kinds, cols, width), F32)],
        compiler_params=vmem(60),
        cost_estimate=takes(8),
        name="proj_grads",
    )(n1, dproj)


def dn_kernel(p_ref, w_ref, out_ref):
    total = dot(p_ref[0], w_ref[0], 1, 1) + dot(p_ref[1], w_ref[1], 1, 1)
    out_ref[...] = (total + dot(p_ref[2], w_ref[2], 1, 1)).astype(BF16)


def dn_call(scalars, dproj, w_qkv, parity, rows, step=256):
    kinds, tokens, cols = dproj.shape
    width = w_qkv.shape[1]
    per = rows // step
    return pl.pallas_call(
        lambda s_ref, p_ref, w_ref, out_ref: dn_kernel(p_ref, w_ref, out_ref),
        out_shape=jax.ShapeDtypeStruct((2 * rows, width), BF16),
        grid_spec=pltpu.PrefetchScalarGridSpec(
            num_scalar_prefetch=1,
            grid=(2 * per,),
            in_specs=[
                pl.BlockSpec(
                    (kinds, step, cols),
                    lambda i, s: (0, ((2 * (i // per) + parity) ^ s[0]) * per + i % per, 0),
                ),
                resident((kinds, width, cols)),
            ],
            out_specs=pl.BlockSpec((step, width), lambda i, s: (i, 0)),
        ),
        compiler_params=vmem(60),
        cost_estimate=takes(6),
        name="dn",
    )(scalars, dproj, w_qkv)


def last_kernel(mine_ref, arrived_ref, x_ref, dx_ref, gain_ref, out_ref):
    dn = (mine_ref[...] + arrived_ref[...].astype(F32)).astype(BF16).astype(F32)
    normed, scale = row_stats(x_ref[...].astype(F32))
    out_ref[...] = (dx_ref[...] + pull_norm(normed, scale, dn * gain_ref[...])).astype(BF16)


def last_call(mine, arrived, x, dx, gain, step=256):
    rows, width = x.shape
    per = rows // step
    flat = pl.BlockSpec((step, width), lambda i: (i, 0))
    return pl.pallas_call(
        last_kernel,
        out_shape=jax.ShapeDtypeStruct((rows, width), BF16),
        grid=(per,),
        in_specs=[flat, flat, flat, flat, resident(gain.shape)],
        out_specs=flat,
        compiler_params=vmem(60),
        cost_estimate=takes(5),
        name="last",
    )(mine, arrived, x, dx, gain)


def bits_of(count):
    return [1 << i for i in range(count.bit_length() - 1)]


def pick(values, axis, index):
    return lax.dynamic_index_in_dim(values, index, axis, keepdims=False)


def by_device(values, count):
    blocks = values.shape[0]
    if blocks == count:
        return values
    axis = values.shape.index(LANES, 2)
    shape = values.shape[:axis] + (count // blocks, LANES * blocks // count) + values.shape[axis + 1 :]
    values = jnp.moveaxis(values.reshape(shape), axis, 1)
    return values.reshape((count,) + values.shape[2:])


def halve(values, axis_name, point):
    me = lax.axis_index(axis_name)
    carried = values
    for bit in bits_of(lax.axis_size(axis_name)):
        view = carried.reshape((carried.shape[0] // 2, 2) + carried.shape[1:])
        mine = (me // bit) % 2
        arrived = swap_bit(pick(view, 1, 1 - mine).astype(BF16), axis_name, bit)
        (arrived,) = after(point, arrived)
        carried = pick(view, 1, mine).astype(F32) + arrived.astype(F32)
    return carried[0]


def after(point, *values):
    return lax.optimization_barrier((point, *values))[1:]


def gather_bits(values, axis_name):
    me = lax.axis_index(axis_name)
    count = lax.axis_size(axis_name)
    shape = values.shape
    for bit in reversed(bits_of(count)):
        other = swap_bit(values, axis_name, bit)
        high = (me // bit) % 2 == 1
        values = jnp.stack([jnp.where(high, other, values), jnp.where(high, values, other)])
    lead = values.ndim - len(shape)
    order = tuple(reversed(range(lead))) + tuple(range(lead, values.ndim))
    return values.transpose(order).reshape((count,) + shape)


def scatter_lanes(values):
    me = lax.axis_index("mp")
    for bit in reversed(bits_of(lax.axis_size("mp"))):
        half = values.shape[-1] // 2
        low, top = values[..., :half], values[..., half:]
        high = (me // bit) % 2 == 1
        other = swap_bit(jnp.where(high, low, top), "mp", bit)
        values = jnp.where(high, top, low) + other
    return values


def local(
    hidden_in, out_grad, seq_lengths, dealing, attn_gain, mlp_gain, w_qkv, w_out, w_in, w_down
):
    dp_count = lax.axis_size("dp")
    mp_count = lax.axis_size("mp")
    owner = lax.axis_index("dp")
    lane = lax.axis_index("mp")
    rows, width = hidden_in.shape
    tokens = rows * mp_count
    shards = width // dp_count
    slots = rows // dp_count
    first_len = pick(seq_lengths, 0, 2 * owner)
    scalars = jnp.stack([lane, first_len, lane % 2, lane // 2]).astype(jnp.int32)

    lane_rows = pick(dealing.reshape(dp_count, mp_count, rows), 1, lane)
    local_row = lane_rows - (owner * mp_count + lane) * rows
    inside = (local_row >= 0) & (local_row < rows)
    order = jnp.arange(rows, dtype=jnp.int32)
    upto = (order[:, None] <= order[None, :]).astype(BF16)
    rank = dot(inside.astype(BF16), upto, 1, 0).astype(jnp.int32) - 1
    slot_hit = inside[:, None, :] & (rank[:, None, :] == jnp.arange(slots)[None, :, None])
    send_row = jnp.sum(jnp.where(slot_hit, local_row[:, None, :], 0), axis=2).reshape(rows)
    to_slot = (send_row[:, None] == order[None, :]).astype(BF16)
    source = pick(lane_rows, 0, owner) // (rows * mp_count)
    from_src = source[None, :] == jnp.arange(dp_count, dtype=jnp.int32)[:, None]
    src_rank = dot(from_src.astype(BF16), upto, 1, 0).astype(jnp.int32) - 1
    slot_of = source * slots + jnp.sum(jnp.where(from_src, src_rank, 0), axis=0)
    to_dealt = (slot_of[:, None] == order[None, :]).astype(BF16)

    def exchange(values):
        packed = values.reshape(dp_count, slots, width)
        arrived = lax.all_to_all(packed, "dp", split_axis=0, concat_axis=0, tiled=True)
        return arrived.reshape(rows, width)

    def pack(values):
        return dot(to_slot, values, 1, 0).astype(BF16)

    def unpack(values):
        return dot(to_dealt, values, 1, 0).astype(BF16)

    def pack_back(values):
        return dot(to_dealt, values, 0, 0).astype(BF16)

    def unpack_back(values):
        return dot(to_slot, values, 0, 0).astype(BF16)

    def group(values):
        across = swap_bit(values, "mp", 2)
        return [values, swap_bit(values, "mp", 1), across, swap_bit(across, "mp", 1)]

    gains = gather_bits(gather_bits(jnp.stack([attn_gain, mlp_gain]), "dp"), "mp")
    gains = gains.transpose(2, 1, 0, 3).reshape(2, width)
    w_mlp = jnp.concatenate([w_in, w_down.T[None]], axis=0)
    x_arrived = exchange(pack(hidden_in))
    x_arrived, g_packed, gains, w_mlp = lax.optimization_barrier(
        (x_arrived, pack(out_grad), gains, w_mlp)
    )
    w_mlp = lax.all_gather(w_mlp, "dp", axis=1, tiled=True)
    gain_one, gain_two = gains[0:1], gains[1:2]
    x_mine = unpack(x_arrived)
    x_rel = group(x_mine)
    attn_weights = jnp.concatenate([w_qkv, w_out.T[None]], axis=0)
    attn_weights = jnp.moveaxis(gather_bits(attn_weights, "dp"), 0, 1).reshape(4, width, -1)
    w_out_rel = group(attn_weights[3])
    g_arrived = exchange(g_packed)

    place = jnp.arange(tokens, dtype=jnp.int32)
    place = jnp.where(place >= first_len, place - first_len, place).astype(F32)
    freq_index = jnp.arange(LANES, dtype=jnp.int32) % (HEAD_DIM // 2)
    freqs = jnp.exp(freq_index.astype(F32) * (-2.0 * math.log(theta_base) / HEAD_DIM))
    angles = place[:, None] * freqs[None, :]
    first_half = jnp.arange(LANES) % HEAD_DIM < HEAD_DIM // 2
    cos = jnp.cos(angles)
    sin = jnp.sin(angles) * jnp.where(first_half, -1.0, 1.0)[None, :]

    held = qkv_call(scalars, x_rel[0], x_rel[1], gain_one, attn_weights, cos, sin, 0, ())
    q, k, v, n1 = qkv_call(scalars, x_rel[2], x_rel[3], gain_one, attn_weights, cos, sin, 2, held)
    (g_arrived,) = after(q, g_arrived)
    g_rel = group(unpack(g_arrived))
    near, q2, near_top = attend_forward(scalars, q, k, v, 0, 2 * rows, ())
    near_across = swap_bit(near, "mp", 2)
    distant, q2, far_top = attend_forward(scalars, q, k, v, 1, 2 * rows, (q2,))
    (distant,) = after(near_across, distant)
    far_across = swap_bit(distant, "mp", 2)
    core = lambda values: swap_bit(values, "mp", 1)
    far_heads = [distant, core(distant), near_across, core(near_across)]
    peaks = [near_top, far_top]
    head_peaks = jnp.max(jnp.stack(peaks), axis=(0, 1, 3, 4)) * score_scale
    peak_bits = bits_of(dp_count)
    peak_swap = swap_bit(head_peaks, "dp", peak_bits[0])

    *held, keep, send, keep_out, send_out = mlp_call(
        scalars,
        (x_rel[3], x_rel[2]),
        (g_rel[3], g_rel[2]),
        far_heads,
        w_out_rel,
        gain_two,
        w_mlp,
        2,
        (),
    )
    far_across, peak_swap, send, near = lax.optimization_barrier(
        (far_across, peak_swap, send, near)
    )
    head_peaks = jnp.maximum(head_peaks, peak_swap)
    peak_swap = swap_bit(head_peaks, "dp", peak_bits[1])
    dn_far = (keep + core(send).astype(F32)).astype(BF16)
    dn_arrived = swap_bit(dn_far, "mp", 2)
    near_heads = [near, core(near), far_across, core(far_across)]
    (near_heads[0],) = after(dn_far, near)
    far_out = (keep_out, send_out)
    a_rel, n2, act, dgate, dup, keep, send, keep_out, send_out = mlp_call(
        scalars,
        (x_rel[1], x_rel[0]),
        (g_rel[1], g_rel[0]),
        near_heads,
        w_out_rel,
        gain_two,
        w_mlp,
        0,
        held,
    )
    dn_arrived, peak_swap, send = lax.optimization_barrier((dn_arrived, peak_swap, send))
    head_peaks = jnp.maximum(head_peaks, peak_swap)
    peak_swap = swap_bit(head_peaks, "dp", peak_bits[2])
    dx, da = resid_call(
        keep + core(send).astype(F32), dn_arrived, x_rel[0], a_rel, g_rel[0], gain_two
    )
    da_core, da_across = core(da), swap_bit(da, "mp", 2)

    flat = lambda values: values.reshape(tokens, values.shape[2])
    (act,) = after(da, act)
    inner_grads = inner_call(flat(n2), g_rel, flat(dgate), flat(dup), flat(act))
    inner_grads, da_across, peak_swap = lax.optimization_barrier((inner_grads, da_across, peak_swap))
    head_peaks = jnp.maximum(head_peaks, peak_swap)
    for bit in peak_bits[3:]:
        head_peaks = jnp.maximum(head_peaks, swap_bit(head_peaks, "dp", bit))
    da_rel = [da, da_core, da_across, core(da_across)]
    inner_grads = lax.psum_scatter(by_device(inner_grads, dp_count), "dp").astype(F32)
    inner_grad, down_grad = inner_grads[:2], inner_grads[2].T

    do, da_near = head_grad_call(
        scalars, da_rel[0], da_rel[1], attn_weights[3], near, 0, tokens, ()
    )
    do, da_far = head_grad_call(
        scalars, da_rel[2], da_rel[3], attn_weights[3], distant, 1, tokens, (do,)
    )
    outer_grad = outer_call((near, distant), (da_near, da_far))
    outer_grad = by_device(outer_grad, dp_count)
    outer_grad = lax.all_to_all(outer_grad, "dp", split_axis=0, concat_axis=0, tiled=True)

    far_out = after(da_across, *far_out)
    add_core = lambda keep, send: keep.astype(F32) + core(send).astype(F32)

    factor = jnp.sqrt(clip_limit / jnp.maximum(head_peaks, clip_limit))
    column_factor = jnp.repeat(factor, HEAD_DIM)
    scaling = jnp.stack([column_factor, column_factor, jnp.ones_like(column_factor)])[:, None, :]
    clipped = (w_qkv.astype(F32) * scaling).astype(BF16)

    out_far = add_core(*far_out).astype(BF16)
    out_arrived = swap_bit(out_far, "mp", 2)
    do, out_sum = after(out_far, do, add_core(keep_out, send_out))
    dproj = attend_backward(scalars, q2, k, v, do, cos, sin)
    send = dn_call(scalars, dproj, attn_weights, 1, rows)
    out_arrived, outer_grad, send = lax.optimization_barrier((out_arrived, outer_grad, send))
    outer_grad = jnp.sum(outer_grad.astype(F32), axis=0)[0]
    keep = dn_call(scalars, dproj, attn_weights, 0, rows)
    both = keep.astype(F32) + core(send).astype(F32)
    dn_own, dn_far = both[:rows], both[rows:].astype(BF16)
    dn_arrived = swap_bit(dn_far, "mp", 2)
    (out_arrived,) = after(dn_far, out_arrived)
    x1 = x_rel[0].astype(F32) + a_rel[0].astype(F32)
    out_packed = pack_back((x1 + (out_sum + out_arrived.astype(F32))).astype(BF16))
    (n1,) = after(out_packed, n1)
    proj_grad = proj_call(n1, dproj)
    (dn_arrived,) = after(proj_grad, dn_arrived)
    grad_packed = pack_back(last_call(dn_own, dn_arrived, x_rel[0], dx, gain_one))
    input_grad = unpack_back(exchange(grad_packed))
    (out_arrived,) = after(grad_packed, exchange(out_packed))
    output = unpack_back(out_arrived)
    proj_grad = halve(by_device(proj_grad, dp_count), "dp", grad_packed)
    proj_grad = jnp.swapaxes(proj_grad, 1, 2)

    by_gain = jnp.stack(
        [
            jnp.sum(proj_grad * w_qkv.astype(F32), axis=(0, 2)),
            jnp.sum(inner_grad * w_in.astype(F32), axis=(0, 2)),
        ]
    )
    gain_part = lax.dynamic_slice_in_dim(gains, owner * shards, shards, 1)
    gain_grads = scatter_lanes(by_gain / gain_part)
    return (
        output,
        input_grad,
        gain_grads[0],
        gain_grads[1],
        proj_grad,
        outer_grad,
        inner_grad,
        down_grad,
        clipped,
    )


def solution(mesh):
    in_specs = (
        P(("dp", "mp"), None),
        P(("dp", "mp"), None),
        P(),
        P(),
        P(("dp", "mp")),
        P(("dp", "mp")),
        P(None, "dp", "mp"),
        P("mp", "dp"),
        P(None, "dp", "mp"),
        P("mp", "dp"),
    )
    out_specs = (
        P(("dp", "mp"), None),
        P(("dp", "mp"), None),
        P(("dp", "mp")),
        P(("dp", "mp")),
        P(None, "dp", "mp"),
        P("mp", "dp"),
        P(None, "dp", "mp"),
        P("mp", "dp"),
        P(None, "dp", "mp"),
    )
    return jax.shard_map(local, mesh=mesh, in_specs=in_specs, out_specs=out_specs, check_vma=False)
```

time: 693 us -> 502 us (0.72)
  local copies, waits for them, and re-layouts: 121 us -> 22.1 us
  blocking collectives: 58.3 us -> 0 us
  Pallas kernels: 190 us -> 226 us
  matrix products: 51.5 us -> 19.3 us
  waiting for transfers between devices: 135 us -> 120 us
  other arithmetic: 40.3 us -> 27.1 us
  starting transfers between devices: 76.7 us -> 67 us
    all_gather x1 -> x0, blocking collectives: 58.3 us -> none  [local(): outer_own = lax.all_gather(w_out, 'dp', axis=1, tiled=True)]
    unnamed x178 -> x80, local copies, waits for them, and re-layouts: 62.5 us -> 11.1 us
    pallas_call x6 -> x8, Pallas kernels: 44.2 us -> 91 us  [the longest x2 40.1 us: attend_forward(): pl.pallas_call(functools.partial(fwd_kernel, far, q_rows, k_rows), out_sh...]
    dot_general x16 -> x10, matrix products: 46.4 us -> 19.3 us  [dot(): lax.dot_general(left, right, (((left_dim,), (right_dim,)), ((), ())), pre...]
    another operation x5 -> x0, local copies, waits for them, and re-layouts: 21.7 us -> none  [the longest x3 14 us: local(): jnp.stack([dot(n2_flat, flat(dgate), 0, 0), dot(n2_flat, flat(dup), 0, 0)])]
    ppermute x62 -> x42, starting transfers between devices: 57.3 us -> 38.7 us  [swap_bit(): return lax.ppermute(values, axis_name, [(i, i ^ bit) for i in range(count)])]
    dynamic_slice x7 -> x2, local copies, waits for them, and re-layouts: 15.5 us -> 0.6 us  [pick(): return lax.dynamic_index_in_dim(values, index, axis, keepdims=False)]
    ppermute x62 -> x42, waiting for transfers between devices: 106 us -> 94.8 us  [swap_bit(): return lax.ppermute(values, axis_name, [(i, i ^ bit) for i in range(count)])]
  transfers between devices with their start and end apart: 69 -> 49, of which waited for: 20 -> 17; matrix products, arithmetic and copies ran while one was open for 22% -> 12% of each run, Pallas kernels for 26% -> 45%
where the time goes in v2:
time: 502 us; the launch traced here: 496 us
  Pallas kernels  226 us (45%)
  waiting for transfers between devices  120 us (24%)
  starting transfers between devices  67 us (13%)
  other arithmetic  27.1 us (5%)
  local copies, waits for them, and re-layouts  22.1 us (4%)
  matrix products  19.3 us (4%)
  between operations  15 us (3%)
    ppermute x42, waiting for transfers between devices, swap_bit(): return lax.ppermute(values, axis_name, [(i, i ^ bit) for i in range(count)])  94.8 us
    pallas_call x1, Pallas kernels, attend_backward(): pl.pallas_call(functools.partial(bwd_kernel, q_rows, k_rows), out_shape=j...  56.8 us
    pallas_call x2, Pallas kernels, mlp_call(): pl.pallas_call(mlp_kernel, out_shape=(wide_out, wide_out, narrow_out, nar...  48.2 us
    pallas_call x2, Pallas kernels, attend_forward(): pl.pallas_call(functools.partial(fwd_kernel, far, q_rows, k_rows), out_sh...  40.1 us
    ppermute x42, starting transfers between devices, swap_bit(): return lax.ppermute(values, axis_name, [(i, i ^ bit) for i in range(count)])  38.7 us
    all_to_all x4, waiting for transfers between devices, exchange(): lax.all_to_all(packed, 'dp', split_axis=0, concat_axis=0, tiled=True)  25.6 us
    all_to_all x4, starting transfers between devices, exchange(): lax.all_to_all(packed, 'dp', split_axis=0, concat_axis=0, tiled=True)  23.7 us
    dot_general x10, matrix products, dot(): lax.dot_general(left, right, (((left_dim,), (right_dim,)), ((), ())), pre...  19.3 us
  transfers between devices with their start and end apart: 49, of which 17 were waited for; matrix products, arithmetic and copies ran while one was open for 12% of the time, Pallas kernels for 45%

profile of v2, /device:TPU:0, one launch (start us, length us, event | category | flops | bytes accessed | tf_op | source)
XLA Modules:
  0.0 496.5 jit_solution(8325676247178184182)
XLA Ops:
  9.2 4.1 collective-permute-start.7
  15.5 1.7 convolution_convert_fusion.7
  17.2 6.3 %all-to-all-start = ((bf16[8,64,1024]{2,1,0:T(8,128)(2,1)}), bf16[8,64,1024]{2,1,0:T(8,128)(2,1)}, u32[]{:S(2)}, u32[]{:S(2)}) async-start(bf16[8,64,1024]{2,1,0:T(8,128)(2,1)} %bitcast.4), calls=%async_computation | async-start | bytes 2097152 | tf_op jit(solution)/shard_map/all_to_all | solution.py:749
  23.7 1.7 convolution_convert_fusion.6
  28.3 2.0 collective-permute-start.1
  30.5 11.3 %collective-permute-done.1 = f32[2,2,32]{2,1,0:T(2,128)S(1)} collective-permute-done((f32[2,2,32]{2,1,0:T(2,128)S(1)}, f32[2,2,32]{2,1,0:T(2,128)S(1)}, u32[]{:S(2)}, u32[]{:S(2)}) %collective-permute-start.1) | collective-permute-done | bytes 544 | tf_op jit(solution)/shard_map/ppermute | solution.py:56
  41.9 2.1 collective-permute-start.2
  44.0 1.6 collective-permute-done.2
  45.6 1.6 collective-permute-start.3
  47.2 6.3 %collective-permute-done.8 = bf16[2,4,128,256]{3,2,1,0:T(8,128)(2,1)S(1)} collective-permute-done((bf16[2,4,128,256]{3,2,1,0:T(8,128)(2,1)S(1)}, bf16[2,4,128,256]{3,2,1,0:T(8,128)(2,1)S(1)}, u32[]{:S(2)}, u32[]{:S(2)}) %collective-permute-start.8) | collective-permute-done | bytes 524320 | tf_op jit(solution)/shard_map/ppermute | solution.py:56
  53.7 1.5 collective-permute-start.9
  56.6 3.0 convolution_convert_fusion.5.xa_ref.xk_ref.x_ref
  59.8 1.5 collective-permute-start.5
  61.3 16.7 %collective-permute-done.9 = bf16[2,2,4,128,256]{4,3,2,0,1:T(8,128)(2,1)S(1)} collective-permute-done((bf16[2,2,4,128,256]{4,3,2,0,1:T(8,128)(2,1)S(1)}, bf16[2,2,4,128,256]{4,3,2,0,1:T(8,128)(2,1)S(1)}, u32[]{:S(2)}, u32[]{:S(2)}) %collective-permute-start.9) | collective-permute-done | bytes 1048608 | tf_op jit(solution)/shard_map/ppermute | solution.py:56
  79.2 1.5 collective-permute-start.18
  80.7 5.6 %fusion.6 = (f32[2048,128]{1,0:T(8,128)}, f32[2048,128]{1,0:T(8,128)}) fusion(f32[128]{0:T(128)S(1)} %get-tuple-element.212, f32[128]{0:T(128)S(1)} %get-tuple-element.213, f32[2048]{0:T(1024)S(1)} %select_convert_fusion), kind=kLoop, calls=%fused_computation.27 | loop fusion | flops 524288 | bytes 2106368 | tf_op jit(solution)/shard_map/mul | solution.py:791
  87.5 1.6 copy.76
  89.1 5.5 %all-to-all-start.1 = ((bf16[8,64,1024]{2,1,0:T(8,128)(2,1)}), bf16[8,64,1024]{2,1,0:T(8,128)(2,1)S(1)}, u32[]{:S(2)}, u32[]{:S(2)}) async-start(bf16[8,64,1024]{2,1,0:T(8,128)(2,1)} %bitcast.40), calls=%async_computation.1 | async-start | bytes 2097152 | tf_op jit(solution)/shard_map/all_to_all | solution.py:749
  96.7 8.3 %qkv.2 = (bf16[4,2048,128]{2,1,0:T(8,128)(2,1)}, bf16[4,2048,128]{2,1,0:T(8,128)(2,1)}, bf16[4,2048,128]{2,1,0:T(8,128)(2,1)}, bf16[2048,1024]{1,0:T(8,128)(2,1)}) custom-call(s32[4]{0:T(128)} %pad_add_fusion.s_ref, bf16[512,1024]{1,0:T(8,128)(2,1)} %convolution_convert_fusion.5.xa_ref.xk_ref.x_ref, bf16[512,1024]{1,0:T(8,128)(2,1)} %collective-permute-done.10.xb_ref.xs_ref, ...), custom_call_target="tpu_custom_call" | custom-call | flops 9900000256 | bytes 1048576 | tf_op jit(solution)/shard_map/qkv/pallas_call | solution.py:118
  106.1 8.3 %qkv.3 = (bf16[4,2048,128]{2,1,0:T(8,128)(2,1)}, bf16[4,2048,128]{2,1,0:T(8,128)(2,1)}, bf16[4,2048,128]{2,1,0:T(8,128)(2,1)}, bf16[2048,1024]{1,0:T(8,128)(2,1)}) custom-call(s32[4]{0:T(128)} %pad_add_fusion.s_ref, bf16[512,1024]{1,0:T(8,128)(2,1)} %collective-permute-done.5.xa_ref.xk_ref, ...), custom_call_target="tpu_custom_call", output_to_operand_aliasing={{0}: (7, {}), {1}: (8, {}), {2}: (9, {}), {3}: (10, {})} | custom-call | flops 9900000256 | bytes 1048576 | tf_op jit(solution)/shard_map/qkv/pallas_call | solution.py:118
  114.4 25.6 %all-to-all-done.1 = bf16[8,64,1024]{2,1,0:T(8,128)(2,1)S(1)} async-done(((bf16[8,64,1024]{2,1,0:T(8,128)(2,1)}), bf16[8,64,1024]{2,1,0:T(8,128)(2,1)S(1)}, u32[]{:S(2)}, u32[]{:S(2)}) %all-to-all-start.1) | async-done | bytes 1048608 | tf_op jit(solution)/shard_map/all_to_all | solution.py:749
  141.4 18.8 %attend_forward.2 = (bf16[1024,256]{1,0:T(8,128)(2,1)}, bf16[4,2048,128]{2,1,0:T(8,128)(2,1)}, f32[4,4,8,128]{3,2,1,0:T(8,128)}) custom-call(s32[4]{0:T(128)} %pad_add_fusion.s_ref, bf16[4,2048,128]{2,1,0:T(8,128)(2,1)} %get-tuple-element.85.q_ref, bf16[4,2048,128]{2,1,0:T(8,128)(2,1)} %get-tuple-element.86.k_ref, bf16[4,2048,128]{2,1,0:T(8,128)(2,1)} %get-tuple-element.87.v_ref), custom_call_target="tpu_custom_call" | custom-call | flops 22000001024 | bytes 1048576 | tf_op jit(solution)/shard_map/attend_forward/pallas_call | solution.py:216
  160.2 4.3 collective-permute-start.14
  164.5 1.7 collective-permute-done.12.gk_ref.g2
  166.2 21.3 %attend_forward.3 = (bf16[1024,256]{1,0:T(8,128)(2,1)}, bf16[4,2048,128]{2,1,0:T(8,128)(2,1)}, f32[4,4,8,128]{3,2,1,0:T(8,128)}) custom-call(s32[4]{0:T(128)} %pad_add_fusion.s_ref, bf16[4,2048,128]{2,1,0:T(8,128)(2,1)} %get-tuple-element.85.q_ref, bf16[4,2048,128]{2,1,0:T(8,128)(2,1)} %get-tuple-element.86.k_ref, ...), custom_call_target="tpu_custom_call", output_to_operand_aliasing={{1}: (4, {})} | custom-call | flops 22000001024 | bytes 1048576 | tf_op jit(solution)/shard_map/attend_forward/pallas_call | solution.py:216
  190.6 24.3 %mlp.2 = (bf16[4,512,1024]{2,1,0:T(8,128)(2,1)}, bf16[4,512,1024]{2,1,0:T(8,128)(2,1)}, bf16[4,512,656]{2,1,0:T(8,128)(2,1)}, bf16[4,512,656]{2,1,0:T(8,128)(2,1...) custom-call(s32[4]{0:T(128)} %pad_add_fusion.s_ref, ...), custom_call_target="tpu_custom_call" | custom-call | flops 26400000000 | bytes 1048576 | tf_op jit(solution)/shard_map/mlp/pallas_call | solution.py:398
  216.1 2.0 collective-permute-done.22
  218.1 2.0 add_convert_fusion.1
  222.6 23.9 %mlp.3 = (bf16[4,512,1024]{2,1,0:T(8,128)(2,1)}, bf16[4,512,1024]{2,1,0:T(8,128)(2,1)}, bf16[4,512,656]{2,1,0:T(8,128)(2,1)}, bf16[4,512,656]{2,1,0:T(8,128)(2,1...) custom-call(s32[4]{0:T(128)} %pad_add_fusion.s_ref, ...), custom_call_target="tpu_custom_call", output_to_operand_aliasing={{0}: (15, {}), {1}: (16, {}), {2}: (17, {}), {3}: (18, {}),... | custom-call | flops 26400000000 | bytes 1048576 | tf_op jit(solution)/shard_map/mlp/pallas_call | solution.py:398
  247.1 2.1 collective-permute-start.29
  249.4 3.3 convert_add_fusion.3.mine_ref
  252.8 4.8 resid.1
  258.8 16.9 %inner_grads.1 = bf16[8,3,128,656]{3,2,1,0:T(8,128)(2,1)} custom-call(bf16[2048,1024]{1,0:T(8,128)(2,1)} %bitcast.158, bf16[512,1024]{1,0:T(8,128)(2,1)} %copy-done.23, bf16[512,1024]{1,0:T(8,128)(2,1)} %copy-done.26, bf16[512,1024]{1,0:T(8,128)(2,1)} %copy-done.24, bf16[512,1024]{1,0:T(8,128)(2,1)} %collective-permute-done.13.gs_ref.g3, ...), custom_call_target="tpu_custom_call" | custom-call | flops 18699999232 | bytes 1048576 | tf_op jit(solution)/shard_map/inner_grads/pallas_call | solution.py:537
  275.7 7.3 %collective-permute-done.28.even_ref = bf16[512,1024]{1,0:T(8,128)(2,1)S(1)} collective-permute-done((bf16[512,1024]{1,0:T(8,128)(2,1)}, bf16[512,1024]{1,0:T(8,128)(2,1)S(1)}, u32[]{:S(2)}, u32[]{:S(2)}) %collective-permute-start.28) | collective-permute-done | bytes 1048608 | tf_op jit(solution)/shard_map/ppermute | solution.py:56
  284.5 1.7 convert_add_fusion.2
  286.3 6.5 %head_grad.2 = (bf16[4,2048,128]{2,1,0:T(8,128)(2,1)}, bf16[1024,1024]{1,0:T(8,128)(2,1)}) custom-call(s32[4]{0:T(128)} %pad_add_fusion.s_ref, bf16[512,1024]{1,0:T(8,128)(2,1)} %get-tuple-element.118.even_ref, bf16[512,1024]{1,0:T(8,128)(2,1)} %collective-permute-done.32.odd_ref, bf16[1024,256]{1,0:T(8,128)(2,1)} %bitcast.44.w0.w_ref, ...), custom_call_target="tpu_custom_call" | custom-call | flops 6600000000 | bytes 1048576 | tf_op jit(solution)/shard_map/head_grad/pallas_call | solution.py:495
  293.2 1.3 collective-permute-start.34
  294.5 6.0 %head_grad.3 = (bf16[4,2048,128]{2,1,0:T(8,128)(2,1)}, bf16[1024,1024]{1,0:T(8,128)(2,1)}) custom-call(s32[4]{0:T(128)} %pad_add_fusion.s_ref, bf16[512,1024]{1,0:T(8,128)(2,1)} %copy-done.27, bf16[512,1024]{1,0:T(8,128)(2,1)} %collective-permute-done.31.odd_ref, bf16[1024,256]{1,0:T(8,128)(2,1)} %bitcast.44.w0.w_ref, ...), custom_call_target="tpu_custom_call", output_to_operand_aliasing={{0}: (5, {})} | custom-call | flops 6600000000 | bytes 1048576 | tf_op jit(solution)/shard_map/head_grad/pallas_call | solution.py:495
  300.4 4.6 outer_grad.1
  305.1 4.3 all-to-all-start.2
  309.4 56.8 %attend_backward.1.p_ref.d_ref = bf16[3,2048,256]{2,1,0:T(8,128)(2,1)} custom-call(s32[4]{0:T(128)} %pad_add_fusion.s_ref, bf16[4,2048,128]{2,1,0:T(8,128)(2,1)} %get-tuple-element.89.q2_ref, bf16[4,2048,128]{2,1,0:T(8,128)(2,1)} %get-tuple-element.86.k_ref, bf16[4,2048,128]{2,1,0:T(8,128)(2,1)} %get-tuple-element.87.v_ref, ...), custom_call_target="tpu_custom_call" | custom-call | flops 62699999232 | bytes 1048576 | tf_op jit(solution)/shard_map/attend_backward/pallas_call | solution.py:312
  366.1 6.3 %dn.3 = bf16[1024,1024]{1,0:T(8,128)(2,1)} custom-call(s32[4]{0:T(128)} %pad_add_fusion.s_ref, bf16[3,2048,256]{2,1,0:T(8,128)(2,1)} %attend_backward.1.p_ref.d_ref, bf16[4,1024,256]{2,1,0:T(8,128)(2,1)} %bitcast.135), custom_call_target="tpu_custom_call" | custom-call | flops 6600000000 | bytes 1048576 | tf_op jit(solution)/shard_map/dn/pallas_call | solution.py:617
  372.5 6.1 %dn.2 = bf16[1024,1024]{1,0:T(8,128)(2,1)} custom-call(s32[4]{0:T(128)} %pad_add_fusion.s_ref, bf16[3,2048,256]{2,1,0:T(8,128)(2,1)} %attend_backward.1.p_ref.d_ref, bf16[4,1024,256]{2,1,0:T(8,128)(2,1)} %bitcast.136), custom_call_target="tpu_custom_call" | custom-call | flops 6600000000 | bytes 1048576 | tf_op jit(solution)/shard_map/dn/pallas_call | solution.py:617
  378.6 2.5 convert_add_fusion
  381.3 1.8 collective-permute-start.36
  384.3 3.8 convolution_convert_fusion.3
  388.1 6.2 %all-to-all-start.3 = ((bf16[8,64,1024]{2,1,0:T(8,128)(2,1)}), bf16[8,64,1024]{2,1,0:T(8,128)(2,1)S(1)}, u32[]{:S(2)}, u32[]{:S(2)}) async-start(bf16[8,64,1024]{2,1,0:T(8,128)(2,1)} %bitcast.50), calls=%async_computation.3 | async-start | bytes 2097152 | tf_op jit(solution)/shard_map/all_to_all | solution.py:749
  394.4 3.2 slice.66.mine_ref
  397.5 8.2 %proj_grads.1 = bf16[8,3,256,128]{3,2,1,0:T(8,128)(2,1)} custom-call(bf16[2048,1024]{1,0:T(8,128)(2,1)} %get-tuple-element.139.n_ref, bf16[3,2048,256]{2,1,0:T(8,128)(2,1)} %attend_backward.1.p_ref.d_ref), custom_call_target="tpu_custom_call" | custom-call | flops 8800000000 | bytes 1048576 | tf_op jit(solution)/shard_map/proj_grads/pallas_call | solution.py:592
  405.8 2.1 dynamic-slice_bitcast_fusion
  407.8 2.0 collective-permute-start.37
  409.8 4.4 last.1
  414.2 3.1 convolution_convert_fusion.2
  417.3 13.2 %collective-permute-done.37 = bf16[4,3,256,128]{3,2,1,0:T(8,128)(2,1)} collective-permute-done((bf16[4,3,256,128]{3,2,1,0:T(8,128)(2,1)}, bf16[4,3,256,128]{3,2,1,0:T(8,128)(2,1)}, u32[]{:S(2)}, u32[]{:S(2)}) %collective-permute-start.37) | collective-permute-done | bytes 786464 | tf_op jit(solution)/shard_map/ppermute | solution.py:56
  431.4 5.7 %all-to-all-start.4 = ((bf16[8,64,1024]{2,1,0:T(8,128)(2,1)}), bf16[8,64,1024]{2,1,0:T(8,128)(2,1)}, u32[]{:S(2)}, u32[]{:S(2)}) async-start(bf16[8,64,1024]{2,1,0:T(8,128)(2,1)} %bitcast.52), calls=%async_computation.4 | async-start | bytes 2097152 | tf_op jit(solution)/shard_map/all_to_all | solution.py:749
  437.1 1.6 convert_add_fusion.4
  438.8 2.1 collective-permute-start.38
  441.3 22.8 %collective-permute-done.38 = bf16[2,3,256,128]{3,2,1,0:T(8,128)(2,1)S(1)} collective-permute-done((bf16[2,3,256,128]{3,2,1,0:T(8,128)(2,1)S(1)}, bf16[2,3,256,128]{3,2,1,0:T(8,128)(2,1)S(1)}, u32[]{:S(2)}, u32[]{:S(2)}) %collective-permute-start.38) | collective-permute-done | bytes 393248 | tf_op jit(solution)/shard_map/ppermute | solution.py:56
  464.2 2.6 collective-permute-start.39
  467.6 6.5 %collective-permute-done.39 = bf16[1,3,256,128]{3,2,1,0:T(8,128)(2,1)S(1)} collective-permute-done((bf16[1,3,256,128]{3,2,1,0:T(8,128)(2,1)S(1)}, bf16[1,3,256,128]{3,2,1,0:T(8,128)(2,1)S(1)}, u32[]{:S(2)}, u32[]{:S(2)}) %collective-permute-start.39) | collective-permute-done | bytes 196640 | tf_op jit(solution)/shard_map/ppermute | solution.py:56
  476.1 1.8 convolution_convert_fusion.1
  477.9 3.1 convolution_convert_fusion
  483.1 1.7 collective-permute-start.40
  484.8 1.8 collective-permute-done.40
  (214 shorter events, 37.1 us)
Async XLA Ops:
  7.2 8.3 %copy-start = (bf16[512,1024]{1,0:T(8,128)(2,1)S(1)}, bf16[512,1024]{1,0:T(8,128)(2,1)}, u32[]{:S(2)}) copy-start(bf16[512,1024]{1,0:T(8,128)(2,1)} %param.10) | copy-start | bytes 3145732
  9.2 21.0 %collective-permute-start.7 = (bf16[4,128,256]{2,1,0:T(8,128)(2,1)S(1)}, bf16[4,128,256]{2,1,0:T(8,128)(2,1)S(1)}, u32[]{:S(2)}, u32[]{:S(2)}) collective-permute-start(bf16[4,128,256]{2,1,0:T(8,128)(2,1)S(1)} %pad_maximum_fusion.4), channel_id=1, source_target_pairs={{0,16},{4,20},{8,24},{12,28},{16,0},{20,4},{24,8},{28,12},{1,17},{... | collective-permute-start | bytes 786440 | tf_op jit(solution)/shard_map/ppermute | solution.py:56
  14.0 14.3 %collective-permute-start = (f32[2,32]{1,0:T(2,128)S(1)}, f32[2,32]{1,0:T(2,128)S(1)}, u32[]{:S(2)}, u32[]{:S(2)}) collective-permute-start(f32[2,32]{1,0:T(2,128)S(1)} %pad_maximum_fusion.8), channel_id=1, source_target_pairs={{0,16},{4,20},{8,24},{12,28},{16,0},{20,4},{24,8},{28,12},{1,17},{... | collective-permute-start | bytes 776 | tf_op jit(solution)/shard_map/ppermute | solution.py:56
  15.5 8.1 %copy-start.16 = (s32[512]{0:T(512)}, s32[512]{0:T(512)S(1)}, u32[]{:S(2)}) copy-start(s32[512]{0:T(512)S(1)} %eq.91) | copy-start | bytes 6148
  15.5 8.1 %copy-start.22 = (bf16[512,1024]{1,0:T(8,128)(2,1)S(1)}, bf16[512,1024]{1,0:T(8,128)(2,1)}, u32[]{:S(2)}) copy-start(bf16[512,1024]{1,0:T(8,128)(2,1)} %param.11) | copy-start | bytes 3145732
  17.2 8.2 %copy-start.12 = (bf16[2,128,656]{1,2,0:T(8,128)(2,1)S(1)}, bf16[2,128,656]{1,2,0:T(8,128)(2,1)}, u32[]{:S(2)}) copy-start(bf16[2,128,656]{1,2,0:T(8,128)(2,1)} %param.18) | copy-start | bytes 1007620
  17.2 39.4 %all-to-all-start = ((bf16[8,64,1024]{2,1,0:T(8,128)(2,1)}), bf16[8,64,1024]{2,1,0:T(8,128)(2,1)}, u32[]{:S(2)}, u32[]{:S(2)}) async-start(bf16[8,64,1024]{2,1,0:T(8,128)(2,1)} %bitcast.4), calls=%async_computation | async-start | bytes 2097152 | tf_op jit(solution)/shard_map/all_to_all | solution.py:749
  23.5 167.1 %all-gather.2.cloned.1.call-start = ((), (), s32[]{:S(2)}) async-start(), calls=%async_computation.6 | async-start | bytes 5308416 | tf_op jit(solution)/shard_map/all_gather | solution.py:775
  25.6 21.5 %copy-start.3 = (bf16[2,128,656]{2,1,0:T(8,128)(2,1)}, bf16[2,128,656]{2,1,0:T(8,128)(2,1)S(1)}, u32[]{:S(2)}) copy-start(bf16[2,128,656]{2,1,0:T(8,128)(2,1)S(1)} %copy.72) | copy-start | bytes 1007620
  26.1 113.9 %copy-start.18 = (s32[512]{0:T(512)}, s32[512]{0:T(512)S(1)}, u32[]{:S(2)}) copy-start(s32[512]{0:T(512)S(1)} %multiply_add_fusion) | copy-start | bytes 6148
  28.3 13.6 %collective-permute-start.1 = (f32[2,2,32]{2,1,0:T(2,128)S(1)}, f32[2,2,32]{2,1,0:T(2,128)S(1)}, u32[]{:S(2)}, u32[]{:S(2)}) collective-permute-start(f32[2,2,32]{2,1,0:T(2,128)S(1)} %pad_maximum_fusion.7), channel_id=1, source_target_pairs={{0,8},{4,12},{8,0},{12,4},{16,24},{20,28},{24,16},{28,20},{1,9},{5... | collective-permute-start | bytes 1544 | tf_op jit(solution)/shard_map/ppermute | solution.py:56
  30.3 23.2 %collective-permute-start.8 = (bf16[2,4,128,256]{3,2,1,0:T(8,128)(2,1)S(1)}, bf16[2,4,128,256]{3,2,1,0:T(8,128)(2,1)S(1)}, u32[]{:S(2)}, u32[]{:S(2)}) collective-permute-start(bf16[2,4,128,256]{3,2,1,0:T(8,128)(2,1)S(1)} %pad_maximum_fusion.3), channel_id=1, source_target_pairs={{0,8},{4,12},{8,0},{12,4},{16,24},{20,28},{24,16},{28,20},{1,9},{5... | collective-permute-start | bytes 1572872 | tf_op jit(solution)/shard_map/ppermute | solution.py:56
  41.9 3.7 collective-permute-start.2
  45.6 9.6 %collective-permute-start.3 = (f32[8,2,32]{2,0,1:T(8,128)S(1)}, f32[8,2,32]{2,0,1:T(8,128)S(1)}, u32[]{:S(2)}, u32[]{:S(2)}) collective-permute-start(f32[8,2,32]{2,0,1:T(8,128)S(1)} %bitcast.146), channel_id=1, source_target_pairs={{0,2},{1,3},{2,0},{3,1},{4,6},{5,7},{6,4},{7,5},{8,10},{9,11},{10,... | collective-permute-start | bytes 6152 | tf_op jit(solution)/shard_map/ppermute | solution.py:56
  53.7 24.3 %collective-permute-start.9 = (bf16[2,2,4,128,256]{4,3,2,0,1:T(8,128)(2,1)S(1)}, bf16[2,2,4,128,256]{4,3,2,0,1:T(8,128)(2,1)S(1)}, u32[]{:S(2)}, u32[]{:S(2)}) collective-permute-start(bf16[2,2,4,128,256]{4,3,2,0,1:T(8,128)(2,1)S(1)} %pad_maximum_fusion.1), channel_id=1, source_target_pairs={{0,4},{4,0},{8,12},{12,8},{16,20},{20,16},{24,28},{28,24},{1,5},{5... | collective-permute-start | bytes 3145736 | tf_op jit(solution)/shard_map/ppermute | solution.py:56
  55.2 1.2 collective-permute-start.4
  56.6 38.5 %copy-start.15 = (f32[2,1024]{1,0:T(2,128)}, f32[2,1024]{1,0:T(2,128)S(1)}, u32[]{:S(2)}) copy-start(f32[2,1024]{1,0:T(2,128)S(1)} %reshape.209) | copy-start | bytes 24580
  59.6 37.1 %collective-permute-start.10 = (bf16[512,1024]{1,0:T(8,128)(2,1)}, bf16[512,1024]{1,0:T(8,128)(2,1)}, u32[]{:S(2)}, u32[]{:S(2)}) collective-permute-start(bf16[512,1024]{1,0:T(8,128)(2,1)} %convolution_convert_fusion.5.xa_ref.xk_ref.x_ref), channel_id=1, source_target_pairs={{0,1},{1,0},{2,3},{3,2},{4,5},{5,4},{6,7},{7,6},{8,9},{9,8},{10,11... | collective-permute-start | bytes 3145736 | tf_op jit(solution)/shard_map/ppermute | solution.py:56
  59.8 35.1 %collective-permute-start.5 = (bf16[512,1024]{1,0:T(8,128)(2,1)}, bf16[512,1024]{1,0:T(8,128)(2,1)}, u32[]{:S(2)}, u32[]{:S(2)}) collective-permute-start(bf16[512,1024]{1,0:T(8,128)(2,1)} %convolution_convert_fusion.5.xa_ref.xk_ref.x_ref), channel_id=1, source_target_pairs={{0,2},{1,3},{2,0},{3,1},{4,6},{5,7},{6,4},{7,5},{8,10},{9,11},{10,... | collective-permute-start | bytes 3145736 | tf_op jit(solution)/shard_map/ppermute | solution.py:56
  79.2 17.6 %collective-permute-start.18 = (bf16[1024,256]{1,0:T(8,128)(2,1)}, bf16[1024,256]{1,0:T(8,128)(2,1)}, u32[]{:S(2)}, u32[]{:S(2)}) collective-permute-start(bf16[1024,256]{1,0:T(8,128)(2,1)} %bitcast.44.w0.w_ref), channel_id=1, source_target_pairs={{0,2},{1,3},{2,0},{3,1},{4,6},{5,7},{6,4},{7,5},{8,10},{9,11},{10,... | collective-permute-start | bytes 1572872 | tf_op jit(solution)/shard_map/ppermute | solution.py:56
  89.1 100.3 %collective-permute-start.17 = (bf16[1024,256]{1,0:T(8,128)(2,1)}, bf16[1024,256]{1,0:T(8,128)(2,1)}, u32[]{:S(2)}, u32[]{:S(2)}) collective-permute-start(bf16[1024,256]{1,0:T(8,128)(2,1)} %bitcast.44.w0.w_ref), channel_id=1, source_target_pairs={{0,1},{1,0},{2,3},{3,2},{4,5},{5,4},{6,7},{7,6},{8,9},{9,8},{10,11... | collective-permute-start | bytes 1572872 | tf_op jit(solution)/shard_map/ppermute | solution.py:56
  89.1 50.9 %all-to-all-start.1 = ((bf16[8,64,1024]{2,1,0:T(8,128)(2,1)}), bf16[8,64,1024]{2,1,0:T(8,128)(2,1)S(1)}, u32[]{:S(2)}, u32[]{:S(2)}) async-start(bf16[8,64,1024]{2,1,0:T(8,128)(2,1)} %bitcast.40), calls=%async_computation.1 | async-start | bytes 2097152 | tf_op jit(solution)/shard_map/all_to_all | solution.py:749
  94.6 386.3 %reduce-scatter.2.cloned.1.call-start = ((), (), s32[]{:S(2)}) async-start(), calls=%async_computation.7 | async-start | bytes 5308416 | tf_op jit(solution)/shard_map/reduce_scatter | solution.py:857
  94.8 10.2 %collective-permute-start.6 = (bf16[512,1024]{1,0:T(8,128)(2,1)}, bf16[512,1024]{1,0:T(8,128)(2,1)S(1)}, u32[]{:S(2)}, u32[]{:S(2)}) collective-permute-start(bf16[512,1024]{1,0:T(8,128)(2,1)} %collective-permute-done.5.xa_ref.xk_ref), channel_id=1, source_target_pairs={{0,1},{1,0},{2,3},{3,2},{4,5},{5,4},{6,7},{7,6},{8,9},{9,8},{10,11... | collective-permute-start | bytes 3145736 | tf_op jit(solution)/shard_map/ppermute | solution.py:56
  96.7 92.7 %collective-permute-start.19 = (bf16[1024,256]{1,0:T(8,128)(2,1)}, bf16[1024,256]{1,0:T(8,128)(2,1)}, u32[]{:S(2)}, u32[]{:S(2)}) collective-permute-start(bf16[1024,256]{1,0:T(8,128)(2,1)} %collective-permute-done.18.w2), channel_id=1, source_target_pairs={{0,1},{1,0},{2,3},{3,2},{4,5},{5,4},{6,7},{7,6},{8,9},{9,8},{10,11... | collective-permute-start | bytes 1572872 | tf_op jit(solution)/shard_map/ppermute | solution.py:56
  140.7 74.7 %copy-start.23 = (bf16[512,1024]{1,0:T(8,128)(2,1)}, bf16[512,1024]{1,0:T(8,128)(2,1)S(1)}, u32[]{:S(2)}) copy-start(bf16[512,1024]{1,0:T(8,128)(2,1)S(1)} %convolution_convert_fusion.4.gk_ref.g_ref.g0) | copy-start | bytes 3145732
  140.7 25.5 %collective-permute-start.12 = (bf16[512,1024]{1,0:T(8,128)(2,1)S(1)}, bf16[512,1024]{1,0:T(8,128)(2,1)S(1)}, u32[]{:S(2)}, u32[]{:S(2)}) collective-permute-start(bf16[512,1024]{1,0:T(8,128)(2,1)S(1)} %convolution_convert_fusion.4.gk_ref.g_ref.g0), channel_id=1, source_target_pairs={{0,2},{1,3},{2,0},{3,1},{4,6},{5,7},{6,4},{7,5},{8,10},{9,11},{10,... | collective-permute-start | bytes 3145736 | tf_op jit(solution)/shard_map/ppermute | solution.py:56
  160.2 27.4 %collective-permute-start.14 = (bf16[1024,256]{1,0:T(8,128)(2,1)}, bf16[1024,256]{1,0:T(8,128)(2,1)S(1)}, u32[]{:S(2)}, u32[]{:S(2)}) collective-permute-start(bf16[1024,256]{1,0:T(8,128)(2,1)} %get-tuple-element.102.o0.o_ref), channel_id=1, source_target_pairs={{0,2},{1,3},{2,0},{3,1},{4,6},{5,7},{6,4},{7,5},{8,10},{9,11},{10,... | collective-permute-start | bytes 1572872 | tf_op jit(solution)/shard_map/ppermute | solution.py:56
  166.2 21.4 %copy-start.24 = (bf16[512,1024]{1,0:T(8,128)(2,1)}, bf16[512,1024]{1,0:T(8,128)(2,1)S(1)}, u32[]{:S(2)}) copy-start(bf16[512,1024]{1,0:T(8,128)(2,1)S(1)} %collective-permute-done.12.gk_ref.g2) | copy-start | bytes 3145732
  166.2 24.4 %collective-permute-start.13 = (bf16[512,1024]{1,0:T(8,128)(2,1)S(1)}, bf16[512,1024]{1,0:T(8,128)(2,1)}, u32[]{:S(2)}, u32[]{:S(2)}) collective-permute-start(bf16[512,1024]{1,0:T(8,128)(2,1)S(1)} %collective-permute-done.12.gk_ref.g2), channel_id=1, source_target_pairs={{0,1},{1,0},{2,3},{3,2},{4,5},{5,4},{6,7},{7,6},{8,9},{9,8},{10,11... | collective-permute-start | bytes 3145736 | tf_op jit(solution)/shard_map/ppermute | solution.py:56
  166.2 23.0 %copy-start.14 = (f32[4,4,8,128]{3,2,1,0:T(8,128)S(1)}, f32[4,4,8,128]{3,2,1,0:T(8,128)}, u32[]{:S(2)}) copy-start(f32[4,4,8,128]{3,2,1,0:T(8,128)} %get-tuple-element.97) | copy-start | bytes 196612
  187.6 2.5 collective-permute-start.15
  188.2 2.4 collective-permute-start.16
  189.3 25.6 %collective-permute-start.21 = (f32[4]{0:T(128)S(1)}, f32[4]{0:T(128)S(1)}, u32[]{:S(2)}, u32[]{:S(2)}) collective-permute-start(f32[4]{0:T(128)S(1)} %maximum_multiply_fusion), channel_id=1, source_target_pairs={{0,4},{4,0},{8,12},{12,8},{16,20},{20,16},{24,28},{28,24},{1,5},{5... | collective-permute-start | bytes 56 | tf_op jit(solution)/shard_map/ppermute | solution.py:56
  189.4 25.5 %collective-permute-start.20 = (bf16[1024,256]{1,0:T(8,128)(2,1)}, bf16[1024,256]{1,0:T(8,128)(2,1)}, u32[]{:S(2)}, u32[]{:S(2)}) collective-permute-start(bf16[1024,256]{1,0:T(8,128)(2,1)} %get-tuple-element.94.o0.o_ref.o1), channel_id=1, source_target_pairs={{0,2},{1,3},{2,0},{3,1},{4,6},{5,7},{6,4},{7,5},{8,10},{9,11},{10,... | collective-permute-start | bytes 1572872 | tf_op jit(solution)/shard_map/ppermute | solution.py:56
  190.6 24.9 %copy-start.28 = (bf16[1024,256]{1,0:T(8,128)(2,1)S(1)}, bf16[1024,256]{1,0:T(8,128)(2,1)}, u32[]{:S(2)}) copy-start(bf16[1024,256]{1,0:T(8,128)(2,1)} %get-tuple-element.102.o0.o_ref) | copy-start | bytes 1572868
  215.0 3.1 collective-permute-start.22
  215.4 5.5 %collective-permute-start.11 = (bf16[512,1024]{1,0:T(8,128)(2,1)S(1)}, bf16[512,1024]{1,0:T(8,128)(2,1)S(1)}, u32[]{:S(2)}, u32[]{:S(2)}) collective-permute-start(bf16[512,1024]{1,0:T(8,128)(2,1)S(1)} %convolution_convert_fusion.4.gk_ref.g_ref.g0), channel_id=1, source_target_pairs={{0,1},{1,0},{2,3},{3,2},{4,5},{5,4},{6,7},{7,6},{8,9},{9,8},{10,11... | collective-permute-start | bytes 3145736 | tf_op jit(solution)/shard_map/ppermute | solution.py:56
  215.5 5.4 %collective-permute-start.23 = (bf16[1024,256]{1,0:T(8,128)(2,1)S(1)}, bf16[1024,256]{1,0:T(8,128)(2,1)S(1)}, u32[]{:S(2)}, u32[]{:S(2)}) collective-permute-start(bf16[1024,256]{1,0:T(8,128)(2,1)S(1)} %copy-done.28), channel_id=1, source_target_pairs={{0,1},{1,0},{2,3},{3,2},{4,5},{5,4},{6,7},{7,6},{8,9},{9,8},{10,11... | collective-permute-start | bytes 1572872 | tf_op jit(solution)/shard_map/ppermute | solution.py:56
  215.9 5.8 %collective-permute-start.24 = (bf16[1024,256]{1,0:T(8,128)(2,1)}, bf16[1024,256]{1,0:T(8,128)(2,1)S(1)}, u32[]{:S(2)}, u32[]{:S(2)}) collective-permute-start(bf16[1024,256]{1,0:T(8,128)(2,1)} %collective-permute-done.20.o2), channel_id=1, source_target_pairs={{0,1},{1,0},{2,3},{3,2},{4,5},{5,4},{6,7},{7,6},{8,9},{9,8},{10,11... | collective-permute-start | bytes 1572872 | tf_op jit(solution)/shard_map/ppermute | solution.py:56
  216.1 30.4 %collective-permute-start.26 = (f32[4]{0:T(128)S(1)}, f32[4]{0:T(128)S(1)}, u32[]{:S(2)}, u32[]{:S(2)}) collective-permute-start(f32[4]{0:T(128)S(1)} %max.12), channel_id=1, source_target_pairs={{0,8},{4,12},{8,0},{12,4},{16,24},{20,28},{24,16},{28,20},{1,9},{5... | collective-permute-start | bytes 56 | tf_op jit(solution)/shard_map/ppermute | solution.py:56
  220.1 26.4 %collective-permute-start.25 = (bf16[512,1024]{1,0:T(8,128)(2,1)S(1)}, bf16[512,1024]{1,0:T(8,128)(2,1)}, u32[]{:S(2)}, u32[]{:S(2)}) collective-permute-start(bf16[512,1024]{1,0:T(8,128)(2,1)S(1)} %add_convert_fusion.1), channel_id=1, source_target_pairs={{0,2},{1,3},{2,0},{3,1},{4,6},{5,7},{6,4},{7,5},{8,10},{9,11},{10,... | collective-permute-start | bytes 3145736 | tf_op jit(solution)/shard_map/ppermute | solution.py:56
  246.5 2.9 collective-permute-start.27
  246.8 37.7 %collective-permute-start.33 = (bf16[512,1024]{1,0:T(8,128)(2,1)}, bf16[512,1024]{1,0:T(8,128)(2,1)S(1)}, u32[]{:S(2)}, u32[]{:S(2)}) collective-permute-start(bf16[512,1024]{1,0:T(8,128)(2,1)} %get-tuple-element.130), channel_id=1, source_target_pairs={{0,1},{1,0},{2,3},{3,2},{4,5},{5,4},{6,7},{7,6},{8,9},{9,8},{10,11... | collective-permute-start | bytes 3145736 | tf_op jit(solution)/shard_map/ppermute | solution.py:56
  247.1 28.7 %collective-permute-start.29 = (f32[4]{0:T(128)S(1)}, f32[4]{0:T(128)S(1)}, u32[]{:S(2)}, u32[]{:S(2)}) collective-permute-start(f32[4]{0:T(128)S(1)} %max.13), channel_id=1, source_target_pairs={{0,16},{4,20},{8,24},{12,28},{16,0},{20,4},{24,8},{28,12},{1,17},{... | collective-permute-start | bytes 56 | tf_op jit(solution)/shard_map/ppermute | solution.py:56
  257.5 25.5 %collective-permute-start.28 = (bf16[512,1024]{1,0:T(8,128)(2,1)}, bf16[512,1024]{1,0:T(8,128)(2,1)S(1)}, u32[]{:S(2)}, u32[]{:S(2)}) collective-permute-start(bf16[512,1024]{1,0:T(8,128)(2,1)} %get-tuple-element.118.even_ref), channel_id=1, source_target_pairs={{0,2},{1,3},{2,0},{3,1},{4,6},{5,7},{6,4},{7,5},{8,10},{9,11},{10,... | collective-permute-start | bytes 3145736 | tf_op jit(solution)/shard_map/ppermute | solution.py:56
  258.8 27.5 %collective-permute-start.32 = (bf16[512,1024]{1,0:T(8,128)(2,1)}, bf16[512,1024]{1,0:T(8,128)(2,1)}, u32[]{:S(2)}, u32[]{:S(2)}) collective-permute-start(bf16[512,1024]{1,0:T(8,128)(2,1)} %get-tuple-element.118.even_ref), channel_id=1, source_target_pairs={{0,1},{1,0},{2,3},{3,2},{4,5},{5,4},{6,7},{7,6},{8,9},{9,8},{10,11... | collective-permute-start | bytes 3145736 | tf_op jit(solution)/shard_map/ppermute | solution.py:56
  258.8 25.7 %copy-start.11 = (bf16[512,1024]{1,0:T(8,128)(2,1)S(1)}, bf16[512,1024]{1,0:T(8,128)(2,1)}, u32[]{:S(2)}) copy-start(bf16[512,1024]{1,0:T(8,128)(2,1)} %get-tuple-element.129) | copy-start | bytes 3145732
  284.0 8.8 %collective-permute-start.30 = (bf16[512,1024]{1,0:T(8,128)(2,1)}, bf16[512,1024]{1,0:T(8,128)(2,1)S(1)}, u32[]{:S(2)}, u32[]{:S(2)}) collective-permute-start(bf16[512,1024]{1,0:T(8,128)(2,1)} %get-tuple-element.126), channel_id=1, source_target_pairs={{0,1},{1,0},{2,3},{3,2},{4,5},{5,4},{6,7},{7,6},{8,9},{9,8},{10,11... | collective-permute-start | bytes 3145736 | tf_op jit(solution)/shard_map/ppermute | solution.py:56
  284.0 10.5 %collective-permute-start.31 = (bf16[512,1024]{1,0:T(8,128)(2,1)}, bf16[512,1024]{1,0:T(8,128)(2,1)}, u32[]{:S(2)}, u32[]{:S(2)}) collective-permute-start(bf16[512,1024]{1,0:T(8,128)(2,1)} %copy-done.27), channel_id=1, source_target_pairs={{0,1},{1,0},{2,3},{3,2},{4,5},{5,4},{6,7},{7,6},{8,9},{9,8},{10,11... | collective-permute-start | bytes 3145736 | tf_op jit(solution)/shard_map/ppermute | solution.py:56
  293.2 79.2 %collective-permute-start.34 = (bf16[512,1024]{1,0:T(8,128)(2,1)S(1)}, bf16[512,1024]{1,0:T(8,128)(2,1)}, u32[]{:S(2)}, u32[]{:S(2)}) collective-permute-start(bf16[512,1024]{1,0:T(8,128)(2,1)S(1)} %add_convert_fusion), channel_id=1, source_target_pairs={{0,2},{1,3},{2,0},{3,1},{4,6},{5,7},{6,4},{7,5},{8,10},{9,11},{10,... | collective-permute-start | bytes 3145736 | tf_op jit(solution)/shard_map/ppermute | solution.py:56
  305.1 67.3 %all-to-all-start.2 = ((bf16[8,1,256,128]{3,2,1,0:T(8,128)(2,1)}), bf16[8,1,256,128]{3,2,1,0:T(8,128)(2,1)S(1)}, u32[]{:S(2)}, u32[]{:S(2)}) async-start(bf16[8,1,256,128]{3,2,1,0:T(8,128)(2,1)} %outer_grad.1), calls=%async_computation.2 | async-start | bytes 1048576 | tf_op jit(solution)/shard_map/all_to_all | solution.py:868
  372.4 6.2 %collective-permute-start.35 = (bf16[1024,1024]{1,0:T(8,128)(2,1)}, bf16[1024,1024]{1,0:T(8,128)(2,1)S(1)}, u32[]{:S(2)}, u32[]{:S(2)}) collective-permute-start(bf16[1024,1024]{1,0:T(8,128)(2,1)} %dn.3), channel_id=1, source_target_pairs={{0,1},{1,0},{2,3},{3,2},{4,5},{5,4},{6,7},{7,6},{8,9},{9,8},{10,11... | collective-permute-start | bytes 6291464 | tf_op jit(solution)/shard_map/ppermute | solution.py:56
  381.1 7.0 %copy-start.2 = (f32[1024,1024]{1,0:T(8,128)}, f32[1024,1024]{1,0:T(8,128)S(1)}, u32[]{:S(2)}) copy-start(f32[1024,1024]{1,0:T(8,128)S(1)} %convert_add_fusion) | copy-start | bytes 12582916
  381.3 28.5 %collective-permute-start.36 = (bf16[512,1024]{1,0:T(8,128)(2,1)S(1)}, bf16[512,1024]{1,0:T(8,128)(2,1)}, u32[]{:S(2)}, u32[]{:S(2)}) collective-permute-start(bf16[512,1024]{1,0:T(8,128)(2,1)S(1)} %slice.89), channel_id=1, source_target_pairs={{0,2},{1,3},{2,0},{3,1},{4,6},{5,7},{6,4},{7,5},{8,10},{9,11},{10,... | collective-permute-start | bytes 3145736 | tf_op jit(solution)/shard_map/ppermute | solution.py:56
  388.1 42.4 %all-to-all-start.3 = ((bf16[8,64,1024]{2,1,0:T(8,128)(2,1)}), bf16[8,64,1024]{2,1,0:T(8,128)(2,1)S(1)}, u32[]{:S(2)}, u32[]{:S(2)}) async-start(bf16[8,64,1024]{2,1,0:T(8,128)(2,1)} %bitcast.50), calls=%async_computation.3 | async-start | bytes 2097152 | tf_op jit(solution)/shard_map/all_to_all | solution.py:749
  407.8 22.7 %collective-permute-start.37 = (bf16[4,3,256,128]{3,2,1,0:T(8,128)(2,1)}, bf16[4,3,256,128]{3,2,1,0:T(8,128)(2,1)}, u32[]{:S(2)}, u32[]{:S(2)}) collective-permute-start(bf16[4,3,256,128]{3,2,1,0:T(8,128)(2,1)} %dynamic-slice_bitcast_fusion), channel_id=1, source_target_pairs={{0,4},{4,0},{8,12},{12,8},{16,20},{20,16},{24,28},{28,24},{1,5},{5... | collective-permute-start | bytes 2359304 | tf_op jit(solution)/shard_map/ppermute | solution.py:56
  431.4 46.4 %all-to-all-start.4 = ((bf16[8,64,1024]{2,1,0:T(8,128)(2,1)}), bf16[8,64,1024]{2,1,0:T(8,128)(2,1)}, u32[]{:S(2)}, u32[]{:S(2)}) async-start(bf16[8,64,1024]{2,1,0:T(8,128)(2,1)} %bitcast.52), calls=%async_computation.4 | async-start | bytes 2097152 | tf_op jit(solution)/shard_map/all_to_all | solution.py:749
  438.8 25.2 %collective-permute-start.38 = (bf16[2,3,256,128]{3,2,1,0:T(8,128)(2,1)S(1)}, bf16[2,3,256,128]{3,2,1,0:T(8,128)(2,1)S(1)}, u32[]{:S(2)}, u32[]{:S(2)}) collective-permute-start(bf16[2,3,256,128]{3,2,1,0:T(8,128)(2,1)S(1)} %fusion.21), channel_id=1, source_target_pairs={{0,8},{4,12},{8,0},{12,4},{16,24},{20,28},{24,16},{28,20},{1,9},{5... | collective-permute-start | bytes 1179656 | tf_op jit(solution)/shard_map/ppermute | solution.py:56
  464.1 12.0 %copy-start.10 = (bf16[8,64,1024]{2,1,0:T(8,128)(2,1)S(1)}, bf16[8,64,1024]{2,1,0:T(8,128)(2,1)}, u32[]{:S(2)}) copy-start(bf16[8,64,1024]{2,1,0:T(8,128)(2,1)} %copy-done.9) | copy-start | bytes 3145732
  464.1 11.9 %copy-start.17 = (s32[512]{0:T(512)S(1)}, s32[512]{0:T(512)}, u32[]{:S(2)}) copy-start(s32[512]{0:T(512)} %copy-done.16) | copy-start | bytes 6148
  464.2 10.0 %collective-permute-start.39 = (bf16[1,3,256,128]{3,2,1,0:T(8,128)(2,1)S(1)}, bf16[1,3,256,128]{3,2,1,0:T(8,128)(2,1)S(1)}, u32[]{:S(2)}, u32[]{:S(2)}) collective-permute-start(bf16[1,3,256,128]{3,2,1,0:T(8,128)(2,1)S(1)} %dynamic-slice_convert_fusion.1), channel_id=1, source_target_pairs={{0,16},{4,20},{8,24},{12,28},{16,0},{20,4},{24,8},{28,12},{1,17},{... | collective-permute-start | bytes 589832 | tf_op jit(solution)/shard_map/ppermute | solution.py:56
  483.1 3.6 collective-permute-start.40
  486.8 2.0 collective-permute-start.41
  (20 other events, 67.6 us)
Sparse Core Ops, SparseCore 0:
  86.4 99.7 all-gather.1
  286.4 106.4 reduce-scatter.1

commit v3 on v2

--- a/solution.py
+++ b/solution.py
@@ -65,7 +65,8 @@
 
 
 def takes(micros):
-    return pl.CostEstimate(flops=micros * 1_100_000_000, bytes_accessed=1 << 20, transcendentals=0)
+    flops = max(micros * 1_100_000_000, 1024)
+    return pl.CostEstimate(flops=flops, bytes_accessed=flops // 1024, transcendentals=0)
 
 
 def resident(shape):
@@ -133,8 +134,8 @@
             out_specs=[head_spec] * 3 + [pl.BlockSpec((step, width), place)],
         ),
         input_output_aliases={7 + i: i for i in range(len(held))},
-        compiler_params=vmem(60),
-        cost_estimate=takes(9),
+        compiler_params=vmem(48),
+        cost_estimate=takes(3),
         name="qkv",
     )(scalars, xa, xb, gain, w_qkv, cos, sin, *held)
 
@@ -240,7 +241,7 @@
                 pltpu.VMEM((heads, q_rows, LANES), F32),
             ],
         ),
-        compiler_params=vmem(60),
+        compiler_params=vmem(48),
         cost_estimate=takes(20),
         input_output_aliases={4 + i: 1 + i for i in range(len(held))},
         name="attend_forward",
@@ -329,7 +330,7 @@
                 pltpu.VMEM((heads, tokens, LANES), F32),
             ],
         ),
-        compiler_params=vmem(60),
+        compiler_params=vmem(48),
         cost_estimate=takes(57),
         name="attend_backward",
     )(scalars, q2, k, v, do, cos, sin)
@@ -338,7 +339,8 @@
 def mlp_kernel(
     s_ref, xs_ref, xk_ref, gs_ref, gk_ref, o0, o1, o2, o3, w0, w1, w2, w3, gain_ref, w_ref, *rest
 ):
-    a_ref, n_ref, act_ref, dgate_ref, dup_ref, keep_ref, send_ref, keep_out, send_out = rest[-9:]
+    a_ref, n_ref, g_out, act_ref, dgate_ref, dup_ref = rest[-10:-4]
+    keep_ref, send_ref, keep_out, send_out = rest[-4:]
     units = w_ref.shape[2]
     sending = pl.program_id(0) < pl.num_programs(0) // 2
     x = jnp.where(sending, xs_ref[...], xk_ref[...])
@@ -350,6 +352,7 @@
     normed, _ = row_stats(x.astype(F32) + branch.astype(F32))
     n2 = (normed * gain_ref[...]).astype(BF16)
     n_ref[...] = n2
+    g_out[...] = g
     partial = out_partial = 0.0
     for low in range(0, units, 256):
         cols = slice(low, min(low + 256, units))
@@ -398,6 +401,7 @@
     return pl.pallas_call(
         mlp_kernel,
         out_shape=(
+            wide_out,
             wide_out,
             wide_out,
             narrow_out,
@@ -416,10 +420,10 @@
             + [resident(w.shape) for w in w_out_rel]
             + [resident(gain.shape), resident(w_mlp.shape)]
             + [pl.BlockSpec(memory_space=pl.ANY)] * len(held),
-            out_specs=[wide, wide, narrow, narrow, narrow, keep, send, keep, send],
+            out_specs=[wide, wide, wide, narrow, narrow, narrow, keep, send, keep, send],
         ),
         input_output_aliases={15 + i: i for i in range(len(held))},
-        compiler_params=vmem(60),
+        compiler_params=vmem(48),
         cost_estimate=takes(24),
         name="mlp",
     )(scalars, *x_pair, *g_pair, *heads_rel, *w_out_rel, gain, w_mlp, *held)
@@ -431,16 +435,16 @@
     return (cotangent - mean - normed * along) * scale
 
 
-def resid_kernel(mine_ref, arrived_ref, x_ref, a_ref, g_ref, gain_ref, dx_ref, da_ref):
-    dn = mine_ref[...] + arrived_ref[...].astype(F32)
+def resid_kernel(keep_ref, core_ref, chip_ref, x_ref, a_ref, g_ref, gain_ref, dx_ref, da_ref):
+    dn = keep_ref[...] + core_ref[...].astype(F32) + chip_ref[...].astype(F32)
     normed, scale = row_stats(x_ref[...].astype(F32) + a_ref[...].astype(F32))
     dx = g_ref[...].astype(F32) + pull_norm(normed, scale, dn * gain_ref[...])
     dx_ref[...] = dx
     da_ref[...] = dx.astype(BF16)
 
 
-def resid_call(mine, arrived, x, a_rel, g, gain, step=256):
-    rows, width = mine.shape
+def resid_call(keep, core, chip, x, a_rel, g, gain, step=256):
+    rows, width = keep.shape
     per = rows // step
     flat = pl.BlockSpec((step, width), lambda i: (i, 0))
     return pl.pallas_call(
@@ -454,15 +458,16 @@
             flat,
             flat,
             flat,
+            flat,
             pl.BlockSpec((None, step, width), lambda i: (0, i, 0)),
             flat,
             resident(gain.shape),
         ],
         out_specs=[flat, flat],
-        compiler_params=vmem(60),
+        compiler_params=vmem(48),
         cost_estimate=takes(5),
         name="resid",
-    )(mine, arrived, x, a_rel, g, gain)
+    )(keep, core, chip, x, a_rel, g, gain)
 
 
 def head_grad_kernel(s_ref, even_ref, odd_ref, w_ref, o_ref, *rest):
@@ -496,7 +501,7 @@
         head_grad_kernel,
         out_shape=(
             jax.ShapeDtypeStruct((heads, tokens, LANES), BF16),
-            jax.ShapeDtypeStruct((2 * rows, width), BF16),
+            jax.ShapeDtypeStruct((tokens, width), BF16),
         ),
         grid_spec=pltpu.PrefetchScalarGridSpec(
             num_scalar_prefetch=1,
@@ -510,138 +515,135 @@
             + [pl.BlockSpec(memory_space=pl.ANY)] * len(held),
             out_specs=[
                 pl.BlockSpec((heads, rows, LANES), lambda i, s: (0, 2 * (s[3] ^ far) + i, 0)),
-                pl.BlockSpec((rows, width), lambda i, s: (i, 0)),
+                pl.BlockSpec((rows, width), lambda i, s: (2 * far + i, 0)),
             ],
         ),
         input_output_aliases={5 + i: i for i in range(len(held))},
-        compiler_params=vmem(60),
+        compiler_params=vmem(48),
         cost_estimate=takes(6),
         name="head_grad",
     )(scalars, even, odd, w_out, o_chunk, *held)
 
 
-def inner_kernel(n_ref, g0, g1, g2, g3, dgate_ref, dup_ref, act_ref, out_ref):
-    n2 = n_ref[...]
-    out_ref[0] = dot(n2, dgate_ref[...], 0, 0).astype(BF16)
-    out_ref[1] = dot(n2, dup_ref[...], 0, 0).astype(BF16)
-    rows = g0.shape[0]
-    g = jnp.concatenate([g0[...], g1[...], g2[...], g3[...]], axis=0)
-    out_ref[2] = dot(g, act_ref[...], 0, 0).astype(BF16)
-
-
-def inner_call(n2, g_rel, dgate, dup, act):
-    tokens, width = n2.shape
-    units = act.shape[1]
-    rows = g_rel[0].shape[0]
-    count = width // LANES
-    return pl.pallas_call(
-        inner_kernel,
-        out_shape=jax.ShapeDtypeStruct((count, 3, LANES, units), BF16),
-        grid=(count,),
-        in_specs=[pl.BlockSpec((tokens, LANES), lambda i: (0, i))]
-        + [pl.BlockSpec((rows, LANES), lambda i: (0, i))] * 4
-        + [resident(act.shape)] * 3,
-        out_specs=pl.BlockSpec((None, 3, LANES, units), lambda i: (i, 0, 0, 0)),
-        compiler_params=vmem(60),
-        cost_estimate=takes(17),
-        name="inner_grads",
-    )(n2, *g_rel, dgate, dup, act)
-
-
 def store_slices(out_ref, at, sums):
     for i in range(out_ref.shape[0]):
         out_ref[i, at] = sums[:, i * LANES : (i + 1) * LANES].astype(BF16)
 
 
-def outer_kernel(o0, o1, da0, da1, out_ref):
-    store_slices(out_ref, 0, dot(o0[...], da0[...], 0, 0) + dot(o1[...], da1[...], 0, 0))
-
-
-def outer_call(o_chunks, da_chunks):
-    rows, width = da_chunks[0].shape
-    cols = o_chunks[0].shape[1]
-    out = (width // LANES, 1, cols, LANES)
-    return pl.pallas_call(
-        outer_kernel,
-        out_shape=jax.ShapeDtypeStruct(out, BF16),
-        compiler_params=vmem(60),
-        cost_estimate=takes(5),
-        name="outer_grad",
-    )(*o_chunks, *da_chunks)
-
-
-def proj_kernel(n_ref, d_ref, out_ref, acc):
-    step = pl.program_id(0)
-    for at in range(d_ref.shape[0]):
-        sums = dot(d_ref[at], n_ref[...], 0, 0)
+def inner_kernel(n_ref, g_ref, dgate_ref, dup_ref, act_ref, out_ref, acc):
+    step, last = pl.program_id(0), pl.num_programs(0) - 1
+    for at, (right, left) in enumerate(((dgate_ref, n_ref), (dup_ref, n_ref), (act_ref, g_ref))):
+        sums = dot(right[...], left[...], 0, 0)
 
         @pl.when(step == 0)
         def _(sums=sums, at=at):
             acc[at] = sums
 
-        @pl.when(step > 0)
+        @pl.when((step > 0) & (step < last))
+        def _(sums=sums, at=at):
+            acc[at] += sums
+
+        @pl.when(step == last)
         def _(sums=sums, at=at):
             store_slices(out_ref, at, acc[at] + sums)
 
 
-def proj_call(n1, dproj):
+def inner_call(n2, g_rel, dgate, dup, act, steps=4):
+    tokens, width = n2.shape
+    units = act.shape[1]
+    step = tokens // steps
+    out = (width // LANES, 3, units, LANES)
+    wide = pl.BlockSpec((step, width), lambda i: (i, 0))
+    narrow = pl.BlockSpec((step, units), lambda i: (i, 0))
+    return pl.pallas_call(
+        inner_kernel,
+        out_shape=jax.ShapeDtypeStruct(out, BF16),
+        grid=(steps,),
+        in_specs=[wide, wide, narrow, narrow, narrow],
+        out_specs=resident(out),
+        scratch_shapes=[pltpu.VMEM((3, units, width), F32)],
+        compiler_params=vmem(48),
+        cost_estimate=takes(18),
+        name="inner_grads",
+    )(n2, g_rel, dgate, dup, act)
+
+
+def proj_kernel(n_ref, d_ref, o0, o1, da_ref, out_ref, acc):
+    step = pl.program_id(0)
+    kinds = d_ref.shape[0]
+
+    @pl.when(step == 0)
+    def _():
+        for at in range(kinds):
+            acc[at] = dot(d_ref[at], n_ref[...], 0, 0)
+        acc[kinds] = dot(o0[...], da_ref[...], 0, 0)
+
+    @pl.when(step == 1)
+    def _():
+        for at in range(kinds):
+            store_slices(out_ref, at, acc[at] + dot(d_ref[at], n_ref[...], 0, 0))
+        store_slices(out_ref, kinds, acc[kinds] + dot(o1[...], da_ref[...], 0, 0))
+
+
+def proj_call(n1, dproj, o_chunks, da):
     tokens, width = n1.shape
     kinds, _, cols = dproj.shape
     step = tokens // 2
-    out = (width // LANES, kinds, cols, LANES)
+    out = (width // LANES, kinds + 1, cols, LANES)
+    wide = pl.BlockSpec((step, width), lambda i: (i, 0))
     return pl.pallas_call(
         proj_kernel,
         out_shape=jax.ShapeDtypeStruct(out, BF16),
         grid=(2,),
         in_specs=[
-            pl.BlockSpec((step, width), lambda i: (i, 0)),
+            wide,
             pl.BlockSpec((kinds, step, cols), lambda i: (0, i, 0)),
+            resident(o_chunks[0].shape),
+            resident(o_chunks[1].shape),
+            wide,
         ],
         out_specs=resident(out),
-        scratch_shapes=[pltpu.VMEM((kinds, cols, width), F32)],
-        compiler_params=vmem(60),
-        cost_estimate=takes(8),
+        scratch_shapes=[pltpu.VMEM((kinds + 1, cols, width), F32)],
+        compiler_params=vmem(48),
+        cost_estimate=takes(10),
         name="proj_grads",
-    )(n1, dproj)
-
-
-def dn_kernel(p_ref, w_ref, out_ref):
+    )(n1, dproj, *o_chunks, da)
+
+
+def dn_kernel(s_ref, p_ref, w_ref, out_ref):
     total = dot(p_ref[0], w_ref[0], 1, 1) + dot(p_ref[1], w_ref[1], 1, 1)
     out_ref[...] = (total + dot(p_ref[2], w_ref[2], 1, 1)).astype(BF16)
 
 
-def dn_call(scalars, dproj, w_qkv, parity, rows, step=256):
-    kinds, tokens, cols = dproj.shape
+def dn_call(scalars, dproj, w_qkv, rel, rows):
+    kinds, _, cols = dproj.shape
     width = w_qkv.shape[1]
-    per = rows // step
-    return pl.pallas_call(
-        lambda s_ref, p_ref, w_ref, out_ref: dn_kernel(p_ref, w_ref, out_ref),
-        out_shape=jax.ShapeDtypeStruct((2 * rows, width), BF16),
+    return pl.pallas_call(
+        dn_kernel,
+        out_shape=jax.ShapeDtypeStruct((rows, width), BF16),
         grid_spec=pltpu.PrefetchScalarGridSpec(
             num_scalar_prefetch=1,
-            grid=(2 * per,),
+            grid=(1,),
             in_specs=[
-                pl.BlockSpec(
-                    (kinds, step, cols),
-                    lambda i, s: (0, ((2 * (i // per) + parity) ^ s[0]) * per + i % per, 0),
-                ),
+                pl.BlockSpec((kinds, rows, cols), lambda i, s: (0, rel ^ s[0], 0)),
                 resident((kinds, width, cols)),
             ],
-            out_specs=pl.BlockSpec((step, width), lambda i, s: (i, 0)),
+            out_specs=pl.BlockSpec((rows, width), lambda i, s: (0, 0)),
         ),
-        compiler_params=vmem(60),
-        cost_estimate=takes(6),
+        compiler_params=vmem(48),
+        cost_estimate=takes(0),
         name="dn",
     )(scalars, dproj, w_qkv)
 
 
-def last_kernel(mine_ref, arrived_ref, x_ref, dx_ref, gain_ref, out_ref):
-    dn = (mine_ref[...] + arrived_ref[...].astype(F32)).astype(BF16).astype(F32)
+def last_kernel(keep_ref, core_ref, chip_ref, x_ref, dx_ref, gain_ref, out_ref):
+    dn = keep_ref[...].astype(F32) + core_ref[...].astype(F32) + chip_ref[...].astype(F32)
+    dn = dn.astype(BF16).astype(F32)
     normed, scale = row_stats(x_ref[...].astype(F32))
     out_ref[...] = (dx_ref[...] + pull_norm(normed, scale, dn * gain_ref[...])).astype(BF16)
 
 
-def last_call(mine, arrived, x, dx, gain, step=256):
+def last_call(keep, core, chip, x, dx, gain, step=256):
     rows, width = x.shape
     per = rows // step
     flat = pl.BlockSpec((step, width), lambda i: (i, 0))
@@ -649,12 +651,26 @@
         last_kernel,
         out_shape=jax.ShapeDtypeStruct((rows, width), BF16),
         grid=(per,),
-        in_specs=[flat, flat, flat, flat, resident(gain.shape)],
+        in_specs=[flat] * 5 + [resident(gain.shape)],
         out_specs=flat,
-        compiler_params=vmem(60),
+        compiler_params=vmem(48),
         cost_estimate=takes(5),
         name="last",
-    )(mine, arrived, x, dx, gain)
+    )(keep, core, chip, x, dx, gain)
+
+
+def turn_rows_kernel(hot_ref, rows_ref, out_ref):
+    out_ref[...] = dot(hot_ref[...], rows_ref[...], 0, 0).astype(BF16)
+
+
+def turn_rows(one_hot, values):
+    return pl.pallas_call(
+        turn_rows_kernel,
+        out_shape=jax.ShapeDtypeStruct(values.shape, BF16),
+        compiler_params=vmem(48),
+        cost_estimate=takes(2),
+        name="turn_rows",
+    )(one_hot, values)
 
 
 def bits_of(count):
@@ -673,18 +689,6 @@
     shape = values.shape[:axis] + (count // blocks, LANES * blocks // count) + values.shape[axis + 1 :]
     values = jnp.moveaxis(values.reshape(shape), axis, 1)
     return values.reshape((count,) + values.shape[2:])
-
-
-def halve(values, axis_name, point):
-    me = lax.axis_index(axis_name)
-    carried = values
-    for bit in bits_of(lax.axis_size(axis_name)):
-        view = carried.reshape((carried.shape[0] // 2, 2) + carried.shape[1:])
-        mine = (me // bit) % 2
-        arrived = swap_bit(pick(view, 1, 1 - mine).astype(BF16), axis_name, bit)
-        (arrived,) = after(point, arrived)
-        carried = pick(view, 1, mine).astype(F32) + arrived.astype(F32)
-    return carried[0]
 
 
 def after(point, *values):
@@ -767,20 +771,6 @@
 
     gains = gather_bits(gather_bits(jnp.stack([attn_gain, mlp_gain]), "dp"), "mp")
     gains = gains.transpose(2, 1, 0, 3).reshape(2, width)
-    w_mlp = jnp.concatenate([w_in, w_down.T[None]], axis=0)
-    x_arrived = exchange(pack(hidden_in))
-    x_arrived, g_packed, gains, w_mlp = lax.optimization_barrier(
-        (x_arrived, pack(out_grad), gains, w_mlp)
-    )
-    w_mlp = lax.all_gather(w_mlp, "dp", axis=1, tiled=True)
-    gain_one, gain_two = gains[0:1], gains[1:2]
-    x_mine = unpack(x_arrived)
-    x_rel = group(x_mine)
-    attn_weights = jnp.concatenate([w_qkv, w_out.T[None]], axis=0)
-    attn_weights = jnp.moveaxis(gather_bits(attn_weights, "dp"), 0, 1).reshape(4, width, -1)
-    w_out_rel = group(attn_weights[3])
-    g_arrived = exchange(g_packed)
-
     place = jnp.arange(tokens, dtype=jnp.int32)
     place = jnp.where(place >= first_len, place - first_len, place).astype(F32)
     freq_index = jnp.arange(LANES, dtype=jnp.int32) % (HEAD_DIM // 2)
@@ -790,14 +780,35 @@
     cos = jnp.cos(angles)
     sin = jnp.sin(angles) * jnp.where(first_half, -1.0, 1.0)[None, :]
 
+    w_mlp = jnp.concatenate([w_in, w_down.T[None]], axis=0)
+    x_arrived = exchange(pack(hidden_in))
+    gains, w_mlp = lax.optimization_barrier((gains, w_mlp))
+    x_arrived, gains, cos, sin, scalars, g_packed = lax.optimization_barrier(
+        (x_arrived, gains, cos, sin, scalars, pack(out_grad))
+    )
+    w_mlp = lax.all_gather(w_mlp, "dp", axis=1, tiled=True)
+    gain_one, gain_two = gains[0:1], gains[1:2]
+    x_mine = unpack(x_arrived)
+    x_rel = group(x_mine)
+    attn_weights = jnp.concatenate([w_qkv, w_out.T[None]], axis=0)
+    attn_weights = jnp.moveaxis(gather_bits(attn_weights, "dp"), 0, 1).reshape(4, width, -1)
+    w_out_across = swap_bit(attn_weights[3], "mp", 2)
+    g_packed, attn_weights = lax.optimization_barrier((g_packed, attn_weights))
+    g_arrived = exchange(g_packed)
+
     held = qkv_call(scalars, x_rel[0], x_rel[1], gain_one, attn_weights, cos, sin, 0, ())
     q, k, v, n1 = qkv_call(scalars, x_rel[2], x_rel[3], gain_one, attn_weights, cos, sin, 2, held)
-    (g_arrived,) = after(q, g_arrived)
-    g_rel = group(unpack(g_arrived))
+    q, w_out_across = lax.optimization_barrier((q, w_out_across))
+    w_out_rel = [attn_weights[3], None, w_out_across, None]
+    w_out_rel[1], w_out_rel[3] = swap_bit(w_out_rel[0], "mp", 1), swap_bit(w_out_across, "mp", 1)
     near, q2, near_top = attend_forward(scalars, q, k, v, 0, 2 * rows, ())
+    (g_arrived,) = after(near, g_arrived)
+    g_mine = unpack(g_arrived)
+    g_core, g_across = swap_bit(g_mine, "mp", 1), swap_bit(g_mine, "mp", 2)
     near_across = swap_bit(near, "mp", 2)
     distant, q2, far_top = attend_forward(scalars, q, k, v, 1, 2 * rows, (q2,))
-    (distant,) = after(near_across, distant)
+    distant, near_across, g_across = lax.optimization_barrier((distant, near_across, g_across))
+    g_rel = [g_mine, g_core, g_across, swap_bit(g_across, "mp", 1)]
     far_across = swap_bit(distant, "mp", 2)
     core = lambda values: swap_bit(values, "mp", 1)
     far_heads = [distant, core(distant), near_across, core(near_across)]
@@ -827,7 +838,7 @@
     near_heads = [near, core(near), far_across, core(far_across)]
     (near_heads[0],) = after(dn_far, near)
     far_out = (keep_out, send_out)
-    a_rel, n2, act, dgate, dup, keep, send, keep_out, send_out = mlp_call(
+    a_rel, n2, g_all, act, dgate, dup, keep, send, keep_out, send_out = mlp_call(
         scalars,
         (x_rel[1], x_rel[0]),
         (g_rel[1], g_rel[0]),
@@ -842,30 +853,26 @@
     head_peaks = jnp.maximum(head_peaks, peak_swap)
     peak_swap = swap_bit(head_peaks, "dp", peak_bits[2])
     dx, da = resid_call(
-        keep + core(send).astype(F32), dn_arrived, x_rel[0], a_rel, g_rel[0], gain_two
+        keep, core(send), dn_arrived, x_rel[0], a_rel, g_rel[0], gain_two
     )
     da_core, da_across = core(da), swap_bit(da, "mp", 2)
 
     flat = lambda values: values.reshape(tokens, values.shape[2])
     (act,) = after(da, act)
-    inner_grads = inner_call(flat(n2), g_rel, flat(dgate), flat(dup), flat(act))
-    inner_grads, da_across, peak_swap = lax.optimization_barrier((inner_grads, da_across, peak_swap))
+    inner_grads = inner_call(flat(n2), flat(g_all), flat(dgate), flat(dup), flat(act))
+    held = list(head_grad_call(scalars, da, da_core, attn_weights[3], near, 0, tokens, ()))
+    inner_grads, da_across, peak_swap, held[0] = lax.optimization_barrier(
+        (inner_grads, da_across, peak_swap, held[0])
+    )
+    do, da_all = head_grad_call(
+        scalars, da_across, core(da_across), attn_weights[3], distant, 1, tokens, held
+    )
     head_peaks = jnp.maximum(head_peaks, peak_swap)
     for bit in peak_bits[3:]:
         head_peaks = jnp.maximum(head_peaks, swap_bit(head_peaks, "dp", bit))
-    da_rel = [da, da_core, da_across, core(da_across)]
-    inner_grads = lax.psum_scatter(by_device(inner_grads, dp_count), "dp").astype(F32)
-    inner_grad, down_grad = inner_grads[:2], inner_grads[2].T
-
-    do, da_near = head_grad_call(
-        scalars, da_rel[0], da_rel[1], attn_weights[3], near, 0, tokens, ()
-    )
-    do, da_far = head_grad_call(
-        scalars, da_rel[2], da_rel[3], attn_weights[3], distant, 1, tokens, (do,)
-    )
-    outer_grad = outer_call((near, distant), (da_near, da_far))
-    outer_grad = by_device(outer_grad, dp_count)
-    outer_grad = lax.all_to_all(outer_grad, "dp", split_axis=0, concat_axis=0, tiled=True)
+    inner_grads = by_device(inner_grads, dp_count)
+    inner_grads = lax.all_to_all(inner_grads, "dp", split_axis=0, concat_axis=0, tiled=True)
+
 
     far_out = after(da_across, *far_out)
     add_core = lambda keep, send: keep.astype(F32) + core(send).astype(F32)
@@ -879,25 +886,35 @@
     out_arrived = swap_bit(out_far, "mp", 2)
     do, out_sum = after(out_far, do, add_core(keep_out, send_out))
     dproj = attend_backward(scalars, q2, k, v, do, cos, sin)
-    send = dn_call(scalars, dproj, attn_weights, 1, rows)
-    out_arrived, outer_grad, send = lax.optimization_barrier((out_arrived, outer_grad, send))
-    outer_grad = jnp.sum(outer_grad.astype(F32), axis=0)[0]
-    keep = dn_call(scalars, dproj, attn_weights, 0, rows)
-    both = keep.astype(F32) + core(send).astype(F32)
-    dn_own, dn_far = both[:rows], both[rows:].astype(BF16)
+    proj_grad = proj_call(n1, dproj, (near, distant), da_all)
+    proj_grad, dproj, out_arrived = lax.optimization_barrier((proj_grad, dproj, out_arrived))
+    far_core = core(dn_call(scalars, dproj, attn_weights, 3, rows))
+    far_keep = dn_call(scalars, dproj, attn_weights, 2, rows)
+    dn_far = (far_keep.astype(F32) + far_core.astype(F32)).astype(BF16)
     dn_arrived = swap_bit(dn_far, "mp", 2)
-    (out_arrived,) = after(dn_far, out_arrived)
+    inner_grads, dn_far, out_arrived = lax.optimization_barrier((inner_grads, dn_far, out_arrived))
     x1 = x_rel[0].astype(F32) + a_rel[0].astype(F32)
     out_packed = pack_back((x1 + (out_sum + out_arrived.astype(F32))).astype(BF16))
-    (n1,) = after(out_packed, n1)
-    proj_grad = proj_call(n1, dproj)
-    (dn_arrived,) = after(proj_grad, dn_arrived)
-    grad_packed = pack_back(last_call(dn_own, dn_arrived, x_rel[0], dx, gain_one))
-    input_grad = unpack_back(exchange(grad_packed))
-    (out_arrived,) = after(grad_packed, exchange(out_packed))
-    output = unpack_back(out_arrived)
-    proj_grad = halve(by_device(proj_grad, dp_count), "dp", grad_packed)
-    proj_grad = jnp.swapaxes(proj_grad, 1, 2)
+    (dproj,) = after(out_packed, dproj)
+    out_sent = exchange(out_packed)
+    send = dn_call(scalars, dproj, attn_weights, 1, rows)
+    keep = dn_call(scalars, dproj, attn_weights, 0, rows)
+    dn_core = core(send)
+    out_sent, dn_arrived, dn_core = lax.optimization_barrier((out_sent, dn_arrived, dn_core))
+    grad_packed = pack_back(last_call(keep, dn_core, dn_arrived, x_rel[0], dx, gain_one))
+    grad_arrived = exchange(grad_packed)
+    (out_arrived,) = after(grad_packed, out_sent)
+    output = turn_rows(to_slot, out_arrived)
+    grads = lax.psum_scatter(by_device(proj_grad, dp_count), "dp")
+    inner_grads, grads = after(output, inner_grads, grads)
+    inner_grads = jnp.sum(inner_grads.astype(F32), axis=0)
+    grad_arrived, inner_grads, grads = lax.optimization_barrier(
+        (grad_arrived, inner_grads, grads)
+    )
+    grads = grads.astype(F32)
+    input_grad = unpack_back(grad_arrived)
+    inner_grad, down_grad = jnp.swapaxes(inner_grads[:2], 1, 2), inner_grads[2]
+    proj_grad, outer_grad = jnp.swapaxes(grads[:3], 1, 2), grads[3]
 
     by_gain = jnp.stack(
         [

time: 502 us -> 485 us (0.966)
  starting transfers between devices: 67 us -> 56.4 us
  Pallas kernels: 226 us -> 216 us
  local copies, waits for them, and re-layouts: 22.1 us -> 28.4 us
    ppermute x42 -> x40, waiting for transfers between devices: 94.8 us -> 67 us  [swap_bit(): return lax.ppermute(values, axis_name, [(i, i ^ bit) for i in range(count)])]
    reduce_scatter x1, waiting for transfers between devices: 0.01 us -> 26.9 us  [local(): grads = lax.psum_scatter(by_device(proj_grad, dp_count), 'dp')]
    unnamed x80 -> x98, local copies, waits for them, and re-layouts: 11.1 us -> 21.1 us
    all_to_all x4, waiting for transfers between devices: 25.6 us -> 16.7 us  [exchange(): lax.all_to_all(packed, 'dp', split_axis=0, concat_axis=0, tiled=True)]
    add x4 -> x0, other arithmetic: 7.51 us -> none  [the longest x1 3.35 us: local(): keep + core(send).astype(F32)]
    ppermute x42 -> x40, starting transfers between devices: 38.7 us -> 32.7 us  [swap_bit(): return lax.ppermute(values, axis_name, [(i, i ^ bit) for i in range(count)])]
    another operation x14, other arithmetic: 0.65 us -> 5.95 us  [gather_bits(): jnp.stack([jnp.where(high, other, values), jnp.where(high, values, other)])]
    dot_general x10 -> x9, matrix products: 19.3 us -> 17 us  [dot(): lax.dot_general(left, right, (((left_dim,), (right_dim,)), ((), ())), pre...]
  transfers between devices with their start and end apart: 49 -> 47, of which waited for: 17 -> 18; matrix products, arithmetic and copies ran while one was open for 12% -> 11% of each run, Pallas kernels for 45% -> 45%
where the time goes in v3:
time: 485 us; the launch traced here: 477 us
  Pallas kernels  216 us (45%)
  waiting for transfers between devices  115 us (24%)
  starting transfers between devices  56.4 us (12%)
  other arithmetic  29.4 us (6%)
  local copies, waits for them, and re-layouts  28.4 us (6%)
  matrix products  17 us (4%)
  between operations  15.1 us (3%)
    ppermute x40, waiting for transfers between devices, swap_bit(): return lax.ppermute(values, axis_name, [(i, i ^ bit) for i in range(count)])  67 us
    pallas_call x1, Pallas kernels, attend_backward(): pl.pallas_call(functools.partial(bwd_kernel, q_rows, k_rows), out_shape=j...  55.8 us
    pallas_call x2, Pallas kernels, mlp_call(): pl.pallas_call(mlp_kernel, out_shape=(wide_out, wide_out, wide_out, narro...  47.3 us
    pallas_call x2, Pallas kernels, attend_forward(): pl.pallas_call(functools.partial(fwd_kernel, far, q_rows, k_rows), out_sh...  38.5 us
    ppermute x40, starting transfers between devices, swap_bit(): return lax.ppermute(values, axis_name, [(i, i ^ bit) for i in range(count)])  32.7 us
    reduce_scatter x1, waiting for transfers between devices, local(): grads = lax.psum_scatter(by_device(proj_grad, dp_count), 'dp')  26.9 us
    unnamed x98, local copies, waits for them, and re-layouts  21.1 us
    all_to_all x4, starting transfers between devices, exchange(): lax.all_to_all(packed, 'dp', split_axis=0, concat_axis=0, tiled=True)  19.1 us
  transfers between devices with their start and end apart: 47, of which 18 were waited for; matrix products, arithmetic and copies ran while one was open for 11% of the time, Pallas kernels for 45%

profile of v3, /device:TPU:0, one launch (start us, length us, event | category | flops | bytes accessed | tf_op | source)
XLA Modules:
  0.0 476.8 jit_solution(9356234849935034383)
XLA Ops:
  9.2 4.1 collective-permute-start.8
  15.5 1.7 convolution_convert_fusion.6
  17.2 6.3 %all-to-all-start = ((bf16[8,64,1024]{2,1,0:T(8,128)(2,1)}), bf16[8,64,1024]{2,1,0:T(8,128)(2,1)}, u32[]{:S(2)}, u32[]{:S(2)}) async-start(bf16[8,64,1024]{2,1,0:T(8,128)(2,1)} %bitcast.1), calls=%async_computation | async-start | bytes 2097152 | tf_op jit(solution)/shard_map/all_to_all | solution.py:753
  23.7 1.7 convolution_convert_fusion.5
  26.9 3.7 fusion.6
  30.7 2.0 collective-permute-start.1
  32.7 7.4 %collective-permute-done.1 = f32[2,2,32]{2,1,0:T(2,128)S(1)} collective-permute-done((f32[2,2,32]{2,1,0:T(2,128)S(1)}, f32[2,2,32]{2,1,0:T(2,128)S(1)}, u32[]{:S(2)}, u32[]{:S(2)}) %collective-permute-start.1) | collective-permute-done | bytes 544 | tf_op jit(solution)/shard_map/ppermute | solution.py:56
  40.2 1.9 collective-permute-start.2
  43.9 1.6 collective-permute-start.3
  49.4 2.5 collective-permute-start.9
  53.3 7.8 %collective-permute-done.9 = bf16[2,4,128,256]{3,2,1,0:T(8,128)(2,1)S(1)} collective-permute-done((bf16[2,4,128,256]{3,2,1,0:T(8,128)(2,1)}, bf16[2,4,128,256]{3,2,1,0:T(8,128)(2,1)S(1)}, u32[]{:S(2)}, u32[]{:S(2)}) %collective-permute-start.9) | collective-permute-done | bytes 524320 | tf_op jit(solution)/shard_map/ppermute | solution.py:56
  62.3 3.0 convolution_convert_fusion.4.xa_ref.xk_ref.x_ref
  65.3 1.5 collective-permute-start.6
  69.1 17.7 %collective-permute-done.6.xa_ref.xk_ref = bf16[512,1024]{1,0:T(8,128)(2,1)S(1)} collective-permute-done((bf16[512,1024]{1,0:T(8,128)(2,1)}, bf16[512,1024]{1,0:T(8,128)(2,1)S(1)}, u32[]{:S(2)}, u32[]{:S(2)}) %collective-permute-start.6) | collective-permute-done | bytes 1048608 | tf_op jit(solution)/shard_map/ppermute | solution.py:56
  86.8 8.7 %collective-permute-done.10 = bf16[2,2,4,128,256]{4,3,2,0,1:T(8,128)(2,1)} collective-permute-done((bf16[2,2,4,128,256]{4,3,2,0,1:T(8,128)(2,1)}, bf16[2,2,4,128,256]{4,3,2,0,1:T(8,128)(2,1)}, u32[]{:S(2)}, u32[]{:S(2)}) %collective-permute-start.10) | collective-permute-done | bytes 1048608 | tf_op jit(solution)/shard_map/ppermute | solution.py:56
  95.5 1.7 select_bitcast_fusion.1
  97.4 1.4 copy.70
  100.2 4.5 all-to-all-start.1
  104.8 8.1 %qkv.2 = (bf16[4,2048,128]{2,1,0:T(8,128)(2,1)}, bf16[4,2048,128]{2,1,0:T(8,128)(2,1)}, bf16[4,2048,128]{2,1,0:T(8,128)(2,1)}, bf16[2048,1024]{1,0:T(8,128)(2,1)}) custom-call(s32[4]{0:T(128)S(1)} %pad_add_fusion.s_ref, bf16[512,1024]{1,0:T(8,128)(2,1)} %convolution_convert_fusion.4.xa_ref.xk_ref.x_ref, ...), custom_call_target="tpu_custom_call" | custom-call | flops 3300000000 | bytes 3222656 | tf_op jit(solution)/shard_map/qkv/pallas_call | solution.py:119
  112.9 7.6 %qkv.3 = (bf16[4,2048,128]{2,1,0:T(8,128)(2,1)}, bf16[4,2048,128]{2,1,0:T(8,128)(2,1)}, bf16[4,2048,128]{2,1,0:T(8,128)(2,1)}, bf16[2048,1024]{1,0:T(8,128)(2,1)}) custom-call(s32[4]{0:T(128)S(1)} %pad_add_fusion.s_ref, ...), custom_call_target="tpu_custom_call", output_to_operand_aliasing={{0}: (7, {}), {1}: (8, {}), {2}: (9, {}), {3}: (10, {})} | custom-call | flops 3300000000 | bytes 3222656 | tf_op jit(solution)/shard_map/qkv/pallas_call | solution.py:119
  120.5 1.6 copy-done.4
  122.1 20.2 %attend_forward.2 = (bf16[1024,256]{1,0:T(8,128)(2,1)S(1)}, bf16[4,2048,128]{2,1,0:T(8,128)(2,1)S(1)}, f32[4,4,8,128]{3,2,1,0:T(8,128)S(1)}) custom-call(s32[4]{0:T(128)S(1)} %pad_add_fusion.s_ref, bf16[4,2048,128]{2,1,0:T(8,128)(2,1)S(1)} %copy-done.4, bf16[4,2048,128]{2,1,0:T(8,128)(2,1)} %get-tuple-element.111.k_ref, ...), custom_call_target="tpu_custom_call" | custom-call | flops 22000001024 | bytes 21484376 | tf_op jit(solution)/shard_map/attend_forward/pallas_call | solution.py:217
  143.6 8.0 %all-to-all-done.1 = bf16[8,64,1024]{2,1,0:T(8,128)(2,1)} async-done(((bf16[8,64,1024]{2,1,0:T(8,128)(2,1)}), bf16[8,64,1024]{2,1,0:T(8,128)(2,1)}, u32[]{:S(2)}, u32[]{:S(2)}) %all-to-all-start.1) | async-done | bytes 1048608 | tf_op jit(solution)/shard_map/all_to_all | solution.py:753
  151.7 2.1 convolution_convert_fusion.3.gk_ref.g_ref
  154.9 1.6 copy-done.23
  156.5 18.2 %attend_forward.3 = (bf16[1024,256]{1,0:T(8,128)(2,1)}, bf16[4,2048,128]{2,1,0:T(8,128)(2,1)S(1)}, f32[4,4,8,128]{3,2,1,0:T(8,128)S(1)}) custom-call(s32[4]{0:T(128)S(1)} %pad_add_fusion.s_ref, bf16[4,2048,128]{2,1,0:T(8,128)(2,1)S(1)} %copy-done.5, bf16[4,2048,128]{2,1,0:T(8,128)(2,1)} %get-tuple-element.111.k_ref, ...), custom_call_target="tpu_custom_call", output_to_operand_aliasing={{1}: (4, {})} | custom-call | flops 22000001024 | bytes 21484376 | tf_op jit(solution)/shard_map/attend_forward/pallas_call | solution.py:217
  180.6 3.7 collective-permute-start.20
  184.4 24.0 %mlp.2 = (bf16[4,512,1024]{2,1,0:T(8,128)(2,1)}, bf16[4,512,1024]{2,1,0:T(8,128)(2,1)}, bf16[4,512,1024]{2,1,0:T(8,128)(2,1)}, bf16[4,512,656]{2,1,0:T(8,128)(2,...) custom-call(s32[4]{0:T(128)S(1)} %pad_add_fusion.s_ref, ...), custom_call_target="tpu_custom_call" | custom-call | flops 26400000000 | bytes 25781250 | tf_op jit(solution)/shard_map/mlp/pallas_call | solution.py:401
  209.4 1.6 collective-permute-done.22
  211.1 1.9 add_convert_fusion.2
  213.0 1.5 collective-permute-start.25
  215.5 23.3 %mlp.3 = (bf16[4,512,1024]{2,1,0:T(8,128)(2,1)}, bf16[4,512,1024]{2,1,0:T(8,128)(2,1)}, bf16[4,512,1024]{2,1,0:T(8,128)(2,1)}, bf16[4,512,656]{2,1,0:T(8,128)(2,...) custom-call(s32[4]{0:T(128)S(1)} %pad_add_fusion.s_ref, ...), custom_call_target="tpu_custom_call", output_to_operand_aliasing={{0}: (15, {}), {1}: (16, {}), {2}: (17, {}), {3}: (18, {}),... | custom-call | flops 26400000000 | bytes 25781250 | tf_op jit(solution)/shard_map/mlp/pallas_call | solution.py:401
  239.4 1.4 collective-permute-start.29
  242.3 4.4 resid.1
  246.8 1.6 collective-permute-start.28
  248.4 18.8 %inner_grads.1 = bf16[8,3,656,128]{3,2,1,0:T(8,128)(2,1)} custom-call(bf16[2048,1024]{1,0:T(8,128)(2,1)} %bitcast.147, bf16[2048,1024]{1,0:T(8,128)(2,1)} %bitcast.148, bf16[2048,656]{1,0:T(8,128)(2,1)S(1)} %bitcast.124, bf16[2048,656]{1,0:T(8,128)(2,1)} %bitcast.150, bf16[2048,656]{1,0:T(8,128)(2,1)} %bitcast.149), custom_call_target="tpu_custom_call" | custom-call | flops 19800000512 | bytes 19335936 | tf_op jit(solution)/shard_map/inner_grads/pallas_call | solution.py:558
  267.2 3.9 head_grad.2
  272.9 1.7 convert_add_fusion.1
  274.6 4.5 all-to-all-start.2
  279.2 3.1 add_convert_fusion.1
  282.3 1.5 collective-permute-start.34
  283.8 5.7 %head_grad.3 = (bf16[4,2048,128]{2,1,0:T(8,128)(2,1)S(1)}, bf16[2048,1024]{1,0:T(8,128)(2,1)}) custom-call(s32[4]{0:T(128)S(1)} %pad_add_fusion.s_ref, bf16[512,1024]{1,0:T(8,128)(2,1)} %collective-permute-done.28.even_ref, bf16[512,1024]{1,0:T(8,128)(2,1)} %collective-permute-done.32.odd_ref, ...), custom_call_target="tpu_custom_call", output_to_operand_aliasing={{0}: (5, {}), {1}: (6, {})} | custom-call | flops 6600000000 | bytes 6445312 | tf_op jit(solution)/shard_map/head_grad/pallas_call | solution.py:500
  290.9 55.8 %attend_backward.1.d_ref.p_ref = bf16[3,2048,256]{2,1,0:T(8,128)(2,1)} custom-call(s32[4]{0:T(128)S(1)} %pad_add_fusion.s_ref, bf16[4,2048,128]{2,1,0:T(8,128)(2,1)S(1)} %copy-done.25, bf16[4,2048,128]{2,1,0:T(8,128)(2,1)} %get-tuple-element.111.k_ref, bf16[4,2048,128]{2,1,0:T(8,128)(2,1)} %get-tuple-element.112.v_ref, bf16[4,2048,128]{2,1,0:T(8,128)(2,1)} %copy-done.21, ...), custom_call_target="tpu_custom_call" | custom-call | flops 62699999232 | bytes 61230468 | tf_op jit(solution)/shard_map/attend_backward/pallas_call | solution.py:313
  346.8 7.7 %proj_grads.1 = bf16[8,4,256,128]{3,2,1,0:T(8,128)(2,1)S(1)} custom-call(bf16[2048,1024]{1,0:T(8,128)(2,1)} %get-tuple-element.164.n_ref, bf16[3,2048,256]{2,1,0:T(8,128)(2,1)} %attend_backward.1.d_ref.p_ref, bf16[1024,256]{1,0:T(8,128)(2,1)S(1)} %copy-done.17, bf16[1024,256]{1,0:T(8,128)(2,1)} %get-tuple-element.119.o0.o_ref.o1, ...), custom_call_target="tpu_custom_call" | custom-call | flops 11000000512 | bytes 10742187 | tf_op jit(solution)/shard_map/proj_grads/pallas_call | solution.py:594
  355.8 3.7 dn.5
  359.4 2.7 dn.4
  362.4 2.6 add_convert_fusion
  365.0 4.3 all-to-all-done.2
  369.4 4.4 convolution_convert_fusion.2
  373.8 4.5 all-to-all-start.3
  378.3 1.5 collective-permute-start.36
  379.8 2.7 dn.7
  382.5 2.7 dn.6.keep_ref
  385.3 17.7 %collective-permute-done.36.chip_ref = bf16[512,1024]{1,0:T(8,128)(2,1)S(1)} collective-permute-done((bf16[512,1024]{1,0:T(8,128)(2,1)}, bf16[512,1024]{1,0:T(8,128)(2,1)S(1)}, u32[]{:S(2)}, u32[]{:S(2)}) %collective-permute-start.36) | collective-permute-done | bytes 1048608 | tf_op jit(solution)/shard_map/ppermute | solution.py:56
  404.9 8.2 %all-to-all-done.3 = bf16[8,64,1024]{2,1,0:T(8,128)(2,1)} async-done(((bf16[8,64,1024]{2,1,0:T(8,128)(2,1)}), bf16[8,64,1024]{2,1,0:T(8,128)(2,1)}, u32[]{:S(2)}, u32[]{:S(2)}) %all-to-all-start.3) | async-done | bytes 1048608 | tf_op jit(solution)/shard_map/all_to_all | solution.py:753
  415.6 3.2 last.1
  418.8 1.8 convolution_convert_fusion.1
  420.6 3.9 all-to-all-start.4
  425.8 2.9 turn_rows.1
  428.8 26.9 %reduce-scatter.2.cloned.1.call-done = bf16[1,4,256,128]{3,2,1,0:T(8,128)(2,1)} async-done(((bf16[8,4,256,128]{3,2,1,0:T(8,128)(2,1)}), bf16[1,4,256,128]{3,2,1,0:T(8,128)(2,1)}) %reduce-scatter.2.cloned.1.call-update) | async-done | bytes 262160 | tf_op jit(solution)/shard_map/reduce_scatter | solution.py:908
  455.7 2.8 convert_reduce_fusion
  461.6 1.4 collective-permute-start.38
  463.1 1.8 convolution_convert_fusion
  466.5 1.7 copy.73
  (224 shorter events, 47.2 us)
Async XLA Ops:
  7.2 8.3 %copy-start = (bf16[512,1024]{1,0:T(8,128)(2,1)S(1)}, bf16[512,1024]{1,0:T(8,128)(2,1)}, u32[]{:S(2)}) copy-start(bf16[512,1024]{1,0:T(8,128)(2,1)} %param.10) | copy-start | bytes 3145732
  9.2 38.4 %collective-permute-start.8 = (bf16[4,128,256]{2,1,0:T(8,128)(2,1)S(1)}, bf16[4,128,256]{2,1,0:T(8,128)(2,1)}, u32[]{:S(2)}, u32[]{:S(2)}) collective-permute-start(bf16[4,128,256]{2,1,0:T(8,128)(2,1)S(1)} %pad_maximum_fusion.4), channel_id=1, source_target_pairs={{0,16},{4,20},{8,24},{12,28},{16,0},{20,4},{24,8},{28,12},{1,17},{... | collective-permute-start | bytes 786440 | tf_op jit(solution)/shard_map/ppermute | solution.py:56
  14.0 16.7 %collective-permute-start = (f32[2,32]{1,0:T(2,128)S(1)}, f32[2,32]{1,0:T(2,128)S(1)}, u32[]{:S(2)}, u32[]{:S(2)}) collective-permute-start(f32[2,32]{1,0:T(2,128)S(1)} %pad_maximum_fusion.8), channel_id=1, source_target_pairs={{0,16},{4,20},{8,24},{12,28},{16,0},{20,4},{24,8},{28,12},{1,17},{... | collective-permute-start | bytes 776 | tf_op jit(solution)/shard_map/ppermute | solution.py:56
  15.5 8.1 %copy-start.42 = (bf16[512,1024]{1,0:T(8,128)(2,1)S(1)}, bf16[512,1024]{1,0:T(8,128)(2,1)}, u32[]{:S(2)}) copy-start(bf16[512,1024]{1,0:T(8,128)(2,1)} %param.11) | copy-start | bytes 3145732
  17.2 8.2 %copy-start.44 = (s32[16]{0:T(128)S(1)}, s32[16]{0:T(128)}, u32[]{:S(2)}) copy-start(s32[16]{0:T(128)} %param.12) | copy-start | bytes 196
  17.2 45.0 %all-to-all-start = ((bf16[8,64,1024]{2,1,0:T(8,128)(2,1)}), bf16[8,64,1024]{2,1,0:T(8,128)(2,1)}, u32[]{:S(2)}, u32[]{:S(2)}) async-start(bf16[8,64,1024]{2,1,0:T(8,128)(2,1)} %bitcast.1), calls=%async_computation | async-start | bytes 2097152 | tf_op jit(solution)/shard_map/all_to_all | solution.py:753
  23.5 160.8 %all-gather.2.cloned.1.call-start = ((), (), s32[]{:S(2)}) async-start(), calls=%async_computation.6 | async-start | bytes 5308416 | tf_op jit(solution)/shard_map/all_gather | solution.py:789
  23.7 18.4 %copy-start.30 = (bf16[2,128,656]{1,2,0:T(8,128)(2,1)S(1)}, bf16[2,128,656]{1,2,0:T(8,128)(2,1)}, u32[]{:S(2)}) copy-start(bf16[2,128,656]{1,2,0:T(8,128)(2,1)} %param.18) | copy-start | bytes 1007620
  26.9 20.7 %copy-start.28 = (bf16[3,128,256]{2,1,0:T(8,128)(2,1)S(1)}, bf16[3,128,256]{2,1,0:T(8,128)(2,1)}, u32[]{:S(2)}) copy-start(bf16[3,128,256]{2,1,0:T(8,128)(2,1)} %param.16) | copy-start | bytes 589828
  30.7 9.4 %collective-permute-start.1 = (f32[2,2,32]{2,1,0:T(2,128)S(1)}, f32[2,2,32]{2,1,0:T(2,128)S(1)}, u32[]{:S(2)}, u32[]{:S(2)}) collective-permute-start(f32[2,2,32]{2,1,0:T(2,128)S(1)} %pad_maximum_fusion.7), channel_id=1, source_target_pairs={{0,8},{4,12},{8,0},{12,4},{16,24},{20,28},{24,16},{28,20},{1,9},{5... | collective-permute-start | bytes 1544 | tf_op jit(solution)/shard_map/ppermute | solution.py:56
  40.2 3.7 collective-permute-start.2
  42.1 109.6 %copy-start.38 = (s32[512]{0:T(512)}, s32[512]{0:T(512)S(1)}, u32[]{:S(2)}) copy-start(s32[512]{0:T(512)S(1)} %multiply_add_fusion) | copy-start | bytes 6148
  43.9 3.7 collective-permute-start.3
  49.4 11.7 %collective-permute-start.9 = (bf16[2,4,128,256]{3,2,1,0:T(8,128)(2,1)}, bf16[2,4,128,256]{3,2,1,0:T(8,128)(2,1)S(1)}, u32[]{:S(2)}, u32[]{:S(2)}) collective-permute-start(bf16[2,4,128,256]{3,2,1,0:T(8,128)(2,1)} %pad_maximum_fusion.3), channel_id=1, source_target_pairs={{0,8},{4,12},{8,0},{12,4},{16,24},{20,28},{24,16},{28,20},{1,9},{5... | collective-permute-start | bytes 1572872 | tf_op jit(solution)/shard_map/ppermute | solution.py:56
  52.0 1.2 collective-permute-start.4
  53.3 51.4 %copy-start.35 = (f32[2,1024]{1,0:T(2,128)}, f32[2,1024]{1,0:T(2,128)S(1)}, u32[]{:S(2)}) copy-start(f32[2,1024]{1,0:T(2,128)S(1)} %reshape.190) | copy-start | bytes 24580
  65.3 21.5 %collective-permute-start.6 = (bf16[512,1024]{1,0:T(8,128)(2,1)}, bf16[512,1024]{1,0:T(8,128)(2,1)S(1)}, u32[]{:S(2)}, u32[]{:S(2)}) collective-permute-start(bf16[512,1024]{1,0:T(8,128)(2,1)} %convolution_convert_fusion.4.xa_ref.xk_ref.x_ref), channel_id=1, source_target_pairs={{0,2},{1,3},{2,0},{3,1},{4,6},{5,7},{6,4},{7,5},{8,10},{9,11},{10,... | collective-permute-start | bytes 3145736 | tf_op jit(solution)/shard_map/ppermute | solution.py:56
  67.9 27.7 %collective-permute-start.10 = (bf16[2,2,4,128,256]{4,3,2,0,1:T(8,128)(2,1)}, bf16[2,2,4,128,256]{4,3,2,0,1:T(8,128)(2,1)}, u32[]{:S(2)}, u32[]{:S(2)}) collective-permute-start(bf16[2,2,4,128,256]{4,3,2,0,1:T(8,128)(2,1)} %pad_maximum_fusion.1), channel_id=1, source_target_pairs={{0,4},{4,0},{8,12},{12,8},{16,20},{20,16},{24,28},{28,24},{1,5},{5... | collective-permute-start | bytes 3145736 | tf_op jit(solution)/shard_map/ppermute | solution.py:56
  69.1 35.7 %collective-permute-start.5 = (bf16[512,1024]{1,0:T(8,128)(2,1)}, bf16[512,1024]{1,0:T(8,128)(2,1)}, u32[]{:S(2)}, u32[]{:S(2)}) collective-permute-start(bf16[512,1024]{1,0:T(8,128)(2,1)} %convolution_convert_fusion.4.xa_ref.xk_ref.x_ref), channel_id=1, source_target_pairs={{0,1},{1,0},{2,3},{3,2},{4,5},{5,4},{6,7},{7,6},{8,9},{9,8},{10,11... | collective-permute-start | bytes 3145736 | tf_op jit(solution)/shard_map/ppermute | solution.py:56
  86.8 26.0 %copy-start.6 = (bf16[512,1024]{1,0:T(8,128)(2,1)}, bf16[512,1024]{1,0:T(8,128)(2,1)S(1)}, u32[]{:S(2)}) copy-start(bf16[512,1024]{1,0:T(8,128)(2,1)S(1)} %collective-permute-done.6.xa_ref.xk_ref) | copy-start | bytes 3145732
  86.8 26.0 %collective-permute-start.7 = (bf16[512,1024]{1,0:T(8,128)(2,1)S(1)}, bf16[512,1024]{1,0:T(8,128)(2,1)}, u32[]{:S(2)}, u32[]{:S(2)}) collective-permute-start(bf16[512,1024]{1,0:T(8,128)(2,1)S(1)} %collective-permute-done.6.xa_ref.xk_ref), channel_id=1, source_target_pairs={{0,1},{1,0},{2,3},{3,2},{4,5},{5,4},{6,7},{7,6},{8,9},{9,8},{10,11... | collective-permute-start | bytes 3145736 | tf_op jit(solution)/shard_map/ppermute | solution.py:56
  99.7 20.8 %collective-permute-start.11 = (bf16[1024,256]{1,0:T(8,128)(2,1)}, bf16[1024,256]{1,0:T(8,128)(2,1)}, u32[]{:S(2)}, u32[]{:S(2)}) collective-permute-start(bf16[1024,256]{1,0:T(8,128)(2,1)} %bitcast.42), channel_id=1, source_target_pairs={{0,2},{1,3},{2,0},{3,1},{4,6},{5,7},{6,4},{7,5},{8,10},{9,11},{10,... | collective-permute-start | bytes 1572872 | tf_op jit(solution)/shard_map/ppermute | solution.py:56
  100.2 51.4 %all-to-all-start.1 = ((bf16[8,64,1024]{2,1,0:T(8,128)(2,1)}), bf16[8,64,1024]{2,1,0:T(8,128)(2,1)}, u32[]{:S(2)}, u32[]{:S(2)}) async-start(bf16[8,64,1024]{2,1,0:T(8,128)(2,1)} %bitcast.127), calls=%async_computation.1 | async-start | bytes 2097152 | tf_op jit(solution)/shard_map/all_to_all | solution.py:753
  104.7 8.1 %copy-start.7 = (f32[1,1024]{1,0:T(1,128)}, f32[1,1024]{1,0:T(1,128)S(1)}, u32[]{:S(2)}) copy-start(f32[1,1024]{1,0:T(1,128)S(1)} %get-tuple-element.240.gain_ref) | copy-start | bytes 12292
  143.6 31.1 %copy-start.16 = (bf16[1024,256]{1,0:T(8,128)(2,1)}, bf16[1024,256]{1,0:T(8,128)(2,1)S(1)}, u32[]{:S(2)}) copy-start(bf16[1024,256]{1,0:T(8,128)(2,1)S(1)} %get-tuple-element.129.o0.o_ref) | copy-start | bytes 1572868
  143.6 32.4 %collective-permute-start.13 = (bf16[1024,256]{1,0:T(8,128)(2,1)S(1)}, bf16[1024,256]{1,0:T(8,128)(2,1)}, u32[]{:S(2)}, u32[]{:S(2)}) collective-permute-start(bf16[1024,256]{1,0:T(8,128)(2,1)S(1)} %get-tuple-element.129.o0.o_ref), channel_id=1, source_target_pairs={{0,2},{1,3},{2,0},{3,1},{4,6},{5,7},{6,4},{7,5},{8,10},{9,11},{10,... | collective-permute-start | bytes 1572872 | tf_op jit(solution)/shard_map/ppermute | solution.py:56
  153.8 20.9 %copy-start.9 = (bf16[512,1024]{1,0:T(8,128)(2,1)}, bf16[512,1024]{1,0:T(8,128)(2,1)S(1)}, u32[]{:S(2)}) copy-start(bf16[512,1024]{1,0:T(8,128)(2,1)S(1)} %convolution_convert_fusion.3.gk_ref.g_ref) | copy-start | bytes 3145732
  153.8 22.2 %collective-permute-start.14 = (bf16[512,1024]{1,0:T(8,128)(2,1)S(1)}, bf16[512,1024]{1,0:T(8,128)(2,1)}, u32[]{:S(2)}, u32[]{:S(2)}) collective-permute-start(bf16[512,1024]{1,0:T(8,128)(2,1)S(1)} %convolution_convert_fusion.3.gk_ref.g_ref), channel_id=1, source_target_pairs={{0,2},{1,3},{2,0},{3,1},{4,6},{5,7},{6,4},{7,5},{8,10},{9,11},{10,... | collective-permute-start | bytes 3145736 | tf_op jit(solution)/shard_map/ppermute | solution.py:56
  176.1 8.2 %collective-permute-start.15 = (bf16[512,1024]{1,0:T(8,128)(2,1)}, bf16[512,1024]{1,0:T(8,128)(2,1)}, u32[]{:S(2)}, u32[]{:S(2)}) collective-permute-start(bf16[512,1024]{1,0:T(8,128)(2,1)} %collective-permute-done.14.gk_ref), channel_id=1, source_target_pairs={{0,1},{1,0},{2,3},{3,2},{4,5},{5,4},{6,7},{7,6},{8,9},{9,8},{10,11... | collective-permute-start | bytes 3145736 | tf_op jit(solution)/shard_map/ppermute | solution.py:56
  177.1 2.5 collective-permute-start.18
  177.7 2.8 collective-permute-start.19
  177.8 6.5 %collective-permute-start.16 = (bf16[1024,256]{1,0:T(8,128)(2,1)}, bf16[1024,256]{1,0:T(8,128)(2,1)}, u32[]{:S(2)}, u32[]{:S(2)}) collective-permute-start(bf16[1024,256]{1,0:T(8,128)(2,1)} %get-tuple-element.119.o0.o_ref.o1), channel_id=1, source_target_pairs={{0,1},{1,0},{2,3},{3,2},{4,5},{5,4},{6,7},{7,6},{8,9},{9,8},{10,11... | collective-permute-start | bytes 1572872 | tf_op jit(solution)/shard_map/ppermute | solution.py:56
  178.2 6.1 %collective-permute-start.17 = (bf16[1024,256]{1,0:T(8,128)(2,1)}, bf16[1024,256]{1,0:T(8,128)(2,1)}, u32[]{:S(2)}, u32[]{:S(2)}) collective-permute-start(bf16[1024,256]{1,0:T(8,128)(2,1)} %collective-permute-done.13.o2), channel_id=1, source_target_pairs={{0,1},{1,0},{2,3},{3,2},{4,5},{5,4},{6,7},{7,6},{8,9},{9,8},{10,11... | collective-permute-start | bytes 1572872 | tf_op jit(solution)/shard_map/ppermute | solution.py:56
  179.6 28.7 %collective-permute-start.21 = (f32[4]{0:T(128)S(1)}, f32[4]{0:T(128)S(1)}, u32[]{:S(2)}, u32[]{:S(2)}) collective-permute-start(f32[4]{0:T(128)S(1)} %maximum_multiply_fusion), channel_id=1, source_target_pairs={{0,4},{4,0},{8,12},{12,8},{16,20},{20,16},{24,28},{28,24},{1,5},{5... | collective-permute-start | bytes 56 | tf_op jit(solution)/shard_map/ppermute | solution.py:56
  180.6 27.8 %collective-permute-start.20 = (bf16[1024,256]{1,0:T(8,128)(2,1)}, bf16[1024,256]{1,0:T(8,128)(2,1)}, u32[]{:S(2)}, u32[]{:S(2)}) collective-permute-start(bf16[1024,256]{1,0:T(8,128)(2,1)} %get-tuple-element.119.o0.o_ref.o1), channel_id=1, source_target_pairs={{0,2},{1,3},{2,0},{3,1},{4,6},{5,7},{6,4},{7,5},{8,10},{9,11},{10,... | collective-permute-start | bytes 1572872 | tf_op jit(solution)/shard_map/ppermute | solution.py:56
  184.3 24.1 %copy-start.10 = (bf16[512,1024]{1,0:T(8,128)(2,1)S(1)}, bf16[512,1024]{1,0:T(8,128)(2,1)}, u32[]{:S(2)}) copy-start(bf16[512,1024]{1,0:T(8,128)(2,1)} %copy-done.9) | copy-start | bytes 3145732
  184.3 24.6 %copy-start.17 = (bf16[1024,256]{1,0:T(8,128)(2,1)S(1)}, bf16[1024,256]{1,0:T(8,128)(2,1)}, u32[]{:S(2)}) copy-start(bf16[1024,256]{1,0:T(8,128)(2,1)} %copy-done.16) | copy-start | bytes 1572868
  208.3 2.7 collective-permute-start.22
  208.4 6.1 %collective-permute-start.12 = (bf16[512,1024]{1,0:T(8,128)(2,1)S(1)}, bf16[512,1024]{1,0:T(8,128)(2,1)S(1)}, u32[]{:S(2)}, u32[]{:S(2)}) collective-permute-start(bf16[512,1024]{1,0:T(8,128)(2,1)S(1)} %copy-done.10), channel_id=1, source_target_pairs={{0,1},{1,0},{2,3},{3,2},{4,5},{5,4},{6,7},{7,6},{8,9},{9,8},{10,11... | collective-permute-start | bytes 3145736 | tf_op jit(solution)/shard_map/ppermute | solution.py:56
  208.9 5.6 %collective-permute-start.23 = (bf16[1024,256]{1,0:T(8,128)(2,1)S(1)}, bf16[1024,256]{1,0:T(8,128)(2,1)S(1)}, u32[]{:S(2)}, u32[]{:S(2)}) collective-permute-start(bf16[1024,256]{1,0:T(8,128)(2,1)S(1)} %copy-done.17), channel_id=1, source_target_pairs={{0,1},{1,0},{2,3},{3,2},{4,5},{5,4},{6,7},{7,6},{8,9},{9,8},{10,11... | collective-permute-start | bytes 1572872 | tf_op jit(solution)/shard_map/ppermute | solution.py:56
  209.0 5.5 %collective-permute-start.24 = (bf16[1024,256]{1,0:T(8,128)(2,1)}, bf16[1024,256]{1,0:T(8,128)(2,1)S(1)}, u32[]{:S(2)}, u32[]{:S(2)}) collective-permute-start(bf16[1024,256]{1,0:T(8,128)(2,1)} %collective-permute-done.20.o2), channel_id=1, source_target_pairs={{0,1},{1,0},{2,3},{3,2},{4,5},{5,4},{6,7},{7,6},{8,9},{9,8},{10,11... | collective-permute-start | bytes 1572872 | tf_op jit(solution)/shard_map/ppermute | solution.py:56
  209.4 29.4 %collective-permute-start.26 = (f32[4]{0:T(128)S(1)}, f32[4]{0:T(128)S(1)}, u32[]{:S(2)}, u32[]{:S(2)}) collective-permute-start(f32[4]{0:T(128)S(1)} %max.12), channel_id=1, source_target_pairs={{0,8},{4,12},{8,0},{12,4},{16,24},{20,28},{24,16},{28,20},{1,9},{5... | collective-permute-start | bytes 56 | tf_op jit(solution)/shard_map/ppermute | solution.py:56
  213.0 25.8 %collective-permute-start.25 = (bf16[512,1024]{1,0:T(8,128)(2,1)S(1)}, bf16[512,1024]{1,0:T(8,128)(2,1)S(1)}, u32[]{:S(2)}, u32[]{:S(2)}) collective-permute-start(bf16[512,1024]{1,0:T(8,128)(2,1)S(1)} %add_convert_fusion.2), channel_id=1, source_target_pairs={{0,2},{1,3},{2,0},{3,1},{4,6},{5,7},{6,4},{7,5},{8,10},{9,11},{10,... | collective-permute-start | bytes 3145736 | tf_op jit(solution)/shard_map/ppermute | solution.py:56
  215.5 26.8 %copy-start.11 = (bf16[512,1024]{1,0:T(8,128)(2,1)S(1)}, bf16[512,1024]{1,0:T(8,128)(2,1)}, u32[]{:S(2)}) copy-start(bf16[512,1024]{1,0:T(8,128)(2,1)} %copy-done.9) | copy-start | bytes 3145732
  238.8 3.4 collective-permute-start.27
  238.9 34.0 %collective-permute-start.33 = (bf16[512,1024]{1,0:T(8,128)(2,1)}, bf16[512,1024]{1,0:T(8,128)(2,1)S(1)}, u32[]{:S(2)}, u32[]{:S(2)}) collective-permute-start(bf16[512,1024]{1,0:T(8,128)(2,1)} %get-tuple-element.161), channel_id=1, source_target_pairs={{0,1},{1,0},{2,3},{3,2},{4,5},{5,4},{6,7},{7,6},{8,9},{9,8},{10,11... | collective-permute-start | bytes 3145736 | tf_op jit(solution)/shard_map/ppermute | solution.py:56
  239.4 33.0 %collective-permute-start.29 = (f32[4]{0:T(128)S(1)}, f32[4]{0:T(128)S(1)}, u32[]{:S(2)}, u32[]{:S(2)}) collective-permute-start(f32[4]{0:T(128)S(1)} %max.13), channel_id=1, source_target_pairs={{0,16},{4,20},{8,24},{12,28},{16,0},{20,4},{24,8},{28,12},{1,17},{... | collective-permute-start | bytes 56 | tf_op jit(solution)/shard_map/ppermute | solution.py:56
  246.7 20.5 %collective-permute-start.30 = (bf16[512,1024]{1,0:T(8,128)(2,1)S(1)}, bf16[512,1024]{1,0:T(8,128)(2,1)S(1)}, u32[]{:S(2)}, u32[]{:S(2)}) collective-permute-start(bf16[512,1024]{1,0:T(8,128)(2,1)S(1)} %get-tuple-element.147.even_ref), channel_id=1, source_target_pairs={{0,1},{1,0},{2,3},{3,2},{4,5},{5,4},{6,7},{7,6},{8,9},{9,8},{10,11... | collective-permute-start | bytes 3145736 | tf_op jit(solution)/shard_map/ppermute | solution.py:56
  246.8 25.6 %collective-permute-start.28 = (bf16[512,1024]{1,0:T(8,128)(2,1)S(1)}, bf16[512,1024]{1,0:T(8,128)(2,1)}, u32[]{:S(2)}, u32[]{:S(2)}) collective-permute-start(bf16[512,1024]{1,0:T(8,128)(2,1)S(1)} %get-tuple-element.147.even_ref), channel_id=1, source_target_pairs={{0,2},{1,3},{2,0},{3,1},{4,6},{5,7},{6,4},{7,5},{8,10},{9,11},{10,... | collective-permute-start | bytes 3145736 | tf_op jit(solution)/shard_map/ppermute | solution.py:56
  272.4 6.8 %collective-permute-start.31 = (bf16[512,1024]{1,0:T(8,128)(2,1)}, bf16[512,1024]{1,0:T(8,128)(2,1)}, u32[]{:S(2)}, u32[]{:S(2)}) collective-permute-start(bf16[512,1024]{1,0:T(8,128)(2,1)} %get-tuple-element.156), channel_id=1, source_target_pairs={{0,1},{1,0},{2,3},{3,2},{4,5},{5,4},{6,7},{7,6},{8,9},{9,8},{10,11... | collective-permute-start | bytes 3145736 | tf_op jit(solution)/shard_map/ppermute | solution.py:56
  272.5 11.3 %collective-permute-start.32 = (bf16[512,1024]{1,0:T(8,128)(2,1)}, bf16[512,1024]{1,0:T(8,128)(2,1)}, u32[]{:S(2)}, u32[]{:S(2)}) collective-permute-start(bf16[512,1024]{1,0:T(8,128)(2,1)} %collective-permute-done.28.even_ref), channel_id=1, source_target_pairs={{0,1},{1,0},{2,3},{3,2},{4,5},{5,4},{6,7},{7,6},{8,9},{9,8},{10,11... | collective-permute-start | bytes 3145736 | tf_op jit(solution)/shard_map/ppermute | solution.py:56
  274.6 94.7 %all-to-all-start.2 = ((bf16[8,3,656,128]{3,2,1,0:T(8,128)(2,1)}), bf16[8,3,656,128]{3,2,1,0:T(8,128)(2,1)}, u32[]{:S(2)}, u32[]{:S(2)}) async-start(bf16[8,3,656,128]{3,2,1,0:T(8,128)(2,1)} %inner_grads.1), calls=%async_computation.2 | async-start | bytes 8060928 | tf_op jit(solution)/shard_map/all_to_all | solution.py:874
  279.2 176.5 %reduce-scatter.2.cloned.1.call-start = ((), (), s32[]{:S(2)}) async-start(), calls=%async_computation.7 | async-start | bytes 2359296 | tf_op jit(solution)/shard_map/reduce_scatter | solution.py:908
  282.3 73.5 %collective-permute-start.34 = (bf16[512,1024]{1,0:T(8,128)(2,1)}, bf16[512,1024]{1,0:T(8,128)(2,1)}, u32[]{:S(2)}, u32[]{:S(2)}) collective-permute-start(bf16[512,1024]{1,0:T(8,128)(2,1)} %add_convert_fusion.1), channel_id=1, source_target_pairs={{0,2},{1,3},{2,0},{3,1},{4,6},{5,7},{6,4},{7,5},{8,10},{9,11},{10,... | collective-permute-start | bytes 3145736 | tf_op jit(solution)/shard_map/ppermute | solution.py:56
  346.8 9.0 %copy-start.2 = (bf16[4,8,128,256]{3,2,1,0:T(8,128)(2,1)S(1)}, bf16[4,8,128,256]{3,2,1,0:T(8,128)(2,1)}, u32[]{:S(2)}) copy-start(bf16[4,8,128,256]{3,2,1,0:T(8,128)(2,1)} %copy.70) | copy-start | bytes 6291460
  359.4 3.0 collective-permute-start.35
  373.8 39.4 %all-to-all-start.3 = ((bf16[8,64,1024]{2,1,0:T(8,128)(2,1)}), bf16[8,64,1024]{2,1,0:T(8,128)(2,1)}, u32[]{:S(2)}, u32[]{:S(2)}) async-start(bf16[8,64,1024]{2,1,0:T(8,128)(2,1)} %bitcast.52), calls=%async_computation.3 | async-start | bytes 2097152 | tf_op jit(solution)/shard_map/all_to_all | solution.py:753
  378.3 24.7 %collective-permute-start.36 = (bf16[512,1024]{1,0:T(8,128)(2,1)}, bf16[512,1024]{1,0:T(8,128)(2,1)S(1)}, u32[]{:S(2)}, u32[]{:S(2)}) collective-permute-start(bf16[512,1024]{1,0:T(8,128)(2,1)} %add_convert_fusion), channel_id=1, source_target_pairs={{0,2},{1,3},{2,0},{3,1},{4,6},{5,7},{6,4},{7,5},{8,10},{9,11},{10,... | collective-permute-start | bytes 3145736 | tf_op jit(solution)/shard_map/ppermute | solution.py:56
  382.5 30.7 %copy-start.8 = (f32[1,1024]{1,0:T(1,128)S(1)}, f32[1,1024]{1,0:T(1,128)}, u32[]{:S(2)}) copy-start(f32[1,1024]{1,0:T(1,128)} %copy-done.7) | copy-start | bytes 12292
  382.5 21.5 %collective-permute-start.37 = (bf16[512,1024]{1,0:T(8,128)(2,1)S(1)}, bf16[512,1024]{1,0:T(8,128)(2,1)S(1)}, u32[]{:S(2)}, u32[]{:S(2)}) collective-permute-start(bf16[512,1024]{1,0:T(8,128)(2,1)S(1)} %dn.7), channel_id=1, source_target_pairs={{0,1},{1,0},{2,3},{3,2},{4,5},{5,4},{6,7},{7,6},{8,9},{9,8},{10,11... | collective-permute-start | bytes 3145736 | tf_op jit(solution)/shard_map/ppermute | solution.py:56
  420.6 38.4 %all-to-all-start.4 = ((bf16[8,64,1024]{2,1,0:T(8,128)(2,1)}), bf16[8,64,1024]{2,1,0:T(8,128)(2,1)S(1)}, u32[]{:S(2)}, u32[]{:S(2)}) async-start(bf16[8,64,1024]{2,1,0:T(8,128)(2,1)} %bitcast.54), calls=%async_computation.4 | async-start | bytes 2097152 | tf_op jit(solution)/shard_map/all_to_all | solution.py:753
  461.6 8.2 %copy-start.1 = (bf16[512,1024]{1,0:T(8,128)(2,1)S(1)}, bf16[512,1024]{1,0:T(8,128)(2,1)}, u32[]{:S(2)}) copy-start(bf16[512,1024]{1,0:T(8,128)(2,1)} %param.10) | copy-start | bytes 3145732
  461.6 4.0 collective-permute-start.38
  465.8 3.3 collective-permute-start.39
  (28 other events, 101.1 us)
Sparse Core Ops, SparseCore 0:
  69.2 94.3 all-gather.1
  362.3 93.3 reduce-scatter.1

commit v4 on v3

--- a/solution.py
+++ b/solution.py
@@ -331,7 +331,7 @@
             ],
         ),
         compiler_params=vmem(48),
-        cost_estimate=takes(57),
+        cost_estimate=takes(20),
         name="attend_backward",
     )(scalars, q2, k, v, do, cos, sin)
 
@@ -654,7 +654,7 @@
         in_specs=[flat] * 5 + [resident(gain.shape)],
         out_specs=flat,
         compiler_params=vmem(48),
-        cost_estimate=takes(5),
+        cost_estimate=takes(0),
         name="last",
     )(keep, core, chip, x, dx, gain)
 
@@ -668,7 +668,7 @@
         turn_rows_kernel,
         out_shape=jax.ShapeDtypeStruct(values.shape, BF16),
         compiler_params=vmem(48),
-        cost_estimate=takes(2),
+        cost_estimate=takes(0),
         name="turn_rows",
     )(one_hot, values)
 
@@ -710,13 +710,12 @@
 
 def scatter_lanes(values):
     me = lax.axis_index("mp")
-    for bit in reversed(bits_of(lax.axis_size("mp"))):
-        half = values.shape[-1] // 2
-        low, top = values[..., :half], values[..., half:]
-        high = (me // bit) % 2 == 1
-        other = swap_bit(jnp.where(high, low, top), "mp", bit)
-        values = jnp.where(high, top, low) + other
-    return values
+    count = lax.axis_size("mp")
+    slices = values.reshape(values.shape[0], count, values.shape[1] // count)
+    total = pick(slices, 1, me)
+    for bits in range(1, count):
+        total = total + swap_bit(pick(slices, 1, me ^ bits), "mp", bits)
+    return total
 
 
 def local(
@@ -782,7 +781,6 @@
 
     w_mlp = jnp.concatenate([w_in, w_down.T[None]], axis=0)
     x_arrived = exchange(pack(hidden_in))
-    gains, w_mlp = lax.optimization_barrier((gains, w_mlp))
     x_arrived, gains, cos, sin, scalars, g_packed = lax.optimization_barrier(
         (x_arrived, gains, cos, sin, scalars, pack(out_grad))
     )
@@ -861,15 +859,14 @@
     (act,) = after(da, act)
     inner_grads = inner_call(flat(n2), flat(g_all), flat(dgate), flat(dup), flat(act))
     held = list(head_grad_call(scalars, da, da_core, attn_weights[3], near, 0, tokens, ()))
-    inner_grads, da_across, peak_swap, held[0] = lax.optimization_barrier(
-        (inner_grads, da_across, peak_swap, held[0])
-    )
+    _, da_across, held[0] = lax.optimization_barrier((inner_grads, da_across, held[0]))
     do, da_all = head_grad_call(
         scalars, da_across, core(da_across), attn_weights[3], distant, 1, tokens, held
     )
     head_peaks = jnp.maximum(head_peaks, peak_swap)
     for bit in peak_bits[3:]:
         head_peaks = jnp.maximum(head_peaks, swap_bit(head_peaks, "dp", bit))
+    inner_grads, peak_swap = lax.optimization_barrier((inner_grads, peak_swap))
     inner_grads = by_device(inner_grads, dp_count)
     inner_grads = lax.all_to_all(inner_grads, "dp", split_axis=0, concat_axis=0, tiled=True)
 
@@ -877,15 +874,18 @@
     far_out = after(da_across, *far_out)
     add_core = lambda keep, send: keep.astype(F32) + core(send).astype(F32)
 
+    out_far = add_core(*far_out).astype(BF16)
+    out_arrived = swap_bit(out_far, "mp", 2)
+    do, out_sum = after(out_far, do, add_core(keep_out, send_out))
+    dproj = attend_backward(scalars, q2, k, v, do, cos, sin)
+    head_peaks = jnp.maximum(head_peaks, peak_swap)
+    for bit in peak_bits[3:]:
+        head_peaks = jnp.maximum(head_peaks, swap_bit(head_peaks, "dp", bit))
     factor = jnp.sqrt(clip_limit / jnp.maximum(head_peaks, clip_limit))
     column_factor = jnp.repeat(factor, HEAD_DIM)
     scaling = jnp.stack([column_factor, column_factor, jnp.ones_like(column_factor)])[:, None, :]
     clipped = (w_qkv.astype(F32) * scaling).astype(BF16)
 
-    out_far = add_core(*far_out).astype(BF16)
-    out_arrived = swap_bit(out_far, "mp", 2)
-    do, out_sum = after(out_far, do, add_core(keep_out, send_out))
-    dproj = attend_backward(scalars, q2, k, v, do, cos, sin)
     proj_grad = proj_call(n1, dproj, (near, distant), da_all)
     proj_grad, dproj, out_arrived = lax.optimization_barrier((proj_grad, dproj, out_arrived))
     far_core = core(dn_call(scalars, dproj, attn_weights, 3, rows))
@@ -900,29 +900,26 @@
     send = dn_call(scalars, dproj, attn_weights, 1, rows)
     keep = dn_call(scalars, dproj, attn_weights, 0, rows)
     dn_core = core(send)
+    inner_grads = jnp.sum(inner_grads.astype(F32), axis=0)
+    inner_grad, down_grad = jnp.swapaxes(inner_grads[:2], 1, 2), inner_grads[2]
+    inner_by_gain = jnp.sum(inner_grad * w_in.astype(F32), axis=(0, 2))
+    gain_part = lax.dynamic_slice_in_dim(gains, owner * shards, shards, 1)
+    inner_grad, down_grad, inner_by_gain, gain_part, clipped, keep = lax.optimization_barrier(
+        (inner_grad, down_grad, inner_by_gain, gain_part, clipped, keep)
+    )
     out_sent, dn_arrived, dn_core = lax.optimization_barrier((out_sent, dn_arrived, dn_core))
     grad_packed = pack_back(last_call(keep, dn_core, dn_arrived, x_rel[0], dx, gain_one))
     grad_arrived = exchange(grad_packed)
     (out_arrived,) = after(grad_packed, out_sent)
     output = turn_rows(to_slot, out_arrived)
     grads = lax.psum_scatter(by_device(proj_grad, dp_count), "dp")
-    inner_grads, grads = after(output, inner_grads, grads)
-    inner_grads = jnp.sum(inner_grads.astype(F32), axis=0)
-    grad_arrived, inner_grads, grads = lax.optimization_barrier(
-        (grad_arrived, inner_grads, grads)
-    )
+    (grads,) = after(output, grads)
+    grad_arrived, grads = lax.optimization_barrier((grad_arrived, grads))
     grads = grads.astype(F32)
     input_grad = unpack_back(grad_arrived)
-    inner_grad, down_grad = jnp.swapaxes(inner_grads[:2], 1, 2), inner_grads[2]
     proj_grad, outer_grad = jnp.swapaxes(grads[:3], 1, 2), grads[3]
 
-    by_gain = jnp.stack(
-        [
-            jnp.sum(proj_grad * w_qkv.astype(F32), axis=(0, 2)),
-            jnp.sum(inner_grad * w_in.astype(F32), axis=(0, 2)),
-        ]
-    )
-    gain_part = lax.dynamic_slice_in_dim(gains, owner * shards, shards, 1)
+    by_gain = jnp.stack([jnp.sum(proj_grad * w_qkv.astype(F32), axis=(0, 2)), inner_by_gain])
     gain_grads = scatter_lanes(by_gain / gain_part)
     return (
         output,

time: 485 us -> 476 us (0.981)
  Pallas kernels: 216 us -> 202 us
  starting transfers between devices: 56.4 us -> 62.8 us
    pallas_call x1, Pallas kernels: 55.8 us -> 45.8 us  [attend_backward(): pl.pallas_call(functools.partial(bwd_kernel, q_rows, k_rows), out_shape=j...]
    pallas_call x2, Pallas kernels: 38.5 us -> 33 us  [attend_forward(): pl.pallas_call(functools.partial(fwd_kernel, far, q_rows, k_rows), out_sh...]
    all_to_all x4, starting transfers between devices: 19.1 us -> 24.1 us  [exchange(): lax.all_to_all(packed, 'dp', split_axis=0, concat_axis=0, tiled=True)]
    ppermute x40 -> x41, waiting for transfers between devices: 67 us -> 62.5 us  [swap_bit(): return lax.ppermute(values, axis_name, [(i, i ^ bit) for i in range(count)])]
    unnamed x98 -> x96, local copies, waits for them, and re-layouts: 21.1 us -> 19.7 us
    ppermute x40 -> x41, starting transfers between devices: 32.7 us -> 32.4 us  [swap_bit(): return lax.ppermute(values, axis_name, [(i, i ^ bit) for i in range(count)])]
  transfers between devices with their start and end apart: 47 -> 48, of which waited for: 18 -> 22; matrix products, arithmetic and copies ran while one was open for 11% -> 11% of each run, Pallas kernels for 45% -> 43%
where the time goes in v4:
time: 476 us; the launch traced here: 469 us
  Pallas kernels  202 us (42%)
  waiting for transfers between devices  118 us (25%)
  starting transfers between devices  62.8 us (13%)
  local copies, waits for them, and re-layouts  28.4 us (6%)
  other arithmetic  26.4 us (6%)
  matrix products  16 us (3%)
  between operations  15.3 us (3%)
    ppermute x41, waiting for transfers between devices, swap_bit(): return lax.ppermute(values, axis_name, [(i, i ^ bit) for i in range(count)])  62.5 us
    pallas_call x2, Pallas kernels, mlp_call(): pl.pallas_call(mlp_kernel, out_shape=(wide_out, wide_out, wide_out, narro...  47.5 us
    pallas_call x1, Pallas kernels, attend_backward(): pl.pallas_call(functools.partial(bwd_kernel, q_rows, k_rows), out_shape=j...  45.8 us
    pallas_call x2, Pallas kernels, attend_forward(): pl.pallas_call(functools.partial(fwd_kernel, far, q_rows, k_rows), out_sh...  33 us
    ppermute x41, starting transfers between devices, swap_bit(): return lax.ppermute(values, axis_name, [(i, i ^ bit) for i in range(count)])  32.4 us
    reduce_scatter x1, waiting for transfers between devices, local(): grads = lax.psum_scatter(by_device(proj_grad, dp_count), 'dp')  29 us
    all_to_all x4, starting transfers between devices, exchange(): lax.all_to_all(packed, 'dp', split_axis=0, concat_axis=0, tiled=True)  24.1 us
    all_to_all x4, waiting for transfers between devices, exchange(): lax.all_to_all(packed, 'dp', split_axis=0, concat_axis=0, tiled=True)  19.9 us
  transfers between devices with their start and end apart: 48, of which 22 were waited for; matrix products, arithmetic and copies ran while one was open for 11% of the time, Pallas kernels for 43%

profile of v4, /device:TPU:0, one launch (start us, length us, event | category | flops | bytes accessed | tf_op | source)
XLA Modules:
  0.0 469.3 jit_solution(14605812713195980814)
XLA Ops:
  9.2 4.1 collective-permute-start.8
  15.5 1.7 convolution_convert_fusion.6
  17.2 6.3 %all-to-all-start = ((bf16[8,64,1024]{2,1,0:T(8,128)(2,1)}), bf16[8,64,1024]{2,1,0:T(8,128)(2,1)}, u32[]{:S(2)}, u32[]{:S(2)}) async-start(bf16[8,64,1024]{2,1,0:T(8,128)(2,1)} %bitcast.1), calls=%async_computation | async-start | bytes 2097152 | tf_op jit(solution)/shard_map/all_to_all | solution.py:752
  23.7 1.7 convolution_convert_fusion.5
  26.7 3.7 fusion.6
  30.5 2.0 collective-permute-start.1
  32.5 7.6 %collective-permute-done.1 = f32[2,2,32]{2,1,0:T(2,128)S(1)} collective-permute-done((f32[2,2,32]{2,1,0:T(2,128)S(1)}, f32[2,2,32]{2,1,0:T(2,128)S(1)}, u32[]{:S(2)}, u32[]{:S(2)}) %collective-permute-start.1) | collective-permute-done | bytes 544 | tf_op jit(solution)/shard_map/ppermute | solution.py:56
  40.2 1.9 collective-permute-start.2
  42.3 1.6 collective-permute-done.2
  43.9 1.6 collective-permute-start.3
  45.5 2.1 collective-permute-done.3
  48.5 2.5 collective-permute-start.9
  52.4 7.8 %collective-permute-done.9 = bf16[2,4,128,256]{3,2,1,0:T(8,128)(2,1)S(1)} collective-permute-done((bf16[2,4,128,256]{3,2,1,0:T(8,128)(2,1)}, bf16[2,4,128,256]{3,2,1,0:T(8,128)(2,1)S(1)}, u32[]{:S(2)}, u32[]{:S(2)}) %collective-permute-start.9) | collective-permute-done | bytes 524320 | tf_op jit(solution)/shard_map/ppermute | solution.py:56
  61.3 2.1 convolution_convert_fusion.4.xa_ref.xk_ref.x_ref
  63.3 1.6 collective-permute-start.6
  68.3 1.7 copy.81
  70.1 1.8 pad_maximum_fusion.2
  71.9 12.9 %collective-permute-done.6.xa_ref.xk_ref = bf16[512,1024]{1,0:T(8,128)(2,1)} collective-permute-done((bf16[512,1024]{1,0:T(8,128)(2,1)S(1)}, bf16[512,1024]{1,0:T(8,128)(2,1)}, u32[]{:S(2)}, u32[]{:S(2)}) %collective-permute-start.6) | collective-permute-done | bytes 1048608 | tf_op jit(solution)/shard_map/ppermute | solution.py:56
  84.8 8.8 %collective-permute-done.10 = bf16[2,2,4,128,256]{4,3,2,0,1:T(8,128)(2,1)} collective-permute-done((bf16[2,2,4,128,256]{4,3,2,0,1:T(8,128)(2,1)}, bf16[2,2,4,128,256]{4,3,2,0,1:T(8,128)(2,1)}, u32[]{:S(2)}, u32[]{:S(2)}) %collective-permute-start.10) | collective-permute-done | bytes 1048608 | tf_op jit(solution)/shard_map/ppermute | solution.py:56
  93.6 1.7 select_bitcast_fusion.1
  95.5 1.5 copy.80
  98.4 4.7 %all-to-all-start.1 = ((bf16[8,64,1024]{2,1,0:T(8,128)(2,1)}), bf16[8,64,1024]{2,1,0:T(8,128)(2,1)}, u32[]{:S(2)}, u32[]{:S(2)}) async-start(bf16[8,64,1024]{2,1,0:T(8,128)(2,1)} %bitcast.140), calls=%async_computation.1 | async-start | bytes 2097152 | tf_op jit(solution)/shard_map/all_to_all | solution.py:752
  103.2 7.7 %qkv.2 = (bf16[4,2048,128]{2,1,0:T(8,128)(2,1)}, bf16[4,2048,128]{2,1,0:T(8,128)(2,1)}, bf16[4,2048,128]{2,1,0:T(8,128)(2,1)}, bf16[2048,1024]{1,0:T(8,128)(2,1)}) custom-call(s32[4]{0:T(128)S(1)} %pad_add_fusion.s_ref, bf16[512,1024]{1,0:T(8,128)(2,1)S(1)} %convolution_convert_fusion.4.xa_ref.xk_ref.x_ref, ...), custom_call_target="tpu_custom_call" | custom-call | flops 3300000000 | bytes 3222656 | tf_op jit(solution)/shard_map/qkv/pallas_call | solution.py:119
  110.9 8.2 %qkv.3 = (bf16[4,2048,128]{2,1,0:T(8,128)(2,1)}, bf16[4,2048,128]{2,1,0:T(8,128)(2,1)}, bf16[4,2048,128]{2,1,0:T(8,128)(2,1)}, bf16[2048,1024]{1,0:T(8,128)(2,1)}) custom-call(s32[4]{0:T(128)S(1)} %pad_add_fusion.s_ref, ...), custom_call_target="tpu_custom_call", output_to_operand_aliasing={{0}: (7, {}), {1}: (8, {}), {2}: (9, {}), {3}: (10, {})} | custom-call | flops 3300000000 | bytes 3222656 | tf_op jit(solution)/shard_map/qkv/pallas_call | solution.py:119
  119.1 1.6 copy-done.6
  120.7 15.6 %attend_forward.2 = (bf16[1024,256]{1,0:T(8,128)(2,1)}, bf16[4,2048,128]{2,1,0:T(8,128)(2,1)S(1)}, f32[4,4,8,128]{3,2,1,0:T(8,128)S(1)}) custom-call(s32[4]{0:T(128)S(1)} %pad_add_fusion.s_ref, bf16[4,2048,128]{2,1,0:T(8,128)(2,1)S(1)} %copy-done.6, bf16[4,2048,128]{2,1,0:T(8,128)(2,1)} %get-tuple-element.112.k_ref, ...), custom_call_target="tpu_custom_call" | custom-call | flops 22000001024 | bytes 21484376 | tf_op jit(solution)/shard_map/attend_forward/pallas_call | solution.py:217
  137.6 3.4 collective-permute-start.13
  141.0 8.2 %all-to-all-done.1 = bf16[8,64,1024]{2,1,0:T(8,128)(2,1)} async-done(((bf16[8,64,1024]{2,1,0:T(8,128)(2,1)}), bf16[8,64,1024]{2,1,0:T(8,128)(2,1)}, u32[]{:S(2)}, u32[]{:S(2)}) %all-to-all-start.1) | async-done | bytes 1048608 | tf_op jit(solution)/shard_map/all_to_all | solution.py:752
  149.2 2.1 convolution_convert_fusion.3.gk_ref.g_ref
  151.3 1.9 collective-permute-start.14
  153.2 1.6 copy-done.7
  154.9 17.4 %attend_forward.3 = (bf16[1024,256]{1,0:T(8,128)(2,1)}, bf16[4,2048,128]{2,1,0:T(8,128)(2,1)S(1)}, f32[4,4,8,128]{3,2,1,0:T(8,128)S(1)}) custom-call(s32[4]{0:T(128)S(1)} %pad_add_fusion.s_ref, bf16[4,2048,128]{2,1,0:T(8,128)(2,1)S(1)} %copy-done.7, bf16[4,2048,128]{2,1,0:T(8,128)(2,1)} %get-tuple-element.112.k_ref, ...), custom_call_target="tpu_custom_call", output_to_operand_aliasing={{1}: (4, {})} | custom-call | flops 22000001024 | bytes 21484376 | tf_op jit(solution)/shard_map/attend_forward/pallas_call | solution.py:217
  175.7 1.7 collective-permute-done.18.w1
  179.6 24.0 %mlp.2 = (bf16[4,512,1024]{2,1,0:T(8,128)(2,1)}, bf16[4,512,1024]{2,1,0:T(8,128)(2,1)}, bf16[4,512,1024]{2,1,0:T(8,128)(2,1)}, bf16[4,512,656]{2,1,0:T(8,128)(2,...) custom-call(s32[4]{0:T(128)S(1)} %pad_add_fusion.s_ref, ...), custom_call_target="tpu_custom_call" | custom-call | flops 26400000000 | bytes 25781250 | tf_op jit(solution)/shard_map/mlp/pallas_call | solution.py:401
  206.3 1.9 add_convert_fusion.2
  210.3 23.6 %mlp.3 = (bf16[4,512,1024]{2,1,0:T(8,128)(2,1)}, bf16[4,512,1024]{2,1,0:T(8,128)(2,1)}, bf16[4,512,1024]{2,1,0:T(8,128)(2,1)}, bf16[4,512,656]{2,1,0:T(8,128)(2,...) custom-call(s32[4]{0:T(128)S(1)} %pad_add_fusion.s_ref, ...), custom_call_target="tpu_custom_call", output_to_operand_aliasing={{0}: (15, {}), {1}: (16, {}), {2}: (17, {}), {3}: (18, {}),... | custom-call | flops 26400000000 | bytes 25781250 | tf_op jit(solution)/shard_map/mlp/pallas_call | solution.py:401
  234.1 3.3 collective-permute-start.28
  237.5 4.4 resid.1
  242.3 18.5 %inner_grads.1 = bf16[8,3,656,128]{3,2,1,0:T(8,128)(2,1)} custom-call(bf16[2048,1024]{1,0:T(8,128)(2,1)} %bitcast.165, bf16[2048,1024]{1,0:T(8,128)(2,1)} %bitcast.166, bf16[2048,656]{1,0:T(8,128)(2,1)S(1)} %bitcast.137, bf16[2048,656]{1,0:T(8,128)(2,1)} %bitcast.168, bf16[2048,656]{1,0:T(8,128)(2,1)} %bitcast.167), custom_call_target="tpu_custom_call" | custom-call | flops 19800000512 | bytes 19335936 | tf_op jit(solution)/shard_map/inner_grads/pallas_call | solution.py:558
  260.8 6.3 %all-to-all-start.2 = ((bf16[8,3,656,128]{3,2,1,0:T(8,128)(2,1)}), bf16[8,3,656,128]{3,2,1,0:T(8,128)(2,1)}, u32[]{:S(2)}, u32[]{:S(2)}) async-start(bf16[8,3,656,128]{3,2,1,0:T(8,128)(2,1)} %inner_grads.1), calls=%async_computation.2 | async-start | bytes 8060928 | tf_op jit(solution)/shard_map/all_to_all | solution.py:871
  267.2 5.7 %head_grad.2 = (bf16[4,2048,128]{2,1,0:T(8,128)(2,1)S(1)}, bf16[2048,1024]{1,0:T(8,128)(2,1)}) custom-call(s32[4]{0:T(128)S(1)} %pad_add_fusion.s_ref, bf16[512,1024]{1,0:T(8,128)(2,1)} %get-tuple-element.147.even_ref, bf16[512,1024]{1,0:T(8,128)(2,1)} %collective-permute-done.30.odd_ref, bf16[1024,256]{1,0:T(8,128)(2,1)} %slice_bitcast_fusion.1.w0.w_ref, ...), custom_call_target="tpu_custom_call" | custom-call | flops 6600000000 | bytes 6445312 | tf_op jit(solution)/shard_map/head_grad/pallas_call | solution.py:500
  273.6 1.8 convert_add_fusion.1
  278.9 5.7 %head_grad.3 = (bf16[4,2048,128]{2,1,0:T(8,128)(2,1)S(1)}, bf16[2048,1024]{1,0:T(8,128)(2,1)}) custom-call(s32[4]{0:T(128)S(1)} %pad_add_fusion.s_ref, bf16[512,1024]{1,0:T(8,128)(2,1)} %collective-permute-done.29.even_ref, bf16[512,1024]{1,0:T(8,128)(2,1)S(1)} %collective-permute-done.32.odd_ref, ...), custom_call_target="tpu_custom_call", output_to_operand_aliasing={{0}: (5, {}), {1}: (6, {})} | custom-call | flops 6600000000 | bytes 6445312 | tf_op jit(solution)/shard_map/head_grad/pallas_call | solution.py:500
  285.9 45.8 %attend_backward.1.d_ref.p_ref = bf16[3,2048,256]{2,1,0:T(8,128)(2,1)} custom-call(s32[4]{0:T(128)S(1)} %pad_add_fusion.s_ref, bf16[4,2048,128]{2,1,0:T(8,128)(2,1)S(1)} %copy-done.25, bf16[4,2048,128]{2,1,0:T(8,128)(2,1)} %get-tuple-element.112.k_ref, bf16[4,2048,128]{2,1,0:T(8,128)(2,1)} %get-tuple-element.113.v_ref, bf16[4,2048,128]{2,1,0:T(8,128)(2,1)} %copy-done.21, ...), custom_call_target="tpu_custom_call" | custom-call | flops 22000001024 | bytes 21484376 | tf_op jit(solution)/shard_map/attend_backward/pallas_call | solution.py:313
  331.6 7.9 %proj_grads.1 = bf16[8,4,256,128]{3,2,1,0:T(8,128)(2,1)S(1)} custom-call(bf16[2048,1024]{1,0:T(8,128)(2,1)} %get-tuple-element.152.n_ref, bf16[3,2048,256]{2,1,0:T(8,128)(2,1)} %attend_backward.1.d_ref.p_ref, bf16[1024,256]{1,0:T(8,128)(2,1)} %get-tuple-element.129.o0.o_ref, bf16[1024,256]{1,0:T(8,128)(2,1)} %get-tuple-element.120.o0.o_ref.o1, ...), custom_call_target="tpu_custom_call" | custom-call | flops 11000000512 | bytes 10742187 | tf_op jit(solution)/shard_map/proj_grads/pallas_call | solution.py:594
  340.9 3.7 dn.5
  344.7 2.7 dn.4
  347.6 2.6 add_convert_fusion
  350.2 6.9 %all-to-all-done.2 = bf16[8,3,656,128]{3,2,1,0:T(8,128)(2,1)} async-done(((bf16[8,3,656,128]{3,2,1,0:T(8,128)(2,1)}), bf16[8,3,656,128]{3,2,1,0:T(8,128)(2,1)}, u32[]{:S(2)}, u32[]{:S(2)}) %all-to-all-start.2) | async-done | bytes 4030496 | tf_op jit(solution)/shard_map/all_to_all | solution.py:871
  357.1 4.4 convolution_convert_fusion.2
  361.5 9.3 %all-to-all-start.3 = ((bf16[8,64,1024]{2,1,0:T(8,128)(2,1)}), bf16[8,64,1024]{2,1,0:T(8,128)(2,1)}, u32[]{:S(2)}, u32[]{:S(2)}) async-start(bf16[8,64,1024]{2,1,0:T(8,128)(2,1)} %bitcast.142), calls=%async_computation.3 | async-start | bytes 2097152 | tf_op jit(solution)/shard_map/all_to_all | solution.py:752
  373.0 2.7 dn.7
  375.9 2.7 dn.6.keep_ref
  378.6 2.9 convert_reduce_fusion
  383.4 13.8 %collective-permute-done.36.chip_ref = bf16[512,1024]{1,0:T(8,128)(2,1)S(1)} collective-permute-done((bf16[512,1024]{1,0:T(8,128)(2,1)}, bf16[512,1024]{1,0:T(8,128)(2,1)S(1)}, u32[]{:S(2)}, u32[]{:S(2)}) %collective-permute-start.36) | collective-permute-done | bytes 1048608 | tf_op jit(solution)/shard_map/ppermute | solution.py:56
  399.2 10.2 %all-to-all-done.3 = bf16[8,64,1024]{2,1,0:T(8,128)(2,1)} async-done(((bf16[8,64,1024]{2,1,0:T(8,128)(2,1)}), bf16[8,64,1024]{2,1,0:T(8,128)(2,1)}, u32[]{:S(2)}, u32[]{:S(2)}) %all-to-all-start.3) | async-done | bytes 1048608 | tf_op jit(solution)/shard_map/all_to_all | solution.py:752
  411.9 3.0 last.1
  414.9 1.8 convolution_convert_fusion.1
  416.7 3.8 all-to-all-start.4
  421.5 2.9 turn_rows.1
  424.4 29.0 %reduce-scatter.2.cloned.1.call-done = bf16[1,4,256,128]{3,2,1,0:T(8,128)(2,1)} async-done(((bf16[8,4,256,128]{3,2,1,0:T(8,128)(2,1)}), bf16[1,4,256,128]{3,2,1,0:T(8,128)(2,1)}) %reduce-scatter.2.cloned.1.call-update) | async-done | bytes 262160 | tf_op jit(solution)/shard_map/reduce_scatter | solution.py:915
  453.4 1.5 all-to-all-done.4
  456.3 1.5 collective-permute-start.39
  458.1 1.8 convolution_convert_fusion
  (226 shorter events, 47.1 us)
Async XLA Ops:
  7.2 8.3 %copy-start = (bf16[512,1024]{1,0:T(8,128)(2,1)S(1)}, bf16[512,1024]{1,0:T(8,128)(2,1)}, u32[]{:S(2)}) copy-start(bf16[512,1024]{1,0:T(8,128)(2,1)} %param.10) | copy-start | bytes 3145732
  9.2 38.4 %collective-permute-start.8 = (bf16[4,128,256]{2,1,0:T(8,128)(2,1)S(1)}, bf16[4,128,256]{2,1,0:T(8,128)(2,1)S(1)}, u32[]{:S(2)}, u32[]{:S(2)}) collective-permute-start(bf16[4,128,256]{2,1,0:T(8,128)(2,1)S(1)} %pad_maximum_fusion.4), channel_id=1, source_target_pairs={{0,16},{4,20},{8,24},{12,28},{16,0},{20,4},{24,8},{28,12},{1,17},{... | collective-permute-start | bytes 786440 | tf_op jit(solution)/shard_map/ppermute | solution.py:56
  14.0 16.5 %collective-permute-start = (f32[2,32]{1,0:T(2,128)S(1)}, f32[2,32]{1,0:T(2,128)S(1)}, u32[]{:S(2)}, u32[]{:S(2)}) collective-permute-start(f32[2,32]{1,0:T(2,128)S(1)} %pad_maximum_fusion.8), channel_id=1, source_target_pairs={{0,16},{4,20},{8,24},{12,28},{16,0},{20,4},{24,8},{28,12},{1,17},{... | collective-permute-start | bytes 776 | tf_op jit(solution)/shard_map/ppermute | solution.py:56
  17.2 8.2 %copy-start.43 = (s32[16]{0:T(128)S(1)}, s32[16]{0:T(128)}, u32[]{:S(2)}) copy-start(s32[16]{0:T(128)} %param.12) | copy-start | bytes 196
  17.2 44.0 %all-to-all-start = ((bf16[8,64,1024]{2,1,0:T(8,128)(2,1)}), bf16[8,64,1024]{2,1,0:T(8,128)(2,1)}, u32[]{:S(2)}, u32[]{:S(2)}) async-start(bf16[8,64,1024]{2,1,0:T(8,128)(2,1)} %bitcast.1), calls=%async_computation | async-start | bytes 2097152 | tf_op jit(solution)/shard_map/all_to_all | solution.py:752
  23.5 156.1 %all-gather.2.cloned.1.call-start = ((), (), s32[]{:S(2)}) async-start(), calls=%async_computation.6 | async-start | bytes 5308416 | tf_op jit(solution)/shard_map/all_gather | solution.py:787
  23.7 23.9 %copy-start.28 = (bf16[3,128,256]{2,1,0:T(8,128)(2,1)S(1)}, bf16[3,128,256]{2,1,0:T(8,128)(2,1)}, u32[]{:S(2)}) copy-start(bf16[3,128,256]{2,1,0:T(8,128)(2,1)} %param.16) | copy-start | bytes 589828
  30.4 80.5 %copy-start.3 = (f32[2048,128]{1,0:T(8,128)}, f32[2048,128]{1,0:T(8,128)S(1)}, u32[]{:S(2)}) copy-start(f32[2048,128]{1,0:T(8,128)S(1)} %get-tuple-element.104.cos_ref) | copy-start | bytes 3145732
  30.5 9.6 %collective-permute-start.1 = (f32[2,2,32]{2,1,0:T(2,128)S(1)}, f32[2,2,32]{2,1,0:T(2,128)S(1)}, u32[]{:S(2)}, u32[]{:S(2)}) collective-permute-start(f32[2,2,32]{2,1,0:T(2,128)S(1)} %pad_maximum_fusion.7), channel_id=1, source_target_pairs={{0,8},{4,12},{8,0},{12,4},{16,24},{20,28},{24,16},{28,20},{1,9},{5... | collective-permute-start | bytes 1544 | tf_op jit(solution)/shard_map/ppermute | solution.py:56
  40.2 3.7 collective-permute-start.2
  43.9 3.7 collective-permute-start.3
  45.4 103.8 %copy-start.36 = (s32[512]{0:T(512)}, s32[512]{0:T(512)S(1)}, u32[]{:S(2)}) copy-start(s32[512]{0:T(512)S(1)} %multiply_add_fusion) | copy-start | bytes 6148
  48.5 11.7 %collective-permute-start.9 = (bf16[2,4,128,256]{3,2,1,0:T(8,128)(2,1)}, bf16[2,4,128,256]{3,2,1,0:T(8,128)(2,1)S(1)}, u32[]{:S(2)}, u32[]{:S(2)}) collective-permute-start(bf16[2,4,128,256]{3,2,1,0:T(8,128)(2,1)} %pad_maximum_fusion.3), channel_id=1, source_target_pairs={{0,8},{4,12},{8,0},{12,4},{16,24},{20,28},{24,16},{28,20},{1,9},{5... | collective-permute-start | bytes 1572872 | tf_op jit(solution)/shard_map/ppermute | solution.py:56
  51.0 1.2 collective-permute-start.4
  52.4 50.8 %copy-start.33 = (f32[2,1024]{1,0:T(2,128)}, f32[2,1024]{1,0:T(2,128)S(1)}, u32[]{:S(2)}) copy-start(f32[2,1024]{1,0:T(2,128)S(1)} %reshape.193) | copy-start | bytes 24580
  63.3 39.8 %copy-start.8 = (bf16[512,1024]{1,0:T(8,128)(2,1)}, bf16[512,1024]{1,0:T(8,128)(2,1)S(1)}, u32[]{:S(2)}) copy-start(bf16[512,1024]{1,0:T(8,128)(2,1)S(1)} %convolution_convert_fusion.4.xa_ref.xk_ref.x_ref) | copy-start | bytes 3145732
  63.3 21.5 %collective-permute-start.6 = (bf16[512,1024]{1,0:T(8,128)(2,1)S(1)}, bf16[512,1024]{1,0:T(8,128)(2,1)}, u32[]{:S(2)}, u32[]{:S(2)}) collective-permute-start(bf16[512,1024]{1,0:T(8,128)(2,1)S(1)} %convolution_convert_fusion.4.xa_ref.xk_ref.x_ref), channel_id=1, source_target_pairs={{0,2},{1,3},{2,0},{3,1},{4,6},{5,7},{6,4},{7,5},{8,10},{9,11},{10,... | collective-permute-start | bytes 3145736 | tf_op jit(solution)/shard_map/ppermute | solution.py:56
  66.0 27.7 %collective-permute-start.10 = (bf16[2,2,4,128,256]{4,3,2,0,1:T(8,128)(2,1)}, bf16[2,2,4,128,256]{4,3,2,0,1:T(8,128)(2,1)}, u32[]{:S(2)}, u32[]{:S(2)}) collective-permute-start(bf16[2,2,4,128,256]{4,3,2,0,1:T(8,128)(2,1)} %pad_maximum_fusion.1), channel_id=1, source_target_pairs={{0,4},{4,0},{8,12},{12,8},{16,20},{20,16},{24,28},{28,24},{1,5},{5... | collective-permute-start | bytes 3145736 | tf_op jit(solution)/shard_map/ppermute | solution.py:56
  70.1 33.1 %collective-permute-start.5 = (bf16[512,1024]{1,0:T(8,128)(2,1)S(1)}, bf16[512,1024]{1,0:T(8,128)(2,1)}, u32[]{:S(2)}, u32[]{:S(2)}) collective-permute-start(bf16[512,1024]{1,0:T(8,128)(2,1)S(1)} %convolution_convert_fusion.4.xa_ref.xk_ref.x_ref), channel_id=1, source_target_pairs={{0,1},{1,0},{2,3},{3,2},{4,5},{5,4},{6,7},{7,6},{8,9},{9,8},{10,11... | collective-permute-start | bytes 3145736 | tf_op jit(solution)/shard_map/ppermute | solution.py:56
  84.8 26.1 %collective-permute-start.7 = (bf16[512,1024]{1,0:T(8,128)(2,1)}, bf16[512,1024]{1,0:T(8,128)(2,1)}, u32[]{:S(2)}, u32[]{:S(2)}) collective-permute-start(bf16[512,1024]{1,0:T(8,128)(2,1)} %collective-permute-done.6.xa_ref.xk_ref), channel_id=1, source_target_pairs={{0,1},{1,0},{2,3},{3,2},{4,5},{5,4},{6,7},{7,6},{8,9},{9,8},{10,11... | collective-permute-start | bytes 3145736 | tf_op jit(solution)/shard_map/ppermute | solution.py:56
  97.8 21.2 %collective-permute-start.11 = (bf16[1024,256]{1,0:T(8,128)(2,1)}, bf16[1024,256]{1,0:T(8,128)(2,1)}, u32[]{:S(2)}, u32[]{:S(2)}) collective-permute-start(bf16[1024,256]{1,0:T(8,128)(2,1)} %bitcast.40), channel_id=1, source_target_pairs={{0,2},{1,3},{2,0},{3,1},{4,6},{5,7},{6,4},{7,5},{8,10},{9,11},{10,... | collective-permute-start | bytes 1572872 | tf_op jit(solution)/shard_map/ppermute | solution.py:56
  98.4 50.8 %all-to-all-start.1 = ((bf16[8,64,1024]{2,1,0:T(8,128)(2,1)}), bf16[8,64,1024]{2,1,0:T(8,128)(2,1)}, u32[]{:S(2)}, u32[]{:S(2)}) async-start(bf16[8,64,1024]{2,1,0:T(8,128)(2,1)} %bitcast.140), calls=%async_computation.1 | async-start | bytes 2097152 | tf_op jit(solution)/shard_map/all_to_all | solution.py:752
  137.6 36.0 %collective-permute-start.13 = (bf16[1024,256]{1,0:T(8,128)(2,1)}, bf16[1024,256]{1,0:T(8,128)(2,1)}, u32[]{:S(2)}, u32[]{:S(2)}) collective-permute-start(bf16[1024,256]{1,0:T(8,128)(2,1)} %get-tuple-element.129.o0.o_ref), channel_id=1, source_target_pairs={{0,2},{1,3},{2,0},{3,1},{4,6},{5,7},{6,4},{7,5},{8,10},{9,11},{10,... | collective-permute-start | bytes 1572872 | tf_op jit(solution)/shard_map/ppermute | solution.py:56
  151.3 20.9 %copy-start.17 = (bf16[512,1024]{1,0:T(8,128)(2,1)}, bf16[512,1024]{1,0:T(8,128)(2,1)S(1)}, u32[]{:S(2)}) copy-start(bf16[512,1024]{1,0:T(8,128)(2,1)S(1)} %convolution_convert_fusion.3.gk_ref.g_ref) | copy-start | bytes 3145732
  151.3 22.3 %collective-permute-start.14 = (bf16[512,1024]{1,0:T(8,128)(2,1)S(1)}, bf16[512,1024]{1,0:T(8,128)(2,1)}, u32[]{:S(2)}, u32[]{:S(2)}) collective-permute-start(bf16[512,1024]{1,0:T(8,128)(2,1)S(1)} %convolution_convert_fusion.3.gk_ref.g_ref), channel_id=1, source_target_pairs={{0,2},{1,3},{2,0},{3,1},{4,6},{5,7},{6,4},{7,5},{8,10},{9,11},{10,... | collective-permute-start | bytes 3145736 | tf_op jit(solution)/shard_map/ppermute | solution.py:56
  154.9 18.8 %copy-start.2 = (bf16[4,8,128,256]{3,2,1,0:T(8,128)(2,1)S(1)}, bf16[4,8,128,256]{3,2,1,0:T(8,128)(2,1)}, u32[]{:S(2)}) copy-start(bf16[4,8,128,256]{3,2,1,0:T(8,128)(2,1)} %copy.80) | copy-start | bytes 6291460
  173.6 6.0 %collective-permute-start.15 = (bf16[512,1024]{1,0:T(8,128)(2,1)}, bf16[512,1024]{1,0:T(8,128)(2,1)}, u32[]{:S(2)}, u32[]{:S(2)}) collective-permute-start(bf16[512,1024]{1,0:T(8,128)(2,1)} %collective-permute-done.14.gk_ref), channel_id=1, source_target_pairs={{0,1},{1,0},{2,3},{3,2},{4,5},{5,4},{6,7},{7,6},{8,9},{9,8},{10,11... | collective-permute-start | bytes 3145736 | tf_op jit(solution)/shard_map/ppermute | solution.py:56
  174.4 2.9 collective-permute-start.18
  174.9 3.2 collective-permute-start.19
  174.9 3.9 collective-permute-start.16
  175.4 4.2 collective-permute-start.17
  177.4 26.2 %collective-permute-start.21 = (f32[4]{0:T(128)S(1)}, f32[4]{0:T(128)S(1)}, u32[]{:S(2)}, u32[]{:S(2)}) collective-permute-start(f32[4]{0:T(128)S(1)} %maximum_multiply_fusion), channel_id=1, source_target_pairs={{0,4},{4,0},{8,12},{12,8},{16,20},{20,16},{24,28},{28,24},{1,5},{5... | collective-permute-start | bytes 56 | tf_op jit(solution)/shard_map/ppermute | solution.py:56
  178.1 25.5 %collective-permute-start.20 = (bf16[1024,256]{1,0:T(8,128)(2,1)}, bf16[1024,256]{1,0:T(8,128)(2,1)}, u32[]{:S(2)}, u32[]{:S(2)}) collective-permute-start(bf16[1024,256]{1,0:T(8,128)(2,1)} %get-tuple-element.120.o0.o_ref.o1), channel_id=1, source_target_pairs={{0,2},{1,3},{2,0},{3,1},{4,6},{5,7},{6,4},{7,5},{8,10},{9,11},{10,... | collective-permute-start | bytes 1572872 | tf_op jit(solution)/shard_map/ppermute | solution.py:56
  179.6 24.2 %copy-start.18 = (bf16[512,1024]{1,0:T(8,128)(2,1)S(1)}, bf16[512,1024]{1,0:T(8,128)(2,1)}, u32[]{:S(2)}) copy-start(bf16[512,1024]{1,0:T(8,128)(2,1)} %copy-done.17) | copy-start | bytes 3145732
  203.6 2.7 collective-permute-start.22
  203.8 5.5 %collective-permute-start.12 = (bf16[512,1024]{1,0:T(8,128)(2,1)S(1)}, bf16[512,1024]{1,0:T(8,128)(2,1)S(1)}, u32[]{:S(2)}, u32[]{:S(2)}) collective-permute-start(bf16[512,1024]{1,0:T(8,128)(2,1)S(1)} %copy-done.18), channel_id=1, source_target_pairs={{0,1},{1,0},{2,3},{3,2},{4,5},{5,4},{6,7},{7,6},{8,9},{9,8},{10,11... | collective-permute-start | bytes 3145736 | tf_op jit(solution)/shard_map/ppermute | solution.py:56
  204.2 5.2 %collective-permute-start.23 = (bf16[1024,256]{1,0:T(8,128)(2,1)}, bf16[1024,256]{1,0:T(8,128)(2,1)S(1)}, u32[]{:S(2)}, u32[]{:S(2)}) collective-permute-start(bf16[1024,256]{1,0:T(8,128)(2,1)} %get-tuple-element.129.o0.o_ref), channel_id=1, source_target_pairs={{0,1},{1,0},{2,3},{3,2},{4,5},{5,4},{6,7},{7,6},{8,9},{9,8},{10,11... | collective-permute-start | bytes 1572872 | tf_op jit(solution)/shard_map/ppermute | solution.py:56
  204.3 5.2 %collective-permute-start.24 = (bf16[1024,256]{1,0:T(8,128)(2,1)}, bf16[1024,256]{1,0:T(8,128)(2,1)S(1)}, u32[]{:S(2)}, u32[]{:S(2)}) collective-permute-start(bf16[1024,256]{1,0:T(8,128)(2,1)} %collective-permute-done.20.o2), channel_id=1, source_target_pairs={{0,1},{1,0},{2,3},{3,2},{4,5},{5,4},{6,7},{7,6},{8,9},{9,8},{10,11... | collective-permute-start | bytes 1572872 | tf_op jit(solution)/shard_map/ppermute | solution.py:56
  204.7 29.2 %collective-permute-start.26 = (f32[4]{0:T(128)S(1)}, f32[4]{0:T(128)S(1)}, u32[]{:S(2)}, u32[]{:S(2)}) collective-permute-start(f32[4]{0:T(128)S(1)} %max.15), channel_id=1, source_target_pairs={{0,8},{4,12},{8,0},{12,4},{16,24},{20,28},{24,16},{28,20},{1,9},{5... | collective-permute-start | bytes 56 | tf_op jit(solution)/shard_map/ppermute | solution.py:56
  208.3 25.6 %collective-permute-start.25 = (bf16[512,1024]{1,0:T(8,128)(2,1)S(1)}, bf16[512,1024]{1,0:T(8,128)(2,1)S(1)}, u32[]{:S(2)}, u32[]{:S(2)}) collective-permute-start(bf16[512,1024]{1,0:T(8,128)(2,1)S(1)} %add_convert_fusion.2), channel_id=1, source_target_pairs={{0,2},{1,3},{2,0},{3,1},{4,6},{5,7},{6,4},{7,5},{8,10},{9,11},{10,... | collective-permute-start | bytes 3145736 | tf_op jit(solution)/shard_map/ppermute | solution.py:56
  210.3 27.2 %copy-start.9 = (bf16[512,1024]{1,0:T(8,128)(2,1)S(1)}, bf16[512,1024]{1,0:T(8,128)(2,1)}, u32[]{:S(2)}) copy-start(bf16[512,1024]{1,0:T(8,128)(2,1)} %copy-done.8) | copy-start | bytes 3145732
  210.3 27.2 %copy-start.19 = (bf16[512,1024]{1,0:T(8,128)(2,1)S(1)}, bf16[512,1024]{1,0:T(8,128)(2,1)}, u32[]{:S(2)}) copy-start(bf16[512,1024]{1,0:T(8,128)(2,1)} %copy-done.17) | copy-start | bytes 3145732
  233.9 3.6 collective-permute-start.27
  234.1 26.6 %collective-permute-start.28 = (f32[4]{0:T(128)S(1)}, f32[4]{0:T(128)S(1)}, u32[]{:S(2)}, u32[]{:S(2)}) collective-permute-start(f32[4]{0:T(128)S(1)} %max.16), channel_id=1, source_target_pairs={{0,16},{4,20},{8,24},{12,28},{16,0},{20,4},{24,8},{28,12},{1,17},{... | collective-permute-start | bytes 56 | tf_op jit(solution)/shard_map/ppermute | solution.py:56
  241.9 25.3 %collective-permute-start.30 = (bf16[512,1024]{1,0:T(8,128)(2,1)}, bf16[512,1024]{1,0:T(8,128)(2,1)}, u32[]{:S(2)}, u32[]{:S(2)}) collective-permute-start(bf16[512,1024]{1,0:T(8,128)(2,1)} %get-tuple-element.147.even_ref), channel_id=1, source_target_pairs={{0,1},{1,0},{2,3},{3,2},{4,5},{5,4},{6,7},{7,6},{8,9},{9,8},{10,11... | collective-permute-start | bytes 3145736 | tf_op jit(solution)/shard_map/ppermute | solution.py:56
  242.1 30.9 %collective-permute-start.29 = (bf16[512,1024]{1,0:T(8,128)(2,1)}, bf16[512,1024]{1,0:T(8,128)(2,1)}, u32[]{:S(2)}, u32[]{:S(2)}) collective-permute-start(bf16[512,1024]{1,0:T(8,128)(2,1)} %get-tuple-element.147.even_ref), channel_id=1, source_target_pairs={{0,2},{1,3},{2,0},{3,1},{4,6},{5,7},{6,4},{7,5},{8,10},{9,11},{10,... | collective-permute-start | bytes 3145736 | tf_op jit(solution)/shard_map/ppermute | solution.py:56
  260.8 96.3 %all-to-all-start.2 = ((bf16[8,3,656,128]{3,2,1,0:T(8,128)(2,1)}), bf16[8,3,656,128]{3,2,1,0:T(8,128)(2,1)}, u32[]{:S(2)}, u32[]{:S(2)}) async-start(bf16[8,3,656,128]{3,2,1,0:T(8,128)(2,1)} %inner_grads.1), calls=%async_computation.2 | async-start | bytes 8060928 | tf_op jit(solution)/shard_map/all_to_all | solution.py:871
  267.1 186.3 %reduce-scatter.2.cloned.1.call-start = ((), (), s32[]{:S(2)}) async-start(), calls=%async_computation.7 | async-start | bytes 2359296 | tf_op jit(solution)/shard_map/reduce_scatter | solution.py:915
  267.1 6.4 %collective-permute-start.33 = (bf16[512,1024]{1,0:T(8,128)(2,1)}, bf16[512,1024]{1,0:T(8,128)(2,1)S(1)}, u32[]{:S(2)}, u32[]{:S(2)}) collective-permute-start(bf16[512,1024]{1,0:T(8,128)(2,1)} %get-tuple-element.164), channel_id=1, source_target_pairs={{0,1},{1,0},{2,3},{3,2},{4,5},{5,4},{6,7},{7,6},{8,9},{9,8},{10,11... | collective-permute-start | bytes 3145736 | tf_op jit(solution)/shard_map/ppermute | solution.py:56
  272.9 3.5 collective-permute-start.31
  273.5 5.4 %collective-permute-start.32 = (bf16[512,1024]{1,0:T(8,128)(2,1)}, bf16[512,1024]{1,0:T(8,128)(2,1)S(1)}, u32[]{:S(2)}, u32[]{:S(2)}) collective-permute-start(bf16[512,1024]{1,0:T(8,128)(2,1)} %collective-permute-done.29.even_ref), channel_id=1, source_target_pairs={{0,1},{1,0},{2,3},{3,2},{4,5},{5,4},{6,7},{7,6},{8,9},{9,8},{10,11... | collective-permute-start | bytes 3145736 | tf_op jit(solution)/shard_map/ppermute | solution.py:56
  277.9 63.0 %collective-permute-start.34 = (bf16[512,1024]{1,0:T(8,128)(2,1)}, bf16[512,1024]{1,0:T(8,128)(2,1)}, u32[]{:S(2)}, u32[]{:S(2)}) collective-permute-start(bf16[512,1024]{1,0:T(8,128)(2,1)} %add_convert_fusion.1), channel_id=1, source_target_pairs={{0,2},{1,3},{2,0},{3,1},{4,6},{5,7},{6,4},{7,5},{8,10},{9,11},{10,... | collective-permute-start | bytes 3145736 | tf_op jit(solution)/shard_map/ppermute | solution.py:56
  344.6 3.0 collective-permute-start.35
  347.4 9.7 %copy-start.37 = (s32[512]{0:T(512)S(1)}, s32[512]{0:T(512)}, u32[]{:S(2)}) copy-start(s32[512]{0:T(512)} %copy-done.36) | copy-start | bytes 6148
  361.5 9.3 %copy-start.29 = (bf16[3,128,256]{2,1,0:T(8,128)(2,1)S(1)}, bf16[3,128,256]{2,1,0:T(8,128)(2,1)}, u32[]{:S(2)}) copy-start(bf16[3,128,256]{2,1,0:T(8,128)(2,1)} %param.16) | copy-start | bytes 589828
  361.5 47.9 %all-to-all-start.3 = ((bf16[8,64,1024]{2,1,0:T(8,128)(2,1)}), bf16[8,64,1024]{2,1,0:T(8,128)(2,1)}, u32[]{:S(2)}, u32[]{:S(2)}) async-start(bf16[8,64,1024]{2,1,0:T(8,128)(2,1)} %bitcast.142), calls=%async_computation.3 | async-start | bytes 2097152 | tf_op jit(solution)/shard_map/all_to_all | solution.py:752
  371.9 25.3 %collective-permute-start.36 = (bf16[512,1024]{1,0:T(8,128)(2,1)}, bf16[512,1024]{1,0:T(8,128)(2,1)S(1)}, u32[]{:S(2)}, u32[]{:S(2)}) collective-permute-start(bf16[512,1024]{1,0:T(8,128)(2,1)} %add_convert_fusion), channel_id=1, source_target_pairs={{0,2},{1,3},{2,0},{3,1},{4,6},{5,7},{6,4},{7,5},{8,10},{9,11},{10,... | collective-permute-start | bytes 3145736 | tf_op jit(solution)/shard_map/ppermute | solution.py:56
  375.7 22.5 %collective-permute-start.37 = (bf16[512,1024]{1,0:T(8,128)(2,1)S(1)}, bf16[512,1024]{1,0:T(8,128)(2,1)S(1)}, u32[]{:S(2)}, u32[]{:S(2)}) collective-permute-start(bf16[512,1024]{1,0:T(8,128)(2,1)S(1)} %dn.7), channel_id=1, source_target_pairs={{0,1},{1,0},{2,3},{3,2},{4,5},{5,4},{6,7},{7,6},{8,9},{9,8},{10,11... | collective-permute-start | bytes 3145736 | tf_op jit(solution)/shard_map/ppermute | solution.py:56
  381.5 27.9 %copy-start.10 = (bf16[512,1024]{1,0:T(8,128)(2,1)S(1)}, bf16[512,1024]{1,0:T(8,128)(2,1)}, u32[]{:S(2)}) copy-start(bf16[512,1024]{1,0:T(8,128)(2,1)} %copy-done.8) | copy-start | bytes 3145732
  381.6 27.8 %copy-start.16 = (f32[1,1024]{1,0:T(1,128)S(1)}, f32[1,1024]{1,0:T(1,128)}, u32[]{:S(2)}) copy-start(f32[1,1024]{1,0:T(1,128)} %copy-done.15) | copy-start | bytes 12292
  416.7 38.2 %all-to-all-start.4 = ((bf16[8,64,1024]{2,1,0:T(8,128)(2,1)}), bf16[8,64,1024]{2,1,0:T(8,128)(2,1)S(1)}, u32[]{:S(2)}, u32[]{:S(2)}) async-start(bf16[8,64,1024]{2,1,0:T(8,128)(2,1)} %bitcast.56), calls=%async_computation.4 | async-start | bytes 2097152 | tf_op jit(solution)/shard_map/all_to_all | solution.py:752
  456.2 5.3 %collective-permute-start.38 = (f32[2,32]{1,0:T(2,128)S(1)}, f32[2,32]{1,0:T(2,128)S(1)}, u32[]{:S(2)}, u32[]{:S(2)}) collective-permute-start(f32[2,32]{1,0:T(2,128)S(1)} %bitcast.164), channel_id=1, source_target_pairs={{0,1},{1,0},{2,3},{3,2},{4,5},{5,4},{6,7},{7,6},{8,9},{9,8},{10,11... | collective-permute-start | bytes 776 | tf_op jit(solution)/shard_map/ppermute | solution.py:56
  456.3 5.2 %collective-permute-start.39 = (f32[2,32]{1,0:T(2,128)S(1)}, f32[2,32]{1,0:T(2,128)S(1)}, u32[]{:S(2)}, u32[]{:S(2)}) collective-permute-start(f32[2,32]{1,0:T(2,128)S(1)} %bitcast.163), channel_id=1, source_target_pairs={{0,2},{1,3},{2,0},{3,1},{4,6},{5,7},{6,4},{7,5},{8,10},{9,11},{10,... | collective-permute-start | bytes 776 | tf_op jit(solution)/shard_map/ppermute | solution.py:56
  457.8 3.7 collective-permute-start.40
  (28 other events, 111.4 us)
Sparse Core Ops, SparseCore 0:
  72.0 92.4 all-gather.1
  347.5 105.8 reduce-scatter.1

commit v5 on v4

--- a/solution.py
+++ b/solution.py
@@ -134,7 +134,7 @@
             out_specs=[head_spec] * 3 + [pl.BlockSpec((step, width), place)],
         ),
         input_output_aliases={7 + i: i for i in range(len(held))},
-        compiler_params=vmem(48),
+        compiler_params=vmem(52),
         cost_estimate=takes(3),
         name="qkv",
     )(scalars, xa, xb, gain, w_qkv, cos, sin, *held)
@@ -241,7 +241,7 @@
                 pltpu.VMEM((heads, q_rows, LANES), F32),
             ],
         ),
-        compiler_params=vmem(48),
+        compiler_params=vmem(52),
         cost_estimate=takes(20),
         input_output_aliases={4 + i: 1 + i for i in range(len(held))},
         name="attend_forward",
@@ -330,7 +330,7 @@
                 pltpu.VMEM((heads, tokens, LANES), F32),
             ],
         ),
-        compiler_params=vmem(48),
+        compiler_params=vmem(52),
         cost_estimate=takes(20),
         name="attend_backward",
     )(scalars, q2, k, v, do, cos, sin)
@@ -423,7 +423,7 @@
             out_specs=[wide, wide, wide, narrow, narrow, narrow, keep, send, keep, send],
         ),
         input_output_aliases={15 + i: i for i in range(len(held))},
-        compiler_params=vmem(48),
+        compiler_params=vmem(52),
         cost_estimate=takes(24),
         name="mlp",
     )(scalars, *x_pair, *g_pair, *heads_rel, *w_out_rel, gain, w_mlp, *held)
@@ -464,7 +464,7 @@
             resident(gain.shape),
         ],
         out_specs=[flat, flat],
-        compiler_params=vmem(48),
+        compiler_params=vmem(52),
         cost_estimate=takes(5),
         name="resid",
     )(keep, core, chip, x, a_rel, g, gain)
@@ -519,7 +519,7 @@
             ],
         ),
         input_output_aliases={5 + i: i for i in range(len(held))},
-        compiler_params=vmem(48),
+        compiler_params=vmem(52),
         cost_estimate=takes(6),
         name="head_grad",
     )(scalars, even, odd, w_out, o_chunk, *held)
@@ -562,7 +562,7 @@
         in_specs=[wide, wide, narrow, narrow, narrow],
         out_specs=resident(out),
         scratch_shapes=[pltpu.VMEM((3, units, width), F32)],
-        compiler_params=vmem(48),
+        compiler_params=vmem(52),
         cost_estimate=takes(18),
         name="inner_grads",
     )(n2, g_rel, dgate, dup, act)
@@ -604,7 +604,7 @@
         ],
         out_specs=resident(out),
         scratch_shapes=[pltpu.VMEM((kinds + 1, cols, width), F32)],
-        compiler_params=vmem(48),
+        compiler_params=vmem(52),
         cost_estimate=takes(10),
         name="proj_grads",
     )(n1, dproj, *o_chunks, da)
@@ -630,7 +630,7 @@
             ],
             out_specs=pl.BlockSpec((rows, width), lambda i, s: (0, 0)),
         ),
-        compiler_params=vmem(48),
+        compiler_params=vmem(52),
         cost_estimate=takes(0),
         name="dn",
     )(scalars, dproj, w_qkv)
@@ -653,7 +653,7 @@
         grid=(per,),
         in_specs=[flat] * 5 + [resident(gain.shape)],
         out_specs=flat,
-        compiler_params=vmem(48),
+        compiler_params=vmem(52),
         cost_estimate=takes(0),
         name="last",
     )(keep, core, chip, x, dx, gain)
@@ -667,7 +667,7 @@
     return pl.pallas_call(
         turn_rows_kernel,
         out_shape=jax.ShapeDtypeStruct(values.shape, BF16),
-        compiler_params=vmem(48),
+        compiler_params=vmem(52),
         cost_estimate=takes(0),
         name="turn_rows",
     )(one_hot, values)

time: 476 us -> 473 us (level)
  Pallas kernels: 202 us -> 221 us
  local copies, waits for them, and re-layouts: 28.4 us -> 18.1 us
  starting transfers between devices: 62.8 us -> 57.2 us
    pallas_call x1, Pallas kernels: 45.8 us -> 56.1 us  [attend_backward(): pl.pallas_call(functools.partial(bwd_kernel, q_rows, k_rows), out_shape=j...]
    unnamed x96 -> x80, local copies, waits for them, and re-layouts: 19.7 us -> 9.99 us
    all_to_all x1, waiting for transfers between devices: 6.92 us -> 0.01 us  [local(): lax.all_to_all(inner_grads, 'dp', split_axis=0, concat_axis=0, tiled=True)]
    pallas_call x2, Pallas kernels: 33 us -> 39.3 us  [attend_forward(): pl.pallas_call(functools.partial(fwd_kernel, far, q_rows, k_rows), out_sh...]
  transfers between devices with their start and end apart: 48 -> 48, of which waited for: 22 -> 18; matrix products, arithmetic and copies ran while one was open for 11% -> 11% of each run, Pallas kernels for 43% -> 47%
where the time goes in v5:
time: 473 us; the launch traced here: 467 us
  Pallas kernels  221 us (47%)
  waiting for transfers between devices  114 us (24%)
  starting transfers between devices  57.2 us (12%)
  other arithmetic  25.6 us (5%)
  local copies, waits for them, and re-layouts  18.1 us (4%)
  matrix products  15.4 us (3%)
  between operations  15.2 us (3%)
    ppermute x41, waiting for transfers between devices, swap_bit(): return lax.ppermute(values, axis_name, [(i, i ^ bit) for i in range(count)])  62.8 us
    pallas_call x1, Pallas kernels, attend_backward(): pl.pallas_call(functools.partial(bwd_kernel, q_rows, k_rows), out_shape=j...  56.1 us
    pallas_call x2, Pallas kernels, mlp_call(): pl.pallas_call(mlp_kernel, out_shape=(wide_out, wide_out, wide_out, narro...  47.9 us
    pallas_call x2, Pallas kernels, attend_forward(): pl.pallas_call(functools.partial(fwd_kernel, far, q_rows, k_rows), out_sh...  39.3 us
    ppermute x41, starting transfers between devices, swap_bit(): return lax.ppermute(values, axis_name, [(i, i ^ bit) for i in range(count)])  31.8 us
    reduce_scatter x1, waiting for transfers between devices, local(): grads = lax.psum_scatter(by_device(proj_grad, dp_count), 'dp')  30.8 us
    all_to_all x4, waiting for transfers between devices, exchange(): lax.all_to_all(packed, 'dp', split_axis=0, concat_axis=0, tiled=True)  20.7 us
    all_to_all x4, starting transfers between devices, exchange(): lax.all_to_all(packed, 'dp', split_axis=0, concat_axis=0, tiled=True)  20.6 us
  transfers between devices with their start and end apart: 48, of which 18 were waited for; matrix products, arithmetic and copies ran while one was open for 11% of the time, Pallas kernels for 47%

profile of v5, /device:TPU:0, one launch (start us, length us, event | category | flops | bytes accessed | tf_op | source)
XLA Modules:
  0.0 467.2 jit_solution(5216367510614714461)
XLA Ops:
  9.2 4.1 collective-permute-start.8
  15.5 1.7 convolution_convert_fusion.6
  17.2 6.3 %all-to-all-start = ((bf16[8,64,1024]{2,1,0:T(8,128)(2,1)}), bf16[8,64,1024]{2,1,0:T(8,128)(2,1)}, u32[]{:S(2)}, u32[]{:S(2)}) async-start(bf16[8,64,1024]{2,1,0:T(8,128)(2,1)} %bitcast.1), calls=%async_computation | async-start | bytes 2097152 | tf_op jit(solution)/shard_map/all_to_all | solution.py:752
  23.7 1.7 convolution_convert_fusion.5
  26.7 5.6 %fusion.6 = (f32[2048,128]{1,0:T(8,128)}, f32[2048,128]{1,0:T(8,128)}) fusion(f32[128]{0:T(128)S(1)} %get-tuple-element.253, f32[128]{0:T(128)S(1)} %get-tuple-element.254, f32[2048]{0:T(1024)S(1)} %select_convert_fusion), kind=kLoop, calls=%fused_computation.24 | loop fusion | flops 524288 | bytes 2106368 | tf_op jit(solution)/shard_map/mul | solution.py:780
  32.4 2.0 collective-permute-start.1
  34.4 5.8 %collective-permute-done.1 = f32[2,2,32]{2,1,0:T(2,128)S(1)} collective-permute-done((f32[2,2,32]{2,1,0:T(2,128)S(1)}, f32[2,2,32]{2,1,0:T(2,128)S(1)}, u32[]{:S(2)}, u32[]{:S(2)}) %collective-permute-start.1) | collective-permute-done | bytes 544 | tf_op jit(solution)/shard_map/ppermute | solution.py:56
  40.2 1.9 collective-permute-start.2
  42.3 1.6 collective-permute-done.2
  43.9 1.6 collective-permute-start.3
  45.5 2.1 collective-permute-done.3
  47.7 2.6 collective-permute-start.9
  51.6 8.5 %collective-permute-done.9 = bf16[2,4,128,256]{3,2,1,0:T(8,128)(2,1)S(1)} collective-permute-done((bf16[2,4,128,256]{3,2,1,0:T(8,128)(2,1)S(1)}, bf16[2,4,128,256]{3,2,1,0:T(8,128)(2,1)S(1)}, u32[]{:S(2)}, u32[]{:S(2)}) %collective-permute-start.9) | collective-permute-done | bytes 524320 | tf_op jit(solution)/shard_map/ppermute | solution.py:56
  60.2 2.0 convolution_convert_fusion.4.xa_ref.xk_ref.x_ref
  62.2 1.6 collective-permute-start.6
  64.8 1.2 collective-permute-start.10
  67.2 1.7 copy.81
  69.0 1.8 pad_maximum_fusion.2
  70.8 13.7 %collective-permute-done.6.xa_ref.xk_ref = bf16[512,1024]{1,0:T(8,128)(2,1)S(1)} collective-permute-done((bf16[512,1024]{1,0:T(8,128)(2,1)S(1)}, bf16[512,1024]{1,0:T(8,128)(2,1)S(1)}, u32[]{:S(2)}, u32[]{:S(2)}) %collective-permute-start.6) | collective-permute-done | bytes 1048608 | tf_op jit(solution)/shard_map/ppermute | solution.py:56
  84.5 8.9 %collective-permute-done.10 = bf16[2,2,4,128,256]{4,3,2,0,1:T(8,128)(2,1)} collective-permute-done((bf16[2,2,4,128,256]{4,3,2,0,1:T(8,128)(2,1)}, bf16[2,2,4,128,256]{4,3,2,0,1:T(8,128)(2,1)}, u32[]{:S(2)}, u32[]{:S(2)}) %collective-permute-start.10) | collective-permute-done | bytes 1048608 | tf_op jit(solution)/shard_map/ppermute | solution.py:56
  93.4 1.4 select_bitcast_fusion.1
  94.9 1.4 copy.80
  97.0 4.5 all-to-all-start.1
  101.6 7.9 %qkv.2 = (bf16[4,2048,128]{2,1,0:T(8,128)(2,1)}, bf16[4,2048,128]{2,1,0:T(8,128)(2,1)}, bf16[4,2048,128]{2,1,0:T(8,128)(2,1)}, bf16[2048,1024]{1,0:T(8,128)(2,1)}) custom-call(s32[4]{0:T(128)S(1)} %pad_add_fusion.s_ref, bf16[512,1024]{1,0:T(8,128)(2,1)S(1)} %convolution_convert_fusion.4.xa_ref.xk_ref.x_ref, ...), custom_call_target="tpu_custom_call" | custom-call | flops 3300000000 | bytes 3222656 | tf_op jit(solution)/shard_map/qkv/pallas_call | solution.py:119
  109.6 8.0 %qkv.3 = (bf16[4,2048,128]{2,1,0:T(8,128)(2,1)}, bf16[4,2048,128]{2,1,0:T(8,128)(2,1)}, bf16[4,2048,128]{2,1,0:T(8,128)(2,1)}, bf16[2048,1024]{1,0:T(8,128)(2,1)}) custom-call(s32[4]{0:T(128)S(1)} %pad_add_fusion.s_ref, ...), custom_call_target="tpu_custom_call", output_to_operand_aliasing={{0}: (7, {}), {1}: (8, {}), {2}: (9, {}), {3}: (10, {})} | custom-call | flops 3300000000 | bytes 3222656 | tf_op jit(solution)/shard_map/qkv/pallas_call | solution.py:119
  117.5 18.3 %attend_forward.2 = (bf16[1024,256]{1,0:T(8,128)(2,1)S(1)}, bf16[4,2048,128]{2,1,0:T(8,128)(2,1)}, f32[4,4,8,128]{3,2,1,0:T(8,128)S(1)}) custom-call(s32[4]{0:T(128)S(1)} %pad_add_fusion.s_ref, bf16[4,2048,128]{2,1,0:T(8,128)(2,1)} %get-tuple-element.111.q_ref, bf16[4,2048,128]{2,1,0:T(8,128)(2,1)} %get-tuple-element.112.k_ref, ...), custom_call_target="tpu_custom_call" | custom-call | flops 22000001024 | bytes 21484376 | tf_op jit(solution)/shard_map/attend_forward/pallas_call | solution.py:217
  135.8 4.2 collective-permute-start.13
  140.1 7.7 %all-to-all-done.1 = bf16[8,64,1024]{2,1,0:T(8,128)(2,1)} async-done(((bf16[8,64,1024]{2,1,0:T(8,128)(2,1)}), bf16[8,64,1024]{2,1,0:T(8,128)(2,1)}, u32[]{:S(2)}, u32[]{:S(2)}) %all-to-all-start.1) | async-done | bytes 1048608 | tf_op jit(solution)/shard_map/all_to_all | solution.py:752
  147.7 2.0 convolution_convert_fusion.3.gk_ref.g_ref
  149.7 1.6 collective-permute-start.14
  151.3 21.0 %attend_forward.3 = (bf16[1024,256]{1,0:T(8,128)(2,1)S(1)}, bf16[4,2048,128]{2,1,0:T(8,128)(2,1)}, f32[4,4,8,128]{3,2,1,0:T(8,128)S(1)}) custom-call(s32[4]{0:T(128)S(1)} %pad_add_fusion.s_ref, bf16[4,2048,128]{2,1,0:T(8,128)(2,1)} %get-tuple-element.111.q_ref, bf16[4,2048,128]{2,1,0:T(8,128)(2,1)} %get-tuple-element.112.k_ref, ...), custom_call_target="tpu_custom_call", output_to_operand_aliasing={{1}: (4, {})} | custom-call | flops 22000001024 | bytes 21484376 | tf_op jit(solution)/shard_map/attend_forward/pallas_call | solution.py:217
  176.2 1.4 collective-permute-done.19.w3
  178.2 24.3 %mlp.2 = (bf16[4,512,1024]{2,1,0:T(8,128)(2,1)}, bf16[4,512,1024]{2,1,0:T(8,128)(2,1)}, bf16[4,512,1024]{2,1,0:T(8,128)(2,1)}, bf16[4,512,656]{2,1,0:T(8,128)(2,...) custom-call(s32[4]{0:T(128)S(1)} %pad_add_fusion.s_ref, ...), custom_call_target="tpu_custom_call" | custom-call | flops 26400000000 | bytes 25781250 | tf_op jit(solution)/shard_map/mlp/pallas_call | solution.py:401
  203.6 1.8 collective-permute-done.22
  205.4 1.9 add_convert_fusion.2
  207.4 2.2 collective-permute-start.25
  210.7 23.7 %mlp.3 = (bf16[4,512,1024]{2,1,0:T(8,128)(2,1)}, bf16[4,512,1024]{2,1,0:T(8,128)(2,1)}, bf16[4,512,1024]{2,1,0:T(8,128)(2,1)}, bf16[4,512,656]{2,1,0:T(8,128)(2,...) custom-call(s32[4]{0:T(128)S(1)} %pad_add_fusion.s_ref, ...), custom_call_target="tpu_custom_call", output_to_operand_aliasing={{0}: (15, {}), {1}: (16, {}), {2}: (17, {}), {3}: (18, {}),... | custom-call | flops 26400000000 | bytes 25781250 | tf_op jit(solution)/shard_map/mlp/pallas_call | solution.py:401
  234.6 2.8 collective-permute-done.27.core_ref
  238.3 5.0 %resid.1 = (f32[512,1024]{1,0:T(8,128)}, bf16[512,1024]{1,0:T(8,128)(2,1)S(1)}) custom-call(f32[512,1024]{1,0:T(8,128)} %get-tuple-element.141.keep_ref, bf16[512,1024]{1,0:T(8,128)(2,1)} %copy-done.33, bf16[512,1024]{1,0:T(8,128)(2,1)} %copy-done.29, bf16[512,1024]{1,0:T(8,128)(2,1)} %copy-done.4, bf16[4,512,1024]{2,1,0:T(8,128)(2,1)} %get-tuple-element.146.a_ref, ...), custom_call_target="tpu_custom_call" | custom-call | flops 5500000256 | bytes 5371093 | tf_op jit(solution)/shard_map/resid/pallas_call | solution.py:450
  243.7 18.6 %inner_grads.1 = bf16[8,3,656,128]{3,2,1,0:T(8,128)(2,1)} custom-call(bf16[2048,1024]{1,0:T(8,128)(2,1)} %bitcast.166, bf16[2048,1024]{1,0:T(8,128)(2,1)} %bitcast.167, bf16[2048,656]{1,0:T(8,128)(2,1)} %bitcast.169, bf16[2048,656]{1,0:T(8,128)(2,1)} %bitcast.170, bf16[2048,656]{1,0:T(8,128)(2,1)} %bitcast.168), custom_call_target="tpu_custom_call" | custom-call | flops 19800000512 | bytes 19335936 | tf_op jit(solution)/shard_map/inner_grads/pallas_call | solution.py:558
  262.4 4.7 %all-to-all-start.2 = ((bf16[8,3,656,128]{3,2,1,0:T(8,128)(2,1)}), bf16[8,3,656,128]{3,2,1,0:T(8,128)(2,1)}, u32[]{:S(2)}, u32[]{:S(2)}) async-start(bf16[8,3,656,128]{3,2,1,0:T(8,128)(2,1)} %inner_grads.1), calls=%async_computation.2 | async-start | bytes 8060928 | tf_op jit(solution)/shard_map/all_to_all | solution.py:871
  267.3 5.6 %head_grad.2 = (bf16[4,2048,128]{2,1,0:T(8,128)(2,1)}, bf16[2048,1024]{1,0:T(8,128)(2,1)}) custom-call(s32[4]{0:T(128)S(1)} %pad_add_fusion.s_ref, bf16[512,1024]{1,0:T(8,128)(2,1)} %copy-done.11, bf16[512,1024]{1,0:T(8,128)(2,1)} %collective-permute-done.30.odd_ref, bf16[1024,256]{1,0:T(8,128)(2,1)S(1)} %copy-done.8, ...), custom_call_target="tpu_custom_call" | custom-call | flops 6600000000 | bytes 6445312 | tf_op jit(solution)/shard_map/head_grad/pallas_call | solution.py:500
  273.5 1.7 convert_add_fusion.1
  276.4 1.4 add_convert_fusion.1
  277.8 1.7 collective-permute-start.34
  280.5 5.6 %head_grad.3 = (bf16[4,2048,128]{2,1,0:T(8,128)(2,1)}, bf16[2048,1024]{1,0:T(8,128)(2,1)}) custom-call(s32[4]{0:T(128)S(1)} %pad_add_fusion.s_ref, bf16[512,1024]{1,0:T(8,128)(2,1)} %collective-permute-done.29.even_ref, bf16[512,1024]{1,0:T(8,128)(2,1)} %copy-done.32, bf16[1024,256]{1,0:T(8,128)(2,1)S(1)} %copy-done.8, ...), custom_call_target="tpu_custom_call", output_to_operand_aliasing={{0}: (5, {}), {1}: (6, {})} | custom-call | flops 6600000000 | bytes 6445312 | tf_op jit(solution)/shard_map/head_grad/pallas_call | solution.py:500
  286.1 56.1 %attend_backward.1.d_ref.p_ref = bf16[3,2048,256]{2,1,0:T(8,128)(2,1)} custom-call(s32[4]{0:T(128)S(1)} %pad_add_fusion.s_ref, bf16[4,2048,128]{2,1,0:T(8,128)(2,1)} %get-tuple-element.153.q2_ref, bf16[4,2048,128]{2,1,0:T(8,128)(2,1)} %get-tuple-element.112.k_ref, bf16[4,2048,128]{2,1,0:T(8,128)(2,1)} %get-tuple-element.113.v_ref, ...), custom_call_target="tpu_custom_call" | custom-call | flops 22000001024 | bytes 21484376 | tf_op jit(solution)/shard_map/attend_backward/pallas_call | solution.py:313
  342.2 9.0 %proj_grads.1 = bf16[8,4,256,128]{3,2,1,0:T(8,128)(2,1)} custom-call(bf16[2048,1024]{1,0:T(8,128)(2,1)} %get-tuple-element.152.n_ref, bf16[3,2048,256]{2,1,0:T(8,128)(2,1)} %attend_backward.1.d_ref.p_ref, bf16[1024,256]{1,0:T(8,128)(2,1)S(1)} %get-tuple-element.129.o0.o_ref, bf16[1024,256]{1,0:T(8,128)(2,1)S(1)} %get-tuple-element.120.o0.o_ref.o1, ...), custom_call_target="tpu_custom_call" | custom-call | flops 11000000512 | bytes 10742187 | tf_op jit(solution)/shard_map/proj_grads/pallas_call | solution.py:594
  351.3 3.2 dn.5
  354.6 3.2 dn.4
  357.9 1.7 add_convert_fusion
  359.7 4.1 convolution_convert_fusion.2
  363.7 6.0 %all-to-all-start.3 = ((bf16[8,64,1024]{2,1,0:T(8,128)(2,1)}), bf16[8,64,1024]{2,1,0:T(8,128)(2,1)S(1)}, u32[]{:S(2)}, u32[]{:S(2)}) async-start(bf16[8,64,1024]{2,1,0:T(8,128)(2,1)} %bitcast.141), calls=%async_computation.3 | async-start | bytes 2097152 | tf_op jit(solution)/shard_map/all_to_all | solution.py:752
  371.2 3.2 dn.7
  374.7 3.2 dn.6.keep_ref
  378.0 3.3 convert_reduce_fusion
  383.1 13.0 %collective-permute-done.36.chip_ref = bf16[512,1024]{1,0:T(8,128)(2,1)S(1)} collective-permute-done((bf16[512,1024]{1,0:T(8,128)(2,1)S(1)}, bf16[512,1024]{1,0:T(8,128)(2,1)S(1)}, u32[]{:S(2)}, u32[]{:S(2)}) %collective-permute-start.36) | collective-permute-done | bytes 1048608 | tf_op jit(solution)/shard_map/ppermute | solution.py:56
  397.1 12.0 %all-to-all-done.3 = bf16[8,64,1024]{2,1,0:T(8,128)(2,1)S(1)} async-done(((bf16[8,64,1024]{2,1,0:T(8,128)(2,1)}), bf16[8,64,1024]{2,1,0:T(8,128)(2,1)S(1)}, u32[]{:S(2)}, u32[]{:S(2)}) %all-to-all-start.3) | async-done | bytes 1048608 | tf_op jit(solution)/shard_map/all_to_all | solution.py:752
  409.1 3.7 last.1
  412.9 1.8 convolution_convert_fusion.1
  414.7 3.8 all-to-all-start.4
  419.5 1.7 turn_rows.1
  421.2 30.8 %reduce-scatter.2.cloned.1.call-done = bf16[1,4,256,128]{3,2,1,0:T(8,128)(2,1)} async-done(((bf16[8,4,256,128]{3,2,1,0:T(8,128)(2,1)}), bf16[1,4,256,128]{3,2,1,0:T(8,128)(2,1)}) %reduce-scatter.2.cloned.1.call-update) | async-done | bytes 262160 | tf_op jit(solution)/shard_map/reduce_scatter | solution.py:915
  456.2 1.8 convolution_convert_fusion
  (210 shorter events, 33.5 us)
Async XLA Ops:
  7.2 8.3 %copy-start = (bf16[512,1024]{1,0:T(8,128)(2,1)S(1)}, bf16[512,1024]{1,0:T(8,128)(2,1)}, u32[]{:S(2)}) copy-start(bf16[512,1024]{1,0:T(8,128)(2,1)} %param.10) | copy-start | bytes 3145732
  9.2 38.4 %collective-permute-start.8 = (bf16[4,128,256]{2,1,0:T(8,128)(2,1)S(1)}, bf16[4,128,256]{2,1,0:T(8,128)(2,1)S(1)}, u32[]{:S(2)}, u32[]{:S(2)}) collective-permute-start(bf16[4,128,256]{2,1,0:T(8,128)(2,1)S(1)} %pad_maximum_fusion.4), channel_id=1, source_target_pairs={{0,16},{4,20},{8,24},{12,28},{16,0},{20,4},{24,8},{28,12},{1,17},{... | collective-permute-start | bytes 786440 | tf_op jit(solution)/shard_map/ppermute | solution.py:56
  14.0 18.3 %collective-permute-start = (f32[2,32]{1,0:T(2,128)S(1)}, f32[2,32]{1,0:T(2,128)S(1)}, u32[]{:S(2)}, u32[]{:S(2)}) collective-permute-start(f32[2,32]{1,0:T(2,128)S(1)} %pad_maximum_fusion.8), channel_id=1, source_target_pairs={{0,16},{4,20},{8,24},{12,28},{16,0},{20,4},{24,8},{28,12},{1,17},{... | collective-permute-start | bytes 776 | tf_op jit(solution)/shard_map/ppermute | solution.py:56
  15.5 8.1 %copy-start.19 = (s32[512]{0:T(512)}, s32[512]{0:T(512)S(1)}, u32[]{:S(2)}) copy-start(s32[512]{0:T(512)S(1)} %eq.84) | copy-start | bytes 6148
  15.5 8.1 %copy-start.25 = (bf16[512,1024]{1,0:T(8,128)(2,1)S(1)}, bf16[512,1024]{1,0:T(8,128)(2,1)}, u32[]{:S(2)}) copy-start(bf16[512,1024]{1,0:T(8,128)(2,1)} %param.11) | copy-start | bytes 3145732
  17.2 8.2 %copy-start.35 = (s32[16]{0:T(128)S(1)}, s32[16]{0:T(128)}, u32[]{:S(2)}) copy-start(s32[16]{0:T(128)} %param.12) | copy-start | bytes 196
  17.2 43.0 %all-to-all-start = ((bf16[8,64,1024]{2,1,0:T(8,128)(2,1)}), bf16[8,64,1024]{2,1,0:T(8,128)(2,1)}, u32[]{:S(2)}, u32[]{:S(2)}) async-start(bf16[8,64,1024]{2,1,0:T(8,128)(2,1)} %bitcast.1), calls=%async_computation | async-start | bytes 2097152 | tf_op jit(solution)/shard_map/all_to_all | solution.py:752
  23.5 154.6 %all-gather.2.cloned.1.call-start = ((), (), s32[]{:S(2)}) async-start(), calls=%async_computation.6 | async-start | bytes 5308416 | tf_op jit(solution)/shard_map/all_gather | solution.py:787
  23.6 8.7 %copy-start.23 = (f32[32]{0:T(128)S(1)}, f32[32]{0:T(128)}, u32[]{:S(2)}) copy-start(f32[32]{0:T(128)} %param.15) | copy-start | bytes 388
  23.7 8.7 %copy-start.24 = (f32[32]{0:T(128)S(1)}, f32[32]{0:T(128)}, u32[]{:S(2)}) copy-start(f32[32]{0:T(128)} %param.14) | copy-start | bytes 388
  23.7 23.9 %copy-start.12 = (bf16[3,128,256]{2,1,0:T(8,128)(2,1)S(1)}, bf16[3,128,256]{2,1,0:T(8,128)(2,1)}, u32[]{:S(2)}) copy-start(bf16[3,128,256]{2,1,0:T(8,128)(2,1)} %param.16) | copy-start | bytes 589828
  32.4 7.8 %collective-permute-start.1 = (f32[2,2,32]{2,1,0:T(2,128)S(1)}, f32[2,2,32]{2,1,0:T(2,128)S(1)}, u32[]{:S(2)}, u32[]{:S(2)}) collective-permute-start(f32[2,2,32]{2,1,0:T(2,128)S(1)} %pad_maximum_fusion.7), channel_id=1, source_target_pairs={{0,8},{4,12},{8,0},{12,4},{16,24},{20,28},{24,16},{28,20},{1,9},{5... | collective-permute-start | bytes 1544 | tf_op jit(solution)/shard_map/ppermute | solution.py:56
  40.2 3.7 collective-permute-start.2
  43.9 3.7 collective-permute-start.3
  45.4 102.3 %copy-start.21 = (s32[512]{0:T(512)}, s32[512]{0:T(512)S(1)}, u32[]{:S(2)}) copy-start(s32[512]{0:T(512)S(1)} %multiply_add_fusion) | copy-start | bytes 6148
  47.7 12.4 %collective-permute-start.9 = (bf16[2,4,128,256]{3,2,1,0:T(8,128)(2,1)S(1)}, bf16[2,4,128,256]{3,2,1,0:T(8,128)(2,1)S(1)}, u32[]{:S(2)}, u32[]{:S(2)}) collective-permute-start(bf16[2,4,128,256]{3,2,1,0:T(8,128)(2,1)S(1)} %pad_maximum_fusion.3), channel_id=1, source_target_pairs={{0,8},{4,12},{8,0},{12,4},{16,24},{20,28},{24,16},{28,20},{1,9},{5... | collective-permute-start | bytes 1572872 | tf_op jit(solution)/shard_map/ppermute | solution.py:56
  50.3 1.2 collective-permute-start.4
  51.6 49.9 %copy-start.18 = (f32[2,1024]{1,0:T(2,128)}, f32[2,1024]{1,0:T(2,128)S(1)}, u32[]{:S(2)}) copy-start(f32[2,1024]{1,0:T(2,128)S(1)} %reshape.193) | copy-start | bytes 24580
  62.2 39.4 %copy-start.4 = (bf16[512,1024]{1,0:T(8,128)(2,1)}, bf16[512,1024]{1,0:T(8,128)(2,1)S(1)}, u32[]{:S(2)}) copy-start(bf16[512,1024]{1,0:T(8,128)(2,1)S(1)} %convolution_convert_fusion.4.xa_ref.xk_ref.x_ref) | copy-start | bytes 3145732
  62.2 22.2 %collective-permute-start.6 = (bf16[512,1024]{1,0:T(8,128)(2,1)S(1)}, bf16[512,1024]{1,0:T(8,128)(2,1)S(1)}, u32[]{:S(2)}, u32[]{:S(2)}) collective-permute-start(bf16[512,1024]{1,0:T(8,128)(2,1)S(1)} %convolution_convert_fusion.4.xa_ref.xk_ref.x_ref), channel_id=1, source_target_pairs={{0,2},{1,3},{2,0},{3,1},{4,6},{5,7},{6,4},{7,5},{8,10},{9,11},{10,... | collective-permute-start | bytes 3145736 | tf_op jit(solution)/shard_map/ppermute | solution.py:56
  64.8 28.5 %collective-permute-start.10 = (bf16[2,2,4,128,256]{4,3,2,0,1:T(8,128)(2,1)}, bf16[2,2,4,128,256]{4,3,2,0,1:T(8,128)(2,1)}, u32[]{:S(2)}, u32[]{:S(2)}) collective-permute-start(bf16[2,2,4,128,256]{4,3,2,0,1:T(8,128)(2,1)} %pad_maximum_fusion.1), channel_id=1, source_target_pairs={{0,4},{4,0},{8,12},{12,8},{16,20},{20,16},{24,28},{28,24},{1,5},{5... | collective-permute-start | bytes 3145736 | tf_op jit(solution)/shard_map/ppermute | solution.py:56
  69.0 32.6 %collective-permute-start.5 = (bf16[512,1024]{1,0:T(8,128)(2,1)S(1)}, bf16[512,1024]{1,0:T(8,128)(2,1)}, u32[]{:S(2)}, u32[]{:S(2)}) collective-permute-start(bf16[512,1024]{1,0:T(8,128)(2,1)S(1)} %convolution_convert_fusion.4.xa_ref.xk_ref.x_ref), channel_id=1, source_target_pairs={{0,1},{1,0},{2,3},{3,2},{4,5},{5,4},{6,7},{7,6},{8,9},{9,8},{10,11... | collective-permute-start | bytes 3145736 | tf_op jit(solution)/shard_map/ppermute | solution.py:56
  84.5 25.1 %copy-start.6 = (bf16[512,1024]{1,0:T(8,128)(2,1)}, bf16[512,1024]{1,0:T(8,128)(2,1)S(1)}, u32[]{:S(2)}) copy-start(bf16[512,1024]{1,0:T(8,128)(2,1)S(1)} %collective-permute-done.6.xa_ref.xk_ref) | copy-start | bytes 3145732
  84.5 25.1 %collective-permute-start.7 = (bf16[512,1024]{1,0:T(8,128)(2,1)S(1)}, bf16[512,1024]{1,0:T(8,128)(2,1)}, u32[]{:S(2)}, u32[]{:S(2)}) collective-permute-start(bf16[512,1024]{1,0:T(8,128)(2,1)S(1)} %collective-permute-done.6.xa_ref.xk_ref), channel_id=1, source_target_pairs={{0,1},{1,0},{2,3},{3,2},{4,5},{5,4},{6,7},{7,6},{8,9},{9,8},{10,11... | collective-permute-start | bytes 3145736 | tf_op jit(solution)/shard_map/ppermute | solution.py:56
  96.4 21.1 %collective-permute-start.11 = (bf16[1024,256]{1,0:T(8,128)(2,1)S(1)}, bf16[1024,256]{1,0:T(8,128)(2,1)}, u32[]{:S(2)}, u32[]{:S(2)}) collective-permute-start(bf16[1024,256]{1,0:T(8,128)(2,1)S(1)} %bitcast.146), channel_id=1, source_target_pairs={{0,2},{1,3},{2,0},{3,1},{4,6},{5,7},{6,4},{7,5},{8,10},{9,11},{10,... | collective-permute-start | bytes 1572872 | tf_op jit(solution)/shard_map/ppermute | solution.py:56
  97.0 50.7 %all-to-all-start.1 = ((bf16[8,64,1024]{2,1,0:T(8,128)(2,1)}), bf16[8,64,1024]{2,1,0:T(8,128)(2,1)}, u32[]{:S(2)}, u32[]{:S(2)}) async-start(bf16[8,64,1024]{2,1,0:T(8,128)(2,1)} %bitcast.41), calls=%async_computation.1 | async-start | bytes 2097152 | tf_op jit(solution)/shard_map/all_to_all | solution.py:752
  101.6 8.0 %copy-start.9 = (f32[1,1024]{1,0:T(1,128)}, f32[1,1024]{1,0:T(1,128)S(1)}, u32[]{:S(2)}) copy-start(f32[1,1024]{1,0:T(1,128)S(1)} %get-tuple-element.240.gain_ref) | copy-start | bytes 12292
  135.8 36.5 %collective-permute-start.13 = (bf16[1024,256]{1,0:T(8,128)(2,1)S(1)}, bf16[1024,256]{1,0:T(8,128)(2,1)S(1)}, u32[]{:S(2)}, u32[]{:S(2)}) collective-permute-start(bf16[1024,256]{1,0:T(8,128)(2,1)S(1)} %get-tuple-element.129.o0.o_ref), channel_id=1, source_target_pairs={{0,2},{1,3},{2,0},{3,1},{4,6},{5,7},{6,4},{7,5},{8,10},{9,11},{10,... | collective-permute-start | bytes 1572872 | tf_op jit(solution)/shard_map/ppermute | solution.py:56
  149.7 22.6 %copy-start.26 = (bf16[512,1024]{1,0:T(8,128)(2,1)}, bf16[512,1024]{1,0:T(8,128)(2,1)S(1)}, u32[]{:S(2)}) copy-start(bf16[512,1024]{1,0:T(8,128)(2,1)S(1)} %convolution_convert_fusion.3.gk_ref.g_ref) | copy-start | bytes 3145732
  149.7 22.6 %collective-permute-start.14 = (bf16[512,1024]{1,0:T(8,128)(2,1)S(1)}, bf16[512,1024]{1,0:T(8,128)(2,1)}, u32[]{:S(2)}, u32[]{:S(2)}) collective-permute-start(bf16[512,1024]{1,0:T(8,128)(2,1)S(1)} %convolution_convert_fusion.3.gk_ref.g_ref), channel_id=1, source_target_pairs={{0,2},{1,3},{2,0},{3,1},{4,6},{5,7},{6,4},{7,5},{8,10},{9,11},{10,... | collective-permute-start | bytes 3145736 | tf_op jit(solution)/shard_map/ppermute | solution.py:56
  172.3 5.9 %collective-permute-start.15 = (bf16[512,1024]{1,0:T(8,128)(2,1)}, bf16[512,1024]{1,0:T(8,128)(2,1)}, u32[]{:S(2)}, u32[]{:S(2)}) collective-permute-start(bf16[512,1024]{1,0:T(8,128)(2,1)} %collective-permute-done.14.gk_ref), channel_id=1, source_target_pairs={{0,1},{1,0},{2,3},{3,2},{4,5},{5,4},{6,7},{7,6},{8,9},{9,8},{10,11... | collective-permute-start | bytes 3145736 | tf_op jit(solution)/shard_map/ppermute | solution.py:56
  173.5 2.4 collective-permute-start.18
  174.0 3.6 collective-permute-start.19
  174.1 3.5 collective-permute-start.16
  174.6 3.6 collective-permute-start.17
  175.9 26.6 %collective-permute-start.21 = (f32[4]{0:T(128)S(1)}, f32[4]{0:T(128)S(1)}, u32[]{:S(2)}, u32[]{:S(2)}) collective-permute-start(f32[4]{0:T(128)S(1)} %maximum_multiply_fusion), channel_id=1, source_target_pairs={{0,4},{4,0},{8,12},{12,8},{16,20},{20,16},{24,28},{28,24},{1,5},{5... | collective-permute-start | bytes 56 | tf_op jit(solution)/shard_map/ppermute | solution.py:56
  177.6 24.9 %collective-permute-start.20 = (bf16[1024,256]{1,0:T(8,128)(2,1)S(1)}, bf16[1024,256]{1,0:T(8,128)(2,1)S(1)}, u32[]{:S(2)}, u32[]{:S(2)}) collective-permute-start(bf16[1024,256]{1,0:T(8,128)(2,1)S(1)} %get-tuple-element.120.o0.o_ref.o1), channel_id=1, source_target_pairs={{0,2},{1,3},{2,0},{3,1},{4,6},{5,7},{6,4},{7,5},{8,10},{9,11},{10,... | collective-permute-start | bytes 1572872 | tf_op jit(solution)/shard_map/ppermute | solution.py:56
  178.2 24.5 %copy-start.27 = (bf16[512,1024]{1,0:T(8,128)(2,1)S(1)}, bf16[512,1024]{1,0:T(8,128)(2,1)}, u32[]{:S(2)}) copy-start(bf16[512,1024]{1,0:T(8,128)(2,1)} %copy-done.26) | copy-start | bytes 3145732
  202.5 2.9 collective-permute-start.22
  202.7 6.9 %collective-permute-start.12 = (bf16[512,1024]{1,0:T(8,128)(2,1)S(1)}, bf16[512,1024]{1,0:T(8,128)(2,1)S(1)}, u32[]{:S(2)}, u32[]{:S(2)}) collective-permute-start(bf16[512,1024]{1,0:T(8,128)(2,1)S(1)} %copy-done.27), channel_id=1, source_target_pairs={{0,1},{1,0},{2,3},{3,2},{4,5},{5,4},{6,7},{7,6},{8,9},{9,8},{10,11... | collective-permute-start | bytes 3145736 | tf_op jit(solution)/shard_map/ppermute | solution.py:56
  203.1 6.5 %collective-permute-start.23 = (bf16[1024,256]{1,0:T(8,128)(2,1)S(1)}, bf16[1024,256]{1,0:T(8,128)(2,1)S(1)}, u32[]{:S(2)}, u32[]{:S(2)}) collective-permute-start(bf16[1024,256]{1,0:T(8,128)(2,1)S(1)} %get-tuple-element.129.o0.o_ref), channel_id=1, source_target_pairs={{0,1},{1,0},{2,3},{3,2},{4,5},{5,4},{6,7},{7,6},{8,9},{9,8},{10,11... | collective-permute-start | bytes 1572872 | tf_op jit(solution)/shard_map/ppermute | solution.py:56
  203.2 6.4 %collective-permute-start.24 = (bf16[1024,256]{1,0:T(8,128)(2,1)S(1)}, bf16[1024,256]{1,0:T(8,128)(2,1)S(1)}, u32[]{:S(2)}, u32[]{:S(2)}) collective-permute-start(bf16[1024,256]{1,0:T(8,128)(2,1)S(1)} %collective-permute-done.20.o2), channel_id=1, source_target_pairs={{0,1},{1,0},{2,3},{3,2},{4,5},{5,4},{6,7},{7,6},{8,9},{9,8},{10,11... | collective-permute-start | bytes 1572872 | tf_op jit(solution)/shard_map/ppermute | solution.py:56
  203.6 30.8 %collective-permute-start.26 = (f32[4]{0:T(128)S(1)}, f32[4]{0:T(128)S(1)}, u32[]{:S(2)}, u32[]{:S(2)}) collective-permute-start(f32[4]{0:T(128)S(1)} %max.15), channel_id=1, source_target_pairs={{0,8},{4,12},{8,0},{12,4},{16,24},{20,28},{24,16},{28,20},{1,9},{5... | collective-permute-start | bytes 56 | tf_op jit(solution)/shard_map/ppermute | solution.py:56
  207.4 27.0 %collective-permute-start.25 = (bf16[512,1024]{1,0:T(8,128)(2,1)S(1)}, bf16[512,1024]{1,0:T(8,128)(2,1)S(1)}, u32[]{:S(2)}, u32[]{:S(2)}) collective-permute-start(bf16[512,1024]{1,0:T(8,128)(2,1)S(1)} %add_convert_fusion.2), channel_id=1, source_target_pairs={{0,2},{1,3},{2,0},{3,1},{4,6},{5,7},{6,4},{7,5},{8,10},{9,11},{10,... | collective-permute-start | bytes 3145736 | tf_op jit(solution)/shard_map/ppermute | solution.py:56
  234.4 2.9 collective-permute-start.27
  234.5 27.9 %collective-permute-start.28 = (f32[4]{0:T(128)S(1)}, f32[4]{0:T(128)S(1)}, u32[]{:S(2)}, u32[]{:S(2)}) collective-permute-start(f32[4]{0:T(128)S(1)} %max.16), channel_id=1, source_target_pairs={{0,16},{4,20},{8,24},{12,28},{16,0},{20,4},{24,8},{28,12},{1,17},{... | collective-permute-start | bytes 56 | tf_op jit(solution)/shard_map/ppermute | solution.py:56
  243.3 19.1 %copy-start.11 = (bf16[512,1024]{1,0:T(8,128)(2,1)}, bf16[512,1024]{1,0:T(8,128)(2,1)S(1)}, u32[]{:S(2)}) copy-start(bf16[512,1024]{1,0:T(8,128)(2,1)S(1)} %get-tuple-element.147.even_ref) | copy-start | bytes 3145732
  243.3 24.0 %collective-permute-start.30 = (bf16[512,1024]{1,0:T(8,128)(2,1)S(1)}, bf16[512,1024]{1,0:T(8,128)(2,1)}, u32[]{:S(2)}, u32[]{:S(2)}) collective-permute-start(bf16[512,1024]{1,0:T(8,128)(2,1)S(1)} %get-tuple-element.147.even_ref), channel_id=1, source_target_pairs={{0,1},{1,0},{2,3},{3,2},{4,5},{5,4},{6,7},{7,6},{8,9},{9,8},{10,11... | collective-permute-start | bytes 3145736 | tf_op jit(solution)/shard_map/ppermute | solution.py:56
  243.4 29.5 %collective-permute-start.29 = (bf16[512,1024]{1,0:T(8,128)(2,1)S(1)}, bf16[512,1024]{1,0:T(8,128)(2,1)}, u32[]{:S(2)}, u32[]{:S(2)}) collective-permute-start(bf16[512,1024]{1,0:T(8,128)(2,1)S(1)} %get-tuple-element.147.even_ref), channel_id=1, source_target_pairs={{0,2},{1,3},{2,0},{3,1},{4,6},{5,7},{6,4},{7,5},{8,10},{9,11},{10,... | collective-permute-start | bytes 3145736 | tf_op jit(solution)/shard_map/ppermute | solution.py:56
  262.4 97.2 %all-to-all-start.2 = ((bf16[8,3,656,128]{3,2,1,0:T(8,128)(2,1)}), bf16[8,3,656,128]{3,2,1,0:T(8,128)(2,1)}, u32[]{:S(2)}, u32[]{:S(2)}) async-start(bf16[8,3,656,128]{3,2,1,0:T(8,128)(2,1)} %inner_grads.1), calls=%async_computation.2 | async-start | bytes 8060928 | tf_op jit(solution)/shard_map/all_to_all | solution.py:871
  267.1 184.9 %reduce-scatter.2.cloned.1.call-start = ((), (), s32[]{:S(2)}) async-start(), calls=%async_computation.7 | async-start | bytes 2359296 | tf_op jit(solution)/shard_map/reduce_scatter | solution.py:915
  267.2 6.3 %collective-permute-start.33 = (bf16[512,1024]{1,0:T(8,128)(2,1)}, bf16[512,1024]{1,0:T(8,128)(2,1)S(1)}, u32[]{:S(2)}, u32[]{:S(2)}) collective-permute-start(bf16[512,1024]{1,0:T(8,128)(2,1)} %get-tuple-element.164), channel_id=1, source_target_pairs={{0,1},{1,0},{2,3},{3,2},{4,5},{5,4},{6,7},{7,6},{8,9},{9,8},{10,11... | collective-permute-start | bytes 3145736 | tf_op jit(solution)/shard_map/ppermute | solution.py:56
  272.9 3.5 collective-permute-start.31
  273.4 6.1 %collective-permute-start.32 = (bf16[512,1024]{1,0:T(8,128)(2,1)}, bf16[512,1024]{1,0:T(8,128)(2,1)S(1)}, u32[]{:S(2)}, u32[]{:S(2)}) collective-permute-start(bf16[512,1024]{1,0:T(8,128)(2,1)} %collective-permute-done.29.even_ref), channel_id=1, source_target_pairs={{0,1},{1,0},{2,3},{3,2},{4,5},{5,4},{6,7},{7,6},{8,9},{9,8},{10,11... | collective-permute-start | bytes 3145736 | tf_op jit(solution)/shard_map/ppermute | solution.py:56
  277.8 73.4 %collective-permute-start.34 = (bf16[512,1024]{1,0:T(8,128)(2,1)}, bf16[512,1024]{1,0:T(8,128)(2,1)S(1)}, u32[]{:S(2)}, u32[]{:S(2)}) collective-permute-start(bf16[512,1024]{1,0:T(8,128)(2,1)} %add_convert_fusion.1), channel_id=1, source_target_pairs={{0,2},{1,3},{2,0},{3,1},{4,6},{5,7},{6,4},{7,5},{8,10},{9,11},{10,... | collective-permute-start | bytes 3145736 | tf_op jit(solution)/shard_map/ppermute | solution.py:56
  354.5 3.4 collective-permute-start.35
  363.7 45.4 %all-to-all-start.3 = ((bf16[8,64,1024]{2,1,0:T(8,128)(2,1)}), bf16[8,64,1024]{2,1,0:T(8,128)(2,1)S(1)}, u32[]{:S(2)}, u32[]{:S(2)}) async-start(bf16[8,64,1024]{2,1,0:T(8,128)(2,1)} %bitcast.141), calls=%async_computation.3 | async-start | bytes 2097152 | tf_op jit(solution)/shard_map/all_to_all | solution.py:752
  370.9 25.2 %collective-permute-start.36 = (bf16[512,1024]{1,0:T(8,128)(2,1)S(1)}, bf16[512,1024]{1,0:T(8,128)(2,1)S(1)}, u32[]{:S(2)}, u32[]{:S(2)}) collective-permute-start(bf16[512,1024]{1,0:T(8,128)(2,1)S(1)} %add_convert_fusion), channel_id=1, source_target_pairs={{0,2},{1,3},{2,0},{3,1},{4,6},{5,7},{6,4},{7,5},{8,10},{9,11},{10,... | collective-permute-start | bytes 3145736 | tf_op jit(solution)/shard_map/ppermute | solution.py:56
  374.5 22.6 %collective-permute-start.37 = (bf16[512,1024]{1,0:T(8,128)(2,1)S(1)}, bf16[512,1024]{1,0:T(8,128)(2,1)}, u32[]{:S(2)}, u32[]{:S(2)}) collective-permute-start(bf16[512,1024]{1,0:T(8,128)(2,1)S(1)} %dn.7), channel_id=1, source_target_pairs={{0,1},{1,0},{2,3},{3,2},{4,5},{5,4},{6,7},{7,6},{8,9},{9,8},{10,11... | collective-permute-start | bytes 3145736 | tf_op jit(solution)/shard_map/ppermute | solution.py:56
  381.3 27.9 %copy-start.10 = (f32[1,1024]{1,0:T(1,128)S(1)}, f32[1,1024]{1,0:T(1,128)}, u32[]{:S(2)}) copy-start(f32[1,1024]{1,0:T(1,128)} %copy-done.9) | copy-start | bytes 12292
  414.7 38.3 %all-to-all-start.4 = ((bf16[8,64,1024]{2,1,0:T(8,128)(2,1)}), bf16[8,64,1024]{2,1,0:T(8,128)(2,1)S(1)}, u32[]{:S(2)}, u32[]{:S(2)}) async-start(bf16[8,64,1024]{2,1,0:T(8,128)(2,1)} %bitcast.142), calls=%async_computation.4 | async-start | bytes 2097152 | tf_op jit(solution)/shard_map/all_to_all | solution.py:752
  454.2 5.3 %collective-permute-start.38 = (f32[2,32]{1,0:T(2,128)S(1)}, f32[2,32]{1,0:T(2,128)S(1)}, u32[]{:S(2)}, u32[]{:S(2)}) collective-permute-start(f32[2,32]{1,0:T(2,128)S(1)} %bitcast.165), channel_id=1, source_target_pairs={{0,1},{1,0},{2,3},{3,2},{4,5},{5,4},{6,7},{7,6},{8,9},{9,8},{10,11... | collective-permute-start | bytes 776 | tf_op jit(solution)/shard_map/ppermute | solution.py:56
  454.3 5.2 %collective-permute-start.39 = (f32[2,32]{1,0:T(2,128)S(1)}, f32[2,32]{1,0:T(2,128)S(1)}, u32[]{:S(2)}, u32[]{:S(2)}) collective-permute-start(f32[2,32]{1,0:T(2,128)S(1)} %bitcast.164), channel_id=1, source_target_pairs={{0,2},{1,3},{2,0},{3,1},{4,6},{5,7},{6,4},{7,5},{8,10},{9,11},{10,... | collective-permute-start | bytes 776 | tf_op jit(solution)/shard_map/ppermute | solution.py:56
  455.3 4.3 collective-permute-start.40
  (20 other events, 69.2 us)
Sparse Core Ops, SparseCore 0:
  70.9 91.6 all-gather.1
  358.0 93.9 reduce-scatter.1

commit v6 on v5

--- a/solution.py
+++ b/solution.py
@@ -210,7 +210,7 @@
             o_ref[:, (h // 2) * LANES : (h // 2 + 1) * LANES] = both.astype(BF16)
 
 
-def attend_forward(scalars, q, k, v, far, rows, held, q_rows=256, k_rows=512):
+def attend_forward(scalars, q, k, v, far, rows, held, q_rows=256, k_rows=1024):
     heads, tokens, _ = k.shape
     count = rows // q_rows
     k_rows = min(k_rows, tokens)

time: 473 us -> 469 us (level)
  transfers between devices with their start and end apart: 48 -> 48, of which waited for: 18 -> 19; matrix products, arithmetic and copies ran while one was open for 11% -> 11% of each run, Pallas kernels for 47% -> 47%
where the time goes in v6:
time: 469 us; the launch traced here: 462 us
  Pallas kernels  218 us (46%)
  waiting for transfers between devices  118 us (25%)
  starting transfers between devices  52.7 us (11%)
  other arithmetic  25.6 us (5%)
  local copies, waits for them, and re-layouts  17.9 us (4%)
  matrix products  15.4 us (3%)
  between operations  15.2 us (3%)
    ppermute x41, waiting for transfers between devices, swap_bit(): return lax.ppermute(values, axis_name, [(i, i ^ bit) for i in range(count)])  61.8 us
    pallas_call x1, Pallas kernels, attend_backward(): pl.pallas_call(functools.partial(bwd_kernel, q_rows, k_rows), out_shape=j...  56.1 us
    pallas_call x2, Pallas kernels, mlp_call(): pl.pallas_call(mlp_kernel, out_shape=(wide_out, wide_out, wide_out, narro...  47.9 us
    pallas_call x2, Pallas kernels, attend_forward(): pl.pallas_call(functools.partial(fwd_kernel, far, q_rows, k_rows), out_sh...  35.5 us
    reduce_scatter x1, waiting for transfers between devices, local(): grads = lax.psum_scatter(by_device(proj_grad, dp_count), 'dp')  30.8 us
    ppermute x41, starting transfers between devices, swap_bit(): return lax.ppermute(values, axis_name, [(i, i ^ bit) for i in range(count)])  29.1 us
    all_to_all x4, waiting for transfers between devices, exchange(): lax.all_to_all(packed, 'dp', split_axis=0, concat_axis=0, tiled=True)  25.3 us
    all_to_all x4, starting transfers between devices, exchange(): lax.all_to_all(packed, 'dp', split_axis=0, concat_axis=0, tiled=True)  18.7 us
  transfers between devices with their start and end apart: 48, of which 19 were waited for; matrix products, arithmetic and copies ran while one was open for 11% of the time, Pallas kernels for 47%

profile of v6, /device:TPU:0, one launch (start us, length us, event | category | flops | bytes accessed | tf_op | source)
XLA Modules:
  0.0 462.3 jit_solution(13843452743949701844)
XLA Ops:
  9.2 4.1 collective-permute-start.8
  15.5 1.7 convolution_convert_fusion.6
  17.2 6.3 %all-to-all-start = ((bf16[8,64,1024]{2,1,0:T(8,128)(2,1)}), bf16[8,64,1024]{2,1,0:T(8,128)(2,1)}, u32[]{:S(2)}, u32[]{:S(2)}) async-start(bf16[8,64,1024]{2,1,0:T(8,128)(2,1)} %bitcast.1), calls=%async_computation | async-start | bytes 2097152 | tf_op jit(solution)/shard_map/all_to_all | solution.py:752
  23.7 1.7 convolution_convert_fusion.5
  26.7 5.6 %fusion.6 = (f32[2048,128]{1,0:T(8,128)}, f32[2048,128]{1,0:T(8,128)}) fusion(f32[128]{0:T(128)S(1)} %get-tuple-element.253, f32[128]{0:T(128)S(1)} %get-tuple-element.254, f32[2048]{0:T(1024)S(1)} %select_convert_fusion), kind=kLoop, calls=%fused_computation.24 | loop fusion | flops 524288 | bytes 2106368 | tf_op jit(solution)/shard_map/mul | solution.py:780
  32.4 2.0 collective-permute-start.1
  34.4 5.8 %collective-permute-done.1 = f32[2,2,32]{2,1,0:T(2,128)S(1)} collective-permute-done((f32[2,2,32]{2,1,0:T(2,128)S(1)}, f32[2,2,32]{2,1,0:T(2,128)S(1)}, u32[]{:S(2)}, u32[]{:S(2)}) %collective-permute-start.1) | collective-permute-done | bytes 544 | tf_op jit(solution)/shard_map/ppermute | solution.py:56
  40.2 1.9 collective-permute-start.2
  42.3 1.6 collective-permute-done.2
  43.9 1.6 collective-permute-start.3
  45.5 2.1 collective-permute-done.3
  47.7 2.6 collective-permute-start.9
  51.6 8.5 %collective-permute-done.9 = bf16[2,4,128,256]{3,2,1,0:T(8,128)(2,1)S(1)} collective-permute-done((bf16[2,4,128,256]{3,2,1,0:T(8,128)(2,1)S(1)}, bf16[2,4,128,256]{3,2,1,0:T(8,128)(2,1)S(1)}, u32[]{:S(2)}, u32[]{:S(2)}) %collective-permute-start.9) | collective-permute-done | bytes 524320 | tf_op jit(solution)/shard_map/ppermute | solution.py:56
  60.2 2.0 convolution_convert_fusion.4.xa_ref.xk_ref.x_ref
  62.2 1.6 collective-permute-start.6
  67.2 1.7 copy.81
  69.0 1.8 pad_maximum_fusion.2
  70.8 13.7 %collective-permute-done.6.xa_ref.xk_ref = bf16[512,1024]{1,0:T(8,128)(2,1)S(1)} collective-permute-done((bf16[512,1024]{1,0:T(8,128)(2,1)S(1)}, bf16[512,1024]{1,0:T(8,128)(2,1)S(1)}, u32[]{:S(2)}, u32[]{:S(2)}) %collective-permute-start.6) | collective-permute-done | bytes 1048608 | tf_op jit(solution)/shard_map/ppermute | solution.py:56
  84.5 8.9 %collective-permute-done.10 = bf16[2,2,4,128,256]{4,3,2,0,1:T(8,128)(2,1)} collective-permute-done((bf16[2,2,4,128,256]{4,3,2,0,1:T(8,128)(2,1)}, bf16[2,2,4,128,256]{4,3,2,0,1:T(8,128)(2,1)}, u32[]{:S(2)}, u32[]{:S(2)}) %collective-permute-start.10) | collective-permute-done | bytes 1048608 | tf_op jit(solution)/shard_map/ppermute | solution.py:56
  93.4 1.4 select_bitcast_fusion.1
  94.9 1.4 copy.80
  97.0 4.5 all-to-all-start.1
  101.6 7.9 %qkv.2 = (bf16[4,2048,128]{2,1,0:T(8,128)(2,1)}, bf16[4,2048,128]{2,1,0:T(8,128)(2,1)}, bf16[4,2048,128]{2,1,0:T(8,128)(2,1)}, bf16[2048,1024]{1,0:T(8,128)(2,1)}) custom-call(s32[4]{0:T(128)S(1)} %pad_add_fusion.s_ref, bf16[512,1024]{1,0:T(8,128)(2,1)S(1)} %convolution_convert_fusion.4.xa_ref.xk_ref.x_ref, ...), custom_call_target="tpu_custom_call" | custom-call | flops 3300000000 | bytes 3222656 | tf_op jit(solution)/shard_map/qkv/pallas_call | solution.py:119
  109.6 8.0 %qkv.3 = (bf16[4,2048,128]{2,1,0:T(8,128)(2,1)}, bf16[4,2048,128]{2,1,0:T(8,128)(2,1)}, bf16[4,2048,128]{2,1,0:T(8,128)(2,1)}, bf16[2048,1024]{1,0:T(8,128)(2,1)}) custom-call(s32[4]{0:T(128)S(1)} %pad_add_fusion.s_ref, ...), custom_call_target="tpu_custom_call", output_to_operand_aliasing={{0}: (7, {}), {1}: (8, {}), {2}: (9, {}), {3}: (10, {})} | custom-call | flops 3300000000 | bytes 3222656 | tf_op jit(solution)/shard_map/qkv/pallas_call | solution.py:119
  117.5 18.5 %attend_forward.2 = (bf16[1024,256]{1,0:T(8,128)(2,1)S(1)}, bf16[4,2048,128]{2,1,0:T(8,128)(2,1)}, f32[4,4,8,128]{3,2,1,0:T(8,128)S(1)}) custom-call(s32[4]{0:T(128)S(1)} %pad_add_fusion.s_ref, bf16[4,2048,128]{2,1,0:T(8,128)(2,1)} %get-tuple-element.111.q_ref, bf16[4,2048,128]{2,1,0:T(8,128)(2,1)} %get-tuple-element.112.k_ref, ...), custom_call_target="tpu_custom_call" | custom-call | flops 22000001024 | bytes 21484376 | tf_op jit(solution)/shard_map/attend_forward/pallas_call | solution.py:217
  136.1 11.7 %all-to-all-done.1 = bf16[8,64,1024]{2,1,0:T(8,128)(2,1)} async-done(((bf16[8,64,1024]{2,1,0:T(8,128)(2,1)}), bf16[8,64,1024]{2,1,0:T(8,128)(2,1)}, u32[]{:S(2)}, u32[]{:S(2)}) %all-to-all-start.1) | async-done | bytes 1048608 | tf_op jit(solution)/shard_map/all_to_all | solution.py:752
  147.7 2.0 convolution_convert_fusion.3.gk_ref.g_ref
  149.7 1.6 collective-permute-start.14
  151.3 17.0 %attend_forward.3 = (bf16[1024,256]{1,0:T(8,128)(2,1)S(1)}, bf16[4,2048,128]{2,1,0:T(8,128)(2,1)}, f32[4,4,8,128]{3,2,1,0:T(8,128)S(1)}) custom-call(s32[4]{0:T(128)S(1)} %pad_add_fusion.s_ref, bf16[4,2048,128]{2,1,0:T(8,128)(2,1)} %get-tuple-element.111.q_ref, bf16[4,2048,128]{2,1,0:T(8,128)(2,1)} %get-tuple-element.112.k_ref, ...), custom_call_target="tpu_custom_call", output_to_operand_aliasing={{1}: (4, {})} | custom-call | flops 22000001024 | bytes 21484376 | tf_op jit(solution)/shard_map/attend_forward/pallas_call | solution.py:217
  171.9 1.7 collective-permute-done.19.w3
  173.6 2.0 collective-permute-start.20
  175.7 24.3 %mlp.2 = (bf16[4,512,1024]{2,1,0:T(8,128)(2,1)}, bf16[4,512,1024]{2,1,0:T(8,128)(2,1)}, bf16[4,512,1024]{2,1,0:T(8,128)(2,1)}, bf16[4,512,656]{2,1,0:T(8,128)(2,...) custom-call(s32[4]{0:T(128)S(1)} %pad_add_fusion.s_ref, ...), custom_call_target="tpu_custom_call" | custom-call | flops 26400000000 | bytes 25781250 | tf_op jit(solution)/shard_map/mlp/pallas_call | solution.py:401
  201.1 2.5 collective-permute-done.22
  203.6 1.9 add_convert_fusion.2
  206.8 23.7 %mlp.3 = (bf16[4,512,1024]{2,1,0:T(8,128)(2,1)}, bf16[4,512,1024]{2,1,0:T(8,128)(2,1)}, bf16[4,512,1024]{2,1,0:T(8,128)(2,1)}, bf16[4,512,656]{2,1,0:T(8,128)(2,...) custom-call(s32[4]{0:T(128)S(1)} %pad_add_fusion.s_ref, ...), custom_call_target="tpu_custom_call", output_to_operand_aliasing={{0}: (15, {}), {1}: (16, {}), {2}: (17, {}), {3}: (18, {}),... | custom-call | flops 26400000000 | bytes 25781250 | tf_op jit(solution)/shard_map/mlp/pallas_call | solution.py:401
  231.5 2.2 collective-permute-done.27.core_ref
  234.6 5.0 %resid.1 = (f32[512,1024]{1,0:T(8,128)}, bf16[512,1024]{1,0:T(8,128)(2,1)S(1)}) custom-call(f32[512,1024]{1,0:T(8,128)} %get-tuple-element.141.keep_ref, bf16[512,1024]{1,0:T(8,128)(2,1)} %copy-done.33, bf16[512,1024]{1,0:T(8,128)(2,1)} %copy-done.29, bf16[512,1024]{1,0:T(8,128)(2,1)} %copy-done.4, bf16[4,512,1024]{2,1,0:T(8,128)(2,1)} %get-tuple-element.146.a_ref, ...), custom_call_target="tpu_custom_call" | custom-call | flops 5500000256 | bytes 5371093 | tf_op jit(solution)/shard_map/resid/pallas_call | solution.py:450
  239.7 1.7 collective-permute-start.29
  241.5 18.6 %inner_grads.1 = bf16[8,3,656,128]{3,2,1,0:T(8,128)(2,1)} custom-call(bf16[2048,1024]{1,0:T(8,128)(2,1)} %bitcast.166, bf16[2048,1024]{1,0:T(8,128)(2,1)} %bitcast.167, bf16[2048,656]{1,0:T(8,128)(2,1)} %bitcast.169, bf16[2048,656]{1,0:T(8,128)(2,1)} %bitcast.170, bf16[2048,656]{1,0:T(8,128)(2,1)} %bitcast.168), custom_call_target="tpu_custom_call" | custom-call | flops 19800000512 | bytes 19335936 | tf_op jit(solution)/shard_map/inner_grads/pallas_call | solution.py:558
  260.1 4.7 %all-to-all-start.2 = ((bf16[8,3,656,128]{3,2,1,0:T(8,128)(2,1)}), bf16[8,3,656,128]{3,2,1,0:T(8,128)(2,1)}, u32[]{:S(2)}, u32[]{:S(2)}) async-start(bf16[8,3,656,128]{3,2,1,0:T(8,128)(2,1)} %inner_grads.1), calls=%async_computation.2 | async-start | bytes 8060928 | tf_op jit(solution)/shard_map/all_to_all | solution.py:871
  265.1 5.6 %head_grad.2 = (bf16[4,2048,128]{2,1,0:T(8,128)(2,1)}, bf16[2048,1024]{1,0:T(8,128)(2,1)}) custom-call(s32[4]{0:T(128)S(1)} %pad_add_fusion.s_ref, bf16[512,1024]{1,0:T(8,128)(2,1)} %copy-done.11, bf16[512,1024]{1,0:T(8,128)(2,1)} %collective-permute-done.30.odd_ref, bf16[1024,256]{1,0:T(8,128)(2,1)S(1)} %copy-done.8, ...), custom_call_target="tpu_custom_call" | custom-call | flops 6600000000 | bytes 6445312 | tf_op jit(solution)/shard_map/head_grad/pallas_call | solution.py:500
  271.3 1.7 convert_add_fusion.1
  274.2 1.4 add_convert_fusion.1
  276.7 5.6 %head_grad.3 = (bf16[4,2048,128]{2,1,0:T(8,128)(2,1)}, bf16[2048,1024]{1,0:T(8,128)(2,1)}) custom-call(s32[4]{0:T(128)S(1)} %pad_add_fusion.s_ref, bf16[512,1024]{1,0:T(8,128)(2,1)} %collective-permute-done.29.even_ref, bf16[512,1024]{1,0:T(8,128)(2,1)} %copy-done.32, bf16[1024,256]{1,0:T(8,128)(2,1)S(1)} %copy-done.8, ...), custom_call_target="tpu_custom_call", output_to_operand_aliasing={{0}: (5, {}), {1}: (6, {})} | custom-call | flops 6600000000 | bytes 6445312 | tf_op jit(solution)/shard_map/head_grad/pallas_call | solution.py:500
  282.3 56.1 %attend_backward.1.d_ref.p_ref = bf16[3,2048,256]{2,1,0:T(8,128)(2,1)} custom-call(s32[4]{0:T(128)S(1)} %pad_add_fusion.s_ref, bf16[4,2048,128]{2,1,0:T(8,128)(2,1)} %get-tuple-element.153.q2_ref, bf16[4,2048,128]{2,1,0:T(8,128)(2,1)} %get-tuple-element.112.k_ref, bf16[4,2048,128]{2,1,0:T(8,128)(2,1)} %get-tuple-element.113.v_ref, ...), custom_call_target="tpu_custom_call" | custom-call | flops 22000001024 | bytes 21484376 | tf_op jit(solution)/shard_map/attend_backward/pallas_call | solution.py:313
  338.4 9.0 %proj_grads.1 = bf16[8,4,256,128]{3,2,1,0:T(8,128)(2,1)} custom-call(bf16[2048,1024]{1,0:T(8,128)(2,1)} %get-tuple-element.152.n_ref, bf16[3,2048,256]{2,1,0:T(8,128)(2,1)} %attend_backward.1.d_ref.p_ref, bf16[1024,256]{1,0:T(8,128)(2,1)S(1)} %get-tuple-element.129.o0.o_ref, bf16[1024,256]{1,0:T(8,128)(2,1)S(1)} %get-tuple-element.120.o0.o_ref.o1, ...), custom_call_target="tpu_custom_call" | custom-call | flops 11000000512 | bytes 10742187 | tf_op jit(solution)/shard_map/proj_grads/pallas_call | solution.py:594
  347.5 3.2 dn.5
  351.0 3.2 dn.4
  354.2 1.7 add_convert_fusion
  356.0 4.1 convolution_convert_fusion.2
  360.0 4.2 all-to-all-start.3
  365.4 1.8 collective-permute-start.36
  367.2 3.2 dn.7
  370.6 3.2 dn.6.keep_ref
  373.9 3.2 convert_reduce_fusion
  379.0 11.7 %collective-permute-done.36.chip_ref = bf16[512,1024]{1,0:T(8,128)(2,1)S(1)} collective-permute-done((bf16[512,1024]{1,0:T(8,128)(2,1)S(1)}, bf16[512,1024]{1,0:T(8,128)(2,1)S(1)}, u32[]{:S(2)}, u32[]{:S(2)}) %collective-permute-start.36) | collective-permute-done | bytes 1048608 | tf_op jit(solution)/shard_map/ppermute | solution.py:56
  391.6 12.8 %all-to-all-done.3 = bf16[8,64,1024]{2,1,0:T(8,128)(2,1)S(1)} async-done(((bf16[8,64,1024]{2,1,0:T(8,128)(2,1)}), bf16[8,64,1024]{2,1,0:T(8,128)(2,1)S(1)}, u32[]{:S(2)}, u32[]{:S(2)}) %all-to-all-start.3) | async-done | bytes 1048608 | tf_op jit(solution)/shard_map/all_to_all | solution.py:752
  404.4 3.7 last.1
  408.1 1.8 convolution_convert_fusion.1
  409.9 3.8 all-to-all-start.4
  414.7 1.7 turn_rows.1
  416.4 30.8 %reduce-scatter.2.cloned.1.call-done = bf16[1,4,256,128]{3,2,1,0:T(8,128)(2,1)} async-done(((bf16[8,4,256,128]{3,2,1,0:T(8,128)(2,1)}), bf16[1,4,256,128]{3,2,1,0:T(8,128)(2,1)}) %reduce-scatter.2.cloned.1.call-update) | async-done | bytes 262160 | tf_op jit(solution)/shard_map/reduce_scatter | solution.py:915
  449.5 1.7 collective-permute-start.39
  451.3 1.8 convolution_convert_fusion
  (210 shorter events, 32.9 us)
Async XLA Ops:
  7.2 8.3 %copy-start = (bf16[512,1024]{1,0:T(8,128)(2,1)S(1)}, bf16[512,1024]{1,0:T(8,128)(2,1)}, u32[]{:S(2)}) copy-start(bf16[512,1024]{1,0:T(8,128)(2,1)} %param.10) | copy-start | bytes 3145732
  9.2 38.4 %collective-permute-start.8 = (bf16[4,128,256]{2,1,0:T(8,128)(2,1)S(1)}, bf16[4,128,256]{2,1,0:T(8,128)(2,1)S(1)}, u32[]{:S(2)}, u32[]{:S(2)}) collective-permute-start(bf16[4,128,256]{2,1,0:T(8,128)(2,1)S(1)} %pad_maximum_fusion.4), channel_id=1, source_target_pairs={{0,16},{4,20},{8,24},{12,28},{16,0},{20,4},{24,8},{28,12},{1,17},{... | collective-permute-start | bytes 786440 | tf_op jit(solution)/shard_map/ppermute | solution.py:56
  14.0 18.3 %collective-permute-start = (f32[2,32]{1,0:T(2,128)S(1)}, f32[2,32]{1,0:T(2,128)S(1)}, u32[]{:S(2)}, u32[]{:S(2)}) collective-permute-start(f32[2,32]{1,0:T(2,128)S(1)} %pad_maximum_fusion.8), channel_id=1, source_target_pairs={{0,16},{4,20},{8,24},{12,28},{16,0},{20,4},{24,8},{28,12},{1,17},{... | collective-permute-start | bytes 776 | tf_op jit(solution)/shard_map/ppermute | solution.py:56
  15.5 8.1 %copy-start.19 = (s32[512]{0:T(512)}, s32[512]{0:T(512)S(1)}, u32[]{:S(2)}) copy-start(s32[512]{0:T(512)S(1)} %eq.84) | copy-start | bytes 6148
  15.5 8.1 %copy-start.25 = (bf16[512,1024]{1,0:T(8,128)(2,1)S(1)}, bf16[512,1024]{1,0:T(8,128)(2,1)}, u32[]{:S(2)}) copy-start(bf16[512,1024]{1,0:T(8,128)(2,1)} %param.11) | copy-start | bytes 3145732
  17.2 8.2 %copy-start.35 = (s32[16]{0:T(128)S(1)}, s32[16]{0:T(128)}, u32[]{:S(2)}) copy-start(s32[16]{0:T(128)} %param.12) | copy-start | bytes 196
  17.2 43.0 %all-to-all-start = ((bf16[8,64,1024]{2,1,0:T(8,128)(2,1)}), bf16[8,64,1024]{2,1,0:T(8,128)(2,1)}, u32[]{:S(2)}, u32[]{:S(2)}) async-start(bf16[8,64,1024]{2,1,0:T(8,128)(2,1)} %bitcast.1), calls=%async_computation | async-start | bytes 2097152 | tf_op jit(solution)/shard_map/all_to_all | solution.py:752
  23.5 152.2 %all-gather.2.cloned.1.call-start = ((), (), s32[]{:S(2)}) async-start(), calls=%async_computation.6 | async-start | bytes 5308416 | tf_op jit(solution)/shard_map/all_gather | solution.py:787
  23.6 8.7 %copy-start.23 = (f32[32]{0:T(128)S(1)}, f32[32]{0:T(128)}, u32[]{:S(2)}) copy-start(f32[32]{0:T(128)} %param.15) | copy-start | bytes 388
  23.7 8.7 %copy-start.24 = (f32[32]{0:T(128)S(1)}, f32[32]{0:T(128)}, u32[]{:S(2)}) copy-start(f32[32]{0:T(128)} %param.14) | copy-start | bytes 388
  23.7 23.9 %copy-start.12 = (bf16[3,128,256]{2,1,0:T(8,128)(2,1)S(1)}, bf16[3,128,256]{2,1,0:T(8,128)(2,1)}, u32[]{:S(2)}) copy-start(bf16[3,128,256]{2,1,0:T(8,128)(2,1)} %param.16) | copy-start | bytes 589828
  32.4 7.8 %collective-permute-start.1 = (f32[2,2,32]{2,1,0:T(2,128)S(1)}, f32[2,2,32]{2,1,0:T(2,128)S(1)}, u32[]{:S(2)}, u32[]{:S(2)}) collective-permute-start(f32[2,2,32]{2,1,0:T(2,128)S(1)} %pad_maximum_fusion.7), channel_id=1, source_target_pairs={{0,8},{4,12},{8,0},{12,4},{16,24},{20,28},{24,16},{28,20},{1,9},{5... | collective-permute-start | bytes 1544 | tf_op jit(solution)/shard_map/ppermute | solution.py:56
  40.2 3.7 collective-permute-start.2
  43.9 3.7 collective-permute-start.3
  45.4 102.3 %copy-start.21 = (s32[512]{0:T(512)}, s32[512]{0:T(512)S(1)}, u32[]{:S(2)}) copy-start(s32[512]{0:T(512)S(1)} %multiply_add_fusion) | copy-start | bytes 6148
  47.7 12.4 %collective-permute-start.9 = (bf16[2,4,128,256]{3,2,1,0:T(8,128)(2,1)S(1)}, bf16[2,4,128,256]{3,2,1,0:T(8,128)(2,1)S(1)}, u32[]{:S(2)}, u32[]{:S(2)}) collective-permute-start(bf16[2,4,128,256]{3,2,1,0:T(8,128)(2,1)S(1)} %pad_maximum_fusion.3), channel_id=1, source_target_pairs={{0,8},{4,12},{8,0},{12,4},{16,24},{20,28},{24,16},{28,20},{1,9},{5... | collective-permute-start | bytes 1572872 | tf_op jit(solution)/shard_map/ppermute | solution.py:56
  50.3 1.2 collective-permute-start.4
  51.6 49.9 %copy-start.18 = (f32[2,1024]{1,0:T(2,128)}, f32[2,1024]{1,0:T(2,128)S(1)}, u32[]{:S(2)}) copy-start(f32[2,1024]{1,0:T(2,128)S(1)} %reshape.193) | copy-start | bytes 24580
  62.2 39.4 %copy-start.4 = (bf16[512,1024]{1,0:T(8,128)(2,1)}, bf16[512,1024]{1,0:T(8,128)(2,1)S(1)}, u32[]{:S(2)}) copy-start(bf16[512,1024]{1,0:T(8,128)(2,1)S(1)} %convolution_convert_fusion.4.xa_ref.xk_ref.x_ref) | copy-start | bytes 3145732
  62.2 22.2 %collective-permute-start.6 = (bf16[512,1024]{1,0:T(8,128)(2,1)S(1)}, bf16[512,1024]{1,0:T(8,128)(2,1)S(1)}, u32[]{:S(2)}, u32[]{:S(2)}) collective-permute-start(bf16[512,1024]{1,0:T(8,128)(2,1)S(1)} %convolution_convert_fusion.4.xa_ref.xk_ref.x_ref), channel_id=1, source_target_pairs={{0,2},{1,3},{2,0},{3,1},{4,6},{5,7},{6,4},{7,5},{8,10},{9,11},{10,... | collective-permute-start | bytes 3145736 | tf_op jit(solution)/shard_map/ppermute | solution.py:56
  64.8 28.5 %collective-permute-start.10 = (bf16[2,2,4,128,256]{4,3,2,0,1:T(8,128)(2,1)}, bf16[2,2,4,128,256]{4,3,2,0,1:T(8,128)(2,1)}, u32[]{:S(2)}, u32[]{:S(2)}) collective-permute-start(bf16[2,2,4,128,256]{4,3,2,0,1:T(8,128)(2,1)} %pad_maximum_fusion.1), channel_id=1, source_target_pairs={{0,4},{4,0},{8,12},{12,8},{16,20},{20,16},{24,28},{28,24},{1,5},{5... | collective-permute-start | bytes 3145736 | tf_op jit(solution)/shard_map/ppermute | solution.py:56
  69.0 32.6 %collective-permute-start.5 = (bf16[512,1024]{1,0:T(8,128)(2,1)S(1)}, bf16[512,1024]{1,0:T(8,128)(2,1)}, u32[]{:S(2)}, u32[]{:S(2)}) collective-permute-start(bf16[512,1024]{1,0:T(8,128)(2,1)S(1)} %convolution_convert_fusion.4.xa_ref.xk_ref.x_ref), channel_id=1, source_target_pairs={{0,1},{1,0},{2,3},{3,2},{4,5},{5,4},{6,7},{7,6},{8,9},{9,8},{10,11... | collective-permute-start | bytes 3145736 | tf_op jit(solution)/shard_map/ppermute | solution.py:56
  84.5 25.1 %copy-start.6 = (bf16[512,1024]{1,0:T(8,128)(2,1)}, bf16[512,1024]{1,0:T(8,128)(2,1)S(1)}, u32[]{:S(2)}) copy-start(bf16[512,1024]{1,0:T(8,128)(2,1)S(1)} %collective-permute-done.6.xa_ref.xk_ref) | copy-start | bytes 3145732
  84.5 25.1 %collective-permute-start.7 = (bf16[512,1024]{1,0:T(8,128)(2,1)S(1)}, bf16[512,1024]{1,0:T(8,128)(2,1)}, u32[]{:S(2)}, u32[]{:S(2)}) collective-permute-start(bf16[512,1024]{1,0:T(8,128)(2,1)S(1)} %collective-permute-done.6.xa_ref.xk_ref), channel_id=1, source_target_pairs={{0,1},{1,0},{2,3},{3,2},{4,5},{5,4},{6,7},{7,6},{8,9},{9,8},{10,11... | collective-permute-start | bytes 3145736 | tf_op jit(solution)/shard_map/ppermute | solution.py:56
  96.4 21.1 %collective-permute-start.11 = (bf16[1024,256]{1,0:T(8,128)(2,1)S(1)}, bf16[1024,256]{1,0:T(8,128)(2,1)}, u32[]{:S(2)}, u32[]{:S(2)}) collective-permute-start(bf16[1024,256]{1,0:T(8,128)(2,1)S(1)} %bitcast.146), channel_id=1, source_target_pairs={{0,2},{1,3},{2,0},{3,1},{4,6},{5,7},{6,4},{7,5},{8,10},{9,11},{10,... | collective-permute-start | bytes 1572872 | tf_op jit(solution)/shard_map/ppermute | solution.py:56
  97.0 50.7 %all-to-all-start.1 = ((bf16[8,64,1024]{2,1,0:T(8,128)(2,1)}), bf16[8,64,1024]{2,1,0:T(8,128)(2,1)}, u32[]{:S(2)}, u32[]{:S(2)}) async-start(bf16[8,64,1024]{2,1,0:T(8,128)(2,1)} %bitcast.41), calls=%async_computation.1 | async-start | bytes 2097152 | tf_op jit(solution)/shard_map/all_to_all | solution.py:752
  101.6 8.0 %copy-start.9 = (f32[1,1024]{1,0:T(1,128)}, f32[1,1024]{1,0:T(1,128)S(1)}, u32[]{:S(2)}) copy-start(f32[1,1024]{1,0:T(1,128)S(1)} %get-tuple-element.240.gain_ref) | copy-start | bytes 12292
  136.0 32.3 %collective-permute-start.13 = (bf16[1024,256]{1,0:T(8,128)(2,1)S(1)}, bf16[1024,256]{1,0:T(8,128)(2,1)S(1)}, u32[]{:S(2)}, u32[]{:S(2)}) collective-permute-start(bf16[1024,256]{1,0:T(8,128)(2,1)S(1)} %get-tuple-element.129.o0.o_ref), channel_id=1, source_target_pairs={{0,2},{1,3},{2,0},{3,1},{4,6},{5,7},{6,4},{7,5},{8,10},{9,11},{10,... | collective-permute-start | bytes 1572872 | tf_op jit(solution)/shard_map/ppermute | solution.py:56
  149.7 18.6 %copy-start.26 = (bf16[512,1024]{1,0:T(8,128)(2,1)}, bf16[512,1024]{1,0:T(8,128)(2,1)S(1)}, u32[]{:S(2)}) copy-start(bf16[512,1024]{1,0:T(8,128)(2,1)S(1)} %convolution_convert_fusion.3.gk_ref.g_ref) | copy-start | bytes 3145732
  149.7 18.6 %collective-permute-start.14 = (bf16[512,1024]{1,0:T(8,128)(2,1)S(1)}, bf16[512,1024]{1,0:T(8,128)(2,1)}, u32[]{:S(2)}, u32[]{:S(2)}) collective-permute-start(bf16[512,1024]{1,0:T(8,128)(2,1)S(1)} %convolution_convert_fusion.3.gk_ref.g_ref), channel_id=1, source_target_pairs={{0,2},{1,3},{2,0},{3,1},{4,6},{5,7},{6,4},{7,5},{8,10},{9,11},{10,... | collective-permute-start | bytes 3145736 | tf_op jit(solution)/shard_map/ppermute | solution.py:56
  168.3 7.4 %collective-permute-start.15 = (bf16[512,1024]{1,0:T(8,128)(2,1)}, bf16[512,1024]{1,0:T(8,128)(2,1)}, u32[]{:S(2)}, u32[]{:S(2)}) collective-permute-start(bf16[512,1024]{1,0:T(8,128)(2,1)} %collective-permute-done.14.gk_ref), channel_id=1, source_target_pairs={{0,1},{1,0},{2,3},{3,2},{4,5},{5,4},{6,7},{7,6},{8,9},{9,8},{10,11... | collective-permute-start | bytes 3145736 | tf_op jit(solution)/shard_map/ppermute | solution.py:56
  169.5 2.4 collective-permute-start.18
  170.0 3.6 collective-permute-start.19
  170.1 5.5 %collective-permute-start.16 = (bf16[1024,256]{1,0:T(8,128)(2,1)S(1)}, bf16[1024,256]{1,0:T(8,128)(2,1)}, u32[]{:S(2)}, u32[]{:S(2)}) collective-permute-start(bf16[1024,256]{1,0:T(8,128)(2,1)S(1)} %get-tuple-element.120.o0.o_ref.o1), channel_id=1, source_target_pairs={{0,1},{1,0},{2,3},{3,2},{4,5},{5,4},{6,7},{7,6},{8,9},{9,8},{10,11... | collective-permute-start | bytes 1572872 | tf_op jit(solution)/shard_map/ppermute | solution.py:56
  170.6 5.1 %collective-permute-start.17 = (bf16[1024,256]{1,0:T(8,128)(2,1)S(1)}, bf16[1024,256]{1,0:T(8,128)(2,1)}, u32[]{:S(2)}, u32[]{:S(2)}) collective-permute-start(bf16[1024,256]{1,0:T(8,128)(2,1)S(1)} %collective-permute-done.13.o2), channel_id=1, source_target_pairs={{0,1},{1,0},{2,3},{3,2},{4,5},{5,4},{6,7},{7,6},{8,9},{9,8},{10,11... | collective-permute-start | bytes 1572872 | tf_op jit(solution)/shard_map/ppermute | solution.py:56
  171.9 28.1 %collective-permute-start.21 = (f32[4]{0:T(128)S(1)}, f32[4]{0:T(128)S(1)}, u32[]{:S(2)}, u32[]{:S(2)}) collective-permute-start(f32[4]{0:T(128)S(1)} %maximum_multiply_fusion), channel_id=1, source_target_pairs={{0,4},{4,0},{8,12},{12,8},{16,20},{20,16},{24,28},{28,24},{1,5},{5... | collective-permute-start | bytes 56 | tf_op jit(solution)/shard_map/ppermute | solution.py:56
  173.6 26.4 %collective-permute-start.20 = (bf16[1024,256]{1,0:T(8,128)(2,1)S(1)}, bf16[1024,256]{1,0:T(8,128)(2,1)S(1)}, u32[]{:S(2)}, u32[]{:S(2)}) collective-permute-start(bf16[1024,256]{1,0:T(8,128)(2,1)S(1)} %get-tuple-element.120.o0.o_ref.o1), channel_id=1, source_target_pairs={{0,2},{1,3},{2,0},{3,1},{4,6},{5,7},{6,4},{7,5},{8,10},{9,11},{10,... | collective-permute-start | bytes 1572872 | tf_op jit(solution)/shard_map/ppermute | solution.py:56
  175.7 24.4 %copy-start.27 = (bf16[512,1024]{1,0:T(8,128)(2,1)S(1)}, bf16[512,1024]{1,0:T(8,128)(2,1)}, u32[]{:S(2)}) copy-start(bf16[512,1024]{1,0:T(8,128)(2,1)} %copy-done.26) | copy-start | bytes 3145732
  200.0 3.6 collective-permute-start.22
  200.1 5.5 %collective-permute-start.12 = (bf16[512,1024]{1,0:T(8,128)(2,1)S(1)}, bf16[512,1024]{1,0:T(8,128)(2,1)S(1)}, u32[]{:S(2)}, u32[]{:S(2)}) collective-permute-start(bf16[512,1024]{1,0:T(8,128)(2,1)S(1)} %copy-done.27), channel_id=1, source_target_pairs={{0,1},{1,0},{2,3},{3,2},{4,5},{5,4},{6,7},{7,6},{8,9},{9,8},{10,11... | collective-permute-start | bytes 3145736 | tf_op jit(solution)/shard_map/ppermute | solution.py:56
  200.6 5.0 %collective-permute-start.23 = (bf16[1024,256]{1,0:T(8,128)(2,1)S(1)}, bf16[1024,256]{1,0:T(8,128)(2,1)S(1)}, u32[]{:S(2)}, u32[]{:S(2)}) collective-permute-start(bf16[1024,256]{1,0:T(8,128)(2,1)S(1)} %get-tuple-element.129.o0.o_ref), channel_id=1, source_target_pairs={{0,1},{1,0},{2,3},{3,2},{4,5},{5,4},{6,7},{7,6},{8,9},{9,8},{10,11... | collective-permute-start | bytes 1572872 | tf_op jit(solution)/shard_map/ppermute | solution.py:56
  200.7 5.1 %collective-permute-start.24 = (bf16[1024,256]{1,0:T(8,128)(2,1)S(1)}, bf16[1024,256]{1,0:T(8,128)(2,1)S(1)}, u32[]{:S(2)}, u32[]{:S(2)}) collective-permute-start(bf16[1024,256]{1,0:T(8,128)(2,1)S(1)} %collective-permute-done.20.o2), channel_id=1, source_target_pairs={{0,1},{1,0},{2,3},{3,2},{4,5},{5,4},{6,7},{7,6},{8,9},{9,8},{10,11... | collective-permute-start | bytes 1572872 | tf_op jit(solution)/shard_map/ppermute | solution.py:56
  201.1 29.3 %collective-permute-start.26 = (f32[4]{0:T(128)S(1)}, f32[4]{0:T(128)S(1)}, u32[]{:S(2)}, u32[]{:S(2)}) collective-permute-start(f32[4]{0:T(128)S(1)} %max.15), channel_id=1, source_target_pairs={{0,8},{4,12},{8,0},{12,4},{16,24},{20,28},{24,16},{28,20},{1,9},{5... | collective-permute-start | bytes 56 | tf_op jit(solution)/shard_map/ppermute | solution.py:56
  205.5 25.3 %collective-permute-start.25 = (bf16[512,1024]{1,0:T(8,128)(2,1)S(1)}, bf16[512,1024]{1,0:T(8,128)(2,1)S(1)}, u32[]{:S(2)}, u32[]{:S(2)}) collective-permute-start(bf16[512,1024]{1,0:T(8,128)(2,1)S(1)} %add_convert_fusion.2), channel_id=1, source_target_pairs={{0,2},{1,3},{2,0},{3,1},{4,6},{5,7},{6,4},{7,5},{8,10},{9,11},{10,... | collective-permute-start | bytes 3145736 | tf_op jit(solution)/shard_map/ppermute | solution.py:56
  230.8 2.9 collective-permute-start.27
  230.8 29.3 %collective-permute-start.28 = (f32[4]{0:T(128)S(1)}, f32[4]{0:T(128)S(1)}, u32[]{:S(2)}, u32[]{:S(2)}) collective-permute-start(f32[4]{0:T(128)S(1)} %max.16), channel_id=1, source_target_pairs={{0,16},{4,20},{8,24},{12,28},{16,0},{20,4},{24,8},{28,12},{1,17},{... | collective-permute-start | bytes 56 | tf_op jit(solution)/shard_map/ppermute | solution.py:56
  239.6 20.5 %copy-start.11 = (bf16[512,1024]{1,0:T(8,128)(2,1)}, bf16[512,1024]{1,0:T(8,128)(2,1)S(1)}, u32[]{:S(2)}) copy-start(bf16[512,1024]{1,0:T(8,128)(2,1)S(1)} %get-tuple-element.147.even_ref) | copy-start | bytes 3145732
  239.6 25.4 %collective-permute-start.30 = (bf16[512,1024]{1,0:T(8,128)(2,1)S(1)}, bf16[512,1024]{1,0:T(8,128)(2,1)}, u32[]{:S(2)}, u32[]{:S(2)}) collective-permute-start(bf16[512,1024]{1,0:T(8,128)(2,1)S(1)} %get-tuple-element.147.even_ref), channel_id=1, source_target_pairs={{0,1},{1,0},{2,3},{3,2},{4,5},{5,4},{6,7},{7,6},{8,9},{9,8},{10,11... | collective-permute-start | bytes 3145736 | tf_op jit(solution)/shard_map/ppermute | solution.py:56
  239.7 30.9 %collective-permute-start.29 = (bf16[512,1024]{1,0:T(8,128)(2,1)S(1)}, bf16[512,1024]{1,0:T(8,128)(2,1)}, u32[]{:S(2)}, u32[]{:S(2)}) collective-permute-start(bf16[512,1024]{1,0:T(8,128)(2,1)S(1)} %get-tuple-element.147.even_ref), channel_id=1, source_target_pairs={{0,2},{1,3},{2,0},{3,1},{4,6},{5,7},{6,4},{7,5},{8,10},{9,11},{10,... | collective-permute-start | bytes 3145736 | tf_op jit(solution)/shard_map/ppermute | solution.py:56
  260.1 95.8 %all-to-all-start.2 = ((bf16[8,3,656,128]{3,2,1,0:T(8,128)(2,1)}), bf16[8,3,656,128]{3,2,1,0:T(8,128)(2,1)}, u32[]{:S(2)}, u32[]{:S(2)}) async-start(bf16[8,3,656,128]{3,2,1,0:T(8,128)(2,1)} %inner_grads.1), calls=%async_computation.2 | async-start | bytes 8060928 | tf_op jit(solution)/shard_map/all_to_all | solution.py:871
  264.8 182.4 %reduce-scatter.2.cloned.1.call-start = ((), (), s32[]{:S(2)}) async-start(), calls=%async_computation.7 | async-start | bytes 2359296 | tf_op jit(solution)/shard_map/reduce_scatter | solution.py:915
  264.9 6.3 %collective-permute-start.33 = (bf16[512,1024]{1,0:T(8,128)(2,1)}, bf16[512,1024]{1,0:T(8,128)(2,1)S(1)}, u32[]{:S(2)}, u32[]{:S(2)}) collective-permute-start(bf16[512,1024]{1,0:T(8,128)(2,1)} %get-tuple-element.164), channel_id=1, source_target_pairs={{0,1},{1,0},{2,3},{3,2},{4,5},{5,4},{6,7},{7,6},{8,9},{9,8},{10,11... | collective-permute-start | bytes 3145736 | tf_op jit(solution)/shard_map/ppermute | solution.py:56
  270.7 3.5 collective-permute-start.31
  271.2 4.5 collective-permute-start.32
  275.6 71.9 %collective-permute-start.34 = (bf16[512,1024]{1,0:T(8,128)(2,1)}, bf16[512,1024]{1,0:T(8,128)(2,1)S(1)}, u32[]{:S(2)}, u32[]{:S(2)}) collective-permute-start(bf16[512,1024]{1,0:T(8,128)(2,1)} %add_convert_fusion.1), channel_id=1, source_target_pairs={{0,2},{1,3},{2,0},{3,1},{4,6},{5,7},{6,4},{7,5},{8,10},{9,11},{10,... | collective-permute-start | bytes 3145736 | tf_op jit(solution)/shard_map/ppermute | solution.py:56
  350.7 3.5 collective-permute-start.35
  360.0 44.3 %all-to-all-start.3 = ((bf16[8,64,1024]{2,1,0:T(8,128)(2,1)}), bf16[8,64,1024]{2,1,0:T(8,128)(2,1)S(1)}, u32[]{:S(2)}, u32[]{:S(2)}) async-start(bf16[8,64,1024]{2,1,0:T(8,128)(2,1)} %bitcast.141), calls=%async_computation.3 | async-start | bytes 2097152 | tf_op jit(solution)/shard_map/all_to_all | solution.py:752
  365.4 25.3 %collective-permute-start.36 = (bf16[512,1024]{1,0:T(8,128)(2,1)S(1)}, bf16[512,1024]{1,0:T(8,128)(2,1)S(1)}, u32[]{:S(2)}, u32[]{:S(2)}) collective-permute-start(bf16[512,1024]{1,0:T(8,128)(2,1)S(1)} %add_convert_fusion), channel_id=1, source_target_pairs={{0,2},{1,3},{2,0},{3,1},{4,6},{5,7},{6,4},{7,5},{8,10},{9,11},{10,... | collective-permute-start | bytes 3145736 | tf_op jit(solution)/shard_map/ppermute | solution.py:56
  370.4 21.2 %collective-permute-start.37 = (bf16[512,1024]{1,0:T(8,128)(2,1)S(1)}, bf16[512,1024]{1,0:T(8,128)(2,1)}, u32[]{:S(2)}, u32[]{:S(2)}) collective-permute-start(bf16[512,1024]{1,0:T(8,128)(2,1)S(1)} %dn.7), channel_id=1, source_target_pairs={{0,1},{1,0},{2,3},{3,2},{4,5},{5,4},{6,7},{7,6},{8,9},{9,8},{10,11... | collective-permute-start | bytes 3145736 | tf_op jit(solution)/shard_map/ppermute | solution.py:56
  377.1 27.3 %copy-start.10 = (f32[1,1024]{1,0:T(1,128)S(1)}, f32[1,1024]{1,0:T(1,128)}, u32[]{:S(2)}) copy-start(f32[1,1024]{1,0:T(1,128)} %copy-done.9) | copy-start | bytes 12292
  409.9 38.2 %all-to-all-start.4 = ((bf16[8,64,1024]{2,1,0:T(8,128)(2,1)}), bf16[8,64,1024]{2,1,0:T(8,128)(2,1)S(1)}, u32[]{:S(2)}, u32[]{:S(2)}) async-start(bf16[8,64,1024]{2,1,0:T(8,128)(2,1)} %bitcast.142), calls=%async_computation.4 | async-start | bytes 2097152 | tf_op jit(solution)/shard_map/all_to_all | solution.py:752
  449.4 5.3 %collective-permute-start.38 = (f32[2,32]{1,0:T(2,128)S(1)}, f32[2,32]{1,0:T(2,128)S(1)}, u32[]{:S(2)}, u32[]{:S(2)}) collective-permute-start(f32[2,32]{1,0:T(2,128)S(1)} %bitcast.165), channel_id=1, source_target_pairs={{0,1},{1,0},{2,3},{3,2},{4,5},{5,4},{6,7},{7,6},{8,9},{9,8},{10,11... | collective-permute-start | bytes 776 | tf_op jit(solution)/shard_map/ppermute | solution.py:56
  449.5 5.2 %collective-permute-start.39 = (f32[2,32]{1,0:T(2,128)S(1)}, f32[2,32]{1,0:T(2,128)S(1)}, u32[]{:S(2)}, u32[]{:S(2)}) collective-permute-start(f32[2,32]{1,0:T(2,128)S(1)} %bitcast.164), channel_id=1, source_target_pairs={{0,2},{1,3},{2,0},{3,1},{4,6},{5,7},{6,4},{7,5},{8,10},{9,11},{10,... | collective-permute-start | bytes 776 | tf_op jit(solution)/shard_map/ppermute | solution.py:56
  451.1 3.6 collective-permute-start.40
  (20 other events, 68.6 us)
Sparse Core Ops, SparseCore 0:
  70.9 91.6 all-gather.1
  354.3 92.8 reduce-scatter.1
